TPU v7x, 128 devices: a whole 4x4x4 slice. The times are simulated.
128 devices in a mesh: dp: 8 (over z, core), mp: 16 (over x, y).
Axes of the slice: x: 4, y: 4, z: 4, core: 2. Of those that a mesh axis runs over, the one named last changes fastest.
Arguments:
- activations: bfloat16 [16384, 5120], P(('dp', 'mp')), may hold values from -10 to 10
- cotangent: bfloat16 [16384, 5120], P('dp', 'mp'), may hold values from -1 to 1
- master_weights: float32 [5120, 5120], P('dp', 'mp'), may hold values from -32 to 32
- first_moment: float32 [5120, 5120], P('dp', 'mp'), may hold values from -1 to 1
- second_moment: float32 [5120, 5120], P('dp', 'mp'), may hold values from 0.25 to 4
- step_count: int32 [1], replicated, may hold values from 1 to 23
- language_ids: int32 [1], replicated, may hold values from 0 to 7
- language_rates: float32 [8], replicated, may hold values from 0.25 to 2
Outputs:
- new_master: float32 [5120, 5120], P('dp', 'mp')
- new_first: float32 [5120, 5120], P('dp', 'mp')
- new_second: float32 [5120, 5120], P('dp', 'mp')
- new_weights: bfloat16 [5120, 5120], P(None, 'mp')
All inputs are finite; a program needn't handle non-finite values.
Results may differ from a plain program's by a relative error of at most 0.0004.
Values may be sent and summed in bfloat16 or wider, within the bound.
No kernel may reach another device: no remote copies, remote signals or barrier semaphores. Data moves between devices by JAX's collectives and lax.ppermute only.
A program may use at most 128 MiB of HBM per device.

v0:
```python
import jax
import jax.numpy as jnp
from jax import lax
from jax.sharding import PartitionSpec as P

beta_one = 0.9
beta_two = 0.999
epsilon = 1e-06
decay_weight = 0.1
base_rate = 0.25


def on_device(
    activations,
    cotangent,
    master_weights,
    first_moment,
    second_moment,
    step_count,
    language_ids,
    language_rates,
):
    gathered = lax.all_gather(activations, "mp", axis=0, tiled=True)
    gradient = lax.psum_scatter(
        lax.dot_general(
            gathered, cotangent, (((0,), (0,)), ((), ())), preferred_element_type=jnp.float32
        ),
        "dp",
        scatter_dimension=0,
        tiled=True,
    )
    steps_done = step_count[0].astype(jnp.float32)
    corr_one = 1.0 - jnp.power(jnp.float32(beta_one), steps_done)
    corr_two = 1.0 - jnp.power(jnp.float32(beta_two), steps_done)
    new_first = beta_one * first_moment + (1.0 - beta_one) * gradient
    new_second = beta_two * second_moment + (1.0 - beta_two) * gradient * gradient
    update = (
        new_first / corr_one / (jnp.sqrt(new_second / corr_two) + epsilon)
        + decay_weight * master_weights
    )
    weight_sq, update_sq = lax.psum(
        (jnp.sum(master_weights * master_weights), jnp.sum(update * update)), ("dp", "mp")
    )
    trust = jnp.sqrt(weight_sq) / jnp.sqrt(update_sq)
    picked = jnp.arange(language_rates.shape[0], dtype=jnp.int32) == language_ids[0]
    rate = base_rate * jnp.sum(jnp.where(picked, language_rates, jnp.float32(0.0)))
    new_master = master_weights - rate * trust * update
    new_weights = lax.all_gather(new_master.astype(jnp.bfloat16), "dp", axis=0, tiled=True)
    return (new_master, new_first, new_second, new_weights)


def solution(mesh):
    return jax.shard_map(
        on_device,
        mesh=mesh,
        in_specs=(
            P(("dp", "mp"), None),
            P("dp", "mp"),
            P("dp", "mp"),
            P("dp", "mp"),
            P("dp", "mp"),
            P(),
            P(),
            P(),
        ),
        out_specs=(P("dp", "mp"), P("dp", "mp"), P("dp", "mp"), P(None, "mp")),
        check_vma=False,
    )
```

profile of v0, /device:TPU:1, one launch (start us, length us, event | category | flops | bytes accessed | tf_op | source)
XLA Modules:
  0.0 311.8 jit_solution(5477487466860797035)
XLA Ops:
  7.2 0.0 copy-start
  7.2 0.0 all-gather.3.cloned.1.call-start
  7.2 0.7 all-gather.3.cloned.1.call-update
  7.9 0.0 reduce-scatter.2.cloned.1.call-start
  8.0 138.1 %all-gather.3.cloned.1.call-done = bf16[2048,5120]{1,0:T(8,128)(2,1)} async-done(((bf16[128,5120]{1,0:T(8,128)(2,1)}), bf16[2048,5120]{1,0:T(8,128)(2,1)}) %all-gather.3.cloned.1.call-update) | async-done | bytes 20971536 | tf_op jit(solution)/shard_map/all_gather | solution.py:23
  146.0 0.0 copy-done
  146.0 13.9 %fusion.4 = f32[5120,320]{0,1:T(8,128)} fusion(bf16[2048,320]{0,1:T(8,128)(2,1)S(1)} %copy-done, bf16[2048,5120]{1,0:T(8,128)(2,1)} %all-gather.3.cloned.1.call-done), kind=kOutput, calls=%fused_computation.10 | convolution fusion | flops 6710886400 | bytes 28835840 | tf_op jit(solution)/shard_map/dot_general | solution.py:25
  159.9 0.0 copy-start.2
  159.9 0.0 copy-start.1
  159.9 0.0 reduce-scatter.2.cloned.1.call-update
  160.0 0.0 all-gather.5.cloned.1.call-start
  161.5 0.0 copy-done.2
  161.5 0.6 fusion.1
  162.7 40.4 %reduce-scatter.2.cloned.1.call-done = f32[640,320]{0,1:T(8,128)} async-done(((f32[5120,320]{0,1:T(8,128)}), f32[640,320]{0,1:T(8,128)}) %reduce-scatter.2.cloned.1.call-update) | async-done | bytes 819216 | tf_op jit(solution)/shard_map/reduce_scatter | solution.py:24
  203.1 0.0 copy-done.1
  203.1 4.1 %multiply_reduce_fusion = (f32[]{:T(128)}, f32[640,320]{0,1:T(8,128)S(1)}, f32[640,320]{0,1:T(8,128)}, f32[640,320]{0,1:T(8,128)}, f32[]{:T(128)}) fusion(f32[640,320]{0,1:T(8,128)S(1)} %copy-done.1, f32[]{:T(128)} %bitcast.2, f32[]{:T(128)} %bitcast.1, f32[640,320]{0,1:T(8,128)} %reduce-scatter.2.cloned.1.call-done, f32[640,320]{0,1:T(8,128)} %param.12, ...), kind=kLoop, calls=%fused_computation.3 | loop fusion | flops 3481598 | bytes 5734416 | tf_op jit(solution)/shard_map/reduce_sum | solution.py:42
  207.2 66.1 %all-reduce = (f32[]{:T(128)}, f32[]{:T(128)}) all-reduce(f32[]{:T(128)} %get-tuple-element.12, f32[]{:T(128)} %get-tuple-element.8), channel_id=1, replica_groups=mesh['dp'=8,'mp'=16] {'dp','mp'}, use_global_device_ids=true, to_apply=%region_2.0 | all-reduce | flops 2 | bytes 16 | tf_op jit(solution)/shard_map/psum | solution.py:41
  274.7 1.1 fusion.2
  275.8 0.0 all-gather.5.cloned.1.call-update
  275.8 25.6 %all-gather.5.cloned.1.call-done = bf16[5120,320]{0,1:T(8,128)(2,1)} async-done(((bf16[640,320]{0,1:T(8,128)(2,1)}), bf16[5120,320]{0,1:T(8,128)(2,1)}) %all-gather.5.cloned.1.call-update) | async-done | bytes 3276816 | tf_op jit(solution)/shard_map/all_gather | solution.py:48
  301.4 3.8 %copy.15 = bf16[5120,320]{0,1:T(8,128)(2,1)} copy(bf16[5120,320]{0,1:T(8,128)(2,1)} %all-gather.5.cloned.1.call-done) | data formatting | bytes 6553600
Async XLA Ops:
  7.2 138.9 %copy-start = (bf16[2048,320]{0,1:T(8,128)(2,1)S(1)}, bf16[2048,320]{0,1:T(8,128)(2,1)}, u32[]{:S(2)}) copy-start(bf16[2048,320]{0,1:T(8,128)(2,1)} %param.9) | copy-start | bytes 3932164
  7.2 138.9 %all-gather.3.cloned.1.call-start = ((), (), s32[]{:S(2)}) async-start(), calls=%async_computation.1 | async-start | bytes 22282240 | tf_op jit(solution)/shard_map/all_gather | solution.py:23
  7.9 195.2 %reduce-scatter.2.cloned.1.call-start = ((), (), s32[]{:S(2)}) async-start(), calls=%async_computation.2 | async-start | bytes 7372800 | tf_op jit(solution)/shard_map/reduce_scatter | solution.py:24
  159.9 1.5 copy-start.2
  159.9 43.2 %copy-start.1 = (f32[640,320]{0,1:T(8,128)S(1)}, f32[640,320]{0,1:T(8,128)}, u32[]{:S(2)}) copy-start(f32[640,320]{0,1:T(8,128)} %param.10) | copy-start | bytes 2457604
  160.0 141.4 %all-gather.5.cloned.1.call-start = ((), (), s32[]{:S(2)}) async-start(), calls=%async_computation.3 | async-start | bytes 3686400 | tf_op jit(solution)/shard_map/all_gather | solution.py:48
Sparse Core Ops, SparseCore 0:
  10.2 135.8 all-gather.2
  160.1 42.9 reduce-scatter.1
  276.0 25.3 all-gather.4
where the time goes:
time: 312 us
  waiting for transfers between devices  205 us (66%)
  blocking collectives  66.1 us (21%)
  between operations  17.2 us (6%)
  matrix products  13.9 us (4%)
  other arithmetic  5.83 us (2%)
  local copies, waits for them, and re-layouts  3.86 us (1%)
    all_gather x1, waiting for transfers between devices, on_device(): gathered = lax.all_gather(activations, 'mp', axis=0, tiled=True)  138 us
    psum x1, blocking collectives, on_device(): lax.psum((jnp.sum(master_weights * master_weights), jnp.sum(update * upda...  66.1 us
    reduce_scatter x1, waiting for transfers between devices, on_device(): lax.psum_scatter(lax.dot_general(gathered, cotangent, (((0,), (0,)), ((),...  40.4 us
    all_gather x1, waiting for transfers between devices, on_device(): lax.all_gather(new_master.astype(jnp.bfloat16), 'dp', axis=0, tiled=True)  25.6 us
    dot_general x1, matrix products, on_device(): lax.dot_general(gathered, cotangent, (((0,), (0,)), ((), ())), preferred_...  13.9 us
  transfers between devices with their start and end apart: 3, of which 3 were waited for; matrix products, arithmetic and copies ran while one was open for 0% of the time, Pallas kernels for 0%

commit v1 on v0

--- a/solution.py
+++ b/solution.py
@@ -1,6 +1,8 @@
 import jax
 import jax.numpy as jnp
 from jax import lax
+from jax.experimental import pallas as pl
+from jax.experimental.pallas import tpu as pltpu
 from jax.sharding import PartitionSpec as P
 
 beta_one = 0.9
@@ -8,6 +10,141 @@
 epsilon = 1e-06
 decay_weight = 0.1
 base_rate = 0.25
+
+ROWS = 640
+COLS = 320
+BLOCK = 128
+GROUP = 2 * ROWS
+
+
+def moved(array, dz=0, dc=0, dx=0, dy=0):
+    pairs = []
+    for z in range(4):
+        for c in range(2):
+            for x in range(4):
+                for y in range(4):
+                    src = (2 * z + c) * 16 + 4 * x + y
+                    dst = (2 * ((z + dz) % 4) + (c + dc) % 2) * 16 + 4 * ((x + dx) % 4) + (y + dy) % 4
+                    pairs.append((src, dst))
+    return lax.ppermute(array, ("dp", "mp"), pairs)
+
+
+def place():
+    d = lax.axis_index("dp")
+    m = lax.axis_index("mp")
+    return d // 2, d % 2, m // 4, m % 4
+
+
+def prepare_kernel(act, cot, a0, a1, a2, a3, c0, c1, c2, c3):
+    z, c, x, y = place()
+    for kz, out in enumerate((a0, a1, a2, a3)):
+        first = lax.rem(z + kz, 4) * GROUP
+        mine = pl.multiple_of(first + c * ROWS, 128)
+        other = pl.multiple_of(first + (1 - c) * ROWS, 128)
+        out[:, :ROWS] = act[:, pl.ds(mine, ROWS)]
+        out[:, ROWS:] = act[:, pl.ds(other, ROWS)]
+    for ky, out in enumerate((c0, c1, c2, c3)):
+        for dx in range(4):
+            start = (4 * lax.rem(x + dx, 4) + lax.rem(y + ky, 4)) * BLOCK
+            out[:, dx * BLOCK : (dx + 1) * BLOCK] = cot[:, pl.ds(pl.multiple_of(start, 128), BLOCK)]
+
+
+def prepare(activations, cotangent_t):
+    bf16 = jnp.bfloat16
+    return pl.pallas_call(
+        prepare_kernel,
+        out_shape=[jax.ShapeDtypeStruct((BLOCK, GROUP), bf16)] * 4
+        + [jax.ShapeDtypeStruct((COLS, 4 * BLOCK), bf16)] * 4,
+        compiler_params=pltpu.CompilerParams(vmem_limit_bytes=32 * 2**20),
+        name="prepare",
+    )(activations, cotangent_t)
+
+
+def product_kernel(*refs):
+    x0, xp, xm, xd0, xd1, z0, zp, zm, zd0, zd1 = refs[:10]
+    outs = refs[10:18]
+    a_all, c_all, stage, in_sems, out_sems = refs[18:]
+    copies = []
+    for kz in range(4):
+        for dx, block in ((0, x0), (1, xp), (2, None), (3, xm)):
+            if block is None:
+                src = (xd0 if kz < 2 else xd1).at[pl.ds((kz % 2) * BLOCK, BLOCK)]
+            else:
+                src = block.at[pl.ds(kz * BLOCK, BLOCK)]
+            copies.append((src, a_all.at[pl.ds((4 * kz + dx) * BLOCK, BLOCK)]))
+    width = 4 * BLOCK
+    for kz, block in ((0, z0), (1, zm), (3, zp)):
+        copies.append((block, c_all.at[:, pl.ds(kz * width, width)]))
+    copies.append((zd0, c_all.at[pl.ds(0, 2 * COLS), pl.ds(2 * width, width)]))
+    copies.append((zd1, c_all.at[pl.ds(2 * COLS, 2 * COLS), pl.ds(2 * width, width)]))
+    started = []
+    for k, (src, dst) in enumerate(copies):
+        copy = pltpu.make_async_copy(src, dst, in_sems.at[k])
+        copy.start()
+        started.append(copy)
+    for copy in started:
+        copy.wait()
+    writes = []
+    for step, ky in enumerate((2, 1, 3, 0)):
+        total = jnp.dot(
+            c_all[ky * COLS : (ky + 1) * COLS, :], a_all[...], preferred_element_type=jnp.float32
+        )
+        for half in (1, 0):
+            stage[2 * step + half] = total[:, half * ROWS : (half + 1) * ROWS]
+            write = pltpu.make_async_copy(
+                stage.at[2 * step + half], outs[2 * ky + half], out_sems.at[2 * step + half]
+            )
+            write.start()
+            writes.append(write)
+    for write in writes:
+        write.wait()
+
+
+def product(pieces):
+    any_space = pl.BlockSpec(memory_space=pl.ANY)
+    return pl.pallas_call(
+        product_kernel,
+        out_shape=[jax.ShapeDtypeStruct((COLS, ROWS), jnp.float32)] * 8,
+        in_specs=[any_space] * 10,
+        out_specs=[any_space] * 8,
+        scratch_shapes=[
+            pltpu.VMEM((16 * BLOCK, GROUP), jnp.bfloat16),
+            pltpu.VMEM((4 * COLS, 16 * BLOCK), jnp.bfloat16),
+            pltpu.VMEM((8, COLS, ROWS), jnp.float32),
+            pltpu.SemaphoreType.DMA((21,)),
+            pltpu.SemaphoreType.DMA((8,)),
+        ],
+        compiler_params=pltpu.CompilerParams(vmem_limit_bytes=40 * 2**20),
+        name="product",
+    )(*pieces)
+
+
+def ring_gather(block, axis):
+    half = block.shape[0] // 2
+    plus = moved(block, **{axis: -1})
+    minus = moved(block, **{axis: 1})
+    far_first = moved(plus[:half], **{axis: -1})
+    far_second = moved(minus[half:], **{axis: 1})
+    return [block, plus, minus, far_first, far_second]
+
+
+def gradient_t(activations, cotangent):
+    parts = prepare(activations, cotangent.T)
+    acts, cots = parts[:4], parts[4:]
+    a_block = jnp.concatenate([acts[0]] + [moved(acts[k], dz=k) for k in (1, 2, 3)], axis=0)
+    c_block = jnp.concatenate([cots[0]] + [moved(cots[k], dy=k) for k in (1, 2, 3)], axis=0)
+    outs = product(ring_gather(a_block, "dx") + ring_gather(c_block, "dz"))
+    sums = {}
+    for ky in (2, 1, 3, 0):
+        sums[ky] = outs[2 * ky] + moved(outs[2 * ky + 1], dc=1)
+    return sums[0] + moved(sums[1], dy=-1) + moved(sums[2], dy=-2) + moved(sums[3], dy=-3)
+
+
+def total_over_devices(values):
+    values = values + moved(values, dc=1)
+    for axis in ("dx", "dy", "dz"):
+        values = values + moved(values, **{axis: 1}) + moved(values, **{axis: 2}) + moved(values, **{axis: 3})
+    return values
 
 
 def on_device(
@@ -20,15 +157,7 @@
     language_ids,
     language_rates,
 ):
-    gathered = lax.all_gather(activations, "mp", axis=0, tiled=True)
-    gradient = lax.psum_scatter(
-        lax.dot_general(
-            gathered, cotangent, (((0,), (0,)), ((), ())), preferred_element_type=jnp.float32
-        ),
-        "dp",
-        scatter_dimension=0,
-        tiled=True,
-    )
+    gradient = gradient_t(activations, cotangent).T
     steps_done = step_count[0].astype(jnp.float32)
     corr_one = 1.0 - jnp.power(jnp.float32(beta_one), steps_done)
     corr_two = 1.0 - jnp.power(jnp.float32(beta_two), steps_done)
@@ -38,10 +167,10 @@
         new_first / corr_one / (jnp.sqrt(new_second / corr_two) + epsilon)
         + decay_weight * master_weights
     )
-    weight_sq, update_sq = lax.psum(
-        (jnp.sum(master_weights * master_weights), jnp.sum(update * update)), ("dp", "mp")
+    sums = total_over_devices(
+        jnp.stack([jnp.sum(master_weights * master_weights), jnp.sum(update * update)])
     )
-    trust = jnp.sqrt(weight_sq) / jnp.sqrt(update_sq)
+    trust = jnp.sqrt(sums[0]) / jnp.sqrt(sums[1])
     picked = jnp.arange(language_rates.shape[0], dtype=jnp.int32) == language_ids[0]
     rate = base_rate * jnp.sum(jnp.where(picked, language_rates, jnp.float32(0.0)))
     new_master = master_weights - rate * trust * update

time: 312 us -> 217 us (0.70)
  waiting for transfers between devices: 205 us -> 120 us
  blocking collectives: 66.1 us -> 0 us
  starting transfers between devices: 0.12 us -> 45.6 us
  Pallas kernels: 0 us -> 14.2 us
  matrix products: 13.9 us -> 0 us
  other arithmetic: 5.83 us -> 12.2 us
  local copies, waits for them, and re-layouts: 3.86 us -> 7.43 us
    all_gather x1 -> x0, waiting for transfers between devices: 138 us -> none  [on_device(): gathered = lax.all_gather(activations, 'mp', axis=0, tiled=True)]
    ppermute x0 -> x31, waiting for transfers between devices: none -> 86.5 us  [moved(): return lax.ppermute(array, ('dp', 'mp'), pairs)]
    psum x1 -> x0, blocking collectives: 66.1 us -> none  [on_device(): lax.psum((jnp.sum(master_weights * master_weights), jnp.sum(update * upda...]
    ppermute x0 -> x31, starting transfers between devices: none -> 45.5 us  [moved(): return lax.ppermute(array, ('dp', 'mp'), pairs)]
    reduce_scatter x1 -> x0, waiting for transfers between devices: 40.4 us -> none  [on_device(): lax.psum_scatter(lax.dot_general(gathered, cotangent, (((0,), (0,)), ((),...]
    pallas_call x0 -> x2, Pallas kernels: none -> 14.2 us  [the longest x1 13.8 us: product(): pl.pallas_call(product_kernel, out_shape=[jax.ShapeDtypeStruct((COLS, ROW...]
    dot_general x1 -> x0, matrix products: 13.9 us -> none  [on_device(): lax.dot_general(gathered, cotangent, (((0,), (0,)), ((), ())), preferred_...]
    all_gather x1, waiting for transfers between devices: 25.6 us -> 33.2 us  [on_device(): lax.all_gather(new_master.astype(jnp.bfloat16), 'dp', axis=0, tiled=True)]
  transfers between devices with their start and end apart: 3 -> 32, of which waited for: 3 -> 20; matrix products, arithmetic and copies ran while one was open for 0% -> 2% of each run, Pallas kernels for 0% -> 0%
where the time goes in v1:
time: 217 us
  waiting for transfers between devices  120 us (55%)
  starting transfers between devices  45.6 us (21%)
  between operations  17.6 us (8%)
  Pallas kernels  14.2 us (7%)
  other arithmetic  12.2 us (6%)
  local copies, waits for them, and re-layouts  7.43 us (3%)
    ppermute x31, waiting for transfers between devices, moved(): return lax.ppermute(array, ('dp', 'mp'), pairs)  86.5 us
    ppermute x31, starting transfers between devices, moved(): return lax.ppermute(array, ('dp', 'mp'), pairs)  45.5 us
    all_gather x1, waiting for transfers between devices, on_device(): lax.all_gather(new_master.astype(jnp.bfloat16), 'dp', axis=0, tiled=True)  33.2 us
    pallas_call x1, Pallas kernels, product(): pl.pallas_call(product_kernel, out_shape=[jax.ShapeDtypeStruct((COLS, ROW...  13.8 us
    unnamed x21, local copies, waits for them, and re-layouts  6.62 us
    reduce_sum x1, other arithmetic, on_device(): jnp.sum(update * update)  4.73 us
  transfers between devices with their start and end apart: 32, of which 20 were waited for; matrix products, arithmetic and copies ran while one was open for 2% of the time, Pallas kernels for 0%

profile of v1, /device:TPU:1, one launch (start us, length us, event | category | flops | bytes accessed | tf_op | source)
XLA Modules:
  0.0 216.8 jit_solution(7037432443748128882)
XLA Ops:
  7.2 1.3 copy-done
  8.5 1.3 copy-done.1
  10.3 2.2 %collective-permute-start.7 = (bf16[320,512]{1,0:T(8,128)(2,1)S(1)}, bf16[320,512]{1,0:T(8,128)(2,1)S(1)}, u32[]{:S(2)}, u32[]{:S(2)}) collective-permute-start(bf16[320,512]{1,0:T(8,128)(2,1)S(1)} %get-tuple-element.25), channel_id=1, source_target_pairs={{0,1},{1,2},{2,3},{3,0},{4,5},{5,6},{6,7},{7,4},{8,9},{9,10},{10,1... | collective-permute-start | bytes 983048 | tf_op jit(solution)/shard_map/ppermute | solution.py:29
  12.5 2.6 %collective-permute-start.8 = (bf16[320,512]{1,0:T(8,128)(2,1)S(1)}, bf16[320,512]{1,0:T(8,128)(2,1)S(1)}, u32[]{:S(2)}, u32[]{:S(2)}) collective-permute-start(bf16[320,512]{1,0:T(8,128)(2,1)S(1)} %get-tuple-element.26), channel_id=1, source_target_pairs={{0,2},{1,3},{2,0},{3,1},{4,6},{5,7},{6,4},{7,5},{8,10},{9,11},{10,... | collective-permute-start | bytes 983048 | tf_op jit(solution)/shard_map/ppermute | solution.py:29
  15.1 1.1 collective-permute-start.9
  16.2 1.6 collective-permute-start
  17.8 3.3 %collective-permute-start.1 = (bf16[128,1280]{1,0:T(8,128)(2,1)S(1)}, bf16[128,1280]{1,0:T(8,128)(2,1)S(1)}, u32[]{:S(2)}, u32[]{:S(2)}) collective-permute-start(bf16[128,1280]{1,0:T(8,128)(2,1)S(1)} %get-tuple-element.22), channel_id=1, source_target_pairs={{0,64},{1,65},{2,66},{3,67},{4,68},{5,69},{6,70},{7,71},{8,72},{9,... | collective-permute-start | bytes 983048 | tf_op jit(solution)/shard_map/ppermute | solution.py:29
  21.2 3.7 %collective-permute-start.2 = (bf16[128,1280]{1,0:T(8,128)(2,1)S(1)}, bf16[128,1280]{1,0:T(8,128)(2,1)S(1)}, u32[]{:S(2)}, u32[]{:S(2)}) collective-permute-start(bf16[128,1280]{1,0:T(8,128)(2,1)S(1)} %get-tuple-element.23), channel_id=1, source_target_pairs={{0,96},{1,97},{2,98},{3,99},{4,100},{5,101},{6,102},{7,103},{8,104... | collective-permute-start | bytes 983048 | tf_op jit(solution)/shard_map/ppermute | solution.py:29
  24.9 4.3 %collective-permute-done.8 = bf16[320,512]{1,0:T(8,128)(2,1)S(1)} collective-permute-done((bf16[320,512]{1,0:T(8,128)(2,1)S(1)}, bf16[320,512]{1,0:T(8,128)(2,1)S(1)}, u32[]{:S(2)}, u32[]{:S(2)}) %collective-permute-start.8) | collective-permute-done | bytes 327712 | tf_op jit(solution)/shard_map/ppermute | solution.py:29
  29.3 3.8 %collective-permute-start.10 = (bf16[1280,512]{1,0:T(8,128)(2,1)S(1)}, bf16[1280,512]{1,0:T(8,128)(2,1)S(1)}, u32[]{:S(2)}, u32[]{:S(2)}) collective-permute-start(bf16[1280,512]{1,0:T(8,128)(2,1)S(1)} %constant_dynamic-update-slice_fusion.4.refs_5_), channel_id=1, source_target_pairs={{0,96},{1,97},{2,98},{3,99},{4,100},{5,101},{6,102},{7,103},{8,104... | collective-permute-start | bytes 3932168 | tf_op jit(solution)/shard_map/ppermute | solution.py:29
  33.2 1.2 collective-permute-done.1
  34.4 2.5 %collective-permute-start.3 = (bf16[512,1280]{1,0:T(8,128)(2,1)S(1)}, bf16[512,1280]{1,0:T(8,128)(2,1)S(1)}, u32[]{:S(2)}, u32[]{:S(2)}) collective-permute-start(bf16[512,1280]{1,0:T(8,128)(2,1)S(1)} %constant_dynamic-update-slice_fusion.refs_0_), channel_id=1, source_target_pairs={{0,12},{1,13},{2,14},{3,15},{4,0},{5,1},{6,2},{7,3},{8,4},{9,5},{1... | collective-permute-start | bytes 3932168 | tf_op jit(solution)/shard_map/ppermute | solution.py:29
  37.0 25.0 %collective-permute-done.10.refs_6_ = bf16[1280,512]{1,0:T(8,128)(2,1)S(1)} collective-permute-done((bf16[1280,512]{1,0:T(8,128)(2,1)S(1)}, bf16[1280,512]{1,0:T(8,128)(2,1)S(1)}, u32[]{:S(2)}, u32[]{:S(2)}) %collective-permute-start.10) | collective-permute-done | bytes 1310752 | tf_op jit(solution)/shard_map/ppermute | solution.py:29
  62.0 3.5 %collective-permute-start.12 = (bf16[640,512]{1,0:T(8,128)(2,1)S(1)}, bf16[640,512]{1,0:T(8,128)(2,1)S(1)}, u32[]{:S(2)}, u32[]{:S(2)}) collective-permute-start(bf16[640,512]{1,0:T(8,128)(2,1)S(1)} %slice.26), channel_id=1, source_target_pairs={{0,96},{1,97},{2,98},{3,99},{4,100},{5,101},{6,102},{7,103},{8,104... | collective-permute-start | bytes 1966088 | tf_op jit(solution)/shard_map/ppermute | solution.py:29
  65.5 1.2 collective-permute-start.13
  66.8 2.5 %collective-permute-start.5 = (bf16[256,1280]{1,0:T(8,128)(2,1)S(1)}, bf16[256,1280]{1,0:T(8,128)(2,1)S(1)}, u32[]{:S(2)}, u32[]{:S(2)}) collective-permute-start(bf16[256,1280]{1,0:T(8,128)(2,1)S(1)} %slice.24), channel_id=1, source_target_pairs={{0,12},{1,13},{2,14},{3,15},{4,0},{5,1},{6,2},{7,3},{8,4},{9,5},{1... | collective-permute-start | bytes 1966088 | tf_op jit(solution)/shard_map/ppermute | solution.py:29
  69.7 10.8 %collective-permute-done.12.refs_8_ = bf16[640,512]{1,0:T(8,128)(2,1)S(1)} collective-permute-done((bf16[640,512]{1,0:T(8,128)(2,1)S(1)}, bf16[640,512]{1,0:T(8,128)(2,1)S(1)}, u32[]{:S(2)}, u32[]{:S(2)}) %collective-permute-start.12) | collective-permute-done | bytes 655392 | tf_op jit(solution)/shard_map/ppermute | solution.py:29
  80.5 0.9 collective-permute-done.13.refs_9_
  81.4 0.7 collective-permute-done.5.refs_3_
  82.1 3.4 %collective-permute-done.6.refs_4_ = bf16[256,1280]{1,0:T(8,128)(2,1)S(1)} collective-permute-done((bf16[256,1280]{1,0:T(8,128)(2,1)S(1)}, bf16[256,1280]{1,0:T(8,128)(2,1)S(1)}, u32[]{:S(2)}, u32[]{:S(2)}) %collective-permute-start.6) | collective-permute-done | bytes 655392 | tf_op jit(solution)/shard_map/ppermute | solution.py:29
  85.6 13.8 %product.1 = (f32[320,640]{1,0:T(8,128)S(1)}, f32[320,640]{1,0:T(8,128)S(1)}, f32[320,640]{1,0:T(8,128)S(1)}, f32[320,640]{1,0:T(8,128)S(1)}, f32[320,640]{1,0:T...) custom-call(bf16[512,1280]{1,0:T(8,128)(2,1)S(1)} %constant_dynamic-update-slice_fusion.refs_0_,, ...), custom_call_target="tpu_custom_call" | custom-call | tf_op jit(solution)/shard_map/product/pallas_call | solution.py:105
  99.3 2.6 %collective-permute-start.15 = (f32[320,640]{1,0:T(8,128)S(1)}, f32[320,640]{1,0:T(8,128)S(1)}, u32[]{:S(2)}, u32[]{:S(2)}) collective-permute-start(f32[320,640]{1,0:T(8,128)S(1)} %get-tuple-element.31), channel_id=1, source_target_pairs={{0,16},{1,17},{2,18},{3,19},{4,20},{5,21},{6,22},{7,23},{8,24},{9,... | collective-permute-start | bytes 2457608 | tf_op jit(solution)/shard_map/ppermute | solution.py:29
  102.5 1.4 collective-permute-done.15
  103.8 1.0 add.67
  104.8 1.4 collective-permute-start.16
  106.2 1.0 add.69
  107.2 1.1 collective-permute-start.18
  108.3 1.0 add.71
  109.2 0.9 collective-permute-start.20
  112.8 11.8 %collective-permute-done.16 = f32[320,640]{1,0:T(8,128)} collective-permute-done((f32[320,640]{1,0:T(8,128)}, f32[320,640]{1,0:T(8,128)}, u32[]{:S(2)}, u32[]{:S(2)}) %collective-permute-start.16) | collective-permute-done | bytes 819232 | tf_op jit(solution)/shard_map/ppermute | solution.py:29
  124.6 3.6 %collective-permute-done.18 = f32[320,640]{1,0:T(8,128)} collective-permute-done((f32[320,640]{1,0:T(8,128)}, f32[320,640]{1,0:T(8,128)}, u32[]{:S(2)}, u32[]{:S(2)}) %collective-permute-start.18) | collective-permute-done | bytes 819232 | tf_op jit(solution)/shard_map/ppermute | solution.py:29
  128.2 18.5 %collective-permute-done.20 = f32[320,640]{1,0:T(8,128)} collective-permute-done((f32[320,640]{1,0:T(8,128)}, f32[320,640]{1,0:T(8,128)}, u32[]{:S(2)}, u32[]{:S(2)}) %collective-permute-start.20) | collective-permute-done | bytes 819232 | tf_op jit(solution)/shard_map/ppermute | solution.py:29
  146.8 4.7 %multiply_reduce_fusion = (f32[]{:T(128)}, f32[640,320]{0,1:T(8,128)S(1)}, f32[640,320]{0,1:T(8,128)}, f32[640,320]{0,1:T(8,128)}, f32[]{:T(128)}) fusion(f32[640,320]{0,1:T(8,128)S(1)} %copy-done.2, f32[]{:T(128)} %bitcast.5, f32[]{:T(128)} %bitcast.4, f32[640,320]{0,1:T(8,128)S(1)} %copy-done.5, f32[640,320]{0,1:T(8,128)} %param.11, ...), kind=kLoop, calls=%fused_computation.5 | loop fusion | flops 4300798 | bytes 9011216 | tf_op jit(solution)/shard_map/reduce_sum | solution.py:171
  151.5 1.4 pad_maximum_fusion
  153.4 0.8 collective-permute-done.21
  154.2 1.4 fusion.7
  155.6 0.9 collective-permute-start.23
  156.5 1.8 collective-permute-start.24
  158.3 0.9 collective-permute-done.22
  159.8 1.5 collective-permute-start.26
  161.3 1.6 collective-permute-start.27
  164.0 1.9 collective-permute-start.28
  165.9 1.2 collective-permute-start.29
  167.0 1.3 collective-permute-start.30
  168.3 1.4 collective-permute-done.29
  171.7 1.1 fusion.3
  172.9 33.2 %all-gather.2.cloned.1.call-done = bf16[5120,320]{0,1:T(8,128)(2,1)} async-done(((bf16[640,320]{0,1:T(8,128)(2,1)}), bf16[5120,320]{0,1:T(8,128)(2,1)}) %all-gather.2.cloned.1.call-update) | async-done | bytes 3276816 | tf_op jit(solution)/shard_map/all_gather | solution.py:177
  206.1 3.8 %copy.21 = bf16[5120,320]{0,1:T(8,128)(2,1)} copy(bf16[5120,320]{0,1:T(8,128)(2,1)} %all-gather.2.cloned.1.call-done) | data formatting | bytes 6553600
  (58 shorter events, 5.2 us)
Async XLA Ops:
  7.2 198.9 %all-gather.2.cloned.1.call-start = ((), (), s32[]{:S(2)}) async-start(), calls=%async_computation | async-start | bytes 3686400 | tf_op jit(solution)/shard_map/all_gather | solution.py:177
  7.2 1.3 copy-start
  8.5 1.3 copy-start.1
  10.3 10.9 %collective-permute-start.7 = (bf16[320,512]{1,0:T(8,128)(2,1)S(1)}, bf16[320,512]{1,0:T(8,128)(2,1)S(1)}, u32[]{:S(2)}, u32[]{:S(2)}) collective-permute-start(bf16[320,512]{1,0:T(8,128)(2,1)S(1)} %get-tuple-element.25), channel_id=1, source_target_pairs={{0,1},{1,2},{2,3},{3,0},{4,5},{5,6},{6,7},{7,4},{8,9},{9,10},{10,1... | collective-permute-start | bytes 983048 | tf_op jit(solution)/shard_map/ppermute | solution.py:29
  12.5 16.8 %collective-permute-start.8 = (bf16[320,512]{1,0:T(8,128)(2,1)S(1)}, bf16[320,512]{1,0:T(8,128)(2,1)S(1)}, u32[]{:S(2)}, u32[]{:S(2)}) collective-permute-start(bf16[320,512]{1,0:T(8,128)(2,1)S(1)} %get-tuple-element.26), channel_id=1, source_target_pairs={{0,2},{1,3},{2,0},{3,1},{4,6},{5,7},{6,4},{7,5},{8,10},{9,11},{10,... | collective-permute-start | bytes 983048 | tf_op jit(solution)/shard_map/ppermute | solution.py:29
  15.1 14.2 %collective-permute-start.9 = (bf16[320,512]{1,0:T(8,128)(2,1)S(1)}, bf16[320,512]{1,0:T(8,128)(2,1)S(1)}, u32[]{:S(2)}, u32[]{:S(2)}) collective-permute-start(bf16[320,512]{1,0:T(8,128)(2,1)S(1)} %get-tuple-element.27), channel_id=1, source_target_pairs={{0,3},{1,0},{2,1},{3,2},{4,7},{5,4},{6,5},{7,6},{8,11},{9,8},{10,9... | collective-permute-start | bytes 983048 | tf_op jit(solution)/shard_map/ppermute | solution.py:29
  16.2 17.0 %collective-permute-start = (bf16[128,1280]{1,0:T(8,128)(2,1)S(1)}, bf16[128,1280]{1,0:T(8,128)(2,1)S(1)}, u32[]{:S(2)}, u32[]{:S(2)}) collective-permute-start(bf16[128,1280]{1,0:T(8,128)(2,1)S(1)} %get-tuple-element.21), channel_id=1, source_target_pairs={{0,32},{1,33},{2,34},{3,35},{4,36},{5,37},{6,38},{7,39},{8,40},{9,... | collective-permute-start | bytes 983048 | tf_op jit(solution)/shard_map/ppermute | solution.py:29
  17.8 16.5 %collective-permute-start.1 = (bf16[128,1280]{1,0:T(8,128)(2,1)S(1)}, bf16[128,1280]{1,0:T(8,128)(2,1)S(1)}, u32[]{:S(2)}, u32[]{:S(2)}) collective-permute-start(bf16[128,1280]{1,0:T(8,128)(2,1)S(1)} %get-tuple-element.22), channel_id=1, source_target_pairs={{0,64},{1,65},{2,66},{3,67},{4,68},{5,69},{6,70},{7,71},{8,72},{9,... | collective-permute-start | bytes 983048 | tf_op jit(solution)/shard_map/ppermute | solution.py:29
  21.2 13.2 %collective-permute-start.2 = (bf16[128,1280]{1,0:T(8,128)(2,1)S(1)}, bf16[128,1280]{1,0:T(8,128)(2,1)S(1)}, u32[]{:S(2)}, u32[]{:S(2)}) collective-permute-start(bf16[128,1280]{1,0:T(8,128)(2,1)S(1)} %get-tuple-element.23), channel_id=1, source_target_pairs={{0,96},{1,97},{2,98},{3,99},{4,100},{5,101},{6,102},{7,103},{8,104... | collective-permute-start | bytes 983048 | tf_op jit(solution)/shard_map/ppermute | solution.py:29
  29.3 32.6 %collective-permute-start.10 = (bf16[1280,512]{1,0:T(8,128)(2,1)S(1)}, bf16[1280,512]{1,0:T(8,128)(2,1)S(1)}, u32[]{:S(2)}, u32[]{:S(2)}) collective-permute-start(bf16[1280,512]{1,0:T(8,128)(2,1)S(1)} %constant_dynamic-update-slice_fusion.4.refs_5_), channel_id=1, source_target_pairs={{0,96},{1,97},{2,98},{3,99},{4,100},{5,101},{6,102},{7,103},{8,104... | collective-permute-start | bytes 3932168 | tf_op jit(solution)/shard_map/ppermute | solution.py:29
  33.1 32.3 %collective-permute-start.11 = (bf16[1280,512]{1,0:T(8,128)(2,1)S(1)}, bf16[1280,512]{1,0:T(8,128)(2,1)S(1)}, u32[]{:S(2)}, u32[]{:S(2)}) collective-permute-start(bf16[1280,512]{1,0:T(8,128)(2,1)S(1)} %constant_dynamic-update-slice_fusion.4.refs_5_), channel_id=1, source_target_pairs={{0,32},{1,33},{2,34},{3,35},{4,36},{5,37},{6,38},{7,39},{8,40},{9,... | collective-permute-start | bytes 3932168 | tf_op jit(solution)/shard_map/ppermute | solution.py:29
  34.4 32.3 %collective-permute-start.3 = (bf16[512,1280]{1,0:T(8,128)(2,1)S(1)}, bf16[512,1280]{1,0:T(8,128)(2,1)S(1)}, u32[]{:S(2)}, u32[]{:S(2)}) collective-permute-start(bf16[512,1280]{1,0:T(8,128)(2,1)S(1)} %constant_dynamic-update-slice_fusion.refs_0_), channel_id=1, source_target_pairs={{0,12},{1,13},{2,14},{3,15},{4,0},{5,1},{6,2},{7,3},{8,4},{9,5},{1... | collective-permute-start | bytes 3932168 | tf_op jit(solution)/shard_map/ppermute | solution.py:29
  37.0 32.4 %collective-permute-start.4 = (bf16[512,1280]{1,0:T(8,128)(2,1)S(1)}, bf16[512,1280]{1,0:T(8,128)(2,1)S(1)}, u32[]{:S(2)}, u32[]{:S(2)}) collective-permute-start(bf16[512,1280]{1,0:T(8,128)(2,1)S(1)} %constant_dynamic-update-slice_fusion.refs_0_), channel_id=1, source_target_pairs={{0,4},{1,5},{2,6},{3,7},{4,8},{5,9},{6,10},{7,11},{8,12},{9,13},{1... | collective-permute-start | bytes 3932168 | tf_op jit(solution)/shard_map/ppermute | solution.py:29
  61.9 3.6 %copy-start.3 = (bf16[1280,512]{1,0:T(8,128)(2,1)}, bf16[1280,512]{1,0:T(8,128)(2,1)S(1)}, u32[]{:S(2)}) copy-start(bf16[1280,512]{1,0:T(8,128)(2,1)S(1)} %collective-permute-done.10.refs_6_) | copy-start | bytes 3932164
  62.0 18.5 %collective-permute-start.12 = (bf16[640,512]{1,0:T(8,128)(2,1)S(1)}, bf16[640,512]{1,0:T(8,128)(2,1)S(1)}, u32[]{:S(2)}, u32[]{:S(2)}) collective-permute-start(bf16[640,512]{1,0:T(8,128)(2,1)S(1)} %slice.26), channel_id=1, source_target_pairs={{0,96},{1,97},{2,98},{3,99},{4,100},{5,101},{6,102},{7,103},{8,104... | collective-permute-start | bytes 1966088 | tf_op jit(solution)/shard_map/ppermute | solution.py:29
  65.5 1.3 copy-start.4
  65.5 15.9 %collective-permute-start.13 = (bf16[640,512]{1,0:T(8,128)(2,1)S(1)}, bf16[640,512]{1,0:T(8,128)(2,1)S(1)}, u32[]{:S(2)}, u32[]{:S(2)}) collective-permute-start(bf16[640,512]{1,0:T(8,128)(2,1)S(1)} %slice.27), channel_id=1, source_target_pairs={{0,32},{1,33},{2,34},{3,35},{4,36},{5,37},{6,38},{7,39},{8,40},{9,... | collective-permute-start | bytes 1966088 | tf_op jit(solution)/shard_map/ppermute | solution.py:29
  66.8 15.3 %collective-permute-start.5 = (bf16[256,1280]{1,0:T(8,128)(2,1)S(1)}, bf16[256,1280]{1,0:T(8,128)(2,1)S(1)}, u32[]{:S(2)}, u32[]{:S(2)}) collective-permute-start(bf16[256,1280]{1,0:T(8,128)(2,1)S(1)} %slice.24), channel_id=1, source_target_pairs={{0,12},{1,13},{2,14},{3,15},{4,0},{5,1},{6,2},{7,3},{8,4},{9,5},{1... | collective-permute-start | bytes 1966088 | tf_op jit(solution)/shard_map/ppermute | solution.py:29
  69.4 16.1 %collective-permute-start.6 = (bf16[256,1280]{1,0:T(8,128)(2,1)S(1)}, bf16[256,1280]{1,0:T(8,128)(2,1)S(1)}, u32[]{:S(2)}, u32[]{:S(2)}) collective-permute-start(bf16[256,1280]{1,0:T(8,128)(2,1)S(1)} %slice.25), channel_id=1, source_target_pairs={{0,4},{1,5},{2,6},{3,7},{4,8},{5,9},{6,10},{7,11},{8,12},{9,13},{1... | collective-permute-start | bytes 1966088 | tf_op jit(solution)/shard_map/ppermute | solution.py:29
  99.3 4.5 %collective-permute-start.15 = (f32[320,640]{1,0:T(8,128)S(1)}, f32[320,640]{1,0:T(8,128)S(1)}, u32[]{:S(2)}, u32[]{:S(2)}) collective-permute-start(f32[320,640]{1,0:T(8,128)S(1)} %get-tuple-element.31), channel_id=1, source_target_pairs={{0,16},{1,17},{2,18},{3,19},{4,20},{5,21},{6,22},{7,23},{8,24},{9,... | collective-permute-start | bytes 2457608 | tf_op jit(solution)/shard_map/ppermute | solution.py:29
  101.9 4.3 %collective-permute-start.17 = (f32[320,640]{1,0:T(8,128)S(1)}, f32[320,640]{1,0:T(8,128)S(1)}, u32[]{:S(2)}, u32[]{:S(2)}) collective-permute-start(f32[320,640]{1,0:T(8,128)S(1)} %get-tuple-element.33), channel_id=1, source_target_pairs={{0,16},{1,17},{2,18},{3,19},{4,20},{5,21},{6,22},{7,23},{8,24},{9,... | collective-permute-start | bytes 2457608 | tf_op jit(solution)/shard_map/ppermute | solution.py:29
  102.0 6.3 %collective-permute-start.19 = (f32[320,640]{1,0:T(8,128)S(1)}, f32[320,640]{1,0:T(8,128)S(1)}, u32[]{:S(2)}, u32[]{:S(2)}) collective-permute-start(f32[320,640]{1,0:T(8,128)S(1)} %get-tuple-element.35), channel_id=1, source_target_pairs={{0,16},{1,17},{2,18},{3,19},{4,20},{5,21},{6,22},{7,23},{8,24},{9,... | collective-permute-start | bytes 2457608 | tf_op jit(solution)/shard_map/ppermute | solution.py:29
  102.4 10.4 %collective-permute-start.14 = (f32[320,640]{1,0:T(8,128)S(1)}, f32[320,640]{1,0:T(8,128)}, u32[]{:S(2)}, u32[]{:S(2)}) collective-permute-start(f32[320,640]{1,0:T(8,128)S(1)} %get-tuple-element.29), channel_id=1, source_target_pairs={{0,16},{1,17},{2,18},{3,19},{4,20},{5,21},{6,22},{7,23},{8,24},{9,... | collective-permute-start | bytes 2457608 | tf_op jit(solution)/shard_map/ppermute | solution.py:29
  104.8 19.8 %collective-permute-start.16 = (f32[320,640]{1,0:T(8,128)}, f32[320,640]{1,0:T(8,128)}, u32[]{:S(2)}, u32[]{:S(2)}) collective-permute-start(f32[320,640]{1,0:T(8,128)} %add.67), channel_id=1, source_target_pairs={{0,3},{1,0},{2,1},{3,2},{4,7},{5,4},{6,5},{7,6},{8,11},{9,8},{10,9... | collective-permute-start | bytes 2457608 | tf_op jit(solution)/shard_map/ppermute | solution.py:29
  107.2 4.3 %copy-start.6 = (f32[8]{0:T(128)S(1)}, f32[8]{0:T(128)}, u32[]{:S(2)}) copy-start(f32[8]{0:T(128)} %param.15) | copy-start | bytes 100
  107.2 39.5 %copy-start.2 = (f32[640,320]{0,1:T(8,128)S(1)}, f32[640,320]{0,1:T(8,128)}, u32[]{:S(2)}) copy-start(f32[640,320]{0,1:T(8,128)} %param.10) | copy-start | bytes 2457604
  107.2 39.5 %copy-start.5 = (f32[640,320]{0,1:T(8,128)S(1)}, f32[640,320]{0,1:T(8,128)}, u32[]{:S(2)}) copy-start(f32[640,320]{0,1:T(8,128)} %param.12) | copy-start | bytes 2457604
  107.2 21.0 %collective-permute-start.18 = (f32[320,640]{1,0:T(8,128)}, f32[320,640]{1,0:T(8,128)}, u32[]{:S(2)}, u32[]{:S(2)}) collective-permute-start(f32[320,640]{1,0:T(8,128)} %add.69), channel_id=1, source_target_pairs={{0,2},{1,3},{2,0},{3,1},{4,6},{5,7},{6,4},{7,5},{8,10},{9,11},{10,... | collective-permute-start | bytes 2457608 | tf_op jit(solution)/shard_map/ppermute | solution.py:29
  109.2 37.5 %collective-permute-start.20 = (f32[320,640]{1,0:T(8,128)}, f32[320,640]{1,0:T(8,128)}, u32[]{:S(2)}, u32[]{:S(2)}) collective-permute-start(f32[320,640]{1,0:T(8,128)} %add.71), channel_id=1, source_target_pairs={{0,1},{1,2},{2,3},{3,0},{4,5},{5,6},{6,7},{7,4},{8,9},{9,10},{10,1... | collective-permute-start | bytes 2457608 | tf_op jit(solution)/shard_map/ppermute | solution.py:29
  152.9 1.3 collective-permute-start.21
  155.6 3.6 %collective-permute-start.22 = (f32[2]{0:T(128)S(1)}, f32[2]{0:T(128)S(1)}, u32[]{:S(2)}, u32[]{:S(2)}) collective-permute-start(f32[2]{0:T(128)S(1)} %fusion.7), channel_id=1, source_target_pairs={{0,4},{1,5},{2,6},{3,7},{4,8},{5,9},{6,10},{7,11},{8,12},{9,13},{1... | collective-permute-start | bytes 32 | tf_op jit(solution)/shard_map/ppermute | solution.py:29
  155.6 4.0 %collective-permute-start.23 = (f32[2]{0:T(128)S(1)}, f32[2]{0:T(128)S(1)}, u32[]{:S(2)}, u32[]{:S(2)}) collective-permute-start(f32[2]{0:T(128)S(1)} %fusion.7), channel_id=1, source_target_pairs={{0,8},{1,9},{2,10},{3,11},{4,12},{5,13},{6,14},{7,15},{8,0},{9,1},... | collective-permute-start | bytes 32 | tf_op jit(solution)/shard_map/ppermute | solution.py:29
  156.5 3.3 %collective-permute-start.24 = (f32[2]{0:T(128)S(1)}, f32[2]{0:T(128)S(1)}, u32[]{:S(2)}, u32[]{:S(2)}) collective-permute-start(f32[2]{0:T(128)S(1)} %fusion.7), channel_id=1, source_target_pairs={{0,12},{1,13},{2,14},{3,15},{4,0},{5,1},{6,2},{7,3},{8,4},{9,5},{1... | collective-permute-start | bytes 32 | tf_op jit(solution)/shard_map/ppermute | solution.py:29
  159.8 3.6 %collective-permute-start.25 = (f32[2]{0:T(128)S(1)}, f32[2]{0:T(128)S(1)}, u32[]{:S(2)}, u32[]{:S(2)}) collective-permute-start(f32[2]{0:T(128)S(1)} %add_add_fusion.3), channel_id=1, source_target_pairs={{0,1},{1,2},{2,3},{3,0},{4,5},{5,6},{6,7},{7,4},{8,9},{9,10},{10,1... | collective-permute-start | bytes 32 | tf_op jit(solution)/shard_map/ppermute | solution.py:29
  159.8 4.0 %collective-permute-start.26 = (f32[2]{0:T(128)S(1)}, f32[2]{0:T(128)S(1)}, u32[]{:S(2)}, u32[]{:S(2)}) collective-permute-start(f32[2]{0:T(128)S(1)} %add_add_fusion.3), channel_id=1, source_target_pairs={{0,2},{1,3},{2,0},{3,1},{4,6},{5,7},{6,4},{7,5},{8,10},{9,11},{10,... | collective-permute-start | bytes 32 | tf_op jit(solution)/shard_map/ppermute | solution.py:29
  161.3 2.7 %collective-permute-start.27 = (f32[2]{0:T(128)S(1)}, f32[2]{0:T(128)S(1)}, u32[]{:S(2)}, u32[]{:S(2)}) collective-permute-start(f32[2]{0:T(128)S(1)} %add_add_fusion.3), channel_id=1, source_target_pairs={{0,3},{1,0},{2,1},{3,2},{4,7},{5,4},{6,5},{7,6},{8,11},{9,8},{10,9... | collective-permute-start | bytes 32 | tf_op jit(solution)/shard_map/ppermute | solution.py:29
  164.0 4.3 %collective-permute-start.28 = (f32[2]{0:T(128)S(1)}, f32[2]{0:T(128)S(1)}, u32[]{:S(2)}, u32[]{:S(2)}) collective-permute-start(f32[2]{0:T(128)S(1)} %add_add_fusion.2), channel_id=1, source_target_pairs={{0,32},{1,33},{2,34},{3,35},{4,36},{5,37},{6,38},{7,39},{8,40},{9,... | collective-permute-start | bytes 32 | tf_op jit(solution)/shard_map/ppermute | solution.py:29
  165.9 3.9 %collective-permute-start.29 = (f32[2]{0:T(128)S(1)}, f32[2]{0:T(128)S(1)}, u32[]{:S(2)}, u32[]{:S(2)}) collective-permute-start(f32[2]{0:T(128)S(1)} %add_add_fusion.2), channel_id=1, source_target_pairs={{0,64},{1,65},{2,66},{3,67},{4,68},{5,69},{6,70},{7,71},{8,72},{9,... | collective-permute-start | bytes 32 | tf_op jit(solution)/shard_map/ppermute | solution.py:29
  167.0 2.7 %collective-permute-start.30 = (f32[2]{0:T(128)S(1)}, f32[2]{0:T(128)S(1)}, u32[]{:S(2)}, u32[]{:S(2)}) collective-permute-start(f32[2]{0:T(128)S(1)} %add_add_fusion.2), channel_id=1, source_target_pairs={{0,96},{1,97},{2,98},{3,99},{4,100},{5,101},{6,102},{7,103},{8,104... | collective-permute-start | bytes 32 | tf_op jit(solution)/shard_map/ppermute | solution.py:29
Sparse Core Ops, SparseCore 0:
  173.0 33.0 all-gather.1

commit v2 on v1

v2 whole, which is shorter than its diff:
```python
import jax
import jax.numpy as jnp
from jax import lax
from jax.experimental import pallas as pl
from jax.experimental.pallas import tpu as pltpu
from jax.sharding import PartitionSpec as P

beta_one = 0.9
beta_two = 0.999
epsilon = 1e-06
decay_weight = 0.1
base_rate = 0.25

ROWS = 640
COLS = 320
BLOCK = 128
GROUP = 2 * ROWS


def moved(array, dz=0, dc=0, dx=0, dy=0):
    pairs = []
    for z in range(4):
        for c in range(2):
            for x in range(4):
                for y in range(4):
                    src = (2 * z + c) * 16 + 4 * x + y
                    dst = (2 * ((z + dz) % 4) + (c + dc) % 2) * 16 + 4 * ((x + dx) % 4) + (y + dy) % 4
                    pairs.append((src, dst))
    return lax.ppermute(array, ("dp", "mp"), pairs)


def place():
    d = lax.axis_index("dp")
    m = lax.axis_index("mp")
    return d // 2, d % 2, m // 4, m % 4


def prepare_kernel(act, cot, a0, a1, a2, a3, c0, c1, c2, c3, sems):
    z, c, x, y = place()
    copies = []
    for kz, out in enumerate((a0, a1, a2, a3)):
        first = lax.rem(z + kz, 4) * GROUP
        for half, core in enumerate((c, 1 - c)):
            start = pl.multiple_of(first + core * ROWS, 128)
            copies.append((act.at[:, pl.ds(start, ROWS)], out.at[:, pl.ds(half * ROWS, ROWS)]))
    for ky, out in enumerate((c0, c1, c2, c3)):
        for dx in range(4):
            start = (4 * lax.rem(x + dx, 4) + lax.rem(y + ky, 4)) * BLOCK
            start = pl.multiple_of(start, 128)
            copies.append((cot.at[:, pl.ds(start, BLOCK)], out.at[:, pl.ds(dx * BLOCK, BLOCK)]))
    started = [pltpu.make_async_copy(src, dst, sems.at[k]) for k, (src, dst) in enumerate(copies)]
    for copy in started:
        copy.start()
    for copy in started:
        copy.wait()


ANY = pl.BlockSpec(memory_space=pl.ANY)
VMEM = pl.BlockSpec(memory_space=pltpu.VMEM)
SMEM = pl.BlockSpec(memory_space=pltpu.SMEM)


def params(mib):
    return pltpu.CompilerParams(vmem_limit_bytes=mib * 2**20)


def prepare(activations, cotangent_t):
    bf16 = jnp.bfloat16
    return pl.pallas_call(
        prepare_kernel,
        out_shape=[jax.ShapeDtypeStruct((BLOCK, GROUP), bf16)] * 4
        + [jax.ShapeDtypeStruct((COLS, 4 * BLOCK), bf16)] * 4,
        in_specs=[pl.BlockSpec(memory_space=pltpu.HBM)] * 2,
        out_specs=[VMEM] * 8,
        scratch_shapes=[pltpu.SemaphoreType.DMA((24,))],
        compiler_params=params(4),
        name="prepare",
    )(activations, cotangent_t)


def dot(a, b):
    return jnp.dot(a, b, preferred_element_type=jnp.float32)


def near_kernel(x0, xp, xm, z0, zp, zm, *outs):
    acts = jnp.concatenate(
        [x[kz * BLOCK : (kz + 1) * BLOCK, :] for kz in (0, 1, 3) for x in (x0, xp, xm)], axis=0
    )
    for ky, out in enumerate(outs):
        rows = slice(ky * COLS, (ky + 1) * COLS)
        parts = []
        for z in (z0, zm, zp):
            parts += [z[rows, : 2 * BLOCK], z[rows, 3 * BLOCK :]]
        out[...] = dot(jnp.concatenate(parts, axis=1), acts)


def near_product(x0, xp, xm, z0, zp, zm):
    return pl.pallas_call(
        near_kernel,
        out_shape=[jax.ShapeDtypeStruct((COLS, GROUP), jnp.float32)] * 4,
        in_specs=[VMEM] * 6,
        out_specs=[VMEM] * 4,
        compiler_params=params(14),
        name="near_product",
    )(x0, xp, xm, z0, zp, zm)


def far_kernel(*refs):
    x0, xp, xm, xd0, xd1, z0, zp, zm, zd0, zd1 = refs[:10]
    totals = refs[10:14]
    outs = refs[14:]
    acts = jnp.concatenate(
        [x[2 * BLOCK : 3 * BLOCK, :] for x in (x0, xp)]
        + [xd1[:BLOCK, :]]
        + [xm[2 * BLOCK : 3 * BLOCK, :]]
        + [xd0[:BLOCK, :], xd0[BLOCK:, :], xd1[BLOCK:, :]],
        axis=0,
    )
    middle = slice(2 * BLOCK, 3 * BLOCK)
    for ky in (2, 1, 3, 0):
        rows = slice(ky * COLS, (ky + 1) * COLS)
        far = zd0 if ky < 2 else zd1
        parts = [far[(ky % 2) * COLS : (ky % 2 + 1) * COLS, :]]
        parts += [z[rows, middle] for z in (z0, zm, zp)]
        total = totals[ky][...] + dot(jnp.concatenate(parts, axis=1), acts)
        outs[2 * ky][...] = total[:, :ROWS]
        outs[2 * ky + 1][...] = total[:, ROWS:]


def far_product(pieces, totals):
    return pl.pallas_call(
        far_kernel,
        out_shape=[jax.ShapeDtypeStruct((COLS, ROWS), jnp.float32)] * 8,
        in_specs=[VMEM] * 14,
        out_specs=[VMEM] * 8,
        compiler_params=params(14),
        name="far_product",
    )(*pieces, *totals)


def ring_gather(block, axis):
    half = block.shape[0] // 2
    plus = moved(block, **{axis: -1})
    minus = moved(block, **{axis: 1})
    far_first = moved(plus[:half], **{axis: -1})
    far_second = moved(minus[half:], **{axis: 1})
    return [block, plus, minus, far_first, far_second]


def gradient_terms(activations, cotangent):
    parts = prepare(activations, cotangent.T)
    acts, cots = parts[:4], parts[4:]
    a_block = jnp.concatenate([acts[0]] + [moved(acts[k], dz=k) for k in (1, 2, 3)], axis=0)
    c_block = jnp.concatenate([cots[0]] + [moved(cots[k], dy=k) for k in (1, 2, 3)], axis=0)
    a_pieces = ring_gather(a_block, "dx")
    c_pieces = ring_gather(c_block, "dz")
    totals = near_product(*a_pieces[:3], *c_pieces[:3])
    outs = far_product(a_pieces + c_pieces, totals)
    sums = {}
    for ky in (2, 1, 3, 0):
        sums[ky] = outs[2 * ky] + moved(outs[2 * ky + 1], dc=1)
    return [sums[0], moved(sums[1], dy=-1), moved(sums[2], dy=-2), moved(sums[3], dy=-3)]


STRIP = 32


def update_kernel(g0, g1, g2, g3, weights, first, second, scale, new_first, new_second, update, sums):
    inv_one, inv_two = scale[0], scale[1]

    def strip(i, carry):
        rows = pl.ds(pl.multiple_of(i * STRIP, STRIP), STRIP)
        g = (g0[rows, :] + g1[rows, :]) + (g2[rows, :] + g3[rows, :])
        w = weights[rows, :]
        m = beta_one * first[rows, :] + (1.0 - beta_one) * g
        v = beta_two * second[rows, :] + (1.0 - beta_two) * g * g
        u = m * inv_one / (jnp.sqrt(v * inv_two) + epsilon) + decay_weight * w
        new_first[rows, :] = m
        new_second[rows, :] = v
        update[rows, :] = u
        out = []
        for total, term in zip(carry, (w * w, u * u)):
            part = term[:8]
            for k in range(8, STRIP, 8):
                part = part + term[k : k + 8]
            out.append(total + part)
        return tuple(out)

    zero = jnp.zeros((8, ROWS), jnp.float32)
    for k, total in enumerate(lax.fori_loop(0, COLS // STRIP, strip, (zero, zero))):
        part = total[:, :128]
        for j in range(128, ROWS, 128):
            part = part + total[:, j : j + 128]
        sums[8 * k : 8 * k + 8, :] = part


def updated(terms, weights, first, second, scale):
    block = jax.ShapeDtypeStruct((COLS, ROWS), jnp.float32)
    return pl.pallas_call(
        update_kernel,
        out_shape=[block] * 3 + [jax.ShapeDtypeStruct((16, 128), jnp.float32)],
        in_specs=[VMEM] * 7 + [SMEM],
        out_specs=[VMEM] * 4,
        compiler_params=params(6),
        name="update",
    )(*terms, weights, first, second, scale)


def total_over_devices(values):
    values = values + moved(values, dc=1)
    for axis in ("dx", "dy", "dz"):
        values = values + moved(values, **{axis: 1}) + moved(values, **{axis: 2}) + moved(values, **{axis: 3})
    return values


def step_kernel(weights, update, sums, rate, new_master, new_weights):
    weight_sq = jnp.sum(jnp.sum(sums[:8, :], axis=0, keepdims=True), axis=1, keepdims=True)
    update_sq = jnp.sum(jnp.sum(sums[8:, :], axis=0, keepdims=True), axis=1, keepdims=True)
    scale = rate[0] * (jnp.sqrt(weight_sq) / jnp.sqrt(update_sq))

    def strip(i, carry):
        rows = pl.ds(pl.multiple_of(i * STRIP, STRIP), STRIP)
        w = weights[rows, :] - scale * update[rows, :]
        new_master[rows, :] = w
        new_weights[rows, :] = w.astype(jnp.bfloat16)
        return carry

    lax.fori_loop(0, COLS // STRIP, strip, 0)


def stepped(weights, update, sums, rate):
    return pl.pallas_call(
        step_kernel,
        out_shape=[
            jax.ShapeDtypeStruct((COLS, ROWS), jnp.float32),
            jax.ShapeDtypeStruct((COLS, ROWS), jnp.bfloat16),
        ],
        in_specs=[VMEM] * 3 + [SMEM],
        out_specs=[VMEM] * 2,
        compiler_params=params(6),
        name="step",
    )(weights, update, sums, rate)


def assemble_kernel(*refs):
    pieces, out, sems = refs[:8], refs[8], refs[9]
    z, c, x, y = place()
    copies = []
    for k in range(4):
        for half, core in enumerate((c, 1 - c)):
            start = pl.multiple_of((2 * lax.rem(z + k, 4) + core) * ROWS, 128)
            copies.append(
                pltpu.make_async_copy(
                    pieces[2 * k + half], out.at[:, pl.ds(start, ROWS)], sems.at[2 * k + half]
                )
            )
    for copy in copies:
        copy.start()
    for copy in copies:
        copy.wait()


def gathered_rows(block):
    pieces = []
    for k in range(4):
        mine = moved(block, dz=-k) if k else block
        pieces += [mine, moved(mine, dc=1)]
    return pl.pallas_call(
        assemble_kernel,
        out_shape=jax.ShapeDtypeStruct((COLS, 8 * ROWS), block.dtype),
        in_specs=[VMEM] * 8,
        out_specs=ANY,
        scratch_shapes=[pltpu.SemaphoreType.DMA((8,))],
        compiler_params=params(4),
        name="assemble",
    )(*pieces)


def on_device(
    activations,
    cotangent,
    master_weights,
    first_moment,
    second_moment,
    step_count,
    language_ids,
    language_rates,
):
    steps_done = step_count.astype(jnp.float32)
    corr_one = 1.0 - jnp.power(jnp.float32(beta_one), steps_done)
    corr_two = 1.0 - jnp.power(jnp.float32(beta_two), steps_done)
    scale = jnp.concatenate([1.0 / corr_one, 1.0 / corr_two])
    picked = jnp.arange(language_rates.shape[0], dtype=jnp.int32) == language_ids[0]
    rate = base_rate * jnp.sum(jnp.where(picked, language_rates, jnp.float32(0.0)))
    weights = master_weights.T
    terms = gradient_terms(activations, cotangent)
    new_first, new_second, update, sums = updated(
        terms, weights, first_moment.T, second_moment.T, scale
    )
    new_master, mine = stepped(weights, update, total_over_devices(sums), rate.reshape(1))
    return (new_master.T, new_first.T, new_second.T, gathered_rows(mine).T)


def solution(mesh):
    return jax.shard_map(
        on_device,
        mesh=mesh,
        in_specs=(
            P(("dp", "mp"), None),
            P("dp", "mp"),
            P("dp", "mp"),
            P("dp", "mp"),
            P("dp", "mp"),
            P(),
            P(),
            P(),
        ),
        out_specs=(P("dp", "mp"), P("dp", "mp"), P("dp", "mp"), P(None, "mp")),
        check_vma=False,
    )
```

time: 217 us -> 177 us (0.82)
  waiting for transfers between devices: 120 us -> 86.6 us
  starting transfers between devices: 45.6 us -> 68.3 us
  between operations: 17.6 us -> 3.14 us
  other arithmetic: 12.2 us -> 1.03 us
  local copies, waits for them, and re-layouts: 7.43 us -> 3 us
    all_gather x1 -> x0, waiting for transfers between devices: 33.2 us -> none  [on_device(): lax.all_gather(new_master.astype(jnp.bfloat16), 'dp', axis=0, tiled=True)]
    ppermute x31 -> x38, starting transfers between devices: 45.5 us -> 68.3 us  [moved(): return lax.ppermute(array, ('dp', 'mp'), pairs)]
    reduce_sum x1 -> x0, other arithmetic: 4.73 us -> none  [on_device(): jnp.sum(update * update)]
    unnamed x21 -> x18, local copies, waits for them, and re-layouts: 6.62 us -> 2.78 us
    add x3 -> x4, other arithmetic: 2.92 us -> 0.34 us  [gradient_terms(): sums[ky] = outs[2 * ky] + moved(outs[2 * ky + 1], dc=1)]
    pallas_call x1 -> x5, Pallas kernels: 13.8 us -> 13.4 us  [the longest x1 4.39 us: near_product(): pl.pallas_call(near_kernel, out_shape=[jax.ShapeDtypeStruct((COLS, GROUP)...]
    ppermute x31 -> x38, waiting for transfers between devices: 86.5 us -> 86.6 us  [moved(): return lax.ppermute(array, ('dp', 'mp'), pairs)]
  transfers between devices with their start and end apart: 32 -> 38, of which waited for: 20 -> 21; matrix products, arithmetic and copies ran while one was open for 2% -> 1% of each run, Pallas kernels for 0% -> 2%
where the time goes in v2:
time: 177 us; the launch traced here: 176 us
  waiting for transfers between devices  86.6 us (49%)
  starting transfers between devices  68.3 us (39%)
  Pallas kernels  14.3 us (8%)
  between operations  3.14 us (2%)
  local copies, waits for them, and re-layouts  3 us (2%)
    ppermute x38, waiting for transfers between devices, moved(): return lax.ppermute(array, ('dp', 'mp'), pairs)  86.6 us
    ppermute x38, starting transfers between devices, moved(): return lax.ppermute(array, ('dp', 'mp'), pairs)  68.3 us
    pallas_call x1, Pallas kernels, near_product(): pl.pallas_call(near_kernel, out_shape=[jax.ShapeDtypeStruct((COLS, GROUP)...  4.39 us
    pallas_call x1, Pallas kernels, far_product(): pl.pallas_call(far_kernel, out_shape=[jax.ShapeDtypeStruct((COLS, ROWS),...  3.55 us
  transfers between devices with their start and end apart: 38, of which 21 were waited for; matrix products, arithmetic and copies ran while one was open for 1% of the time, Pallas kernels for 2%

profile of v2, /device:TPU:1, one launch (start us, length us, event | category | flops | bytes accessed | tf_op | source)
XLA Modules:
  0.0 176.4 jit_solution(8273005749368125853)
XLA Ops:
  0.6 1.3 copy-done.1
  1.9 1.3 copy-done.2
  3.3 0.9 prepare.1
  4.1 2.2 %collective-permute-start.7 = (bf16[320,512]{1,0:T(8,128)(2,1)S(1)}, bf16[320,512]{1,0:T(8,128)(2,1)S(1)}, u32[]{:S(2)}, u32[]{:S(2)}) collective-permute-start(bf16[320,512]{1,0:T(8,128)(2,1)S(1)} %get-tuple-element.35), channel_id=1, source_target_pairs={{0,1},{1,2},{2,3},{3,0},{4,5},{5,6},{6,7},{7,4},{8,9},{9,10},{10,1... | collective-permute-start | bytes 983048 | tf_op jit(solution)/shard_map/ppermute | solution.py:29
  6.3 2.6 %collective-permute-start.8 = (bf16[320,512]{1,0:T(8,128)(2,1)S(1)}, bf16[320,512]{1,0:T(8,128)(2,1)S(1)}, u32[]{:S(2)}, u32[]{:S(2)}) collective-permute-start(bf16[320,512]{1,0:T(8,128)(2,1)S(1)} %get-tuple-element.36), channel_id=1, source_target_pairs={{0,2},{1,3},{2,0},{3,1},{4,6},{5,7},{6,4},{7,5},{8,10},{9,11},{10,... | collective-permute-start | bytes 983048 | tf_op jit(solution)/shard_map/ppermute | solution.py:29
  8.9 1.1 collective-permute-start.9
  10.0 1.6 collective-permute-start
  11.6 3.3 %collective-permute-start.1 = (bf16[128,1280]{1,0:T(8,128)(2,1)S(1)}, bf16[128,1280]{1,0:T(8,128)(2,1)S(1)}, u32[]{:S(2)}, u32[]{:S(2)}) collective-permute-start(bf16[128,1280]{1,0:T(8,128)(2,1)S(1)} %get-tuple-element.32), channel_id=1, source_target_pairs={{0,64},{1,65},{2,66},{3,67},{4,68},{5,69},{6,70},{7,71},{8,72},{9,... | collective-permute-start | bytes 983048 | tf_op jit(solution)/shard_map/ppermute | solution.py:29
  15.0 3.7 %collective-permute-start.2 = (bf16[128,1280]{1,0:T(8,128)(2,1)S(1)}, bf16[128,1280]{1,0:T(8,128)(2,1)S(1)}, u32[]{:S(2)}, u32[]{:S(2)}) collective-permute-start(bf16[128,1280]{1,0:T(8,128)(2,1)S(1)} %get-tuple-element.33), channel_id=1, source_target_pairs={{0,96},{1,97},{2,98},{3,99},{4,100},{5,101},{6,102},{7,103},{8,104... | collective-permute-start | bytes 983048 | tf_op jit(solution)/shard_map/ppermute | solution.py:29
  18.7 4.3 %collective-permute-done.8 = bf16[320,512]{1,0:T(8,128)(2,1)S(1)} collective-permute-done((bf16[320,512]{1,0:T(8,128)(2,1)S(1)}, bf16[320,512]{1,0:T(8,128)(2,1)S(1)}, u32[]{:S(2)}, u32[]{:S(2)}) %collective-permute-start.8) | collective-permute-done | bytes 327712 | tf_op jit(solution)/shard_map/ppermute | solution.py:29
  23.1 3.8 %collective-permute-start.10 = (bf16[1280,512]{1,0:T(8,128)(2,1)S(1)}, bf16[1280,512]{1,0:T(8,128)(2,1)S(1)}, u32[]{:S(2)}, u32[]{:S(2)}) collective-permute-start(bf16[1280,512]{1,0:T(8,128)(2,1)S(1)} %constant_dynamic-update-slice_fusion.4.z0.refs_5_), channel_id=1, source_target_pairs={{0,96},{1,97},{2,98},{3,99},{4,100},{5,101},{6,102},{7,103},{8,104... | collective-permute-start | bytes 3932168 | tf_op jit(solution)/shard_map/ppermute | solution.py:29
  27.0 1.2 collective-permute-done.1
  28.3 2.5 %collective-permute-start.3 = (bf16[512,1280]{1,0:T(8,128)(2,1)S(1)}, bf16[512,1280]{1,0:T(8,128)(2,1)S(1)}, u32[]{:S(2)}, u32[]{:S(2)}) collective-permute-start(bf16[512,1280]{1,0:T(8,128)(2,1)S(1)} %constant_dynamic-update-slice_fusion.x0.refs_0_), channel_id=1, source_target_pairs={{0,12},{1,13},{2,14},{3,15},{4,0},{5,1},{6,2},{7,3},{8,4},{9,5},{1... | collective-permute-start | bytes 3932168 | tf_op jit(solution)/shard_map/ppermute | solution.py:29
  30.8 25.0 %collective-permute-done.10.zp.refs_6_ = bf16[1280,512]{1,0:T(8,128)(2,1)S(1)} collective-permute-done((bf16[1280,512]{1,0:T(8,128)(2,1)S(1)}, bf16[1280,512]{1,0:T(8,128)(2,1)S(1)}, u32[]{:S(2)}, u32[]{:S(2)}) %collective-permute-start.10) | collective-permute-done | bytes 1310752 | tf_op jit(solution)/shard_map/ppermute | solution.py:29
  55.8 3.5 %collective-permute-start.12 = (bf16[640,512]{1,0:T(8,128)(2,1)S(1)}, bf16[640,512]{1,0:T(8,128)(2,1)S(1)}, u32[]{:S(2)}, u32[]{:S(2)}) collective-permute-start(bf16[640,512]{1,0:T(8,128)(2,1)S(1)} %slice.18), channel_id=1, source_target_pairs={{0,96},{1,97},{2,98},{3,99},{4,100},{5,101},{6,102},{7,103},{8,104... | collective-permute-start | bytes 1966088 | tf_op jit(solution)/shard_map/ppermute | solution.py:29
  59.8 2.5 %collective-permute-start.5 = (bf16[256,1280]{1,0:T(8,128)(2,1)S(1)}, bf16[256,1280]{1,0:T(8,128)(2,1)S(1)}, u32[]{:S(2)}, u32[]{:S(2)}) collective-permute-start(bf16[256,1280]{1,0:T(8,128)(2,1)S(1)} %slice.16), channel_id=1, source_target_pairs={{0,12},{1,13},{2,14},{3,15},{4,0},{5,1},{6,2},{7,3},{8,4},{9,5},{1... | collective-permute-start | bytes 1966088 | tf_op jit(solution)/shard_map/ppermute | solution.py:29
  62.5 4.4 %near_product.1 = (f32[320,1280]{1,0:T(8,128)S(1)}, f32[320,1280]{1,0:T(8,128)S(1)}, f32[320,1280]{1,0:T(8,128)S(1)}, f32[320,1280]{1,0:T(8,128)S(1)}) custom-call(bf16[512,1280]{1,0:T(8,128)(2,1)S(1)} %constant_dynamic-update-slice_fusion.x0.refs_0_, bf16[512,1280]{1,0:T(8,128)(2,1)S(1)} %collective-permute-done.3.xp.refs_1_, ...), custom_call_target="tpu_custom_call" | custom-call | tf_op jit(solution)/shard_map/near_product/pallas_call | solution.py:98
  66.9 7.4 %collective-permute-done.12.refs_8_ = bf16[640,512]{1,0:T(8,128)(2,1)S(1)} collective-permute-done((bf16[640,512]{1,0:T(8,128)(2,1)S(1)}, bf16[640,512]{1,0:T(8,128)(2,1)S(1)}, u32[]{:S(2)}, u32[]{:S(2)}) %collective-permute-start.12) | collective-permute-done | bytes 655392 | tf_op jit(solution)/shard_map/ppermute | solution.py:29
  74.3 0.9 collective-permute-done.13.refs_9_
  75.3 3.2 %collective-permute-done.6.refs_4_ = bf16[256,1280]{1,0:T(8,128)(2,1)S(1)} collective-permute-done((bf16[256,1280]{1,0:T(8,128)(2,1)S(1)}, bf16[256,1280]{1,0:T(8,128)(2,1)S(1)}, u32[]{:S(2)}, u32[]{:S(2)}) %collective-permute-start.6) | collective-permute-done | bytes 655392 | tf_op jit(solution)/shard_map/ppermute | solution.py:29
  78.4 3.5 %far_product.1 = (f32[320,640]{1,0:T(8,128)S(1)}, f32[320,640]{1,0:T(8,128)S(1)}, f32[320,640]{1,0:T(8,128)S(1)}, f32[320,640]{1,0:T(8,128)S(1)}, f32[320,640]{1...) custom-call(bf16[512,1280]{1,0:T(8,128)(2,1)S(1)} %constant_dynamic-update-slice_fusion.x0.r, ...), custom_call_target="tpu_custom_call" | custom-call | tf_op jit(solution)/shard_map/far_product/pallas_call | solution.py:131
  82.0 2.7 %collective-permute-start.19 = (f32[320,640]{1,0:T(8,128)S(1)}, f32[320,640]{1,0:T(8,128)S(1)}, u32[]{:S(2)}, u32[]{:S(2)}) collective-permute-start(f32[320,640]{1,0:T(8,128)S(1)} %get-tuple-element.49), channel_id=1, source_target_pairs={{0,16},{1,17},{2,18},{3,19},{4,20},{5,21},{6,22},{7,23},{8,24},{9,... | collective-permute-start | bytes 2457608 | tf_op jit(solution)/shard_map/ppermute | solution.py:29
  85.3 1.4 collective-permute-done.19
  87.9 1.6 collective-permute-start.18
  89.7 1.3 collective-permute-start.16
  92.0 15.6 %collective-permute-done.20.g3 = f32[320,640]{1,0:T(8,128)S(1)} collective-permute-done((f32[320,640]{1,0:T(8,128)S(1)}, f32[320,640]{1,0:T(8,128)S(1)}, u32[]{:S(2)}, u32[]{:S(2)}) %collective-permute-start.20) | collective-permute-done | bytes 819232 | tf_op jit(solution)/shard_map/ppermute | solution.py:29
  107.6 17.4 %collective-permute-done.18.g2 = f32[320,640]{1,0:T(8,128)S(1)} collective-permute-done((f32[320,640]{1,0:T(8,128)S(1)}, f32[320,640]{1,0:T(8,128)S(1)}, u32[]{:S(2)}, u32[]{:S(2)}) %collective-permute-start.18) | collective-permute-done | bytes 819232 | tf_op jit(solution)/shard_map/ppermute | solution.py:29
  125.5 2.6 %update.1 = (f32[320,640]{1,0:T(8,128)}, f32[320,640]{1,0:T(8,128)}, f32[320,640]{1,0:T(8,128)S(1)}, f32[16,128]{1,0:T(8,128)S(1)}) custom-call(f32[320,640]{1,0:T(8,128)S(1)} %add.42.g0, f32[320,640]{1,0:T(8,128)S(1)} %collective-permute-done.16.g1, f32[320,640]{1,0:T(8,128)S(1)} %collective-permute-done.18.g2, f32[320,640]{1,0:T(8,128)S(1)} %collective-permute-done.20.g3, ...), custom_call_target="tpu_custom_call" | custom-call | tf_op jit(solution)/shard_map/update/pallas_call | solution.py:199
  128.1 1.5 collective-permute-start.21
  129.6 0.8 collective-permute-done.21
  130.4 1.1 collective-permute-start.23
  131.5 1.6 collective-permute-start.24
  133.1 1.0 collective-permute-done.22
  135.1 1.1 collective-permute-start.25
  136.2 2.5 %collective-permute-start.26 = (f32[16,128]{1,0:T(8,128)S(1)}, f32[16,128]{1,0:T(8,128)S(1)}, u32[]{:S(2)}, u32[]{:S(2)}) collective-permute-start(f32[16,128]{1,0:T(8,128)S(1)} %add_add_fusion.2), channel_id=1, source_target_pairs={{0,2},{1,3},{2,0},{3,1},{4,6},{5,7},{6,4},{7,5},{8,10},{9,11},{10,... | collective-permute-start | bytes 24584 | tf_op jit(solution)/shard_map/ppermute | solution.py:29
  140.2 0.9 collective-permute-done.27
  141.2 2.7 %collective-permute-start.28 = (f32[16,128]{1,0:T(8,128)S(1)}, f32[16,128]{1,0:T(8,128)S(1)}, u32[]{:S(2)}, u32[]{:S(2)}) collective-permute-start(f32[16,128]{1,0:T(8,128)S(1)} %add_add_fusion.1), channel_id=1, source_target_pairs={{0,32},{1,33},{2,34},{3,35},{4,36},{5,37},{6,38},{7,39},{8,40},{9,... | collective-permute-start | bytes 24584 | tf_op jit(solution)/shard_map/ppermute | solution.py:29
  143.9 1.2 collective-permute-start.29
  145.0 1.3 collective-permute-start.30
  147.9 1.1 step.1
  149.0 2.2 %collective-permute-start.32 = (bf16[320,640]{1,0:T(8,128)(2,1)S(1)}, bf16[320,640]{1,0:T(8,128)(2,1)S(1)}, u32[]{:S(2)}, u32[]{:S(2)}) collective-permute-start(bf16[320,640]{1,0:T(8,128)(2,1)S(1)} %get-tuple-element.55.refs_0_), channel_id=1, source_target_pairs={{0,96},{1,97},{2,98},{3,99},{4,100},{5,101},{6,102},{7,103},{8,104... | collective-permute-start | bytes 1228808 | tf_op jit(solution)/shard_map/ppermute | solution.py:29
  151.8 5.4 %collective-permute-start.31 = (bf16[320,640]{1,0:T(8,128)(2,1)S(1)}, bf16[320,640]{1,0:T(8,128)(2,1)S(1)}, u32[]{:S(2)}, u32[]{:S(2)}) collective-permute-start(bf16[320,640]{1,0:T(8,128)(2,1)S(1)} %get-tuple-element.55.refs_0_), channel_id=1, source_target_pairs={{0,16},{1,17},{2,18},{3,19},{4,20},{5,21},{6,22},{7,23},{8,24},{9,... | collective-permute-start | bytes 1228808 | tf_op jit(solution)/shard_map/ppermute | solution.py:29
  157.2 1.1 collective-permute-done.32.refs_2_
  158.3 11.4 %collective-permute-start.33 = (bf16[320,640]{1,0:T(8,128)(2,1)S(1)}, bf16[320,640]{1,0:T(8,128)(2,1)S(1)}, u32[]{:S(2)}, u32[]{:S(2)}) collective-permute-start(bf16[320,640]{1,0:T(8,128)(2,1)S(1)} %collective-permute-done.32.refs_2_), channel_id=1, source_target_pairs={{0,16},{1,17},{2,18},{3,19},{4,20},{5,21},{6,22},{7,23},{8,24},{9,... | collective-permute-start | bytes 1228808 | tf_op jit(solution)/shard_map/ppermute | solution.py:29
  169.7 1.9 %collective-permute-done.36.refs_6_ = bf16[320,640]{1,0:T(8,128)(2,1)S(1)} collective-permute-done((bf16[320,640]{1,0:T(8,128)(2,1)S(1)}, bf16[320,640]{1,0:T(8,128)(2,1)S(1)}, u32[]{:S(2)}, u32[]{:S(2)}) %collective-permute-start.36) | collective-permute-done | bytes 409632 | tf_op jit(solution)/shard_map/ppermute | solution.py:29
  171.6 1.4 collective-permute-start.37
  173.1 1.4 collective-permute-done.37.refs_7_
  174.4 1.8 %assemble.1 = bf16[320,5120]{1,0:T(8,128)(2,1)} custom-call(bf16[320,640]{1,0:T(8,128)(2,1)S(1)} %get-tuple-element.55.refs_0_, bf16[320,640]{1,0:T(8,128)(2,1)S(1)} %collective-permute-done.31.refs_1_, bf16[320,640]{1,0:T(8,128)(2,1)S(1)} %collective-permute-done.32.refs_2_, bf16[320,640]{1,0:T(8,128)(2,1)S(1)} %collective-permute-done.33.refs_3_, ...), custom_call_target="tpu_custom_call" | custom-call | tf_op jit(solution)/shard_map/assemble/pallas_call | solution.py:268
  (68 shorter events, 6.9 us)
Async XLA Ops:
  0.6 1.3 copy-start.1
  1.9 1.3 copy-start.2
  4.1 10.9 %collective-permute-start.7 = (bf16[320,512]{1,0:T(8,128)(2,1)S(1)}, bf16[320,512]{1,0:T(8,128)(2,1)S(1)}, u32[]{:S(2)}, u32[]{:S(2)}) collective-permute-start(bf16[320,512]{1,0:T(8,128)(2,1)S(1)} %get-tuple-element.35), channel_id=1, source_target_pairs={{0,1},{1,2},{2,3},{3,0},{4,5},{5,6},{6,7},{7,4},{8,9},{9,10},{10,1... | collective-permute-start | bytes 983048 | tf_op jit(solution)/shard_map/ppermute | solution.py:29
  6.3 16.8 %collective-permute-start.8 = (bf16[320,512]{1,0:T(8,128)(2,1)S(1)}, bf16[320,512]{1,0:T(8,128)(2,1)S(1)}, u32[]{:S(2)}, u32[]{:S(2)}) collective-permute-start(bf16[320,512]{1,0:T(8,128)(2,1)S(1)} %get-tuple-element.36), channel_id=1, source_target_pairs={{0,2},{1,3},{2,0},{3,1},{4,6},{5,7},{6,4},{7,5},{8,10},{9,11},{10,... | collective-permute-start | bytes 983048 | tf_op jit(solution)/shard_map/ppermute | solution.py:29
  8.9 14.2 %collective-permute-start.9 = (bf16[320,512]{1,0:T(8,128)(2,1)S(1)}, bf16[320,512]{1,0:T(8,128)(2,1)S(1)}, u32[]{:S(2)}, u32[]{:S(2)}) collective-permute-start(bf16[320,512]{1,0:T(8,128)(2,1)S(1)} %get-tuple-element.37), channel_id=1, source_target_pairs={{0,3},{1,0},{2,1},{3,2},{4,7},{5,4},{6,5},{7,6},{8,11},{9,8},{10,9... | collective-permute-start | bytes 983048 | tf_op jit(solution)/shard_map/ppermute | solution.py:29
  10.0 17.0 %collective-permute-start = (bf16[128,1280]{1,0:T(8,128)(2,1)S(1)}, bf16[128,1280]{1,0:T(8,128)(2,1)S(1)}, u32[]{:S(2)}, u32[]{:S(2)}) collective-permute-start(bf16[128,1280]{1,0:T(8,128)(2,1)S(1)} %get-tuple-element.31), channel_id=1, source_target_pairs={{0,32},{1,33},{2,34},{3,35},{4,36},{5,37},{6,38},{7,39},{8,40},{9,... | collective-permute-start | bytes 983048 | tf_op jit(solution)/shard_map/ppermute | solution.py:29
  11.6 16.5 %collective-permute-start.1 = (bf16[128,1280]{1,0:T(8,128)(2,1)S(1)}, bf16[128,1280]{1,0:T(8,128)(2,1)S(1)}, u32[]{:S(2)}, u32[]{:S(2)}) collective-permute-start(bf16[128,1280]{1,0:T(8,128)(2,1)S(1)} %get-tuple-element.32), channel_id=1, source_target_pairs={{0,64},{1,65},{2,66},{3,67},{4,68},{5,69},{6,70},{7,71},{8,72},{9,... | collective-permute-start | bytes 983048 | tf_op jit(solution)/shard_map/ppermute | solution.py:29
  15.0 13.2 %collective-permute-start.2 = (bf16[128,1280]{1,0:T(8,128)(2,1)S(1)}, bf16[128,1280]{1,0:T(8,128)(2,1)S(1)}, u32[]{:S(2)}, u32[]{:S(2)}) collective-permute-start(bf16[128,1280]{1,0:T(8,128)(2,1)S(1)} %get-tuple-element.33), channel_id=1, source_target_pairs={{0,96},{1,97},{2,98},{3,99},{4,100},{5,101},{6,102},{7,103},{8,104... | collective-permute-start | bytes 983048 | tf_op jit(solution)/shard_map/ppermute | solution.py:29
  23.1 32.6 %collective-permute-start.10 = (bf16[1280,512]{1,0:T(8,128)(2,1)S(1)}, bf16[1280,512]{1,0:T(8,128)(2,1)S(1)}, u32[]{:S(2)}, u32[]{:S(2)}) collective-permute-start(bf16[1280,512]{1,0:T(8,128)(2,1)S(1)} %constant_dynamic-update-slice_fusion.4.z0.refs_5_), channel_id=1, source_target_pairs={{0,96},{1,97},{2,98},{3,99},{4,100},{5,101},{6,102},{7,103},{8,104... | collective-permute-start | bytes 3932168 | tf_op jit(solution)/shard_map/ppermute | solution.py:29
  27.0 32.3 %collective-permute-start.11 = (bf16[1280,512]{1,0:T(8,128)(2,1)S(1)}, bf16[1280,512]{1,0:T(8,128)(2,1)S(1)}, u32[]{:S(2)}, u32[]{:S(2)}) collective-permute-start(bf16[1280,512]{1,0:T(8,128)(2,1)S(1)} %constant_dynamic-update-slice_fusion.4.z0.refs_5_), channel_id=1, source_target_pairs={{0,32},{1,33},{2,34},{3,35},{4,36},{5,37},{6,38},{7,39},{8,40},{9,... | collective-permute-start | bytes 3932168 | tf_op jit(solution)/shard_map/ppermute | solution.py:29
  28.3 31.5 %collective-permute-start.3 = (bf16[512,1280]{1,0:T(8,128)(2,1)S(1)}, bf16[512,1280]{1,0:T(8,128)(2,1)S(1)}, u32[]{:S(2)}, u32[]{:S(2)}) collective-permute-start(bf16[512,1280]{1,0:T(8,128)(2,1)S(1)} %constant_dynamic-update-slice_fusion.x0.refs_0_), channel_id=1, source_target_pairs={{0,12},{1,13},{2,14},{3,15},{4,0},{5,1},{6,2},{7,3},{8,4},{9,5},{1... | collective-permute-start | bytes 3932168 | tf_op jit(solution)/shard_map/ppermute | solution.py:29
  30.8 31.6 %collective-permute-start.4 = (bf16[512,1280]{1,0:T(8,128)(2,1)S(1)}, bf16[512,1280]{1,0:T(8,128)(2,1)S(1)}, u32[]{:S(2)}, u32[]{:S(2)}) collective-permute-start(bf16[512,1280]{1,0:T(8,128)(2,1)S(1)} %constant_dynamic-update-slice_fusion.x0.refs_0_), channel_id=1, source_target_pairs={{0,4},{1,5},{2,6},{3,7},{4,8},{5,9},{6,10},{7,11},{8,12},{9,13},{1... | collective-permute-start | bytes 3932168 | tf_op jit(solution)/shard_map/ppermute | solution.py:29
  55.8 18.5 %collective-permute-start.12 = (bf16[640,512]{1,0:T(8,128)(2,1)S(1)}, bf16[640,512]{1,0:T(8,128)(2,1)S(1)}, u32[]{:S(2)}, u32[]{:S(2)}) collective-permute-start(bf16[640,512]{1,0:T(8,128)(2,1)S(1)} %slice.18), channel_id=1, source_target_pairs={{0,96},{1,97},{2,98},{3,99},{4,100},{5,101},{6,102},{7,103},{8,104... | collective-permute-start | bytes 1966088 | tf_op jit(solution)/shard_map/ppermute | solution.py:29
  59.4 15.9 %collective-permute-start.13 = (bf16[640,512]{1,0:T(8,128)(2,1)S(1)}, bf16[640,512]{1,0:T(8,128)(2,1)S(1)}, u32[]{:S(2)}, u32[]{:S(2)}) collective-permute-start(bf16[640,512]{1,0:T(8,128)(2,1)S(1)} %slice.19), channel_id=1, source_target_pairs={{0,32},{1,33},{2,34},{3,35},{4,36},{5,37},{6,38},{7,39},{8,40},{9,... | collective-permute-start | bytes 1966088 | tf_op jit(solution)/shard_map/ppermute | solution.py:29
  59.8 15.4 %collective-permute-start.5 = (bf16[256,1280]{1,0:T(8,128)(2,1)S(1)}, bf16[256,1280]{1,0:T(8,128)(2,1)S(1)}, u32[]{:S(2)}, u32[]{:S(2)}) collective-permute-start(bf16[256,1280]{1,0:T(8,128)(2,1)S(1)} %slice.16), channel_id=1, source_target_pairs={{0,12},{1,13},{2,14},{3,15},{4,0},{5,1},{6,2},{7,3},{8,4},{9,5},{1... | collective-permute-start | bytes 1966088 | tf_op jit(solution)/shard_map/ppermute | solution.py:29
  62.4 16.0 %collective-permute-start.6 = (bf16[256,1280]{1,0:T(8,128)(2,1)S(1)}, bf16[256,1280]{1,0:T(8,128)(2,1)S(1)}, u32[]{:S(2)}, u32[]{:S(2)}) collective-permute-start(bf16[256,1280]{1,0:T(8,128)(2,1)S(1)} %slice.17), channel_id=1, source_target_pairs={{0,4},{1,5},{2,6},{3,7},{4,8},{5,9},{6,10},{7,11},{8,12},{9,13},{1... | collective-permute-start | bytes 1966088 | tf_op jit(solution)/shard_map/ppermute | solution.py:29
  82.0 4.7 %collective-permute-start.19 = (f32[320,640]{1,0:T(8,128)S(1)}, f32[320,640]{1,0:T(8,128)S(1)}, u32[]{:S(2)}, u32[]{:S(2)}) collective-permute-start(f32[320,640]{1,0:T(8,128)S(1)} %get-tuple-element.49), channel_id=1, source_target_pairs={{0,16},{1,17},{2,18},{3,19},{4,20},{5,21},{6,22},{7,23},{8,24},{9,... | collective-permute-start | bytes 2457608 | tf_op jit(solution)/shard_map/ppermute | solution.py:29
  84.7 3.1 %collective-permute-start.17 = (f32[320,640]{1,0:T(8,128)S(1)}, f32[320,640]{1,0:T(8,128)S(1)}, u32[]{:S(2)}, u32[]{:S(2)}) collective-permute-start(f32[320,640]{1,0:T(8,128)S(1)} %get-tuple-element.47), channel_id=1, source_target_pairs={{0,16},{1,17},{2,18},{3,19},{4,20},{5,21},{6,22},{7,23},{8,24},{9,... | collective-permute-start | bytes 2457608 | tf_op jit(solution)/shard_map/ppermute | solution.py:29
  84.8 4.8 %collective-permute-start.15 = (f32[320,640]{1,0:T(8,128)S(1)}, f32[320,640]{1,0:T(8,128)S(1)}, u32[]{:S(2)}, u32[]{:S(2)}) collective-permute-start(f32[320,640]{1,0:T(8,128)S(1)} %get-tuple-element.45), channel_id=1, source_target_pairs={{0,16},{1,17},{2,18},{3,19},{4,20},{5,21},{6,22},{7,23},{8,24},{9,... | collective-permute-start | bytes 2457608 | tf_op jit(solution)/shard_map/ppermute | solution.py:29
  85.2 6.7 %collective-permute-start.14 = (f32[320,640]{1,0:T(8,128)S(1)}, f32[320,640]{1,0:T(8,128)S(1)}, u32[]{:S(2)}, u32[]{:S(2)}) collective-permute-start(f32[320,640]{1,0:T(8,128)S(1)} %get-tuple-element.43), channel_id=1, source_target_pairs={{0,16},{1,17},{2,18},{3,19},{4,20},{5,21},{6,22},{7,23},{8,24},{9,... | collective-permute-start | bytes 2457608 | tf_op jit(solution)/shard_map/ppermute | solution.py:29
  86.7 20.8 %collective-permute-start.20 = (f32[320,640]{1,0:T(8,128)S(1)}, f32[320,640]{1,0:T(8,128)S(1)}, u32[]{:S(2)}, u32[]{:S(2)}) collective-permute-start(f32[320,640]{1,0:T(8,128)S(1)} %add.45), channel_id=1, source_target_pairs={{0,1},{1,2},{2,3},{3,0},{4,5},{5,6},{6,7},{7,4},{8,9},{9,10},{10,1... | collective-permute-start | bytes 2457608 | tf_op jit(solution)/shard_map/ppermute | solution.py:29
  87.9 37.1 %collective-permute-start.18 = (f32[320,640]{1,0:T(8,128)S(1)}, f32[320,640]{1,0:T(8,128)S(1)}, u32[]{:S(2)}, u32[]{:S(2)}) collective-permute-start(f32[320,640]{1,0:T(8,128)S(1)} %add.44), channel_id=1, source_target_pairs={{0,2},{1,3},{2,0},{3,1},{4,6},{5,7},{6,4},{7,5},{8,10},{9,11},{10,... | collective-permute-start | bytes 2457608 | tf_op jit(solution)/shard_map/ppermute | solution.py:29
  89.6 35.9 %copy-start = (f32[640,320]{0,1:T(8,128)S(1)}, f32[640,320]{0,1:T(8,128)}, u32[]{:S(2)}) copy-start(f32[640,320]{0,1:T(8,128)} %param.10) | copy-start | bytes 2457604
  89.7 35.8 %copy-start.3 = (f32[640,320]{0,1:T(8,128)S(1)}, f32[640,320]{0,1:T(8,128)}, u32[]{:S(2)}) copy-start(f32[640,320]{0,1:T(8,128)} %param.11) | copy-start | bytes 2457604
  89.7 35.8 %copy-start.4 = (f32[640,320]{0,1:T(8,128)S(1)}, f32[640,320]{0,1:T(8,128)}, u32[]{:S(2)}) copy-start(f32[640,320]{0,1:T(8,128)} %param.12) | copy-start | bytes 2457604
  89.7 35.8 %collective-permute-start.16 = (f32[320,640]{1,0:T(8,128)S(1)}, f32[320,640]{1,0:T(8,128)S(1)}, u32[]{:S(2)}, u32[]{:S(2)}) collective-permute-start(f32[320,640]{1,0:T(8,128)S(1)} %add.43), channel_id=1, source_target_pairs={{0,3},{1,0},{2,1},{3,2},{4,7},{5,4},{6,5},{7,6},{8,11},{9,8},{10,9... | collective-permute-start | bytes 2457608 | tf_op jit(solution)/shard_map/ppermute | solution.py:29
  125.5 20.8 %copy-start.5 = (f32[8]{0:T(128)S(1)}, f32[8]{0:T(128)}, u32[]{:S(2)}) copy-start(f32[8]{0:T(128)} %param.15) | copy-start | bytes 100
  128.1 2.4 %collective-permute-start.21 = (f32[16,128]{1,0:T(8,128)S(1)}, f32[16,128]{1,0:T(8,128)S(1)}, u32[]{:S(2)}, u32[]{:S(2)}) collective-permute-start(f32[16,128]{1,0:T(8,128)S(1)} %get-tuple-element.51), channel_id=1, source_target_pairs={{0,16},{1,17},{2,18},{3,19},{4,20},{5,21},{6,22},{7,23},{8,24},{9,... | collective-permute-start | bytes 24584 | tf_op jit(solution)/shard_map/ppermute | solution.py:29
  130.4 3.7 %collective-permute-start.22 = (f32[16,128]{1,0:T(8,128)S(1)}, f32[16,128]{1,0:T(8,128)S(1)}, u32[]{:S(2)}, u32[]{:S(2)}) collective-permute-start(f32[16,128]{1,0:T(8,128)S(1)} %add.46), channel_id=1, source_target_pairs={{0,4},{1,5},{2,6},{3,7},{4,8},{5,9},{6,10},{7,11},{8,12},{9,13},{1... | collective-permute-start | bytes 24584 | tf_op jit(solution)/shard_map/ppermute | solution.py:29
  130.4 4.0 %collective-permute-start.23 = (f32[16,128]{1,0:T(8,128)S(1)}, f32[16,128]{1,0:T(8,128)S(1)}, u32[]{:S(2)}, u32[]{:S(2)}) collective-permute-start(f32[16,128]{1,0:T(8,128)S(1)} %add.46), channel_id=1, source_target_pairs={{0,8},{1,9},{2,10},{3,11},{4,12},{5,13},{6,14},{7,15},{8,0},{9,1},... | collective-permute-start | bytes 24584 | tf_op jit(solution)/shard_map/ppermute | solution.py:29
  131.5 3.6 %collective-permute-start.24 = (f32[16,128]{1,0:T(8,128)S(1)}, f32[16,128]{1,0:T(8,128)S(1)}, u32[]{:S(2)}, u32[]{:S(2)}) collective-permute-start(f32[16,128]{1,0:T(8,128)S(1)} %add.46), channel_id=1, source_target_pairs={{0,12},{1,13},{2,14},{3,15},{4,0},{5,1},{6,2},{7,3},{8,4},{9,5},{1... | collective-permute-start | bytes 24584 | tf_op jit(solution)/shard_map/ppermute | solution.py:29
  135.1 4.5 %collective-permute-start.25 = (f32[16,128]{1,0:T(8,128)S(1)}, f32[16,128]{1,0:T(8,128)S(1)}, u32[]{:S(2)}, u32[]{:S(2)}) collective-permute-start(f32[16,128]{1,0:T(8,128)S(1)} %add_add_fusion.2), channel_id=1, source_target_pairs={{0,1},{1,2},{2,3},{3,0},{4,5},{5,6},{6,7},{7,4},{8,9},{9,10},{10,1... | collective-permute-start | bytes 24584 | tf_op jit(solution)/shard_map/ppermute | solution.py:29
  136.2 4.0 %collective-permute-start.26 = (f32[16,128]{1,0:T(8,128)S(1)}, f32[16,128]{1,0:T(8,128)S(1)}, u32[]{:S(2)}, u32[]{:S(2)}) collective-permute-start(f32[16,128]{1,0:T(8,128)S(1)} %add_add_fusion.2), channel_id=1, source_target_pairs={{0,2},{1,3},{2,0},{3,1},{4,6},{5,7},{6,4},{7,5},{8,10},{9,11},{10,... | collective-permute-start | bytes 24584 | tf_op jit(solution)/shard_map/ppermute | solution.py:29
  138.7 2.5 %collective-permute-start.27 = (f32[16,128]{1,0:T(8,128)S(1)}, f32[16,128]{1,0:T(8,128)S(1)}, u32[]{:S(2)}, u32[]{:S(2)}) collective-permute-start(f32[16,128]{1,0:T(8,128)S(1)} %add_add_fusion.2), channel_id=1, source_target_pairs={{0,3},{1,0},{2,1},{3,2},{4,7},{5,4},{6,5},{7,6},{8,11},{9,8},{10,9... | collective-permute-start | bytes 24584 | tf_op jit(solution)/shard_map/ppermute | solution.py:29
  141.2 6.4 %collective-permute-start.28 = (f32[16,128]{1,0:T(8,128)S(1)}, f32[16,128]{1,0:T(8,128)S(1)}, u32[]{:S(2)}, u32[]{:S(2)}) collective-permute-start(f32[16,128]{1,0:T(8,128)S(1)} %add_add_fusion.1), channel_id=1, source_target_pairs={{0,32},{1,33},{2,34},{3,35},{4,36},{5,37},{6,38},{7,39},{8,40},{9,... | collective-permute-start | bytes 24584 | tf_op jit(solution)/shard_map/ppermute | solution.py:29
  143.9 4.0 %collective-permute-start.29 = (f32[16,128]{1,0:T(8,128)S(1)}, f32[16,128]{1,0:T(8,128)S(1)}, u32[]{:S(2)}, u32[]{:S(2)}) collective-permute-start(f32[16,128]{1,0:T(8,128)S(1)} %add_add_fusion.1), channel_id=1, source_target_pairs={{0,64},{1,65},{2,66},{3,67},{4,68},{5,69},{6,70},{7,71},{8,72},{9,... | collective-permute-start | bytes 24584 | tf_op jit(solution)/shard_map/ppermute | solution.py:29
  145.0 2.9 %collective-permute-start.30 = (f32[16,128]{1,0:T(8,128)S(1)}, f32[16,128]{1,0:T(8,128)S(1)}, u32[]{:S(2)}, u32[]{:S(2)}) collective-permute-start(f32[16,128]{1,0:T(8,128)S(1)} %add_add_fusion.1), channel_id=1, source_target_pairs={{0,96},{1,97},{2,98},{3,99},{4,100},{5,101},{6,102},{7,103},{8,104... | collective-permute-start | bytes 24584 | tf_op jit(solution)/shard_map/ppermute | solution.py:29
  149.0 9.2 %collective-permute-start.32 = (bf16[320,640]{1,0:T(8,128)(2,1)S(1)}, bf16[320,640]{1,0:T(8,128)(2,1)S(1)}, u32[]{:S(2)}, u32[]{:S(2)}) collective-permute-start(bf16[320,640]{1,0:T(8,128)(2,1)S(1)} %get-tuple-element.55.refs_0_), channel_id=1, source_target_pairs={{0,96},{1,97},{2,98},{3,99},{4,100},{5,101},{6,102},{7,103},{8,104... | collective-permute-start | bytes 1228808 | tf_op jit(solution)/shard_map/ppermute | solution.py:29
  151.2 18.5 %collective-permute-start.34 = (bf16[320,640]{1,0:T(8,128)(2,1)S(1)}, bf16[320,640]{1,0:T(8,128)(2,1)S(1)}, u32[]{:S(2)}, u32[]{:S(2)}) collective-permute-start(bf16[320,640]{1,0:T(8,128)(2,1)S(1)} %get-tuple-element.55.refs_0_), channel_id=1, source_target_pairs={{0,64},{1,65},{2,66},{3,67},{4,68},{5,69},{6,70},{7,71},{8,72},{9,... | collective-permute-start | bytes 1228808 | tf_op jit(solution)/shard_map/ppermute | solution.py:29
  151.2 20.4 %collective-permute-start.36 = (bf16[320,640]{1,0:T(8,128)(2,1)S(1)}, bf16[320,640]{1,0:T(8,128)(2,1)S(1)}, u32[]{:S(2)}, u32[]{:S(2)}) collective-permute-start(bf16[320,640]{1,0:T(8,128)(2,1)S(1)} %get-tuple-element.55.refs_0_), channel_id=1, source_target_pairs={{0,32},{1,33},{2,34},{3,35},{4,36},{5,37},{6,38},{7,39},{8,40},{9,... | collective-permute-start | bytes 1228808 | tf_op jit(solution)/shard_map/ppermute | solution.py:29
  151.8 21.3 %collective-permute-start.31 = (bf16[320,640]{1,0:T(8,128)(2,1)S(1)}, bf16[320,640]{1,0:T(8,128)(2,1)S(1)}, u32[]{:S(2)}, u32[]{:S(2)}) collective-permute-start(bf16[320,640]{1,0:T(8,128)(2,1)S(1)} %get-tuple-element.55.refs_0_), channel_id=1, source_target_pairs={{0,16},{1,17},{2,18},{3,19},{4,20},{5,21},{6,22},{7,23},{8,24},{9,... | collective-permute-start | bytes 1228808 | tf_op jit(solution)/shard_map/ppermute | solution.py:29
  158.3 14.8 %collective-permute-start.33 = (bf16[320,640]{1,0:T(8,128)(2,1)S(1)}, bf16[320,640]{1,0:T(8,128)(2,1)S(1)}, u32[]{:S(2)}, u32[]{:S(2)}) collective-permute-start(bf16[320,640]{1,0:T(8,128)(2,1)S(1)} %collective-permute-done.32.refs_2_), channel_id=1, source_target_pairs={{0,16},{1,17},{2,18},{3,19},{4,20},{5,21},{6,22},{7,23},{8,24},{9,... | collective-permute-start | bytes 1228808 | tf_op jit(solution)/shard_map/ppermute | solution.py:29
  169.7 3.4 %collective-permute-start.35 = (bf16[320,640]{1,0:T(8,128)(2,1)S(1)}, bf16[320,640]{1,0:T(8,128)(2,1)S(1)}, u32[]{:S(2)}, u32[]{:S(2)}) collective-permute-start(bf16[320,640]{1,0:T(8,128)(2,1)S(1)} %collective-permute-done.34.refs_4_), channel_id=1, source_target_pairs={{0,16},{1,17},{2,18},{3,19},{4,20},{5,21},{6,22},{7,23},{8,24},{9,... | collective-permute-start | bytes 1228808 | tf_op jit(solution)/shard_map/ppermute | solution.py:29
  171.6 2.8 %collective-permute-start.37 = (bf16[320,640]{1,0:T(8,128)(2,1)S(1)}, bf16[320,640]{1,0:T(8,128)(2,1)S(1)}, u32[]{:S(2)}, u32[]{:S(2)}) collective-permute-start(bf16[320,640]{1,0:T(8,128)(2,1)S(1)} %collective-permute-done.36.refs_6_), channel_id=1, source_target_pairs={{0,16},{1,17},{2,18},{3,19},{4,20},{5,21},{6,22},{7,23},{8,24},{9,... | collective-permute-start | bytes 1228808 | tf_op jit(solution)/shard_map/ppermute | solution.py:29

commit v3 on v2

--- a/solution.py
+++ b/solution.py
@@ -35,19 +35,17 @@
     return d // 2, d % 2, m // 4, m % 4
 
 
-def prepare_kernel(act, cot, a0, a1, a2, a3, c0, c1, c2, c3, sems):
-    z, c, x, y = place()
-    copies = []
-    for kz, out in enumerate((a0, a1, a2, a3)):
-        first = lax.rem(z + kz, 4) * GROUP
-        for half, core in enumerate((c, 1 - c)):
-            start = pl.multiple_of(first + core * ROWS, 128)
-            copies.append((act.at[:, pl.ds(start, ROWS)], out.at[:, pl.ds(half * ROWS, ROWS)]))
-    for ky, out in enumerate((c0, c1, c2, c3)):
-        for dx in range(4):
-            start = (4 * lax.rem(x + dx, 4) + lax.rem(y + ky, 4)) * BLOCK
-            start = pl.multiple_of(start, 128)
-            copies.append((cot.at[:, pl.ds(start, BLOCK)], out.at[:, pl.ds(dx * BLOCK, BLOCK)]))
+HBM = pl.BlockSpec(memory_space=pltpu.HBM)
+ANY = pl.BlockSpec(memory_space=pl.ANY)
+VMEM = pl.BlockSpec(memory_space=pltpu.VMEM)
+SMEM = pl.BlockSpec(memory_space=pltpu.SMEM)
+
+
+def params(mib):
+    return pltpu.CompilerParams(vmem_limit_bytes=mib * 2**20)
+
+
+def copy_all(copies, sems):
     started = [pltpu.make_async_copy(src, dst, sems.at[k]) for k, (src, dst) in enumerate(copies)]
     for copy in started:
         copy.start()
@@ -55,27 +53,52 @@
         copy.wait()
 
 
-ANY = pl.BlockSpec(memory_space=pl.ANY)
-VMEM = pl.BlockSpec(memory_space=pltpu.VMEM)
-SMEM = pl.BlockSpec(memory_space=pltpu.SMEM)
-
-
-def params(mib):
-    return pltpu.CompilerParams(vmem_limit_bytes=mib * 2**20)
-
-
-def prepare(activations, cotangent_t):
-    bf16 = jnp.bfloat16
-    return pl.pallas_call(
-        prepare_kernel,
-        out_shape=[jax.ShapeDtypeStruct((BLOCK, GROUP), bf16)] * 4
-        + [jax.ShapeDtypeStruct((COLS, 4 * BLOCK), bf16)] * 4,
-        in_specs=[pl.BlockSpec(memory_space=pltpu.HBM)] * 2,
-        out_specs=[VMEM] * 8,
-        scratch_shapes=[pltpu.SemaphoreType.DMA((24,))],
+def rows_kernel(act, *refs):
+    outs, sems = refs[:4], refs[4]
+    z, c, x, y = place()
+    copies = []
+    for kz, out in enumerate(outs):
+        first = lax.rem(z + kz, 4) * GROUP
+        for half, core in enumerate((c, 1 - c)):
+            start = pl.multiple_of(first + core * ROWS, 128)
+            copies.append((act.at[:, pl.ds(start, ROWS)], out.at[:, pl.ds(half * ROWS, ROWS)]))
+    copy_all(copies, sems)
+
+
+def tokens_kernel(cot, first, *refs):
+    outs, sems = refs[:4], refs[4]
+    z, c, x, y = place()
+    copies = []
+    for ky, out in enumerate(outs):
+        for dx in range(4):
+            start = (4 * lax.rem(x + dx, 4) + lax.rem(y + ky, 4)) * BLOCK
+            start = pl.multiple_of(start, 128)
+            copies.append((cot.at[:, pl.ds(start, BLOCK)], out.at[:, pl.ds(dx * BLOCK, BLOCK)]))
+    copy_all(copies, sems)
+
+
+def rows_by_z(activations):
+    return pl.pallas_call(
+        rows_kernel,
+        out_shape=[jax.ShapeDtypeStruct((BLOCK, GROUP), jnp.bfloat16)] * 4,
+        in_specs=[HBM],
+        out_specs=[VMEM] * 4,
+        scratch_shapes=[pltpu.SemaphoreType.DMA((8,))],
         compiler_params=params(4),
-        name="prepare",
-    )(activations, cotangent_t)
+        name="rows_by_z",
+    )(pltpu.with_memory_space_constraint(activations, pltpu.HBM))
+
+
+def tokens_by_y(cotangent_t, first):
+    return pl.pallas_call(
+        tokens_kernel,
+        out_shape=[jax.ShapeDtypeStruct((COLS, 4 * BLOCK), jnp.bfloat16)] * 4,
+        in_specs=[HBM, ANY],
+        out_specs=[VMEM] * 4,
+        scratch_shapes=[pltpu.SemaphoreType.DMA((16,))],
+        compiler_params=params(4),
+        name="tokens_by_y",
+    )(pltpu.with_memory_space_constraint(cotangent_t, pltpu.HBM), first)
 
 
 def dot(a, b):
@@ -107,8 +130,10 @@
 
 def far_kernel(*refs):
     x0, xp, xm, xd0, xd1, z0, zp, zm, zd0, zd1 = refs[:10]
-    totals = refs[10:14]
-    outs = refs[14:]
+    totals, weights = refs[10:14], refs[14]
+    outs, late_weights, sem = refs[15:23], refs[23], refs[24]
+    keep = pltpu.make_async_copy(weights, late_weights, sem)
+    keep.start()
     acts = jnp.concatenate(
         [x[2 * BLOCK : 3 * BLOCK, :] for x in (x0, xp)]
         + [xd1[:BLOCK, :]]
@@ -125,17 +150,19 @@
         total = totals[ky][...] + dot(jnp.concatenate(parts, axis=1), acts)
         outs[2 * ky][...] = total[:, :ROWS]
         outs[2 * ky + 1][...] = total[:, ROWS:]
-
-
-def far_product(pieces, totals):
+    keep.wait()
+
+
+def far_product(pieces, totals, weights):
     return pl.pallas_call(
         far_kernel,
-        out_shape=[jax.ShapeDtypeStruct((COLS, ROWS), jnp.float32)] * 8,
-        in_specs=[VMEM] * 14,
-        out_specs=[VMEM] * 8,
+        out_shape=[jax.ShapeDtypeStruct((COLS, ROWS), jnp.float32)] * 9,
+        in_specs=[VMEM] * 14 + [HBM],
+        out_specs=[VMEM] * 8 + [HBM],
+        scratch_shapes=[pltpu.SemaphoreType.DMA],
         compiler_params=params(14),
         name="far_product",
-    )(*pieces, *totals)
+    )(*pieces, *totals, pltpu.with_memory_space_constraint(weights, pltpu.HBM))
 
 
 def ring_gather(block, axis):
@@ -147,19 +174,26 @@
     return [block, plus, minus, far_first, far_second]
 
 
-def gradient_terms(activations, cotangent):
-    parts = prepare(activations, cotangent.T)
-    acts, cots = parts[:4], parts[4:]
+def gradient_terms(activations, cotangent, weights):
+    acts = rows_by_z(activations)
+    cots = tokens_by_y(cotangent.T, acts[0])
+    c_block = jnp.concatenate([cots[0]] + [moved(cots[k], dy=k) for k in (1, 2, 3)], axis=0)
     a_block = jnp.concatenate([acts[0]] + [moved(acts[k], dz=k) for k in (1, 2, 3)], axis=0)
-    c_block = jnp.concatenate([cots[0]] + [moved(cots[k], dy=k) for k in (1, 2, 3)], axis=0)
+    c_pieces = ring_gather(c_block, "dz")
     a_pieces = ring_gather(a_block, "dx")
-    c_pieces = ring_gather(c_block, "dz")
     totals = near_product(*a_pieces[:3], *c_pieces[:3])
-    outs = far_product(a_pieces + c_pieces, totals)
-    sums = {}
-    for ky in (2, 1, 3, 0):
-        sums[ky] = outs[2 * ky] + moved(outs[2 * ky + 1], dc=1)
-    return [sums[0], moved(sums[1], dy=-1), moved(sums[2], dy=-2), moved(sums[3], dy=-3)]
+    *outs, weights = far_product(a_pieces + c_pieces, totals, weights)
+    mine, theirs = outs[0::2], outs[1::2]
+    half = COLS // 2
+    far = moved(theirs[2], dc=1)
+    low = moved(mine[2][:half] + far[:half], dy=-1)
+    high = moved(mine[2][half:] + far[half:], dy=1)
+    down = mine[1] + moved(theirs[1], dc=1)
+    up = mine[3] + moved(theirs[3], dc=1)
+    own = moved(theirs[0], dc=1)
+    down = jnp.concatenate([down[:half] + low, down[half:]], axis=0)
+    up = jnp.concatenate([up[:half], up[half:] + high], axis=0)
+    return [mine[0], own, moved(down, dy=-1), moved(up, dy=1)], weights
 
 
 STRIP = 32
@@ -213,67 +247,69 @@
     return values
 
 
-def step_kernel(weights, update, sums, rate, new_master, new_weights):
+def step_kernel(*refs):
+    weights, sums, rate = refs[:3]
+    updates = refs[3:13]
+    new_master, new_weights, held, stage, in_sems, sems = refs[13:]
+    z, c, x, y = place()
+    order = [(dz, core) for core in (c, 1 - c) for dz in (0, 1, 3, 2)]
+    loads = []
+    for k, (dz, core) in enumerate(order):
+        start = pl.multiple_of((2 * lax.rem(z + dz, 4) + core) * ROWS, 128)
+        part = (slice(None), pl.ds(start, ROWS))
+        loads.append(pltpu.make_async_copy(weights.at[part], held.at[k], in_sems.at[k]))
+        loads[-1].start()
     weight_sq = jnp.sum(jnp.sum(sums[:8, :], axis=0, keepdims=True), axis=1, keepdims=True)
     update_sq = jnp.sum(jnp.sum(sums[8:, :], axis=0, keepdims=True), axis=1, keepdims=True)
     scale = rate[0] * (jnp.sqrt(weight_sq) / jnp.sqrt(update_sq))
-
-    def strip(i, carry):
-        rows = pl.ds(pl.multiple_of(i * STRIP, STRIP), STRIP)
-        w = weights[rows, :] - scale * update[rows, :]
-        new_master[rows, :] = w
-        new_weights[rows, :] = w.astype(jnp.bfloat16)
-        return carry
-
-    lax.fori_loop(0, COLS // STRIP, strip, 0)
-
-
-def stepped(weights, update, sums, rate):
+    half = COLS // 2
+    copies = []
+    for core, chosen in ((c, updates[:5]), (1 - c, updates[5:])):
+        own, plus, minus, low, high = chosen
+        plan = [(0, own, 0, COLS), (1, plus, 0, COLS), (3, minus, 0, COLS), (2, low, 0, half), (2, high, half, half)]
+        for dz, update, first, count in plan:
+            start = pl.multiple_of((2 * lax.rem(z + dz, 4) + core) * ROWS, 128)
+            slot = len(copies)
+            load = 4 * (slot // 5) + min(slot % 5, 3)
+            if slot % 5 != 4:
+                loads[load].wait()
+
+            def strip(i, carry):
+                at = pl.multiple_of(i * STRIP, STRIP)
+                rows = pl.ds(first + at, STRIP)
+                w = held[load, rows, :] - scale * update[pl.ds(at, STRIP), :]
+                if slot == 0:
+                    new_master[rows, :] = w
+                stage[rows, pl.ds(start, ROWS)] = w.astype(jnp.bfloat16)
+                return carry
+
+            lax.fori_loop(0, count // STRIP, strip, 0)
+            part = (pl.ds(first, count), pl.ds(start, ROWS))
+            copy = pltpu.make_async_copy(stage.at[part], new_weights.at[part], sems.at[slot])
+            copy.start()
+            copies.append(copy)
+    for copy in copies:
+        copy.wait()
+
+
+def stepped(weights, sums, rate, updates):
     return pl.pallas_call(
         step_kernel,
         out_shape=[
             jax.ShapeDtypeStruct((COLS, ROWS), jnp.float32),
-            jax.ShapeDtypeStruct((COLS, ROWS), jnp.bfloat16),
+            jax.ShapeDtypeStruct((COLS, 8 * ROWS), jnp.bfloat16),
         ],
-        in_specs=[VMEM] * 3 + [SMEM],
-        out_specs=[VMEM] * 2,
-        compiler_params=params(6),
+        in_specs=[HBM, VMEM, SMEM] + [VMEM] * 10,
+        out_specs=[VMEM, HBM],
+        scratch_shapes=[
+            pltpu.VMEM((8, COLS, ROWS), jnp.float32),
+            pltpu.VMEM((COLS, 8 * ROWS), jnp.bfloat16),
+            pltpu.SemaphoreType.DMA((8,)),
+            pltpu.SemaphoreType.DMA((10,)),
+        ],
+        compiler_params=params(14),
         name="step",
-    )(weights, update, sums, rate)
-
-
-def assemble_kernel(*refs):
-    pieces, out, sems = refs[:8], refs[8], refs[9]
-    z, c, x, y = place()
-    copies = []
-    for k in range(4):
-        for half, core in enumerate((c, 1 - c)):
-            start = pl.multiple_of((2 * lax.rem(z + k, 4) + core) * ROWS, 128)
-            copies.append(
-                pltpu.make_async_copy(
-                    pieces[2 * k + half], out.at[:, pl.ds(start, ROWS)], sems.at[2 * k + half]
-                )
-            )
-    for copy in copies:
-        copy.start()
-    for copy in copies:
-        copy.wait()
-
-
-def gathered_rows(block):
-    pieces = []
-    for k in range(4):
-        mine = moved(block, dz=-k) if k else block
-        pieces += [mine, moved(mine, dc=1)]
-    return pl.pallas_call(
-        assemble_kernel,
-        out_shape=jax.ShapeDtypeStruct((COLS, 8 * ROWS), block.dtype),
-        in_specs=[VMEM] * 8,
-        out_specs=ANY,
-        scratch_shapes=[pltpu.SemaphoreType.DMA((8,))],
-        compiler_params=params(4),
-        name="assemble",
-    )(*pieces)
+    )(pltpu.with_memory_space_constraint(weights, pltpu.HBM), sums, rate, *updates)
 
 
 def on_device(
@@ -292,13 +328,17 @@
     scale = jnp.concatenate([1.0 / corr_one, 1.0 / corr_two])
     picked = jnp.arange(language_rates.shape[0], dtype=jnp.int32) == language_ids[0]
     rate = base_rate * jnp.sum(jnp.where(picked, language_rates, jnp.float32(0.0)))
-    weights = master_weights.T
-    terms = gradient_terms(activations, cotangent)
+    terms, late_weights = gradient_terms(activations, cotangent, master_weights.T)
+    all_weights = lax.all_gather(late_weights.T, "dp", axis=0, tiled=True)
     new_first, new_second, update, sums = updated(
-        terms, weights, first_moment.T, second_moment.T, scale
-    )
-    new_master, mine = stepped(weights, update, total_over_devices(sums), rate.reshape(1))
-    return (new_master.T, new_first.T, new_second.T, gathered_rows(mine).T)
+        terms, master_weights.T, first_moment.T, second_moment.T, scale
+    )
+    updates = ring_gather(update, "dz")
+    updates += [moved(piece, dc=1) for piece in updates]
+    new_master, new_weights = stepped(
+        all_weights.T, total_over_devices(sums), rate.reshape(1), updates
+    )
+    return (new_master.T, new_first.T, new_second.T, new_weights.T)
 
 
 def solution(mesh):

time: 177 us -> 209 us (1.18)
  Pallas kernels: 14.3 us -> 43.3 us
  between operations: 3.14 us -> 16.4 us
  starting transfers between devices: 68.3 us -> 61.2 us
  waiting for transfers between devices: 86.6 us -> 83.1 us
    pallas_call x1, Pallas kernels: 3.55 us -> 25.9 us  [far_product(): pl.pallas_call(far_kernel, out_shape=[jax.ShapeDtypeStruct((COLS, ROWS),...]
    ppermute x38 -> x41, starting transfers between devices: 68.3 us -> 61.2 us  [moved(): return lax.ppermute(array, ('dp', 'mp'), pairs)]
    pallas_call x1, Pallas kernels: 1.14 us -> 7.38 us  [stepped(): pl.pallas_call(step_kernel, out_shape=[jax.ShapeDtypeStruct((COLS, ROWS),...]
    ppermute x38 -> x41, waiting for transfers between devices: 86.6 us -> 83 us  [moved(): return lax.ppermute(array, ('dp', 'mp'), pairs)]
  transfers between devices with their start and end apart: 38 -> 42, of which waited for: 21 -> 17; matrix products, arithmetic and copies ran while one was open for 1% -> 1% of each run, Pallas kernels for 2% -> 3%
where the time goes in v3:
time: 209 us
  waiting for transfers between devices  83.1 us (40%)
  starting transfers between devices  61.2 us (29%)
  Pallas kernels  43.3 us (21%)
  between operations  16.4 us (8%)
  local copies, waits for them, and re-layouts  4 us (2%)
    ppermute x41, waiting for transfers between devices, moved(): return lax.ppermute(array, ('dp', 'mp'), pairs)  83 us
    ppermute x41, starting transfers between devices, moved(): return lax.ppermute(array, ('dp', 'mp'), pairs)  61.2 us
    pallas_call x1, Pallas kernels, far_product(): pl.pallas_call(far_kernel, out_shape=[jax.ShapeDtypeStruct((COLS, ROWS),...  25.9 us
    pallas_call x1, Pallas kernels, stepped(): pl.pallas_call(step_kernel, out_shape=[jax.ShapeDtypeStruct((COLS, ROWS),...  7.38 us
    pallas_call x1, Pallas kernels, near_product(): pl.pallas_call(near_kernel, out_shape=[jax.ShapeDtypeStruct((COLS, GROUP)...  4.39 us
  transfers between devices with their start and end apart: 42, of which 17 were waited for; matrix products, arithmetic and copies ran while one was open for 1% of the time, Pallas kernels for 3%

profile of v3, /device:TPU:1, one launch (start us, length us, event | category | flops | bytes accessed | tf_op | source)
XLA Modules:
  0.0 209.3 jit_solution(6583731950650327123)
XLA Ops:
  7.2 1.5 rows_by_z.1
  8.7 1.6 tokens_by_y.1
  10.3 2.2 %collective-permute-start.7 = (bf16[320,512]{1,0:T(8,128)(2,1)S(1)}, bf16[320,512]{1,0:T(8,128)(2,1)S(1)}, u32[]{:S(2)}, u32[]{:S(2)}) collective-permute-start(bf16[320,512]{1,0:T(8,128)(2,1)S(1)} %get-tuple-element.36), channel_id=1, source_target_pairs={{0,1},{1,2},{2,3},{3,0},{4,5},{5,6},{6,7},{7,4},{8,9},{9,10},{10,1... | collective-permute-start | bytes 983048 | tf_op jit(solution)/shard_map/ppermute | solution.py:29
  12.5 2.6 %collective-permute-start.8 = (bf16[320,512]{1,0:T(8,128)(2,1)S(1)}, bf16[320,512]{1,0:T(8,128)(2,1)S(1)}, u32[]{:S(2)}, u32[]{:S(2)}) collective-permute-start(bf16[320,512]{1,0:T(8,128)(2,1)S(1)} %get-tuple-element.37), channel_id=1, source_target_pairs={{0,2},{1,3},{2,0},{3,1},{4,6},{5,7},{6,4},{7,5},{8,10},{9,11},{10,... | collective-permute-start | bytes 983048 | tf_op jit(solution)/shard_map/ppermute | solution.py:29
  15.1 1.1 collective-permute-start.9
  16.2 1.6 collective-permute-start
  17.8 3.3 %collective-permute-start.1 = (bf16[128,1280]{1,0:T(8,128)(2,1)S(1)}, bf16[128,1280]{1,0:T(8,128)(2,1)S(1)}, u32[]{:S(2)}, u32[]{:S(2)}) collective-permute-start(bf16[128,1280]{1,0:T(8,128)(2,1)S(1)} %get-tuple-element.33), channel_id=1, source_target_pairs={{0,64},{1,65},{2,66},{3,67},{4,68},{5,69},{6,70},{7,71},{8,72},{9,... | collective-permute-start | bytes 983048 | tf_op jit(solution)/shard_map/ppermute | solution.py:29
  21.2 3.7 %collective-permute-start.2 = (bf16[128,1280]{1,0:T(8,128)(2,1)S(1)}, bf16[128,1280]{1,0:T(8,128)(2,1)S(1)}, u32[]{:S(2)}, u32[]{:S(2)}) collective-permute-start(bf16[128,1280]{1,0:T(8,128)(2,1)S(1)} %get-tuple-element.34), channel_id=1, source_target_pairs={{0,96},{1,97},{2,98},{3,99},{4,100},{5,101},{6,102},{7,103},{8,104... | collective-permute-start | bytes 983048 | tf_op jit(solution)/shard_map/ppermute | solution.py:29
  24.9 4.3 %collective-permute-done.8 = bf16[320,512]{1,0:T(8,128)(2,1)S(1)} collective-permute-done((bf16[320,512]{1,0:T(8,128)(2,1)S(1)}, bf16[320,512]{1,0:T(8,128)(2,1)S(1)}, u32[]{:S(2)}, u32[]{:S(2)}) %collective-permute-start.8) | collective-permute-done | bytes 327712 | tf_op jit(solution)/shard_map/ppermute | solution.py:29
  29.3 3.8 %collective-permute-start.10 = (bf16[1280,512]{1,0:T(8,128)(2,1)S(1)}, bf16[1280,512]{1,0:T(8,128)(2,1)S(1)}, u32[]{:S(2)}, u32[]{:S(2)}) collective-permute-start(bf16[1280,512]{1,0:T(8,128)(2,1)S(1)} %constant_dynamic-update-slice_fusion.4.z0.refs_5_), channel_id=1, source_target_pairs={{0,96},{1,97},{2,98},{3,99},{4,100},{5,101},{6,102},{7,103},{8,104... | collective-permute-start | bytes 3932168 | tf_op jit(solution)/shard_map/ppermute | solution.py:29
  33.2 1.2 collective-permute-done.1
  34.4 2.5 %collective-permute-start.3 = (bf16[512,1280]{1,0:T(8,128)(2,1)S(1)}, bf16[512,1280]{1,0:T(8,128)(2,1)S(1)}, u32[]{:S(2)}, u32[]{:S(2)}) collective-permute-start(bf16[512,1280]{1,0:T(8,128)(2,1)S(1)} %constant_dynamic-update-slice_fusion.x0.refs_0_), channel_id=1, source_target_pairs={{0,12},{1,13},{2,14},{3,15},{4,0},{5,1},{6,2},{7,3},{8,4},{9,5},{1... | collective-permute-start | bytes 3932168 | tf_op jit(solution)/shard_map/ppermute | solution.py:29
  37.0 25.0 %collective-permute-done.10.zp.refs_6_ = bf16[1280,512]{1,0:T(8,128)(2,1)S(1)} collective-permute-done((bf16[1280,512]{1,0:T(8,128)(2,1)S(1)}, bf16[1280,512]{1,0:T(8,128)(2,1)S(1)}, u32[]{:S(2)}, u32[]{:S(2)}) %collective-permute-start.10) | collective-permute-done | bytes 1310752 | tf_op jit(solution)/shard_map/ppermute | solution.py:29
  62.0 3.5 %collective-permute-start.12 = (bf16[640,512]{1,0:T(8,128)(2,1)S(1)}, bf16[640,512]{1,0:T(8,128)(2,1)S(1)}, u32[]{:S(2)}, u32[]{:S(2)}) collective-permute-start(bf16[640,512]{1,0:T(8,128)(2,1)S(1)} %slice.58), channel_id=1, source_target_pairs={{0,96},{1,97},{2,98},{3,99},{4,100},{5,101},{6,102},{7,103},{8,104... | collective-permute-start | bytes 1966088 | tf_op jit(solution)/shard_map/ppermute | solution.py:29
  66.0 2.5 %collective-permute-start.5 = (bf16[256,1280]{1,0:T(8,128)(2,1)S(1)}, bf16[256,1280]{1,0:T(8,128)(2,1)S(1)}, u32[]{:S(2)}, u32[]{:S(2)}) collective-permute-start(bf16[256,1280]{1,0:T(8,128)(2,1)S(1)} %slice.56), channel_id=1, source_target_pairs={{0,12},{1,13},{2,14},{3,15},{4,0},{5,1},{6,2},{7,3},{8,4},{9,5},{1... | collective-permute-start | bytes 1966088 | tf_op jit(solution)/shard_map/ppermute | solution.py:29
  68.7 4.4 %near_product.1 = (f32[320,1280]{1,0:T(8,128)S(1)}, f32[320,1280]{1,0:T(8,128)S(1)}, f32[320,1280]{1,0:T(8,128)S(1)}, f32[320,1280]{1,0:T(8,128)S(1)}) custom-call(bf16[512,1280]{1,0:T(8,128)(2,1)S(1)} %constant_dynamic-update-slice_fusion.x0.refs_0_, bf16[512,1280]{1,0:T(8,128)(2,1)S(1)} %collective-permute-done.3.xp.refs_1_, ...), custom_call_target="tpu_custom_call" | custom-call | tf_op jit(solution)/shard_map/near_product/pallas_call | solution.py:121
  73.1 7.4 %collective-permute-done.12.refs_8_ = bf16[640,512]{1,0:T(8,128)(2,1)S(1)} collective-permute-done((bf16[640,512]{1,0:T(8,128)(2,1)S(1)}, bf16[640,512]{1,0:T(8,128)(2,1)S(1)}, u32[]{:S(2)}, u32[]{:S(2)}) %collective-permute-start.12) | collective-permute-done | bytes 655392 | tf_op jit(solution)/shard_map/ppermute | solution.py:29
  80.5 0.9 collective-permute-done.13.refs_9_
  81.4 3.2 %collective-permute-done.6.refs_4_ = bf16[256,1280]{1,0:T(8,128)(2,1)S(1)} collective-permute-done((bf16[256,1280]{1,0:T(8,128)(2,1)S(1)}, bf16[256,1280]{1,0:T(8,128)(2,1)S(1)}, u32[]{:S(2)}, u32[]{:S(2)}) %collective-permute-start.6) | collective-permute-done | bytes 655392 | tf_op jit(solution)/shard_map/ppermute | solution.py:29
  84.6 25.9 %far_product.1 = (f32[320,640]{1,0:T(8,128)S(1)}, f32[320,640]{1,0:T(8,128)S(1)}, f32[320,640]{1,0:T(8,128)S(1)}, f32[320,640]{1,0:T(8,128)S(1)}, f32[320,640]{1...) custom-call(bf16[512,1280]{1,0:T(8,128)(2,1)S(1)} %constant_dynamic-, ...), custom_call_target="tpu_custom_call" | custom-call | tf_op jit(solution)/shard_map/far_product/pallas_call | solution.py:157
  111.4 0.9 copy-done.5
  112.3 0.9 copy-done.6
  113.2 0.9 copy-done.7
  114.1 2.5 %collective-permute-start.16 = (f32[320,640]{1,0:T(8,128)}, f32[320,640]{1,0:T(8,128)S(1)}, u32[]{:S(2)}, u32[]{:S(2)}) collective-permute-start(f32[320,640]{1,0:T(8,128)} %copy-done.7), channel_id=1, source_target_pairs={{0,16},{1,17},{2,18},{3,19},{4,20},{5,21},{6,22},{7,23},{8,24},{9,... | collective-permute-start | bytes 2457608 | tf_op jit(solution)/shard_map/ppermute | solution.py:29
  117.2 1.7 collective-permute-done.16
  119.4 2.3 %collective-permute-start.17 = (f32[160,640]{1,0:T(8,128)S(1)}, f32[160,640]{1,0:T(8,128)S(1)}, u32[]{:S(2)}, u32[]{:S(2)}) collective-permute-start(f32[160,640]{1,0:T(8,128)S(1)} %get-tuple-element.59), channel_id=1, source_target_pairs={{0,3},{1,0},{2,1},{3,2},{4,7},{5,4},{6,5},{7,6},{8,11},{9,8},{10,9... | collective-permute-start | bytes 1228808 | tf_op jit(solution)/shard_map/ppermute | solution.py:29
  121.7 0.9 collective-permute-start.14
  122.8 8.2 %collective-permute-done.20 = f32[160,640]{1,0:T(8,128)S(1)} collective-permute-done((f32[160,640]{1,0:T(8,128)S(1)}, f32[160,640]{1,0:T(8,128)S(1)}, u32[]{:S(2)}, u32[]{:S(2)}) %collective-permute-start.20) | collective-permute-done | bytes 409632 | tf_op jit(solution)/shard_map/ppermute | solution.py:29
  131.4 2.7 %collective-permute-start.18 = (f32[320,640]{1,0:T(8,128)S(1)}, f32[320,640]{1,0:T(8,128)S(1)}, u32[]{:S(2)}, u32[]{:S(2)}) collective-permute-start(f32[320,640]{1,0:T(8,128)S(1)} %pad_maximum_fusion), channel_id=1, source_target_pairs={{0,3},{1,0},{2,1},{3,2},{4,7},{5,4},{6,5},{7,6},{8,11},{9,8},{10,9... | collective-permute-start | bytes 2457608 | tf_op jit(solution)/shard_map/ppermute | solution.py:29
  135.0 16.2 %collective-permute-done.21.g3 = f32[320,640]{1,0:T(8,128)S(1)} collective-permute-done((f32[320,640]{1,0:T(8,128)S(1)}, f32[320,640]{1,0:T(8,128)S(1)}, u32[]{:S(2)}, u32[]{:S(2)}) %collective-permute-start.21) | collective-permute-done | bytes 819232 | tf_op jit(solution)/shard_map/ppermute | solution.py:29
  151.2 2.6 %update.1 = (f32[320,640]{1,0:T(8,128)}, f32[320,640]{1,0:T(8,128)}, f32[320,640]{1,0:T(8,128)S(1)}, f32[16,128]{1,0:T(8,128)S(1)}) custom-call(f32[320,640]{1,0:T(8,128)S(1)} %get-tuple-element.44.g0, f32[320,640]{1,0:T(8,128)S(1)} %collective-permute-done.14.g1, f32[320,640]{1,0:T(8,128)S(1)} %collective-permute-done.18.g2, ...), custom_call_target="tpu_custom_call" | custom-call | tf_op jit(solution)/shard_map/update/pallas_call | solution.py:233
  153.8 2.3 %collective-permute-start.32 = (f32[320,640]{1,0:T(8,128)S(1)}, f32[320,640]{1,0:T(8,128)S(1)}, u32[]{:S(2)}, u32[]{:S(2)}) collective-permute-start(f32[320,640]{1,0:T(8,128)S(1)} %get-tuple-element.53.refs_3_), channel_id=1, source_target_pairs={{0,96},{1,97},{2,98},{3,99},{4,100},{5,101},{6,102},{7,103},{8,104... | collective-permute-start | bytes 2457608 | tf_op jit(solution)/shard_map/ppermute | solution.py:29
  156.1 2.4 %collective-permute-start.22 = (f32[16,128]{1,0:T(8,128)S(1)}, f32[16,128]{1,0:T(8,128)S(1)}, u32[]{:S(2)}, u32[]{:S(2)}) collective-permute-start(f32[16,128]{1,0:T(8,128)S(1)} %get-tuple-element.52), channel_id=1, source_target_pairs={{0,16},{1,17},{2,18},{3,19},{4,20},{5,21},{6,22},{7,23},{8,24},{9,... | collective-permute-start | bytes 24584 | tf_op jit(solution)/shard_map/ppermute | solution.py:29
  159.4 1.1 collective-permute-start.24
  160.4 1.6 collective-permute-start.25
  162.1 1.3 collective-permute-done.23
  164.1 4.1 %collective-permute-start.27 = (f32[16,128]{1,0:T(8,128)S(1)}, f32[16,128]{1,0:T(8,128)S(1)}, u32[]{:S(2)}, u32[]{:S(2)}) collective-permute-start(f32[16,128]{1,0:T(8,128)S(1)} %add_add_fusion.2), channel_id=1, source_target_pairs={{0,2},{1,3},{2,0},{3,1},{4,6},{5,7},{6,4},{7,5},{8,10},{9,11},{10,... | collective-permute-start | bytes 24584 | tf_op jit(solution)/shard_map/ppermute | solution.py:29
  168.3 1.0 collective-permute-done.27
  169.3 1.7 collective-permute-done.28
  171.0 1.7 collective-permute-start.29
  172.7 2.1 %collective-permute-start.30 = (f32[16,128]{1,0:T(8,128)S(1)}, f32[16,128]{1,0:T(8,128)S(1)}, u32[]{:S(2)}, u32[]{:S(2)}) collective-permute-start(f32[16,128]{1,0:T(8,128)S(1)} %add_add_fusion.1), channel_id=1, source_target_pairs={{0,64},{1,65},{2,66},{3,67},{4,68},{5,69},{6,70},{7,71},{8,72},{9,... | collective-permute-start | bytes 24584 | tf_op jit(solution)/shard_map/ppermute | solution.py:29
  175.2 3.4 %collective-permute-start.36 = (f32[320,640]{1,0:T(8,128)S(1)}, f32[320,640]{1,0:T(8,128)S(1)}, u32[]{:S(2)}, u32[]{:S(2)}) collective-permute-start(f32[320,640]{1,0:T(8,128)S(1)} %get-tuple-element.53.refs_3_), channel_id=1, source_target_pairs={{0,16},{1,17},{2,18},{3,19},{4,20},{5,21},{6,22},{7,23},{8,24},{9,... | collective-permute-start | bytes 2457608 | tf_op jit(solution)/shard_map/ppermute | solution.py:29
  178.7 1.1 collective-permute-start.34
  181.0 0.9 collective-permute-start.38
  181.9 8.1 %collective-permute-done.34.refs_6_ = f32[160,640]{1,0:T(8,128)} collective-permute-done((f32[160,640]{1,0:T(8,128)S(1)}, f32[160,640]{1,0:T(8,128)}, u32[]{:S(2)}, u32[]{:S(2)}) %collective-permute-start.34) | collective-permute-done | bytes 409632 | tf_op jit(solution)/shard_map/ppermute | solution.py:29
  190.8 1.2 collective-permute-done.35.refs_7_
  192.0 1.1 collective-permute-start.40
  195.0 7.4 %step.1 = (f32[320,640]{1,0:T(8,128)}, bf16[320,5120]{1,0:T(8,128)(2,1)}) custom-call(f32[320,5120]{1,0:T(8,128)} %bitcast.17, f32[16,128]{1,0:T(8,128)S(1)} %add_add_fusion.refs_1_, f32[1]{0:T(128)} %bitcast.7.refs_2_, f32[320,640]{1,0:T(8,128)S(1)} %get-tuple-element.53.refs_3_, f32[320,640]{1,0:T(8,128)S(1)} %collective-permute-done.32.refs_4_, ...), custom_call_target="tpu_custom_call" | custom-call | tf_op jit(solution)/shard_map/step/pallas_call | solution.py:296
  (88 shorter events, 8.3 us)
Async XLA Ops:
  7.2 187.8 %all-gather.2.cloned.1.call-start = ((), (), s32[]{:S(2)}) async-start(), calls=%async_computation | async-start | bytes 7372800 | tf_op jit(solution)/shard_map/all_gather | solution.py:332
  10.3 10.9 %collective-permute-start.7 = (bf16[320,512]{1,0:T(8,128)(2,1)S(1)}, bf16[320,512]{1,0:T(8,128)(2,1)S(1)}, u32[]{:S(2)}, u32[]{:S(2)}) collective-permute-start(bf16[320,512]{1,0:T(8,128)(2,1)S(1)} %get-tuple-element.36), channel_id=1, source_target_pairs={{0,1},{1,2},{2,3},{3,0},{4,5},{5,6},{6,7},{7,4},{8,9},{9,10},{10,1... | collective-permute-start | bytes 983048 | tf_op jit(solution)/shard_map/ppermute | solution.py:29
  12.5 16.8 %collective-permute-start.8 = (bf16[320,512]{1,0:T(8,128)(2,1)S(1)}, bf16[320,512]{1,0:T(8,128)(2,1)S(1)}, u32[]{:S(2)}, u32[]{:S(2)}) collective-permute-start(bf16[320,512]{1,0:T(8,128)(2,1)S(1)} %get-tuple-element.37), channel_id=1, source_target_pairs={{0,2},{1,3},{2,0},{3,1},{4,6},{5,7},{6,4},{7,5},{8,10},{9,11},{10,... | collective-permute-start | bytes 983048 | tf_op jit(solution)/shard_map/ppermute | solution.py:29
  15.1 14.2 %collective-permute-start.9 = (bf16[320,512]{1,0:T(8,128)(2,1)S(1)}, bf16[320,512]{1,0:T(8,128)(2,1)S(1)}, u32[]{:S(2)}, u32[]{:S(2)}) collective-permute-start(bf16[320,512]{1,0:T(8,128)(2,1)S(1)} %get-tuple-element.38), channel_id=1, source_target_pairs={{0,3},{1,0},{2,1},{3,2},{4,7},{5,4},{6,5},{7,6},{8,11},{9,8},{10,9... | collective-permute-start | bytes 983048 | tf_op jit(solution)/shard_map/ppermute | solution.py:29
  16.2 17.0 %collective-permute-start = (bf16[128,1280]{1,0:T(8,128)(2,1)S(1)}, bf16[128,1280]{1,0:T(8,128)(2,1)S(1)}, u32[]{:S(2)}, u32[]{:S(2)}) collective-permute-start(bf16[128,1280]{1,0:T(8,128)(2,1)S(1)} %get-tuple-element.32), channel_id=1, source_target_pairs={{0,32},{1,33},{2,34},{3,35},{4,36},{5,37},{6,38},{7,39},{8,40},{9,... | collective-permute-start | bytes 983048 | tf_op jit(solution)/shard_map/ppermute | solution.py:29
  17.8 16.5 %collective-permute-start.1 = (bf16[128,1280]{1,0:T(8,128)(2,1)S(1)}, bf16[128,1280]{1,0:T(8,128)(2,1)S(1)}, u32[]{:S(2)}, u32[]{:S(2)}) collective-permute-start(bf16[128,1280]{1,0:T(8,128)(2,1)S(1)} %get-tuple-element.33), channel_id=1, source_target_pairs={{0,64},{1,65},{2,66},{3,67},{4,68},{5,69},{6,70},{7,71},{8,72},{9,... | collective-permute-start | bytes 983048 | tf_op jit(solution)/shard_map/ppermute | solution.py:29
  21.2 13.2 %collective-permute-start.2 = (bf16[128,1280]{1,0:T(8,128)(2,1)S(1)}, bf16[128,1280]{1,0:T(8,128)(2,1)S(1)}, u32[]{:S(2)}, u32[]{:S(2)}) collective-permute-start(bf16[128,1280]{1,0:T(8,128)(2,1)S(1)} %get-tuple-element.34), channel_id=1, source_target_pairs={{0,96},{1,97},{2,98},{3,99},{4,100},{5,101},{6,102},{7,103},{8,104... | collective-permute-start | bytes 983048 | tf_op jit(solution)/shard_map/ppermute | solution.py:29
  29.3 32.6 %collective-permute-start.10 = (bf16[1280,512]{1,0:T(8,128)(2,1)S(1)}, bf16[1280,512]{1,0:T(8,128)(2,1)S(1)}, u32[]{:S(2)}, u32[]{:S(2)}) collective-permute-start(bf16[1280,512]{1,0:T(8,128)(2,1)S(1)} %constant_dynamic-update-slice_fusion.4.z0.refs_5_), channel_id=1, source_target_pairs={{0,96},{1,97},{2,98},{3,99},{4,100},{5,101},{6,102},{7,103},{8,104... | collective-permute-start | bytes 3932168 | tf_op jit(solution)/shard_map/ppermute | solution.py:29
  33.1 32.3 %collective-permute-start.11 = (bf16[1280,512]{1,0:T(8,128)(2,1)S(1)}, bf16[1280,512]{1,0:T(8,128)(2,1)S(1)}, u32[]{:S(2)}, u32[]{:S(2)}) collective-permute-start(bf16[1280,512]{1,0:T(8,128)(2,1)S(1)} %constant_dynamic-update-slice_fusion.4.z0.refs_5_), channel_id=1, source_target_pairs={{0,32},{1,33},{2,34},{3,35},{4,36},{5,37},{6,38},{7,39},{8,40},{9,... | collective-permute-start | bytes 3932168 | tf_op jit(solution)/shard_map/ppermute | solution.py:29
  34.4 31.5 %collective-permute-start.3 = (bf16[512,1280]{1,0:T(8,128)(2,1)S(1)}, bf16[512,1280]{1,0:T(8,128)(2,1)S(1)}, u32[]{:S(2)}, u32[]{:S(2)}) collective-permute-start(bf16[512,1280]{1,0:T(8,128)(2,1)S(1)} %constant_dynamic-update-slice_fusion.x0.refs_0_), channel_id=1, source_target_pairs={{0,12},{1,13},{2,14},{3,15},{4,0},{5,1},{6,2},{7,3},{8,4},{9,5},{1... | collective-permute-start | bytes 3932168 | tf_op jit(solution)/shard_map/ppermute | solution.py:29
  37.0 31.6 %collective-permute-start.4 = (bf16[512,1280]{1,0:T(8,128)(2,1)S(1)}, bf16[512,1280]{1,0:T(8,128)(2,1)S(1)}, u32[]{:S(2)}, u32[]{:S(2)}) collective-permute-start(bf16[512,1280]{1,0:T(8,128)(2,1)S(1)} %constant_dynamic-update-slice_fusion.x0.refs_0_), channel_id=1, source_target_pairs={{0,4},{1,5},{2,6},{3,7},{4,8},{5,9},{6,10},{7,11},{8,12},{9,13},{1... | collective-permute-start | bytes 3932168 | tf_op jit(solution)/shard_map/ppermute | solution.py:29
  62.0 18.5 %collective-permute-start.12 = (bf16[640,512]{1,0:T(8,128)(2,1)S(1)}, bf16[640,512]{1,0:T(8,128)(2,1)S(1)}, u32[]{:S(2)}, u32[]{:S(2)}) collective-permute-start(bf16[640,512]{1,0:T(8,128)(2,1)S(1)} %slice.58), channel_id=1, source_target_pairs={{0,96},{1,97},{2,98},{3,99},{4,100},{5,101},{6,102},{7,103},{8,104... | collective-permute-start | bytes 1966088 | tf_op jit(solution)/shard_map/ppermute | solution.py:29
  65.5 15.9 %collective-permute-start.13 = (bf16[640,512]{1,0:T(8,128)(2,1)S(1)}, bf16[640,512]{1,0:T(8,128)(2,1)S(1)}, u32[]{:S(2)}, u32[]{:S(2)}) collective-permute-start(bf16[640,512]{1,0:T(8,128)(2,1)S(1)} %slice.59), channel_id=1, source_target_pairs={{0,32},{1,33},{2,34},{3,35},{4,36},{5,37},{6,38},{7,39},{8,40},{9,... | collective-permute-start | bytes 1966088 | tf_op jit(solution)/shard_map/ppermute | solution.py:29
  66.0 15.4 %collective-permute-start.5 = (bf16[256,1280]{1,0:T(8,128)(2,1)S(1)}, bf16[256,1280]{1,0:T(8,128)(2,1)S(1)}, u32[]{:S(2)}, u32[]{:S(2)}) collective-permute-start(bf16[256,1280]{1,0:T(8,128)(2,1)S(1)} %slice.56), channel_id=1, source_target_pairs={{0,12},{1,13},{2,14},{3,15},{4,0},{5,1},{6,2},{7,3},{8,4},{9,5},{1... | collective-permute-start | bytes 1966088 | tf_op jit(solution)/shard_map/ppermute | solution.py:29
  68.6 16.0 %collective-permute-start.6 = (bf16[256,1280]{1,0:T(8,128)(2,1)S(1)}, bf16[256,1280]{1,0:T(8,128)(2,1)S(1)}, u32[]{:S(2)}, u32[]{:S(2)}) collective-permute-start(bf16[256,1280]{1,0:T(8,128)(2,1)S(1)} %slice.57), channel_id=1, source_target_pairs={{0,4},{1,5},{2,6},{3,7},{4,8},{5,9},{6,10},{7,11},{8,12},{9,13},{1... | collective-permute-start | bytes 1966088 | tf_op jit(solution)/shard_map/ppermute | solution.py:29
  112.3 0.9 copy-start.6
  114.1 7.6 %copy-start.4 = (f32[320,640]{1,0:T(8,128)S(1)}, f32[320,640]{1,0:T(8,128)}, u32[]{:S(2)}) copy-start(f32[320,640]{1,0:T(8,128)} %copy-done.3) | copy-start | bytes 2457604
  114.1 4.7 %collective-permute-start.16 = (f32[320,640]{1,0:T(8,128)}, f32[320,640]{1,0:T(8,128)S(1)}, u32[]{:S(2)}, u32[]{:S(2)}) collective-permute-start(f32[320,640]{1,0:T(8,128)} %copy-done.7), channel_id=1, source_target_pairs={{0,16},{1,17},{2,18},{3,19},{4,20},{5,21},{6,22},{7,23},{8,24},{9,... | collective-permute-start | bytes 2457608 | tf_op jit(solution)/shard_map/ppermute | solution.py:29
  116.6 5.9 %collective-permute-start.19 = (f32[320,640]{1,0:T(8,128)}, f32[320,640]{1,0:T(8,128)S(1)}, u32[]{:S(2)}, u32[]{:S(2)}) collective-permute-start(f32[320,640]{1,0:T(8,128)} %copy-done.6), channel_id=1, source_target_pairs={{0,16},{1,17},{2,18},{3,19},{4,20},{5,21},{6,22},{7,23},{8,24},{9,... | collective-permute-start | bytes 2457608 | tf_op jit(solution)/shard_map/ppermute | solution.py:29
  116.9 5.8 %collective-permute-start.15 = (f32[320,640]{1,0:T(8,128)}, f32[320,640]{1,0:T(8,128)S(1)}, u32[]{:S(2)}, u32[]{:S(2)}) collective-permute-start(f32[320,640]{1,0:T(8,128)} %copy-done.5), channel_id=1, source_target_pairs={{0,16},{1,17},{2,18},{3,19},{4,20},{5,21},{6,22},{7,23},{8,24},{9,... | collective-permute-start | bytes 2457608 | tf_op jit(solution)/shard_map/ppermute | solution.py:29
  118.9 12.1 %collective-permute-start.20 = (f32[160,640]{1,0:T(8,128)S(1)}, f32[160,640]{1,0:T(8,128)S(1)}, u32[]{:S(2)}, u32[]{:S(2)}) collective-permute-start(f32[160,640]{1,0:T(8,128)S(1)} %get-tuple-element.58), channel_id=1, source_target_pairs={{0,1},{1,2},{2,3},{3,0},{4,5},{5,6},{6,7},{7,4},{8,9},{9,10},{10,1... | collective-permute-start | bytes 1228808 | tf_op jit(solution)/shard_map/ppermute | solution.py:29
  119.4 11.8 %collective-permute-start.17 = (f32[160,640]{1,0:T(8,128)S(1)}, f32[160,640]{1,0:T(8,128)S(1)}, u32[]{:S(2)}, u32[]{:S(2)}) collective-permute-start(f32[160,640]{1,0:T(8,128)S(1)} %get-tuple-element.59), channel_id=1, source_target_pairs={{0,3},{1,0},{2,1},{3,2},{4,7},{5,4},{6,5},{7,6},{8,11},{9,8},{10,9... | collective-permute-start | bytes 1228808 | tf_op jit(solution)/shard_map/ppermute | solution.py:29
  121.7 13.3 %collective-permute-start.14 = (f32[320,640]{1,0:T(8,128)S(1)}, f32[320,640]{1,0:T(8,128)S(1)}, u32[]{:S(2)}, u32[]{:S(2)}) collective-permute-start(f32[320,640]{1,0:T(8,128)S(1)} %copy-done.4), channel_id=1, source_target_pairs={{0,16},{1,17},{2,18},{3,19},{4,20},{5,21},{6,22},{7,23},{8,24},{9,... | collective-permute-start | bytes 2457608 | tf_op jit(solution)/shard_map/ppermute | solution.py:29
  131.1 20.0 %collective-permute-start.21 = (f32[320,640]{1,0:T(8,128)S(1)}, f32[320,640]{1,0:T(8,128)S(1)}, u32[]{:S(2)}, u32[]{:S(2)}) collective-permute-start(f32[320,640]{1,0:T(8,128)S(1)} %pad_maximum_fusion.1), channel_id=1, source_target_pairs={{0,1},{1,2},{2,3},{3,0},{4,5},{5,6},{6,7},{7,4},{8,9},{9,10},{10,1... | collective-permute-start | bytes 2457608 | tf_op jit(solution)/shard_map/ppermute | solution.py:29
  131.2 19.9 %copy-start.2 = (f32[640,320]{0,1:T(8,128)S(1)}, f32[640,320]{0,1:T(8,128)}, u32[]{:S(2)}) copy-start(f32[640,320]{0,1:T(8,128)} %param.12) | copy-start | bytes 2457604
  131.3 19.9 %copy-start = (f32[640,320]{0,1:T(8,128)S(1)}, f32[640,320]{0,1:T(8,128)}, u32[]{:S(2)}) copy-start(f32[640,320]{0,1:T(8,128)} %param.10) | copy-start | bytes 2457604
  131.3 19.8 %copy-start.1 = (f32[640,320]{0,1:T(8,128)S(1)}, f32[640,320]{0,1:T(8,128)}, u32[]{:S(2)}) copy-start(f32[640,320]{0,1:T(8,128)} %param.11) | copy-start | bytes 2457604
  131.4 19.8 %collective-permute-start.18 = (f32[320,640]{1,0:T(8,128)S(1)}, f32[320,640]{1,0:T(8,128)S(1)}, u32[]{:S(2)}, u32[]{:S(2)}) collective-permute-start(f32[320,640]{1,0:T(8,128)S(1)} %pad_maximum_fusion), channel_id=1, source_target_pairs={{0,3},{1,0},{2,1},{3,2},{4,7},{5,4},{6,5},{7,6},{8,11},{9,8},{10,9... | collective-permute-start | bytes 2457608 | tf_op jit(solution)/shard_map/ppermute | solution.py:29
  153.8 40.0 %copy-start.8 = (f32[8]{0:T(128)S(1)}, f32[8]{0:T(128)}, u32[]{:S(2)}) copy-start(f32[8]{0:T(128)} %param.15) | copy-start | bytes 100
  153.8 21.4 %collective-permute-start.32 = (f32[320,640]{1,0:T(8,128)S(1)}, f32[320,640]{1,0:T(8,128)S(1)}, u32[]{:S(2)}, u32[]{:S(2)}) collective-permute-start(f32[320,640]{1,0:T(8,128)S(1)} %get-tuple-element.53.refs_3_), channel_id=1, source_target_pairs={{0,96},{1,97},{2,98},{3,99},{4,100},{5,101},{6,102},{7,103},{8,104... | collective-permute-start | bytes 2457608 | tf_op jit(solution)/shard_map/ppermute | solution.py:29
  156.1 22.6 %collective-permute-start.33 = (f32[320,640]{1,0:T(8,128)S(1)}, f32[320,640]{1,0:T(8,128)S(1)}, u32[]{:S(2)}, u32[]{:S(2)}) collective-permute-start(f32[320,640]{1,0:T(8,128)S(1)} %get-tuple-element.53.refs_3_), channel_id=1, source_target_pairs={{0,32},{1,33},{2,34},{3,35},{4,36},{5,37},{6,38},{7,39},{8,40},{9,... | collective-permute-start | bytes 2457608 | tf_op jit(solution)/shard_map/ppermute | solution.py:29
  156.1 3.2 %collective-permute-start.22 = (f32[16,128]{1,0:T(8,128)S(1)}, f32[16,128]{1,0:T(8,128)S(1)}, u32[]{:S(2)}, u32[]{:S(2)}) collective-permute-start(f32[16,128]{1,0:T(8,128)S(1)} %get-tuple-element.52), channel_id=1, source_target_pairs={{0,16},{1,17},{2,18},{3,19},{4,20},{5,21},{6,22},{7,23},{8,24},{9,... | collective-permute-start | bytes 24584 | tf_op jit(solution)/shard_map/ppermute | solution.py:29
  159.4 4.0 %collective-permute-start.23 = (f32[16,128]{1,0:T(8,128)S(1)}, f32[16,128]{1,0:T(8,128)S(1)}, u32[]{:S(2)}, u32[]{:S(2)}) collective-permute-start(f32[16,128]{1,0:T(8,128)S(1)} %add.54), channel_id=1, source_target_pairs={{0,4},{1,5},{2,6},{3,7},{4,8},{5,9},{6,10},{7,11},{8,12},{9,13},{1... | collective-permute-start | bytes 24584 | tf_op jit(solution)/shard_map/ppermute | solution.py:29
  159.4 4.0 %collective-permute-start.24 = (f32[16,128]{1,0:T(8,128)S(1)}, f32[16,128]{1,0:T(8,128)S(1)}, u32[]{:S(2)}, u32[]{:S(2)}) collective-permute-start(f32[16,128]{1,0:T(8,128)S(1)} %add.54), channel_id=1, source_target_pairs={{0,8},{1,9},{2,10},{3,11},{4,12},{5,13},{6,14},{7,15},{8,0},{9,1},... | collective-permute-start | bytes 24584 | tf_op jit(solution)/shard_map/ppermute | solution.py:29
  160.4 3.6 %collective-permute-start.25 = (f32[16,128]{1,0:T(8,128)S(1)}, f32[16,128]{1,0:T(8,128)S(1)}, u32[]{:S(2)}, u32[]{:S(2)}) collective-permute-start(f32[16,128]{1,0:T(8,128)S(1)} %add.54), channel_id=1, source_target_pairs={{0,12},{1,13},{2,14},{3,15},{4,0},{5,1},{6,2},{7,3},{8,4},{9,5},{1... | collective-permute-start | bytes 24584 | tf_op jit(solution)/shard_map/ppermute | solution.py:29
  164.1 4.2 %collective-permute-start.26 = (f32[16,128]{1,0:T(8,128)S(1)}, f32[16,128]{1,0:T(8,128)S(1)}, u32[]{:S(2)}, u32[]{:S(2)}) collective-permute-start(f32[16,128]{1,0:T(8,128)S(1)} %add_add_fusion.2), channel_id=1, source_target_pairs={{0,1},{1,2},{2,3},{3,0},{4,5},{5,6},{6,7},{7,4},{8,9},{9,10},{10,1... | collective-permute-start | bytes 24584 | tf_op jit(solution)/shard_map/ppermute | solution.py:29
  164.1 5.2 %collective-permute-start.27 = (f32[16,128]{1,0:T(8,128)S(1)}, f32[16,128]{1,0:T(8,128)S(1)}, u32[]{:S(2)}, u32[]{:S(2)}) collective-permute-start(f32[16,128]{1,0:T(8,128)S(1)} %add_add_fusion.2), channel_id=1, source_target_pairs={{0,2},{1,3},{2,0},{3,1},{4,6},{5,7},{6,4},{7,5},{8,10},{9,11},{10,... | collective-permute-start | bytes 24584 | tf_op jit(solution)/shard_map/ppermute | solution.py:29
  168.1 2.8 %collective-permute-start.28 = (f32[16,128]{1,0:T(8,128)S(1)}, f32[16,128]{1,0:T(8,128)S(1)}, u32[]{:S(2)}, u32[]{:S(2)}) collective-permute-start(f32[16,128]{1,0:T(8,128)S(1)} %add_add_fusion.2), channel_id=1, source_target_pairs={{0,3},{1,0},{2,1},{3,2},{4,7},{5,4},{6,5},{7,6},{8,11},{9,8},{10,9... | collective-permute-start | bytes 24584 | tf_op jit(solution)/shard_map/ppermute | solution.py:29
  171.0 8.8 %collective-permute-start.29 = (f32[16,128]{1,0:T(8,128)S(1)}, f32[16,128]{1,0:T(8,128)S(1)}, u32[]{:S(2)}, u32[]{:S(2)}) collective-permute-start(f32[16,128]{1,0:T(8,128)S(1)} %add_add_fusion.1), channel_id=1, source_target_pairs={{0,32},{1,33},{2,34},{3,35},{4,36},{5,37},{6,38},{7,39},{8,40},{9,... | collective-permute-start | bytes 24584 | tf_op jit(solution)/shard_map/ppermute | solution.py:29
  172.7 7.6 %collective-permute-start.30 = (f32[16,128]{1,0:T(8,128)S(1)}, f32[16,128]{1,0:T(8,128)S(1)}, u32[]{:S(2)}, u32[]{:S(2)}) collective-permute-start(f32[16,128]{1,0:T(8,128)S(1)} %add_add_fusion.1), channel_id=1, source_target_pairs={{0,64},{1,65},{2,66},{3,67},{4,68},{5,69},{6,70},{7,71},{8,72},{9,... | collective-permute-start | bytes 24584 | tf_op jit(solution)/shard_map/ppermute | solution.py:29
  174.8 6.2 %collective-permute-start.31 = (f32[16,128]{1,0:T(8,128)S(1)}, f32[16,128]{1,0:T(8,128)S(1)}, u32[]{:S(2)}, u32[]{:S(2)}) collective-permute-start(f32[16,128]{1,0:T(8,128)S(1)} %add_add_fusion.1), channel_id=1, source_target_pairs={{0,96},{1,97},{2,98},{3,99},{4,100},{5,101},{6,102},{7,103},{8,104... | collective-permute-start | bytes 24584 | tf_op jit(solution)/shard_map/ppermute | solution.py:29
  175.2 19.7 %collective-permute-start.36 = (f32[320,640]{1,0:T(8,128)S(1)}, f32[320,640]{1,0:T(8,128)S(1)}, u32[]{:S(2)}, u32[]{:S(2)}) collective-permute-start(f32[320,640]{1,0:T(8,128)S(1)} %get-tuple-element.53.refs_3_), channel_id=1, source_target_pairs={{0,16},{1,17},{2,18},{3,19},{4,20},{5,21},{6,22},{7,23},{8,24},{9,... | collective-permute-start | bytes 2457608 | tf_op jit(solution)/shard_map/ppermute | solution.py:29
  178.7 11.4 %collective-permute-start.34 = (f32[160,640]{1,0:T(8,128)S(1)}, f32[160,640]{1,0:T(8,128)}, u32[]{:S(2)}, u32[]{:S(2)}) collective-permute-start(f32[160,640]{1,0:T(8,128)S(1)} %slice.66), channel_id=1, source_target_pairs={{0,96},{1,97},{2,98},{3,99},{4,100},{5,101},{6,102},{7,103},{8,104... | collective-permute-start | bytes 1228808 | tf_op jit(solution)/shard_map/ppermute | solution.py:29
  179.8 12.2 %collective-permute-start.35 = (f32[160,640]{1,0:T(8,128)S(1)}, f32[160,640]{1,0:T(8,128)}, u32[]{:S(2)}, u32[]{:S(2)}) collective-permute-start(f32[160,640]{1,0:T(8,128)S(1)} %slice.67), channel_id=1, source_target_pairs={{0,32},{1,33},{2,34},{3,35},{4,36},{5,37},{6,38},{7,39},{8,40},{9,... | collective-permute-start | bytes 1228808 | tf_op jit(solution)/shard_map/ppermute | solution.py:29
  180.3 14.7 %collective-permute-start.37 = (f32[320,640]{1,0:T(8,128)S(1)}, f32[320,640]{1,0:T(8,128)}, u32[]{:S(2)}, u32[]{:S(2)}) collective-permute-start(f32[320,640]{1,0:T(8,128)S(1)} %collective-permute-done.32.refs_4_), channel_id=1, source_target_pairs={{0,16},{1,17},{2,18},{3,19},{4,20},{5,21},{6,22},{7,23},{8,24},{9,... | collective-permute-start | bytes 2457608 | tf_op jit(solution)/shard_map/ppermute | solution.py:29
  181.0 14.0 %collective-permute-start.38 = (f32[320,640]{1,0:T(8,128)S(1)}, f32[320,640]{1,0:T(8,128)}, u32[]{:S(2)}, u32[]{:S(2)}) collective-permute-start(f32[320,640]{1,0:T(8,128)S(1)} %collective-permute-done.33.refs_5_), channel_id=1, source_target_pairs={{0,16},{1,17},{2,18},{3,19},{4,20},{5,21},{6,22},{7,23},{8,24},{9,... | collective-permute-start | bytes 2457608 | tf_op jit(solution)/shard_map/ppermute | solution.py:29
  190.0 4.9 %collective-permute-start.39 = (f32[160,640]{1,0:T(8,128)}, f32[160,640]{1,0:T(8,128)}, u32[]{:S(2)}, u32[]{:S(2)}) collective-permute-start(f32[160,640]{1,0:T(8,128)} %collective-permute-done.34.refs_6_), channel_id=1, source_target_pairs={{0,16},{1,17},{2,18},{3,19},{4,20},{5,21},{6,22},{7,23},{8,24},{9,... | collective-permute-start | bytes 1228808 | tf_op jit(solution)/shard_map/ppermute | solution.py:29
  192.0 3.0 %collective-permute-start.40 = (f32[160,640]{1,0:T(8,128)}, f32[160,640]{1,0:T(8,128)}, u32[]{:S(2)}, u32[]{:S(2)}) collective-permute-start(f32[160,640]{1,0:T(8,128)} %collective-permute-done.35.refs_7_), channel_id=1, source_target_pairs={{0,16},{1,17},{2,18},{3,19},{4,20},{5,21},{6,22},{7,23},{8,24},{9,... | collective-permute-start | bytes 1228808 | tf_op jit(solution)/shard_map/ppermute | solution.py:29
  (3 other events, 2.7 us)
Sparse Core Ops, SparseCore 0:
  114.2 41.7 all-gather.1

commit v4 on v3

v4 whole, which is shorter than its diff:
```python
import functools

import jax
import jax.numpy as jnp
from jax import lax
from jax.experimental import pallas as pl
from jax.experimental.pallas import tpu as pltpu
from jax.sharding import PartitionSpec as P

beta_one = 0.9
beta_two = 0.999
epsilon = 1e-06
decay_weight = 0.1
base_rate = 0.25

ROWS = 640
COLS = 320
BLOCK = 128
GROUP = 2 * ROWS


def moved(array, dz=0, dc=0, dx=0, dy=0):
    pairs = []
    for z in range(4):
        for c in range(2):
            for x in range(4):
                for y in range(4):
                    src = (2 * z + c) * 16 + 4 * x + y
                    dst = (2 * ((z + dz) % 4) + (c + dc) % 2) * 16 + 4 * ((x + dx) % 4) + (y + dy) % 4
                    pairs.append((src, dst))
    return lax.ppermute(array, ("dp", "mp"), pairs)


def place():
    d = lax.axis_index("dp")
    m = lax.axis_index("mp")
    return d // 2, d % 2, m // 4, m % 4


HBM = pl.BlockSpec(memory_space=pltpu.HBM)
ANY = pl.BlockSpec(memory_space=pl.ANY)
VMEM = pl.BlockSpec(memory_space=pltpu.VMEM)
SMEM = pl.BlockSpec(memory_space=pltpu.SMEM)


def params(mib):
    return pltpu.CompilerParams(vmem_limit_bytes=mib * 2**20)


def copy_all(copies, sems):
    started = [pltpu.make_async_copy(src, dst, sems.at[k]) for k, (src, dst) in enumerate(copies)]
    for copy in started:
        copy.start()
    for copy in started:
        copy.wait()


def rows_kernel(act, first, *refs):
    outs, sems = refs[:4], refs[4]
    z, c, x, y = place()
    copies = []
    for kz, out in enumerate(outs):
        base = lax.rem(z + kz, 4) * GROUP
        for half, core in enumerate((c, 1 - c)):
            start = pl.multiple_of(base + core * ROWS, 128)
            copies.append((act.at[:, pl.ds(start, ROWS)], out.at[:, pl.ds(half * ROWS, ROWS)]))
    copy_all(copies, sems)


def tokens_kernel(cot, *refs):
    outs, sems = refs[:4], refs[4]
    z, c, x, y = place()
    copies = []
    for ky, out in enumerate(outs):
        for dx in range(4):
            start = (4 * lax.rem(x + dx, 4) + lax.rem(y + ky, 4)) * BLOCK
            start = pl.multiple_of(start, 128)
            copies.append((cot.at[:, pl.ds(start, BLOCK)], out.at[:, pl.ds(dx * BLOCK, BLOCK)]))
    copy_all(copies, sems)


def rows_by_z(activations, first):
    return pl.pallas_call(
        rows_kernel,
        out_shape=[jax.ShapeDtypeStruct((BLOCK, GROUP), jnp.bfloat16)] * 4,
        in_specs=[HBM, ANY],
        out_specs=[VMEM] * 4,
        scratch_shapes=[pltpu.SemaphoreType.DMA((8,))],
        compiler_params=params(4),
        name="rows_by_z",
    )(pltpu.with_memory_space_constraint(activations, pltpu.HBM), first)


def tokens_by_y(cotangent_t):
    return pl.pallas_call(
        tokens_kernel,
        out_shape=[jax.ShapeDtypeStruct((COLS, 4 * BLOCK), jnp.bfloat16)] * 4,
        in_specs=[HBM],
        out_specs=[VMEM] * 4,
        scratch_shapes=[pltpu.SemaphoreType.DMA((16,))],
        compiler_params=params(4),
        name="tokens_by_y",
    )(pltpu.with_memory_space_constraint(cotangent_t, pltpu.HBM))


def dot(a, b):
    return jnp.dot(a, b, preferred_element_type=jnp.float32)


def near_kernel(z0, zp, zm, x0, xp, xm, *outs):
    acts = jnp.concatenate(
        [x[kz * BLOCK : (kz + 1) * BLOCK, :] for kz in (0, 1, 3) for x in (x0, xp, xm)], axis=0
    )
    for ky, out in enumerate(outs):
        rows = slice(ky * COLS, (ky + 1) * COLS)
        parts = []
        for z in (z0, zm, zp):
            parts += [z[rows, : 2 * BLOCK], z[rows, 3 * BLOCK :]]
        out[...] = dot(jnp.concatenate(parts, axis=1), acts)


def near_product(z0, zp, zm, x0, xp, xm):
    return pl.pallas_call(
        near_kernel,
        out_shape=[jax.ShapeDtypeStruct((COLS, GROUP), jnp.float32)] * 4,
        in_specs=[VMEM] * 6,
        out_specs=[VMEM] * 4,
        compiler_params=params(14),
        name="near_product",
    )(z0, zp, zm, x0, xp, xm)


def far_kernel(*refs):
    z0, zp, zm, zd0, zd1, x0, xp, xm, xd0, xd1 = refs[:10]
    totals, weights = refs[10:14], refs[14]
    outs, late_weights = refs[15:23], refs[23]
    late_weights[...] = weights[...]
    acts = jnp.concatenate(
        [x[2 * BLOCK : 3 * BLOCK, :] for x in (x0, xp)]
        + [xd1[:BLOCK, :]]
        + [xm[2 * BLOCK : 3 * BLOCK, :]]
        + [xd0[:BLOCK, :], xd0[BLOCK:, :], xd1[BLOCK:, :]],
        axis=0,
    )
    middle = slice(2 * BLOCK, 3 * BLOCK)
    for ky in (2, 1, 3, 0):
        rows = slice(ky * COLS, (ky + 1) * COLS)
        far = zd0 if ky < 2 else zd1
        parts = [far[(ky % 2) * COLS : (ky % 2 + 1) * COLS, :]]
        parts += [z[rows, middle] for z in (z0, zm, zp)]
        total = totals[ky][...] + dot(jnp.concatenate(parts, axis=1), acts)
        outs[2 * ky][...] = total[:, :ROWS]
        outs[2 * ky + 1][...] = total[:, ROWS:]


def far_product(pieces, totals, weights):
    return pl.pallas_call(
        far_kernel,
        out_shape=[jax.ShapeDtypeStruct((COLS, ROWS), jnp.float32)] * 9,
        in_specs=[VMEM] * 15,
        out_specs=[VMEM] * 9,
        compiler_params=params(14),
        name="far_product",
    )(*pieces, *totals, weights)


def ring_gather(block, axis):
    half = block.shape[0] // 2
    plus = moved(block, **{axis: -1})
    minus = moved(block, **{axis: 1})
    far_first = moved(plus[:half], **{axis: -1})
    far_second = moved(minus[half:], **{axis: 1})
    return [block, plus, minus, far_first, far_second]


def gradient_terms(activations, cotangent, weights):
    cots = tokens_by_y(cotangent.T)
    acts = rows_by_z(activations, cots[0])
    c_block = jnp.concatenate([cots[0]] + [moved(cots[k], dy=k) for k in (1, 2, 3)], axis=0)
    a_block = jnp.concatenate([acts[0]] + [moved(acts[k], dz=k) for k in (1, 2, 3)], axis=0)
    c_pieces = ring_gather(c_block, "dz")
    a_pieces = ring_gather(a_block, "dx")
    totals = near_product(*c_pieces[:3], *a_pieces[:3])
    *outs, weights = far_product(c_pieces + a_pieces, totals, weights)
    near = [moved(weights, dz=-1), moved(weights, dz=1)]
    mine, theirs = outs[0::2], outs[1::2]
    half = COLS // 2
    far = moved(theirs[2], dc=1)
    low = moved(mine[2][:half] + far[:half], dy=-1)
    high = moved(mine[2][half:] + far[half:], dy=1)
    down = mine[1] + moved(theirs[1], dc=1)
    up = mine[3] + moved(theirs[3], dc=1)
    own = moved(theirs[0], dc=1)
    down = jnp.concatenate([down[:half] + low, down[half:]], axis=0)
    up = jnp.concatenate([up[:half], up[half:] + high], axis=0)
    return [mine[0], own, moved(down, dy=-1), moved(up, dy=1)], near


STRIP = 32


def update_kernel(g0, g1, g2, g3, weights, first, second, scale, near0, near1, new_first, new_second, update, sums):
    inv_one, inv_two = scale[0], scale[1]

    def strip(i, carry):
        rows = pl.ds(pl.multiple_of(i * STRIP, STRIP), STRIP)
        g = (g0[rows, :] + g1[rows, :]) + (g2[rows, :] + g3[rows, :])
        w = weights[rows, :]
        m = beta_one * first[rows, :] + (1.0 - beta_one) * g
        v = beta_two * second[rows, :] + (1.0 - beta_two) * g * g
        u = m * inv_one / (jnp.sqrt(v * inv_two) + epsilon) + decay_weight * w
        new_first[rows, :] = m
        new_second[rows, :] = v
        update[rows, :] = u
        out = []
        for total, term in zip(carry, (w * w, u * u)):
            part = term[:8]
            for k in range(8, STRIP, 8):
                part = part + term[k : k + 8]
            out.append(total + part)
        return tuple(out)

    zero = jnp.zeros((8, ROWS), jnp.float32)
    for k, total in enumerate(lax.fori_loop(0, COLS // STRIP, strip, (zero, zero))):
        part = total[:, :128]
        for j in range(128, ROWS, 128):
            part = part + total[:, j : j + 128]
        sums[8 * k : 8 * k + 8, :] = part


def updated(terms, weights, first, second, scale, near):
    block = jax.ShapeDtypeStruct((COLS, ROWS), jnp.float32)
    return pl.pallas_call(
        update_kernel,
        out_shape=[block] * 3 + [jax.ShapeDtypeStruct((16, 128), jnp.float32)],
        in_specs=[VMEM] * 7 + [SMEM] + [ANY] * 2,
        out_specs=[VMEM] * 4,
        compiler_params=params(6),
        name="update",
    )(*terms, weights, first, second, scale, *near)


def total_over_devices(values):
    values = values + moved(values, dc=1)
    for axis in ("dx", "dy", "dz"):
        one, two, three = (moved(values, **{axis: k}) for k in (1, 2, 3))
        values = (values + two) + (one + three)
    return values


def scale_of(sums, rate):
    weight_sq = jnp.sum(jnp.sum(sums[:8, :], axis=0, keepdims=True), axis=1, keepdims=True)
    update_sq = jnp.sum(jnp.sum(sums[8:, :], axis=0, keepdims=True), axis=1, keepdims=True)
    return rate[0] * (jnp.sqrt(weight_sq) / jnp.sqrt(update_sq))


def step_kernel(sums, rate, *refs):
    count = len(refs) // 3
    scale = scale_of(sums, rate)

    def strip(i, carry):
        rows = pl.ds(pl.multiple_of(i * STRIP, STRIP), STRIP)
        for weights, update, out in zip(refs[:count], refs[count : 2 * count], refs[2 * count :]):
            out[rows, :] = weights[rows, :] - scale * update[rows, :]
        return carry

    lax.fori_loop(0, COLS // STRIP, strip, 0)


def own_kernel(sums, rate, weights, update, near0, near1, new_master, new_weights):
    step_kernel(sums, rate, weights, update, new_master)
    new_weights[...] = new_master[...].astype(jnp.bfloat16)


def near_step_kernel(sums, rate, *refs):
    step_kernel(sums, rate, *refs[:4], *refs[6:])
    for out, new in zip(refs[4:6], refs[6:]):
        out[...] = new[...].astype(jnp.bfloat16)


def own_step(sums, rate, weights, update, near):
    return pl.pallas_call(
        own_kernel,
        out_shape=[
            jax.ShapeDtypeStruct((COLS, ROWS), jnp.float32),
            jax.ShapeDtypeStruct((COLS, ROWS), jnp.bfloat16),
        ],
        in_specs=[VMEM, SMEM, VMEM, VMEM] + [ANY] * 2,
        out_specs=[VMEM] * 2,
        compiler_params=params(6),
        name="own_step",
    )(sums, rate, weights, update, *near)


def near_step(sums, rate, weights, updates):
    return pl.pallas_call(
        near_step_kernel,
        out_shape=[jax.ShapeDtypeStruct((COLS, ROWS), jnp.bfloat16)] * 2,
        in_specs=[VMEM, SMEM] + [VMEM] * 4,
        out_specs=[VMEM] * 2,
        scratch_shapes=[pltpu.VMEM((COLS, ROWS), jnp.float32)] * 2,
        compiler_params=params(6),
        name="near_step",
    )(sums, rate, *weights, *updates)


def place_kernel(offsets, *refs):
    pieces, out, sems = refs[: 2 * len(offsets)], refs[-2], refs[-1]
    z, c, x, y = place()
    copies = []
    for k, dz in enumerate(offsets):
        for half, core in enumerate((c, 1 - c)):
            start = pl.multiple_of((2 * lax.rem(z + dz, 4) + core) * ROWS, 128)
            copies.append((pieces[2 * k + half], out.at[:, pl.ds(start, ROWS)]))
    copy_all(copies, sems)


def placed(offsets, pieces, held=None):
    count = len(pieces)
    given = [] if held is None else [held]
    return pl.pallas_call(
        functools.partial(place_kernel, offsets),
        out_shape=jax.ShapeDtypeStruct((COLS, 8 * ROWS), jnp.bfloat16),
        in_specs=[VMEM] * count + [HBM] * len(given),
        out_specs=HBM,
        scratch_shapes=[pltpu.SemaphoreType.DMA((count,))],
        input_output_aliases={count: 0} if given else {},
        compiler_params=params(4),
        name="placed",
    )(*pieces, *given)


def on_device(
    activations,
    cotangent,
    master_weights,
    first_moment,
    second_moment,
    step_count,
    language_ids,
    language_rates,
):
    steps_done = step_count.astype(jnp.float32)
    corr_one = 1.0 - jnp.power(jnp.float32(beta_one), steps_done)
    corr_two = 1.0 - jnp.power(jnp.float32(beta_two), steps_done)
    scale = jnp.concatenate([1.0 / corr_one, 1.0 / corr_two])
    picked = jnp.arange(language_rates.shape[0], dtype=jnp.int32) == language_ids[0]
    rate = base_rate * jnp.sum(jnp.where(picked, language_rates, jnp.float32(0.0)))
    weights = master_weights.T
    rate = rate.reshape(1)
    terms, near_weights = gradient_terms(activations, cotangent, weights)
    new_first, new_second, update, sums = updated(
        terms, weights, first_moment.T, second_moment.T, scale, near_weights
    )
    near_updates = [moved(update, dz=-1), moved(update, dz=1)]
    sums = total_over_devices(sums)
    new_master, own = own_step(sums, rate, weights, update, near_updates)
    far = moved(own, dz=2)
    plus, minus = near_step(sums, rate, near_weights, near_updates)
    pieces = []
    for block in (own, plus, minus):
        pieces += [block, moved(block, dc=1)]
    new_weights = placed((0, 1, 3), pieces)
    new_weights = placed((2,), [far, moved(far, dc=1)], new_weights)
    return (new_master.T, new_first.T, new_second.T, new_weights.T)


def solution(mesh):
    return jax.shard_map(
        on_device,
        mesh=mesh,
        in_specs=(
            P(("dp", "mp"), None),
            P("dp", "mp"),
            P("dp", "mp"),
            P("dp", "mp"),
            P("dp", "mp"),
            P(),
            P(),
            P(),
        ),
        out_specs=(P("dp", "mp"), P("dp", "mp"), P("dp", "mp"), P(None, "mp")),
        check_vma=False,
    )
```

time: 209 us -> 161 us (0.77)
  Pallas kernels: 43.3 us -> 19.1 us
  between operations: 16.4 us -> 3.23 us
  waiting for transfers between devices: 83.1 us -> 70.8 us
  starting transfers between devices: 61.2 us -> 65.8 us
  local copies, waits for them, and re-layouts: 4 us -> 0.39 us
    pallas_call x1, Pallas kernels: 25.9 us -> 3.6 us  [far_product(): pl.pallas_call(far_kernel, out_shape=[jax.ShapeDtypeStruct((COLS, ROWS),...]
    ppermute x41, waiting for transfers between devices: 83 us -> 70.8 us  [moved(): return lax.ppermute(array, ('dp', 'mp'), pairs)]
    ppermute x41, starting transfers between devices: 61.2 us -> 65.8 us  [moved(): return lax.ppermute(array, ('dp', 'mp'), pairs)]
    unnamed x24 -> x18, local copies, waits for them, and re-layouts: 3.73 us -> 0.17 us
    pallas_call x1 -> x4, Pallas kernels: 7.38 us -> 5.16 us  [the longest x2 2.43 us: placed(): pl.pallas_call(functools.partial(place_kernel, offsets), out_shape=jax.Sh...]
  transfers between devices with their start and end apart: 42 -> 41, of which waited for: 17 -> 21; matrix products, arithmetic and copies ran while one was open for 1% -> 1% of each run, Pallas kernels for 3% -> 4%
where the time goes in v4:
time: 161 us
  waiting for transfers between devices  70.8 us (44%)
  starting transfers between devices  65.8 us (41%)
  Pallas kernels  19.1 us (12%)
  between operations  3.23 us (2%)
    ppermute x41, waiting for transfers between devices, moved(): return lax.ppermute(array, ('dp', 'mp'), pairs)  70.8 us
    ppermute x41, starting transfers between devices, moved(): return lax.ppermute(array, ('dp', 'mp'), pairs)  65.8 us
    pallas_call x1, Pallas kernels, near_product(): pl.pallas_call(near_kernel, out_shape=[jax.ShapeDtypeStruct((COLS, GROUP)...  4.39 us
    pallas_call x1, Pallas kernels, far_product(): pl.pallas_call(far_kernel, out_shape=[jax.ShapeDtypeStruct((COLS, ROWS),...  3.6 us
  transfers between devices with their start and end apart: 41, of which 21 were waited for; matrix products, arithmetic and copies ran while one was open for 1% of the time, Pallas kernels for 4%

profile of v4, /device:TPU:1, one launch (start us, length us, event | category | flops | bytes accessed | tf_op | source)
XLA Modules:
  0.0 160.6 jit_solution(16782518314070488634)
XLA Ops:
  0.6 1.6 tokens_by_y.1
  2.2 1.5 rows_by_z.1
  3.7 2.5 %collective-permute-start.7 = (bf16[128,1280]{1,0:T(8,128)(2,1)S(1)}, bf16[128,1280]{1,0:T(8,128)(2,1)S(1)}, u32[]{:S(2)}, u32[]{:S(2)}) collective-permute-start(bf16[128,1280]{1,0:T(8,128)(2,1)S(1)} %get-tuple-element.38), channel_id=1, source_target_pairs={{0,32},{1,33},{2,34},{3,35},{4,36},{5,37},{6,38},{7,39},{8,40},{9,... | collective-permute-start | bytes 983048 | tf_op jit(solution)/shard_map/ppermute | solution.py:31
  6.2 3.3 %collective-permute-start.8 = (bf16[128,1280]{1,0:T(8,128)(2,1)S(1)}, bf16[128,1280]{1,0:T(8,128)(2,1)S(1)}, u32[]{:S(2)}, u32[]{:S(2)}) collective-permute-start(bf16[128,1280]{1,0:T(8,128)(2,1)S(1)} %get-tuple-element.39), channel_id=1, source_target_pairs={{0,64},{1,65},{2,66},{3,67},{4,68},{5,69},{6,70},{7,71},{8,72},{9,... | collective-permute-start | bytes 983048 | tf_op jit(solution)/shard_map/ppermute | solution.py:31
  10.3 1.3 collective-permute-start
  11.6 2.6 %collective-permute-start.1 = (bf16[320,512]{1,0:T(8,128)(2,1)S(1)}, bf16[320,512]{1,0:T(8,128)(2,1)S(1)}, u32[]{:S(2)}, u32[]{:S(2)}) collective-permute-start(bf16[320,512]{1,0:T(8,128)(2,1)S(1)} %get-tuple-element.35), channel_id=1, source_target_pairs={{0,2},{1,3},{2,0},{3,1},{4,6},{5,7},{6,4},{7,5},{8,10},{9,11},{10,... | collective-permute-start | bytes 983048 | tf_op jit(solution)/shard_map/ppermute | solution.py:31
  14.2 1.6 collective-permute-done.7
  15.8 2.7 %collective-permute-start.2 = (bf16[320,512]{1,0:T(8,128)(2,1)S(1)}, bf16[320,512]{1,0:T(8,128)(2,1)S(1)}, u32[]{:S(2)}, u32[]{:S(2)}) collective-permute-start(bf16[320,512]{1,0:T(8,128)(2,1)S(1)} %get-tuple-element.36), channel_id=1, source_target_pairs={{0,3},{1,0},{2,1},{3,2},{4,7},{5,4},{6,5},{7,6},{8,11},{9,8},{10,9... | collective-permute-start | bytes 983048 | tf_op jit(solution)/shard_map/ppermute | solution.py:31
  18.6 5.1 %collective-permute-done.8 = bf16[128,1280]{1,0:T(8,128)(2,1)S(1)} collective-permute-done((bf16[128,1280]{1,0:T(8,128)(2,1)S(1)}, bf16[128,1280]{1,0:T(8,128)(2,1)S(1)}, u32[]{:S(2)}, u32[]{:S(2)}) %collective-permute-start.8) | collective-permute-done | bytes 327712 | tf_op jit(solution)/shard_map/ppermute | solution.py:31
  23.7 2.5 %collective-permute-start.10 = (bf16[512,1280]{1,0:T(8,128)(2,1)S(1)}, bf16[512,1280]{1,0:T(8,128)(2,1)S(1)}, u32[]{:S(2)}, u32[]{:S(2)}) collective-permute-start(bf16[512,1280]{1,0:T(8,128)(2,1)S(1)} %constant_dynamic-update-slice_fusion.4.x0.refs_5_), channel_id=1, source_target_pairs={{0,12},{1,13},{2,14},{3,15},{4,0},{5,1},{6,2},{7,3},{8,4},{9,5},{1... | collective-permute-start | bytes 3932168 | tf_op jit(solution)/shard_map/ppermute | solution.py:31
  26.3 1.1 collective-permute-done.1
  27.5 1.9 %collective-permute-start.3 = (bf16[1280,512]{1,0:T(8,128)(2,1)S(1)}, bf16[1280,512]{1,0:T(8,128)(2,1)S(1)}, u32[]{:S(2)}, u32[]{:S(2)}) collective-permute-start(bf16[1280,512]{1,0:T(8,128)(2,1)S(1)} %constant_dynamic-update-slice_fusion.z0.refs_0_), channel_id=1, source_target_pairs={{0,96},{1,97},{2,98},{3,99},{4,100},{5,101},{6,102},{7,103},{8,104... | collective-permute-start | bytes 3932168 | tf_op jit(solution)/shard_map/ppermute | solution.py:31
  29.4 23.4 %collective-permute-done.10.xp.refs_6_ = bf16[512,1280]{1,0:T(8,128)(2,1)S(1)} collective-permute-done((bf16[512,1280]{1,0:T(8,128)(2,1)S(1)}, bf16[512,1280]{1,0:T(8,128)(2,1)S(1)}, u32[]{:S(2)}, u32[]{:S(2)}) %collective-permute-start.10) | collective-permute-done | bytes 1310752 | tf_op jit(solution)/shard_map/ppermute | solution.py:31
  52.9 3.5 %collective-permute-start.12 = (bf16[256,1280]{1,0:T(8,128)(2,1)S(1)}, bf16[256,1280]{1,0:T(8,128)(2,1)S(1)}, u32[]{:S(2)}, u32[]{:S(2)}) collective-permute-start(bf16[256,1280]{1,0:T(8,128)(2,1)S(1)} %slice.50), channel_id=1, source_target_pairs={{0,12},{1,13},{2,14},{3,15},{4,0},{5,1},{6,2},{7,3},{8,4},{9,5},{1... | collective-permute-start | bytes 1966088 | tf_op jit(solution)/shard_map/ppermute | solution.py:31
  56.7 3.9 %collective-permute-start.5 = (bf16[640,512]{1,0:T(8,128)(2,1)S(1)}, bf16[640,512]{1,0:T(8,128)(2,1)S(1)}, u32[]{:S(2)}, u32[]{:S(2)}) collective-permute-start(bf16[640,512]{1,0:T(8,128)(2,1)S(1)} %slice.48), channel_id=1, source_target_pairs={{0,96},{1,97},{2,98},{3,99},{4,100},{5,101},{6,102},{7,103},{8,104... | collective-permute-start | bytes 1966088 | tf_op jit(solution)/shard_map/ppermute | solution.py:31
  60.8 4.4 %near_product.1 = (f32[320,1280]{1,0:T(8,128)S(1)}, f32[320,1280]{1,0:T(8,128)S(1)}, f32[320,1280]{1,0:T(8,128)S(1)}, f32[320,1280]{1,0:T(8,128)S(1)}) custom-call(bf16[1280,512]{1,0:T(8,128)(2,1)S(1)} %constant_dynamic-update-slice_fusion.z0.refs_0_, bf16[1280,512]{1,0:T(8,128)(2,1)S(1)} %collective-permute-done.3.zp.refs_1_, ...), custom_call_target="tpu_custom_call" | custom-call | tf_op jit(solution)/shard_map/near_product/pallas_call | solution.py:123
  65.2 2.7 %collective-permute-done.12.refs_8_ = bf16[256,1280]{1,0:T(8,128)(2,1)S(1)} collective-permute-done((bf16[256,1280]{1,0:T(8,128)(2,1)S(1)}, bf16[256,1280]{1,0:T(8,128)(2,1)S(1)}, u32[]{:S(2)}, u32[]{:S(2)}) %collective-permute-start.12) | collective-permute-done | bytes 655392 | tf_op jit(solution)/shard_map/ppermute | solution.py:31
  67.9 3.3 %collective-permute-done.13.refs_9_ = bf16[256,1280]{1,0:T(8,128)(2,1)S(1)} collective-permute-done((bf16[256,1280]{1,0:T(8,128)(2,1)S(1)}, bf16[256,1280]{1,0:T(8,128)(2,1)S(1)}, u32[]{:S(2)}, u32[]{:S(2)}) %collective-permute-start.13) | collective-permute-done | bytes 655392 | tf_op jit(solution)/shard_map/ppermute | solution.py:31
  71.1 1.9 %collective-permute-done.5.refs_3_ = bf16[640,512]{1,0:T(8,128)(2,1)S(1)} collective-permute-done((bf16[640,512]{1,0:T(8,128)(2,1)S(1)}, bf16[640,512]{1,0:T(8,128)(2,1)S(1)}, u32[]{:S(2)}, u32[]{:S(2)}) %collective-permute-start.5) | collective-permute-done | bytes 655392 | tf_op jit(solution)/shard_map/ppermute | solution.py:31
  73.0 3.3 %collective-permute-done.6.refs_4_ = bf16[640,512]{1,0:T(8,128)(2,1)S(1)} collective-permute-done((bf16[640,512]{1,0:T(8,128)(2,1)S(1)}, bf16[640,512]{1,0:T(8,128)(2,1)S(1)}, u32[]{:S(2)}, u32[]{:S(2)}) %collective-permute-start.6) | collective-permute-done | bytes 655392 | tf_op jit(solution)/shard_map/ppermute | solution.py:31
  76.3 3.6 %far_product.1 = (f32[320,640]{1,0:T(8,128)S(1)}, f32[320,640]{1,0:T(8,128)S(1)}, f32[320,640]{1,0:T(8,128)S(1)}, f32[320,640]{1,0:T(8,128)S(1)}, f32[320,640]{1...) custom-call(bf16[1280,512]{1,0:T(8,128)(2,1)S(1)} %constant_dynamic-, ...), custom_call_target="tpu_custom_call" | custom-call | tf_op jit(solution)/shard_map/far_product/pallas_call | solution.py:157
  79.9 2.9 %collective-permute-start.16 = (f32[320,640]{1,0:T(8,128)S(1)}, f32[320,640]{1,0:T(8,128)S(1)}, u32[]{:S(2)}, u32[]{:S(2)}) collective-permute-start(f32[320,640]{1,0:T(8,128)S(1)} %get-tuple-element.50), channel_id=1, source_target_pairs={{0,16},{1,17},{2,18},{3,19},{4,20},{5,21},{6,22},{7,23},{8,24},{9,... | collective-permute-start | bytes 2457608 | tf_op jit(solution)/shard_map/ppermute | solution.py:31
  83.3 1.4 collective-permute-done.16
  84.9 1.7 %collective-permute-start.20 = (f32[160,640]{1,0:T(8,128)S(1)}, f32[160,640]{1,0:T(8,128)S(1)}, u32[]{:S(2)}, u32[]{:S(2)}) collective-permute-start(f32[160,640]{1,0:T(8,128)S(1)} %get-tuple-element.62), channel_id=1, source_target_pairs={{0,1},{1,2},{2,3},{3,0},{4,5},{5,6},{6,7},{7,4},{8,9},{9,10},{10,1... | collective-permute-start | bytes 1228808 | tf_op jit(solution)/shard_map/ppermute | solution.py:31
  86.6 1.1 collective-permute-start.17
  87.7 1.5 collective-permute-start.23
  89.3 1.4 collective-permute-start.14
  90.8 6.1 %collective-permute-done.20 = f32[160,640]{1,0:T(8,128)S(1)} collective-permute-done((f32[160,640]{1,0:T(8,128)S(1)}, f32[160,640]{1,0:T(8,128)S(1)}, u32[]{:S(2)}, u32[]{:S(2)}) %collective-permute-start.20) | collective-permute-done | bytes 409632 | tf_op jit(solution)/shard_map/ppermute | solution.py:31
  97.6 2.4 %collective-permute-start.18 = (f32[320,640]{1,0:T(8,128)S(1)}, f32[320,640]{1,0:T(8,128)S(1)}, u32[]{:S(2)}, u32[]{:S(2)}) collective-permute-start(f32[320,640]{1,0:T(8,128)S(1)} %pad_maximum_fusion), channel_id=1, source_target_pairs={{0,3},{1,0},{2,1},{3,2},{4,7},{5,4},{6,5},{7,6},{8,11},{9,8},{10,9... | collective-permute-start | bytes 2457608 | tf_op jit(solution)/shard_map/ppermute | solution.py:31
  100.9 5.8 %collective-permute-done.22.near0.refs_0_ = f32[320,640]{1,0:T(8,128)S(1)} collective-permute-done((f32[320,640]{1,0:T(8,128)S(1)}, f32[320,640]{1,0:T(8,128)S(1)}, u32[]{:S(2)}, u32[]{:S(2)}) %collective-permute-start.22) | collective-permute-done | bytes 819232 | tf_op jit(solution)/shard_map/ppermute | solution.py:31
  106.7 1.0 collective-permute-done.23.near1.refs_1_
  107.8 9.2 %collective-permute-done.21.g3 = f32[320,640]{1,0:T(8,128)S(1)} collective-permute-done((f32[320,640]{1,0:T(8,128)S(1)}, f32[320,640]{1,0:T(8,128)S(1)}, u32[]{:S(2)}, u32[]{:S(2)}) %collective-permute-start.21) | collective-permute-done | bytes 819232 | tf_op jit(solution)/shard_map/ppermute | solution.py:31
  117.0 2.9 %update.1 = (f32[320,640]{1,0:T(8,128)}, f32[320,640]{1,0:T(8,128)}, f32[320,640]{1,0:T(8,128)}, f32[16,128]{1,0:T(8,128)S(1)}) custom-call(f32[320,640]{1,0:T(8,128)S(1)} %get-tuple-element.45.g0, f32[320,640]{1,0:T(8,128)S(1)} %collective-permute-done.14.g1, f32[320,640]{1,0:T(8,128)S(1)} %collective-permute-done.18.g2, ...), custom_call_target="tpu_custom_call" | custom-call | tf_op jit(solution)/shard_map/update/pallas_call | solution.py:233
  119.9 1.5 collective-permute-start.35
  121.3 2.6 %collective-permute-start.24 = (f32[16,128]{1,0:T(8,128)S(1)}, f32[16,128]{1,0:T(8,128)S(1)}, u32[]{:S(2)}, u32[]{:S(2)}) collective-permute-start(f32[16,128]{1,0:T(8,128)S(1)} %get-tuple-element.54), channel_id=1, source_target_pairs={{0,16},{1,17},{2,18},{3,19},{4,20},{5,21},{6,22},{7,23},{8,24},{9,... | collective-permute-start | bytes 24584 | tf_op jit(solution)/shard_map/ppermute | solution.py:31
  124.8 2.1 %collective-permute-start.25 = (f32[16,128]{1,0:T(8,128)S(1)}, f32[16,128]{1,0:T(8,128)S(1)}, u32[]{:S(2)}, u32[]{:S(2)}) collective-permute-start(f32[16,128]{1,0:T(8,128)S(1)} %add.54), channel_id=1, source_target_pairs={{0,8},{1,9},{2,10},{3,11},{4,12},{5,13},{6,14},{7,15},{8,0},{9,1},... | collective-permute-start | bytes 24584 | tf_op jit(solution)/shard_map/ppermute | solution.py:31
  126.9 1.1 collective-permute-start.26
  128.0 1.5 collective-permute-start.27
  129.5 1.3 collective-permute-done.26
  130.9 1.5 collective-permute-start.28
  132.4 1.9 %collective-permute-start.29 = (f32[16,128]{1,0:T(8,128)S(1)}, f32[16,128]{1,0:T(8,128)S(1)}, u32[]{:S(2)}, u32[]{:S(2)}) collective-permute-start(f32[16,128]{1,0:T(8,128)S(1)} %add_add_fusion.2), channel_id=1, source_target_pairs={{0,1},{1,2},{2,3},{3,0},{4,5},{5,6},{6,7},{7,4},{8,9},{9,10},{10,1... | collective-permute-start | bytes 24584 | tf_op jit(solution)/shard_map/ppermute | solution.py:31
  137.1 1.7 %collective-permute-start.32 = (f32[16,128]{1,0:T(8,128)S(1)}, f32[16,128]{1,0:T(8,128)S(1)}, u32[]{:S(2)}, u32[]{:S(2)}) collective-permute-start(f32[16,128]{1,0:T(8,128)S(1)} %add_add_fusion.1), channel_id=1, source_target_pairs={{0,32},{1,33},{2,34},{3,35},{4,36},{5,37},{6,38},{7,39},{8,40},{9,... | collective-permute-start | bytes 24584 | tf_op jit(solution)/shard_map/ppermute | solution.py:31
  138.7 1.1 collective-permute-start.33
  141.6 2.3 %own_step.1 = (f32[320,640]{1,0:T(8,128)}, bf16[320,640]{1,0:T(8,128)(2,1)S(1)}) custom-call(f32[16,128]{1,0:T(8,128)S(1)} %add_add_fusion.sums, f32[1]{0:T(128)} %bitcast.5.rate, f32[320,640]{1,0:T(8,128)S(1)} %bitcast.13, f32[320,640]{1,0:T(8,128)} %get-tuple-element.55.update, f32[320,640]{1,0:T(8,128)S(1)} %collective-permute-done.34.near0.refs_2_, ...), custom_call_target="tpu_custom_call" | custom-call | tf_op jit(solution)/shard_map/own_step/pallas_call | solution.py:282
  143.9 1.4 collective-permute-start.36
  145.7 5.2 %collective-permute-start.39 = (bf16[320,640]{1,0:T(8,128)(2,1)S(1)}, bf16[320,640]{1,0:T(8,128)(2,1)S(1)}, u32[]{:S(2)}, u32[]{:S(2)}) collective-permute-start(bf16[320,640]{1,0:T(8,128)(2,1)S(1)} %get-tuple-element.60.refs_2_), channel_id=1, source_target_pairs={{0,16},{1,17},{2,18},{3,19},{4,20},{5,21},{6,22},{7,23},{8,24},{9,... | collective-permute-start | bytes 1228808 | tf_op jit(solution)/shard_map/ppermute | solution.py:31
  152.2 5.7 %collective-permute-start.37 = (bf16[320,640]{1,0:T(8,128)(2,1)S(1)}, bf16[320,640]{1,0:T(8,128)(2,1)S(1)}, u32[]{:S(2)}, u32[]{:S(2)}) collective-permute-start(bf16[320,640]{1,0:T(8,128)(2,1)S(1)} %collective-permute-done.36.refs_0_), channel_id=1, source_target_pairs={{0,16},{1,17},{2,18},{3,19},{4,20},{5,21},{6,22},{7,23},{8,24},{9,... | collective-permute-start | bytes 1228808 | tf_op jit(solution)/shard_map/ppermute | solution.py:31
  158.0 1.5 placed.2.refs_2_
  (80 shorter events, 9.7 us)
Async XLA Ops:
  3.7 12.1 %collective-permute-start.7 = (bf16[128,1280]{1,0:T(8,128)(2,1)S(1)}, bf16[128,1280]{1,0:T(8,128)(2,1)S(1)}, u32[]{:S(2)}, u32[]{:S(2)}) collective-permute-start(bf16[128,1280]{1,0:T(8,128)(2,1)S(1)} %get-tuple-element.38), channel_id=1, source_target_pairs={{0,32},{1,33},{2,34},{3,35},{4,36},{5,37},{6,38},{7,39},{8,40},{9,... | collective-permute-start | bytes 983048 | tf_op jit(solution)/shard_map/ppermute | solution.py:31
  6.2 17.4 %collective-permute-start.8 = (bf16[128,1280]{1,0:T(8,128)(2,1)S(1)}, bf16[128,1280]{1,0:T(8,128)(2,1)S(1)}, u32[]{:S(2)}, u32[]{:S(2)}) collective-permute-start(bf16[128,1280]{1,0:T(8,128)(2,1)S(1)} %get-tuple-element.39), channel_id=1, source_target_pairs={{0,64},{1,65},{2,66},{3,67},{4,68},{5,69},{6,70},{7,71},{8,72},{9,... | collective-permute-start | bytes 983048 | tf_op jit(solution)/shard_map/ppermute | solution.py:31
  9.5 14.2 %collective-permute-start.9 = (bf16[128,1280]{1,0:T(8,128)(2,1)S(1)}, bf16[128,1280]{1,0:T(8,128)(2,1)S(1)}, u32[]{:S(2)}, u32[]{:S(2)}) collective-permute-start(bf16[128,1280]{1,0:T(8,128)(2,1)S(1)} %get-tuple-element.40), channel_id=1, source_target_pairs={{0,96},{1,97},{2,98},{3,99},{4,100},{5,101},{6,102},{7,103},{8,104... | collective-permute-start | bytes 983048 | tf_op jit(solution)/shard_map/ppermute | solution.py:31
  10.3 16.0 %collective-permute-start = (bf16[320,512]{1,0:T(8,128)(2,1)S(1)}, bf16[320,512]{1,0:T(8,128)(2,1)S(1)}, u32[]{:S(2)}, u32[]{:S(2)}) collective-permute-start(bf16[320,512]{1,0:T(8,128)(2,1)S(1)} %get-tuple-element.34), channel_id=1, source_target_pairs={{0,1},{1,2},{2,3},{3,0},{4,5},{5,6},{6,7},{7,4},{8,9},{9,10},{10,1... | collective-permute-start | bytes 983048 | tf_op jit(solution)/shard_map/ppermute | solution.py:31
  11.6 15.9 %collective-permute-start.1 = (bf16[320,512]{1,0:T(8,128)(2,1)S(1)}, bf16[320,512]{1,0:T(8,128)(2,1)S(1)}, u32[]{:S(2)}, u32[]{:S(2)}) collective-permute-start(bf16[320,512]{1,0:T(8,128)(2,1)S(1)} %get-tuple-element.35), channel_id=1, source_target_pairs={{0,2},{1,3},{2,0},{3,1},{4,6},{5,7},{6,4},{7,5},{8,10},{9,11},{10,... | collective-permute-start | bytes 983048 | tf_op jit(solution)/shard_map/ppermute | solution.py:31
  15.8 11.7 %collective-permute-start.2 = (bf16[320,512]{1,0:T(8,128)(2,1)S(1)}, bf16[320,512]{1,0:T(8,128)(2,1)S(1)}, u32[]{:S(2)}, u32[]{:S(2)}) collective-permute-start(bf16[320,512]{1,0:T(8,128)(2,1)S(1)} %get-tuple-element.36), channel_id=1, source_target_pairs={{0,3},{1,0},{2,1},{3,2},{4,7},{5,4},{6,5},{7,6},{8,11},{9,8},{10,9... | collective-permute-start | bytes 983048 | tf_op jit(solution)/shard_map/ppermute | solution.py:31
  23.7 29.1 %collective-permute-start.10 = (bf16[512,1280]{1,0:T(8,128)(2,1)S(1)}, bf16[512,1280]{1,0:T(8,128)(2,1)S(1)}, u32[]{:S(2)}, u32[]{:S(2)}) collective-permute-start(bf16[512,1280]{1,0:T(8,128)(2,1)S(1)} %constant_dynamic-update-slice_fusion.4.x0.refs_5_), channel_id=1, source_target_pairs={{0,12},{1,13},{2,14},{3,15},{4,0},{5,1},{6,2},{7,3},{8,4},{9,5},{1... | collective-permute-start | bytes 3932168 | tf_op jit(solution)/shard_map/ppermute | solution.py:31
  26.3 30.1 %collective-permute-start.11 = (bf16[512,1280]{1,0:T(8,128)(2,1)S(1)}, bf16[512,1280]{1,0:T(8,128)(2,1)S(1)}, u32[]{:S(2)}, u32[]{:S(2)}) collective-permute-start(bf16[512,1280]{1,0:T(8,128)(2,1)S(1)} %constant_dynamic-update-slice_fusion.4.x0.refs_5_), channel_id=1, source_target_pairs={{0,4},{1,5},{2,6},{3,7},{4,8},{5,9},{6,10},{7,11},{8,12},{9,13},{1... | collective-permute-start | bytes 3932168 | tf_op jit(solution)/shard_map/ppermute | solution.py:31
  27.5 29.2 %collective-permute-start.3 = (bf16[1280,512]{1,0:T(8,128)(2,1)S(1)}, bf16[1280,512]{1,0:T(8,128)(2,1)S(1)}, u32[]{:S(2)}, u32[]{:S(2)}) collective-permute-start(bf16[1280,512]{1,0:T(8,128)(2,1)S(1)} %constant_dynamic-update-slice_fusion.z0.refs_0_), channel_id=1, source_target_pairs={{0,96},{1,97},{2,98},{3,99},{4,100},{5,101},{6,102},{7,103},{8,104... | collective-permute-start | bytes 3932168 | tf_op jit(solution)/shard_map/ppermute | solution.py:31
  29.4 31.3 %collective-permute-start.4 = (bf16[1280,512]{1,0:T(8,128)(2,1)S(1)}, bf16[1280,512]{1,0:T(8,128)(2,1)S(1)}, u32[]{:S(2)}, u32[]{:S(2)}) collective-permute-start(bf16[1280,512]{1,0:T(8,128)(2,1)S(1)} %constant_dynamic-update-slice_fusion.z0.refs_0_), channel_id=1, source_target_pairs={{0,32},{1,33},{2,34},{3,35},{4,36},{5,37},{6,38},{7,39},{8,40},{9,... | collective-permute-start | bytes 3932168 | tf_op jit(solution)/shard_map/ppermute | solution.py:31
  52.9 15.0 %collective-permute-start.12 = (bf16[256,1280]{1,0:T(8,128)(2,1)S(1)}, bf16[256,1280]{1,0:T(8,128)(2,1)S(1)}, u32[]{:S(2)}, u32[]{:S(2)}) collective-permute-start(bf16[256,1280]{1,0:T(8,128)(2,1)S(1)} %slice.50), channel_id=1, source_target_pairs={{0,12},{1,13},{2,14},{3,15},{4,0},{5,1},{6,2},{7,3},{8,4},{9,5},{1... | collective-permute-start | bytes 1966088 | tf_op jit(solution)/shard_map/ppermute | solution.py:31
  56.4 14.8 %collective-permute-start.13 = (bf16[256,1280]{1,0:T(8,128)(2,1)S(1)}, bf16[256,1280]{1,0:T(8,128)(2,1)S(1)}, u32[]{:S(2)}, u32[]{:S(2)}) collective-permute-start(bf16[256,1280]{1,0:T(8,128)(2,1)S(1)} %slice.51), channel_id=1, source_target_pairs={{0,4},{1,5},{2,6},{3,7},{4,8},{5,9},{6,10},{7,11},{8,12},{9,13},{1... | collective-permute-start | bytes 1966088 | tf_op jit(solution)/shard_map/ppermute | solution.py:31
  56.7 16.3 %collective-permute-start.5 = (bf16[640,512]{1,0:T(8,128)(2,1)S(1)}, bf16[640,512]{1,0:T(8,128)(2,1)S(1)}, u32[]{:S(2)}, u32[]{:S(2)}) collective-permute-start(bf16[640,512]{1,0:T(8,128)(2,1)S(1)} %slice.48), channel_id=1, source_target_pairs={{0,96},{1,97},{2,98},{3,99},{4,100},{5,101},{6,102},{7,103},{8,104... | collective-permute-start | bytes 1966088 | tf_op jit(solution)/shard_map/ppermute | solution.py:31
  60.7 15.6 %copy-start = (f32[640,320]{0,1:T(8,128)S(1)}, f32[640,320]{0,1:T(8,128)}, u32[]{:S(2)}) copy-start(f32[640,320]{0,1:T(8,128)} %param.10) | copy-start | bytes 2457604
  60.7 15.6 %collective-permute-start.6 = (bf16[640,512]{1,0:T(8,128)(2,1)S(1)}, bf16[640,512]{1,0:T(8,128)(2,1)S(1)}, u32[]{:S(2)}, u32[]{:S(2)}) collective-permute-start(bf16[640,512]{1,0:T(8,128)(2,1)S(1)} %slice.49), channel_id=1, source_target_pairs={{0,32},{1,33},{2,34},{3,35},{4,36},{5,37},{6,38},{7,39},{8,40},{9,... | collective-permute-start | bytes 1966088 | tf_op jit(solution)/shard_map/ppermute | solution.py:31
  79.9 4.9 %collective-permute-start.16 = (f32[320,640]{1,0:T(8,128)S(1)}, f32[320,640]{1,0:T(8,128)S(1)}, u32[]{:S(2)}, u32[]{:S(2)}) collective-permute-start(f32[320,640]{1,0:T(8,128)S(1)} %get-tuple-element.50), channel_id=1, source_target_pairs={{0,16},{1,17},{2,18},{3,19},{4,20},{5,21},{6,22},{7,23},{8,24},{9,... | collective-permute-start | bytes 2457608 | tf_op jit(solution)/shard_map/ppermute | solution.py:31
  82.8 4.9 %collective-permute-start.19 = (f32[320,640]{1,0:T(8,128)S(1)}, f32[320,640]{1,0:T(8,128)S(1)}, u32[]{:S(2)}, u32[]{:S(2)}) collective-permute-start(f32[320,640]{1,0:T(8,128)S(1)} %get-tuple-element.52), channel_id=1, source_target_pairs={{0,16},{1,17},{2,18},{3,19},{4,20},{5,21},{6,22},{7,23},{8,24},{9,... | collective-permute-start | bytes 2457608 | tf_op jit(solution)/shard_map/ppermute | solution.py:31
  82.9 6.4 %collective-permute-start.15 = (f32[320,640]{1,0:T(8,128)S(1)}, f32[320,640]{1,0:T(8,128)S(1)}, u32[]{:S(2)}, u32[]{:S(2)}) collective-permute-start(f32[320,640]{1,0:T(8,128)S(1)} %get-tuple-element.48), channel_id=1, source_target_pairs={{0,16},{1,17},{2,18},{3,19},{4,20},{5,21},{6,22},{7,23},{8,24},{9,... | collective-permute-start | bytes 2457608 | tf_op jit(solution)/shard_map/ppermute | solution.py:31
  84.9 12.1 %collective-permute-start.20 = (f32[160,640]{1,0:T(8,128)S(1)}, f32[160,640]{1,0:T(8,128)S(1)}, u32[]{:S(2)}, u32[]{:S(2)}) collective-permute-start(f32[160,640]{1,0:T(8,128)S(1)} %get-tuple-element.62), channel_id=1, source_target_pairs={{0,1},{1,2},{2,3},{3,0},{4,5},{5,6},{6,7},{7,4},{8,9},{9,10},{10,1... | collective-permute-start | bytes 1228808 | tf_op jit(solution)/shard_map/ppermute | solution.py:31
  86.6 10.9 %collective-permute-start.17 = (f32[160,640]{1,0:T(8,128)S(1)}, f32[160,640]{1,0:T(8,128)S(1)}, u32[]{:S(2)}, u32[]{:S(2)}) collective-permute-start(f32[160,640]{1,0:T(8,128)S(1)} %get-tuple-element.63), channel_id=1, source_target_pairs={{0,3},{1,0},{2,1},{3,2},{4,7},{5,4},{6,5},{7,6},{8,11},{9,8},{10,9... | collective-permute-start | bytes 1228808 | tf_op jit(solution)/shard_map/ppermute | solution.py:31
  87.7 19.0 %collective-permute-start.22 = (f32[320,640]{1,0:T(8,128)S(1)}, f32[320,640]{1,0:T(8,128)S(1)}, u32[]{:S(2)}, u32[]{:S(2)}) collective-permute-start(f32[320,640]{1,0:T(8,128)S(1)} %get-tuple-element.53), channel_id=1, source_target_pairs={{0,96},{1,97},{2,98},{3,99},{4,100},{5,101},{6,102},{7,103},{8,104... | collective-permute-start | bytes 2457608 | tf_op jit(solution)/shard_map/ppermute | solution.py:31
  87.7 20.0 %collective-permute-start.23 = (f32[320,640]{1,0:T(8,128)S(1)}, f32[320,640]{1,0:T(8,128)S(1)}, u32[]{:S(2)}, u32[]{:S(2)}) collective-permute-start(f32[320,640]{1,0:T(8,128)S(1)} %get-tuple-element.53), channel_id=1, source_target_pairs={{0,32},{1,33},{2,34},{3,35},{4,36},{5,37},{6,38},{7,39},{8,40},{9,... | collective-permute-start | bytes 2457608 | tf_op jit(solution)/shard_map/ppermute | solution.py:31
  89.3 11.6 %collective-permute-start.14 = (f32[320,640]{1,0:T(8,128)S(1)}, f32[320,640]{1,0:T(8,128)S(1)}, u32[]{:S(2)}, u32[]{:S(2)}) collective-permute-start(f32[320,640]{1,0:T(8,128)S(1)} %get-tuple-element.46), channel_id=1, source_target_pairs={{0,16},{1,17},{2,18},{3,19},{4,20},{5,21},{6,22},{7,23},{8,24},{9,... | collective-permute-start | bytes 2457608 | tf_op jit(solution)/shard_map/ppermute | solution.py:31
  97.1 19.9 %collective-permute-start.21 = (f32[320,640]{1,0:T(8,128)S(1)}, f32[320,640]{1,0:T(8,128)S(1)}, u32[]{:S(2)}, u32[]{:S(2)}) collective-permute-start(f32[320,640]{1,0:T(8,128)S(1)} %pad_maximum_fusion.1), channel_id=1, source_target_pairs={{0,1},{1,2},{2,3},{3,0},{4,5},{5,6},{6,7},{7,4},{8,9},{9,10},{10,1... | collective-permute-start | bytes 2457608 | tf_op jit(solution)/shard_map/ppermute | solution.py:31
  97.6 19.4 %copy-start.3 = (f32[640,320]{0,1:T(8,128)S(1)}, f32[640,320]{0,1:T(8,128)}, u32[]{:S(2)}) copy-start(f32[640,320]{0,1:T(8,128)} %param.11) | copy-start | bytes 2457604
  97.6 19.4 %copy-start.4 = (f32[640,320]{0,1:T(8,128)S(1)}, f32[640,320]{0,1:T(8,128)}, u32[]{:S(2)}) copy-start(f32[640,320]{0,1:T(8,128)} %param.12) | copy-start | bytes 2457604
  97.6 19.3 %collective-permute-start.18 = (f32[320,640]{1,0:T(8,128)S(1)}, f32[320,640]{1,0:T(8,128)S(1)}, u32[]{:S(2)}, u32[]{:S(2)}) collective-permute-start(f32[320,640]{1,0:T(8,128)S(1)} %pad_maximum_fusion), channel_id=1, source_target_pairs={{0,3},{1,0},{2,1},{3,2},{4,7},{5,4},{6,5},{7,6},{8,11},{9,8},{10,9... | collective-permute-start | bytes 2457608 | tf_op jit(solution)/shard_map/ppermute | solution.py:31
  107.8 12.1 %copy-start.1 = (f32[320,640]{1,0:T(8,128)}, f32[320,640]{1,0:T(8,128)S(1)}, u32[]{:S(2)}) copy-start(f32[320,640]{1,0:T(8,128)S(1)} %collective-permute-done.23.near1.refs_1_) | copy-start | bytes 2457604
  117.0 22.9 %copy-start.5 = (f32[8]{0:T(128)S(1)}, f32[8]{0:T(128)}, u32[]{:S(2)}) copy-start(f32[8]{0:T(128)} %param.15) | copy-start | bytes 100
  119.9 21.7 %collective-permute-start.34 = (f32[320,640]{1,0:T(8,128)}, f32[320,640]{1,0:T(8,128)S(1)}, u32[]{:S(2)}, u32[]{:S(2)}) collective-permute-start(f32[320,640]{1,0:T(8,128)} %get-tuple-element.55.update), channel_id=1, source_target_pairs={{0,96},{1,97},{2,98},{3,99},{4,100},{5,101},{6,102},{7,103},{8,104... | collective-permute-start | bytes 2457608 | tf_op jit(solution)/shard_map/ppermute | solution.py:31
  119.9 21.7 %collective-permute-start.35 = (f32[320,640]{1,0:T(8,128)}, f32[320,640]{1,0:T(8,128)S(1)}, u32[]{:S(2)}, u32[]{:S(2)}) collective-permute-start(f32[320,640]{1,0:T(8,128)} %get-tuple-element.55.update), channel_id=1, source_target_pairs={{0,32},{1,33},{2,34},{3,35},{4,36},{5,37},{6,38},{7,39},{8,40},{9,... | collective-permute-start | bytes 2457608 | tf_op jit(solution)/shard_map/ppermute | solution.py:31
  121.3 3.4 %collective-permute-start.24 = (f32[16,128]{1,0:T(8,128)S(1)}, f32[16,128]{1,0:T(8,128)S(1)}, u32[]{:S(2)}, u32[]{:S(2)}) collective-permute-start(f32[16,128]{1,0:T(8,128)S(1)} %get-tuple-element.54), channel_id=1, source_target_pairs={{0,16},{1,17},{2,18},{3,19},{4,20},{5,21},{6,22},{7,23},{8,24},{9,... | collective-permute-start | bytes 24584 | tf_op jit(solution)/shard_map/ppermute | solution.py:31
  124.8 4.8 %collective-permute-start.25 = (f32[16,128]{1,0:T(8,128)S(1)}, f32[16,128]{1,0:T(8,128)S(1)}, u32[]{:S(2)}, u32[]{:S(2)}) collective-permute-start(f32[16,128]{1,0:T(8,128)S(1)} %add.54), channel_id=1, source_target_pairs={{0,8},{1,9},{2,10},{3,11},{4,12},{5,13},{6,14},{7,15},{8,0},{9,1},... | collective-permute-start | bytes 24584 | tf_op jit(solution)/shard_map/ppermute | solution.py:31
  126.9 4.0 %collective-permute-start.26 = (f32[16,128]{1,0:T(8,128)S(1)}, f32[16,128]{1,0:T(8,128)S(1)}, u32[]{:S(2)}, u32[]{:S(2)}) collective-permute-start(f32[16,128]{1,0:T(8,128)S(1)} %add.54), channel_id=1, source_target_pairs={{0,4},{1,5},{2,6},{3,7},{4,8},{5,9},{6,10},{7,11},{8,12},{9,13},{1... | collective-permute-start | bytes 24584 | tf_op jit(solution)/shard_map/ppermute | solution.py:31
  128.0 2.9 %collective-permute-start.27 = (f32[16,128]{1,0:T(8,128)S(1)}, f32[16,128]{1,0:T(8,128)S(1)}, u32[]{:S(2)}, u32[]{:S(2)}) collective-permute-start(f32[16,128]{1,0:T(8,128)S(1)} %add.54), channel_id=1, source_target_pairs={{0,12},{1,13},{2,14},{3,15},{4,0},{5,1},{6,2},{7,3},{8,4},{9,5},{1... | collective-permute-start | bytes 24584 | tf_op jit(solution)/shard_map/ppermute | solution.py:31
  130.9 4.8 %collective-permute-start.28 = (f32[16,128]{1,0:T(8,128)S(1)}, f32[16,128]{1,0:T(8,128)S(1)}, u32[]{:S(2)}, u32[]{:S(2)}) collective-permute-start(f32[16,128]{1,0:T(8,128)S(1)} %add_add_fusion.2), channel_id=1, source_target_pairs={{0,2},{1,3},{2,0},{3,1},{4,6},{5,7},{6,4},{7,5},{8,10},{9,11},{10,... | collective-permute-start | bytes 24584 | tf_op jit(solution)/shard_map/ppermute | solution.py:31
  132.4 4.0 %collective-permute-start.29 = (f32[16,128]{1,0:T(8,128)S(1)}, f32[16,128]{1,0:T(8,128)S(1)}, u32[]{:S(2)}, u32[]{:S(2)}) collective-permute-start(f32[16,128]{1,0:T(8,128)S(1)} %add_add_fusion.2), channel_id=1, source_target_pairs={{0,1},{1,2},{2,3},{3,0},{4,5},{5,6},{6,7},{7,4},{8,9},{9,10},{10,1... | collective-permute-start | bytes 24584 | tf_op jit(solution)/shard_map/ppermute | solution.py:31
  134.3 2.8 %collective-permute-start.30 = (f32[16,128]{1,0:T(8,128)S(1)}, f32[16,128]{1,0:T(8,128)S(1)}, u32[]{:S(2)}, u32[]{:S(2)}) collective-permute-start(f32[16,128]{1,0:T(8,128)S(1)} %add_add_fusion.2), channel_id=1, source_target_pairs={{0,3},{1,0},{2,1},{3,2},{4,7},{5,4},{6,5},{7,6},{8,11},{9,8},{10,9... | collective-permute-start | bytes 24584 | tf_op jit(solution)/shard_map/ppermute | solution.py:31
  137.1 4.1 %collective-permute-start.31 = (f32[16,128]{1,0:T(8,128)S(1)}, f32[16,128]{1,0:T(8,128)S(1)}, u32[]{:S(2)}, u32[]{:S(2)}) collective-permute-start(f32[16,128]{1,0:T(8,128)S(1)} %add_add_fusion.1), channel_id=1, source_target_pairs={{0,64},{1,65},{2,66},{3,67},{4,68},{5,69},{6,70},{7,71},{8,72},{9,... | collective-permute-start | bytes 24584 | tf_op jit(solution)/shard_map/ppermute | solution.py:31
  137.1 4.2 %collective-permute-start.32 = (f32[16,128]{1,0:T(8,128)S(1)}, f32[16,128]{1,0:T(8,128)S(1)}, u32[]{:S(2)}, u32[]{:S(2)}) collective-permute-start(f32[16,128]{1,0:T(8,128)S(1)} %add_add_fusion.1), channel_id=1, source_target_pairs={{0,32},{1,33},{2,34},{3,35},{4,36},{5,37},{6,38},{7,39},{8,40},{9,... | collective-permute-start | bytes 24584 | tf_op jit(solution)/shard_map/ppermute | solution.py:31
  138.7 2.8 %collective-permute-start.33 = (f32[16,128]{1,0:T(8,128)S(1)}, f32[16,128]{1,0:T(8,128)S(1)}, u32[]{:S(2)}, u32[]{:S(2)}) collective-permute-start(f32[16,128]{1,0:T(8,128)S(1)} %add_add_fusion.1), channel_id=1, source_target_pairs={{0,96},{1,97},{2,98},{3,99},{4,100},{5,101},{6,102},{7,103},{8,104... | collective-permute-start | bytes 24584 | tf_op jit(solution)/shard_map/ppermute | solution.py:31
  141.6 3.7 %copy-start.2 = (f32[320,640]{1,0:T(8,128)S(1)}, f32[320,640]{1,0:T(8,128)}, u32[]{:S(2)}) copy-start(f32[320,640]{1,0:T(8,128)} %copy-done.1) | copy-start | bytes 2457604
  143.9 8.3 %collective-permute-start.36 = (bf16[320,640]{1,0:T(8,128)(2,1)S(1)}, bf16[320,640]{1,0:T(8,128)(2,1)S(1)}, u32[]{:S(2)}, u32[]{:S(2)}) collective-permute-start(bf16[320,640]{1,0:T(8,128)(2,1)S(1)} %get-tuple-element.59.refs_0_), channel_id=1, source_target_pairs={{0,64},{1,65},{2,66},{3,67},{4,68},{5,69},{6,70},{7,71},{8,72},{9,... | collective-permute-start | bytes 1228808 | tf_op jit(solution)/shard_map/ppermute | solution.py:31
  145.7 12.3 %collective-permute-start.39 = (bf16[320,640]{1,0:T(8,128)(2,1)S(1)}, bf16[320,640]{1,0:T(8,128)(2,1)S(1)}, u32[]{:S(2)}, u32[]{:S(2)}) collective-permute-start(bf16[320,640]{1,0:T(8,128)(2,1)S(1)} %get-tuple-element.60.refs_2_), channel_id=1, source_target_pairs={{0,16},{1,17},{2,18},{3,19},{4,20},{5,21},{6,22},{7,23},{8,24},{9,... | collective-permute-start | bytes 1228808 | tf_op jit(solution)/shard_map/ppermute | solution.py:31
  150.9 7.1 %collective-permute-start.40 = (bf16[320,640]{1,0:T(8,128)(2,1)S(1)}, bf16[320,640]{1,0:T(8,128)(2,1)S(1)}, u32[]{:S(2)}, u32[]{:S(2)}) collective-permute-start(bf16[320,640]{1,0:T(8,128)(2,1)S(1)} %get-tuple-element.61.refs_4_), channel_id=1, source_target_pairs={{0,16},{1,17},{2,18},{3,19},{4,20},{5,21},{6,22},{7,23},{8,24},{9,... | collective-permute-start | bytes 1228808 | tf_op jit(solution)/shard_map/ppermute | solution.py:31
  151.0 7.0 %collective-permute-start.38 = (bf16[320,640]{1,0:T(8,128)(2,1)S(1)}, bf16[320,640]{1,0:T(8,128)(2,1)S(1)}, u32[]{:S(2)}, u32[]{:S(2)}) collective-permute-start(bf16[320,640]{1,0:T(8,128)(2,1)S(1)} %get-tuple-element.59.refs_0_), channel_id=1, source_target_pairs={{0,16},{1,17},{2,18},{3,19},{4,20},{5,21},{6,22},{7,23},{8,24},{9,... | collective-permute-start | bytes 1228808 | tf_op jit(solution)/shard_map/ppermute | solution.py:31
  152.2 7.3 %collective-permute-start.37 = (bf16[320,640]{1,0:T(8,128)(2,1)S(1)}, bf16[320,640]{1,0:T(8,128)(2,1)S(1)}, u32[]{:S(2)}, u32[]{:S(2)}) collective-permute-start(bf16[320,640]{1,0:T(8,128)(2,1)S(1)} %collective-permute-done.36.refs_0_), channel_id=1, source_target_pairs={{0,16},{1,17},{2,18},{3,19},{4,20},{5,21},{6,22},{7,23},{8,24},{9,... | collective-permute-start | bytes 1228808 | tf_op jit(solution)/shard_map/ppermute | solution.py:31

commit v5 on v4

v5 whole, which is shorter than its diff:
```python
import functools

import jax
import jax.numpy as jnp
from jax import lax
from jax.experimental import pallas as pl
from jax.experimental.pallas import tpu as pltpu
from jax.sharding import PartitionSpec as P

beta_one = 0.9
beta_two = 0.999
epsilon = 1e-06
decay_weight = 0.1
base_rate = 0.25

ROWS = 640
COLS = 320
BLOCK = 128
GROUP = 2 * ROWS


def moved(array, dz=0, dc=0, dx=0, dy=0):
    pairs = []
    for z in range(4):
        for c in range(2):
            for x in range(4):
                for y in range(4):
                    src = (2 * z + c) * 16 + 4 * x + y
                    dst = (2 * ((z + dz) % 4) + (c + dc) % 2) * 16 + 4 * ((x + dx) % 4) + (y + dy) % 4
                    pairs.append((src, dst))
    return lax.ppermute(array, ("dp", "mp"), pairs)


def place():
    d = lax.axis_index("dp")
    m = lax.axis_index("mp")
    return d // 2, d % 2, m // 4, m % 4


HBM = pl.BlockSpec(memory_space=pltpu.HBM)
ANY = pl.BlockSpec(memory_space=pl.ANY)
VMEM = pl.BlockSpec(memory_space=pltpu.VMEM)
SMEM = pl.BlockSpec(memory_space=pltpu.SMEM)


def params(mib):
    return pltpu.CompilerParams(vmem_limit_bytes=mib * 2**20)


def copy_all(copies, sems):
    started = [pltpu.make_async_copy(src, dst, sems.at[k]) for k, (src, dst) in enumerate(copies)]
    for copy in started:
        copy.start()
    for copy in started:
        copy.wait()


def prepare_kernel(act, cot, *refs):
    acts, cots, sems = refs[:4], refs[4:8], refs[8]
    z, c, x, y = place()
    copies = []
    for kz, out in enumerate(acts):
        base = lax.rem(z + kz, 4) * GROUP
        for half, core in enumerate((c, 1 - c)):
            start = pl.multiple_of(base + core * ROWS, 128)
            copies.append((act.at[:, pl.ds(start, ROWS)], out.at[:, pl.ds(half * ROWS, ROWS)]))
    for ky, out in enumerate(cots):
        for dx in range(4):
            start = (4 * lax.rem(x + dx, 4) + lax.rem(y + ky, 4)) * BLOCK
            start = pl.multiple_of(start, 128)
            copies.append((cot.at[:, pl.ds(start, BLOCK)], out.at[:, pl.ds(dx * BLOCK, BLOCK)]))
    copy_all(copies, sems)


def prepare(activations, cotangent_t):
    bf16 = jnp.bfloat16
    return pl.pallas_call(
        prepare_kernel,
        out_shape=[jax.ShapeDtypeStruct((BLOCK, GROUP), bf16)] * 4
        + [jax.ShapeDtypeStruct((COLS, 4 * BLOCK), bf16)] * 4,
        in_specs=[HBM] * 2,
        out_specs=[VMEM] * 8,
        scratch_shapes=[pltpu.SemaphoreType.DMA((24,))],
        compiler_params=params(4),
        name="prepare",
    )(
        pltpu.with_memory_space_constraint(activations, pltpu.HBM),
        pltpu.with_memory_space_constraint(cotangent_t, pltpu.HBM),
    )


def keep_kernel(*refs):
    pass


def kept(arrays):
    count = len(arrays)
    return pl.pallas_call(
        keep_kernel,
        out_shape=[jax.ShapeDtypeStruct(a.shape, a.dtype) for a in arrays],
        in_specs=[ANY] * count,
        out_specs=[ANY] * count,
        input_output_aliases={k: k for k in range(count)},
        compiler_params=params(1),
        name="kept",
    )(*arrays)


def dot(a, b):
    return jnp.dot(a, b, preferred_element_type=jnp.float32)


def near_kernel(z0, zp, zm, x0, xp, xm, *outs):
    acts = jnp.concatenate(
        [x[kz * BLOCK : (kz + 1) * BLOCK, :] for kz in (0, 1, 3) for x in (x0, xp, xm)], axis=0
    )
    for ky, out in enumerate(outs):
        rows = slice(ky * COLS, (ky + 1) * COLS)
        parts = []
        for z in (z0, zm, zp):
            parts += [z[rows, : 2 * BLOCK], z[rows, 3 * BLOCK :]]
        out[...] = dot(jnp.concatenate(parts, axis=1), acts)


def near_product(z0, zp, zm, x0, xp, xm):
    return pl.pallas_call(
        near_kernel,
        out_shape=[jax.ShapeDtypeStruct((COLS, GROUP), jnp.float32)] * 4,
        in_specs=[VMEM] * 6,
        out_specs=[VMEM] * 4,
        compiler_params=params(10),
        name="near_product",
    )(z0, zp, zm, x0, xp, xm)


def far_kernel(*refs):
    z0, zp, zm, zd0, zd1, x0, xp, xm, xd0, xd1 = refs[:10]
    totals, weights = refs[10:14], refs[14]
    outs, late_weights = refs[15:23], refs[23]
    late_weights[...] = weights[...]
    acts = jnp.concatenate(
        [x[2 * BLOCK : 3 * BLOCK, :] for x in (x0, xp)]
        + [xd1[:BLOCK, :]]
        + [xm[2 * BLOCK : 3 * BLOCK, :]]
        + [xd0[:BLOCK, :], xd0[BLOCK:, :], xd1[BLOCK:, :]],
        axis=0,
    )
    middle = slice(2 * BLOCK, 3 * BLOCK)
    for ky in (2, 1, 3, 0):
        rows = slice(ky * COLS, (ky + 1) * COLS)
        far = zd0 if ky < 2 else zd1
        parts = [far[(ky % 2) * COLS : (ky % 2 + 1) * COLS, :]]
        parts += [z[rows, middle] for z in (z0, zm, zp)]
        total = totals[ky][...] + dot(jnp.concatenate(parts, axis=1), acts)
        outs[2 * ky][...] = total[:, :ROWS]
        outs[2 * ky + 1][...] = total[:, ROWS:]


def far_product(pieces, totals, weights):
    return pl.pallas_call(
        far_kernel,
        out_shape=[jax.ShapeDtypeStruct((COLS, ROWS), jnp.float32)] * 9,
        in_specs=[VMEM] * 15,
        out_specs=[VMEM] * 9,
        compiler_params=params(10),
        name="far_product",
    )(*pieces, *totals, weights)


def ring_gather(block, axis):
    half = block.shape[0] // 2
    plus = moved(block, **{axis: -1})
    minus = moved(block, **{axis: 1})
    far_first = moved(plus[:half], **{axis: -1})
    far_second = moved(minus[half:], **{axis: 1})
    return [block, plus, minus, far_first, far_second]


def exchanged(blocks, axis):
    parts = {k: moved(blocks[k], **{axis: k}) for k in (2, 1, 3)}
    return jnp.concatenate([blocks[0], parts[1], parts[2], parts[3]], axis=0)


def gradient_terms(activations, cotangent, weights):
    parts = prepare(activations, cotangent.T)
    c_block = exchanged(parts[4:], "dy")
    a_block = exchanged(kept(parts[:4]), "dz")
    c_pieces = ring_gather(c_block, "dz")
    a_pieces = ring_gather(a_block, "dx")
    totals = near_product(*c_pieces[:3], *a_pieces[:3])
    *outs, weights = far_product(c_pieces + a_pieces, totals, weights)
    near = [moved(weights, dz=-1), moved(weights, dz=1)]
    mine, theirs = outs[0::2], outs[1::2]
    half = COLS // 2
    far = moved(theirs[2], dc=1)
    low = moved(mine[2][:half] + far[:half], dy=-1)
    high = moved(mine[2][half:] + far[half:], dy=1)
    one = moved(theirs[1], dc=1)
    three = moved(theirs[3], dc=1)
    down_high = moved(mine[1][half:] + one[half:], dy=-1)
    up_low = moved(mine[3][:half] + three[:half], dy=1)
    own = moved(theirs[0], dc=1)
    down_low = moved(mine[1][:half] + one[:half] + low, dy=-1)
    up_high = moved(mine[3][half:] + three[half:] + high, dy=1)
    return [mine[0], own, down_low, down_high, up_low, up_high], near


STRIP = 32


def update_kernel(*refs):
    own0, own1, down_low, down_high, up_low, up_high, weights, first, second, scale = refs[:10]
    update, gradient, sums = refs[-3:]
    inv_one, inv_two = scale[0], scale[1]
    half = COLS // 2
    carry = (jnp.zeros((8, ROWS), jnp.float32),) * 2
    for base, down, up in ((0, down_low, up_low), (half, down_high, up_high)):

        def strip(i, carry):
            at = pl.multiple_of(i * STRIP, STRIP)
            part, rows = pl.ds(at, STRIP), pl.ds(base + at, STRIP)
            g = (own0[rows, :] + own1[rows, :]) + (down[part, :] + up[part, :])
            w = weights[rows, :]
            m = beta_one * first[rows, :] + (1.0 - beta_one) * g
            v = beta_two * second[rows, :] + (1.0 - beta_two) * g * g
            u = m * inv_one / (jnp.sqrt(v * inv_two) + epsilon) + decay_weight * w
            update[rows, :] = u
            gradient[rows, :] = g
            out = []
            for total, term in zip(carry, (w * w, u * u)):
                part = term[:8]
                for k in range(8, STRIP, 8):
                    part = part + term[k : k + 8]
                out.append(total + part)
            return tuple(out)

        carry = lax.fori_loop(0, half // STRIP, strip, carry)
    for k, total in enumerate(carry):
        part = total[:, :128]
        for j in range(128, ROWS, 128):
            part = part + total[:, j : j + 128]
        sums[8 * k : 8 * k + 8, :] = part


def updated(terms, weights, first, second, scale, near):
    block = jax.ShapeDtypeStruct((COLS, ROWS), jnp.float32)
    return pl.pallas_call(
        update_kernel,
        out_shape=[block] * 2 + [jax.ShapeDtypeStruct((16, 128), jnp.float32)],
        in_specs=[VMEM] * 9 + [SMEM] + [VMEM] * 2,
        out_specs=[VMEM] * 3,
        compiler_params=params(6),
        name="update",
    )(*terms, weights, first, second, scale, *near)


def in_vmem(array):
    return pltpu.with_memory_space_constraint(array, pltpu.VMEM)


def total_over_devices(values):
    values = values + moved(values, dc=1)
    for axis in ("dx", "dy", "dz"):
        one, two, three = (moved(values, **{axis: k}) for k in (1, 2, 3))
        values = (values + two) + (one + three)
    return values


def scale_of(sums, rate):
    weight_sq = jnp.sum(jnp.sum(sums[:8, :], axis=0, keepdims=True), axis=1, keepdims=True)
    update_sq = jnp.sum(jnp.sum(sums[8:, :], axis=0, keepdims=True), axis=1, keepdims=True)
    return rate[0] * (jnp.sqrt(weight_sq) / jnp.sqrt(update_sq))


def step_kernel(sums, rate, *refs):
    weights, near_weights, updates, outs = refs[0], refs[1:3], refs[3:6], refs[6:9]
    plus_low, minus_high, held, sems = refs[9:]
    half = COLS // 2
    loads = []
    for k, base in ((0, 0), (1, half), (0, half), (1, 0)):
        part = pl.ds(base, half)
        load = pltpu.make_async_copy(near_weights[k].at[part], held.at[k, part], sems.at[len(loads)])
        load.start()
        loads.append(load)
    scale = scale_of(sums, rate)

    def block(w, u, out, base, also):
        def strip(i, carry):
            at = pl.multiple_of(i * STRIP, STRIP)
            part, rows = pl.ds(at, STRIP), pl.ds(base + at, STRIP)
            new = (w[rows, :] - scale * u[rows, :]).astype(jnp.bfloat16)
            out[rows, :] = new
            if also is not None:
                also[part, :] = new
            return carry

        lax.fori_loop(0, half // STRIP, strip, 0)

    for base in (0, half):
        block(weights, updates[0], outs[0], base, None)
    for (k, base, also), load in zip(
        ((0, 0, plus_low), (1, half, minus_high), (0, half, None), (1, 0, None)), loads
    ):
        load.wait()
        block(held.at[k], updates[1 + k], outs[1 + k], base, also)


def stepped(sums, rate, weights, updates):
    full = jax.ShapeDtypeStruct((COLS, ROWS), jnp.bfloat16)
    part = jax.ShapeDtypeStruct((COLS // 2, ROWS), jnp.bfloat16)
    return pl.pallas_call(
        step_kernel,
        out_shape=[full] * 3 + [part] * 2,
        in_specs=[VMEM, SMEM, VMEM, HBM, HBM] + [VMEM] * 3,
        out_specs=[VMEM] * 5,
        scratch_shapes=[
            pltpu.VMEM((2, COLS, ROWS), jnp.float32),
            pltpu.SemaphoreType.DMA((4,)),
        ],
        compiler_params=params(6),
        name="step",
    )(sums, rate, *weights, *updates)


STATE_ROWS = 64


def state_kernel(sums, rate, weights, first, second, update, gradient, step, new_master, new_first, new_second):
    scale = scale_of(sums, rate)
    for at in range(0, STATE_ROWS, STRIP):
        rows = slice(at, at + STRIP)
        g = gradient[rows, :]
        new_master[rows, :] = weights[rows, :] - scale * update[rows, :]
        new_first[rows, :] = beta_one * first[rows, :] + (1.0 - beta_one) * g
        new_second[rows, :] = beta_two * second[rows, :] + (1.0 - beta_two) * g * g


def new_state(sums, rate, weights, first, second, update, gradient, step):
    block = pl.BlockSpec((STATE_ROWS, ROWS), lambda i: (i, 0))
    whole = pl.BlockSpec((16, 128), lambda i: (0, 0))
    held = [pltpu.with_memory_space_constraint(a, pltpu.HBM) for a in (weights, first, second)]
    return pl.pallas_call(
        state_kernel,
        grid=(COLS // STATE_ROWS,),
        out_shape=[jax.ShapeDtypeStruct((COLS, ROWS), jnp.float32)] * 3,
        in_specs=[whole, SMEM] + [block] * 5 + [ANY],
        out_specs=[block] * 3,
        compiler_params=params(6),
        name="new_state",
    )(sums, rate, *held, update, gradient, step)


def place_kernel(plan, *refs):
    pieces, out, sems = refs[: 2 * len(plan)], refs[-2], refs[-1]
    z, c, x, y = place()
    copies = []
    for k, (dz, first, count) in enumerate(plan):
        for half, core in enumerate((c, 1 - c)):
            start = pl.multiple_of((2 * lax.rem(z + dz, 4) + core) * ROWS, 128)
            copies.append((pieces[2 * k + half], out.at[pl.ds(first, count), pl.ds(start, ROWS)]))
    copy_all(copies, sems)


def placed(plan, blocks, held=None):
    pieces = []
    for block in blocks:
        pieces += [block, moved(block, dc=1)]
    count = len(pieces)
    given = [] if held is None else [held]
    return pl.pallas_call(
        functools.partial(place_kernel, plan),
        out_shape=jax.ShapeDtypeStruct((COLS, 8 * ROWS), jnp.bfloat16),
        in_specs=[VMEM] * count + [HBM] * len(given),
        out_specs=HBM,
        scratch_shapes=[pltpu.SemaphoreType.DMA((count,))],
        input_output_aliases={count: 0} if given else {},
        compiler_params=params(4),
        name="placed",
    )(*pieces, *given)


def on_device(
    activations,
    cotangent,
    master_weights,
    first_moment,
    second_moment,
    step_count,
    language_ids,
    language_rates,
):
    steps_done = step_count.astype(jnp.float32)
    corr_one = 1.0 - jnp.power(jnp.float32(beta_one), steps_done)
    corr_two = 1.0 - jnp.power(jnp.float32(beta_two), steps_done)
    scale = jnp.concatenate([1.0 / corr_one, 1.0 / corr_two])
    picked = jnp.arange(language_rates.shape[0], dtype=jnp.int32) == language_ids[0]
    rate = base_rate * jnp.sum(jnp.where(picked, language_rates, jnp.float32(0.0)))
    weights = master_weights.T
    rate = rate.reshape(1)
    terms, near_weights = gradient_terms(activations, cotangent, weights)
    first, second = first_moment.T, second_moment.T
    update, gradient, sums = updated(terms, weights, first, second, scale, near_weights)
    near_updates = [moved(update, dz=-1), moved(update, dz=1)]
    sums = total_over_devices(sums)
    own, plus, minus, plus_low, minus_high = stepped(
        sums,
        rate,
        [weights] + [pltpu.with_memory_space_constraint(w, pltpu.HBM) for w in near_weights],
        [in_vmem(u) for u in [update] + near_updates],
    )
    half = COLS // 2
    far = [moved(plus_low, dz=-1), moved(minus_high, dz=1)]
    new_master, new_first, new_second = new_state(
        sums, rate, weights, first, second, update, gradient, own
    )
    near = placed(((0, 0, COLS), (1, 0, COLS), (3, 0, COLS)), [own, plus, minus])
    near, new_master, *far = lax.optimization_barrier((near, new_master, *far))
    new_weights = placed(((2, 0, half), (2, half, half)), far, near)
    return (new_master.T, new_first.T, new_second.T, new_weights.T)


def solution(mesh):
    return jax.shard_map(
        on_device,
        mesh=mesh,
        in_specs=(
            P(("dp", "mp"), None),
            P("dp", "mp"),
            P("dp", "mp"),
            P("dp", "mp"),
            P("dp", "mp"),
            P(),
            P(),
            P(),
        ),
        out_specs=(P("dp", "mp"), P("dp", "mp"), P("dp", "mp"), P(None, "mp")),
        check_vma=False,
    )
```

time: 161 us -> 164 us (1.019)
  waiting for transfers between devices: 70.8 us -> 76.2 us
  starting transfers between devices: 65.8 us -> 61.5 us
    ppermute x41 -> x45, waiting for transfers between devices: 70.8 us -> 76.2 us  [moved(): return lax.ppermute(array, ('dp', 'mp'), pairs)]
    ppermute x41 -> x45, starting transfers between devices: 65.8 us -> 61.5 us  [moved(): return lax.ppermute(array, ('dp', 'mp'), pairs)]
  transfers between devices with their start and end apart: 41 -> 45, of which waited for: 21 -> 25; matrix products, arithmetic and copies ran while one was open for 1% -> 1% of each run, Pallas kernels for 4% -> 6%
where the time goes in v5:
time: 164 us; the launch traced here: 163 us
  waiting for transfers between devices  76.2 us (46%)
  starting transfers between devices  61.5 us (38%)
  Pallas kernels  20.2 us (12%)
  between operations  3.12 us (2%)
    ppermute x45, waiting for transfers between devices, moved(): return lax.ppermute(array, ('dp', 'mp'), pairs)  76.2 us
    ppermute x45, starting transfers between devices, moved(): return lax.ppermute(array, ('dp', 'mp'), pairs)  61.5 us
    pallas_call x1, Pallas kernels, new_state(): pl.pallas_call(state_kernel, grid=(COLS // STATE_ROWS,), out_shape=[jax.S...  4.69 us
    pallas_call x1, Pallas kernels, near_product(): pl.pallas_call(near_kernel, out_shape=[jax.ShapeDtypeStruct((COLS, GROUP)...  4.39 us
    pallas_call x1, Pallas kernels, far_product(): pl.pallas_call(far_kernel, out_shape=[jax.ShapeDtypeStruct((COLS, ROWS),...  3.6 us
  transfers between devices with their start and end apart: 45, of which 25 were waited for; matrix products, arithmetic and copies ran while one was open for 1% of the time, Pallas kernels for 6%

profile of v5, /device:TPU:1, one launch (start us, length us, event | category | flops | bytes accessed | tf_op | source)
XLA Modules:
  0.0 163.3 jit_solution(11956924386148261012)
XLA Ops:
  0.6 2.1 %prepare.1 = (bf16[128,1280]{1,0:T(8,128)(2,1)S(1)}, bf16[128,1280]{1,0:T(8,128)(2,1)S(1)}, bf16[128,1280]{1,0:T(8,128)(2,1)S(1)}, bf16[128,1280]{1,0:T(8,128)(2...) custom-call(bf16[128,5120]{1,0:T(8,128)(2,1)} %act.1, ...), custom_call_target="tpu_custom_call" | custom-call | tf_op jit(solution)/shard_map/prepare/pallas_call | solution.py:77
  2.7 2.5 %collective-permute-start.7 = (bf16[128,1280]{1,0:T(8,128)(2,1)S(1)}, bf16[128,1280]{1,0:T(8,128)(2,1)S(1)}, u32[]{:S(2)}, u32[]{:S(2)}) collective-permute-start(bf16[128,1280]{1,0:T(8,128)(2,1)S(1)} %get-tuple-element.53), channel_id=1, source_target_pairs={{0,32},{1,33},{2,34},{3,35},{4,36},{5,37},{6,38},{7,39},{8,40},{9,... | collective-permute-start | bytes 983048 | tf_op jit(solution)/shard_map/ppermute | solution.py:31
  5.3 3.3 %collective-permute-start.8 = (bf16[128,1280]{1,0:T(8,128)(2,1)S(1)}, bf16[128,1280]{1,0:T(8,128)(2,1)S(1)}, u32[]{:S(2)}, u32[]{:S(2)}) collective-permute-start(bf16[128,1280]{1,0:T(8,128)(2,1)S(1)} %get-tuple-element.54), channel_id=1, source_target_pairs={{0,64},{1,65},{2,66},{3,67},{4,68},{5,69},{6,70},{7,71},{8,72},{9,... | collective-permute-start | bytes 983048 | tf_op jit(solution)/shard_map/ppermute | solution.py:31
  9.3 1.3 collective-permute-start
  10.6 2.6 %collective-permute-start.1 = (bf16[320,512]{1,0:T(8,128)(2,1)S(1)}, bf16[320,512]{1,0:T(8,128)(2,1)S(1)}, u32[]{:S(2)}, u32[]{:S(2)}) collective-permute-start(bf16[320,512]{1,0:T(8,128)(2,1)S(1)} %get-tuple-element.46), channel_id=1, source_target_pairs={{0,2},{1,3},{2,0},{3,1},{4,6},{5,7},{6,4},{7,5},{8,10},{9,11},{10,... | collective-permute-start | bytes 983048 | tf_op jit(solution)/shard_map/ppermute | solution.py:31
  13.3 1.6 collective-permute-done.7
  14.8 2.7 %collective-permute-start.2 = (bf16[320,512]{1,0:T(8,128)(2,1)S(1)}, bf16[320,512]{1,0:T(8,128)(2,1)S(1)}, u32[]{:S(2)}, u32[]{:S(2)}) collective-permute-start(bf16[320,512]{1,0:T(8,128)(2,1)S(1)} %get-tuple-element.47), channel_id=1, source_target_pairs={{0,3},{1,0},{2,1},{3,2},{4,7},{5,4},{6,5},{7,6},{8,11},{9,8},{10,9... | collective-permute-start | bytes 983048 | tf_op jit(solution)/shard_map/ppermute | solution.py:31
  17.6 5.1 %collective-permute-done.8 = bf16[128,1280]{1,0:T(8,128)(2,1)S(1)} collective-permute-done((bf16[128,1280]{1,0:T(8,128)(2,1)S(1)}, bf16[128,1280]{1,0:T(8,128)(2,1)S(1)}, u32[]{:S(2)}, u32[]{:S(2)}) %collective-permute-start.8) | collective-permute-done | bytes 327712 | tf_op jit(solution)/shard_map/ppermute | solution.py:31
  22.8 2.5 %collective-permute-start.10 = (bf16[512,1280]{1,0:T(8,128)(2,1)S(1)}, bf16[512,1280]{1,0:T(8,128)(2,1)S(1)}, u32[]{:S(2)}, u32[]{:S(2)}) collective-permute-start(bf16[512,1280]{1,0:T(8,128)(2,1)S(1)} %constant_dynamic-update-slice_fusion.4.x0.refs_5_), channel_id=1, source_target_pairs={{0,12},{1,13},{2,14},{3,15},{4,0},{5,1},{6,2},{7,3},{8,4},{9,5},{1... | collective-permute-start | bytes 3932168 | tf_op jit(solution)/shard_map/ppermute | solution.py:31
  25.3 1.1 collective-permute-done.1
  26.5 1.9 %collective-permute-start.3 = (bf16[1280,512]{1,0:T(8,128)(2,1)S(1)}, bf16[1280,512]{1,0:T(8,128)(2,1)S(1)}, u32[]{:S(2)}, u32[]{:S(2)}) collective-permute-start(bf16[1280,512]{1,0:T(8,128)(2,1)S(1)} %constant_dynamic-update-slice_fusion.z0.refs_0_), channel_id=1, source_target_pairs={{0,96},{1,97},{2,98},{3,99},{4,100},{5,101},{6,102},{7,103},{8,104... | collective-permute-start | bytes 3932168 | tf_op jit(solution)/shard_map/ppermute | solution.py:31
  28.4 23.4 %collective-permute-done.10.xp.refs_6_ = bf16[512,1280]{1,0:T(8,128)(2,1)S(1)} collective-permute-done((bf16[512,1280]{1,0:T(8,128)(2,1)S(1)}, bf16[512,1280]{1,0:T(8,128)(2,1)S(1)}, u32[]{:S(2)}, u32[]{:S(2)}) %collective-permute-start.10) | collective-permute-done | bytes 1310752 | tf_op jit(solution)/shard_map/ppermute | solution.py:31
  51.9 3.5 %collective-permute-start.12 = (bf16[256,1280]{1,0:T(8,128)(2,1)S(1)}, bf16[256,1280]{1,0:T(8,128)(2,1)S(1)}, u32[]{:S(2)}, u32[]{:S(2)}) collective-permute-start(bf16[256,1280]{1,0:T(8,128)(2,1)S(1)} %slice.66), channel_id=1, source_target_pairs={{0,12},{1,13},{2,14},{3,15},{4,0},{5,1},{6,2},{7,3},{8,4},{9,5},{1... | collective-permute-start | bytes 1966088 | tf_op jit(solution)/shard_map/ppermute | solution.py:31
  55.8 3.9 %collective-permute-start.5 = (bf16[640,512]{1,0:T(8,128)(2,1)S(1)}, bf16[640,512]{1,0:T(8,128)(2,1)S(1)}, u32[]{:S(2)}, u32[]{:S(2)}) collective-permute-start(bf16[640,512]{1,0:T(8,128)(2,1)S(1)} %slice.64), channel_id=1, source_target_pairs={{0,96},{1,97},{2,98},{3,99},{4,100},{5,101},{6,102},{7,103},{8,104... | collective-permute-start | bytes 1966088 | tf_op jit(solution)/shard_map/ppermute | solution.py:31
  59.8 4.4 %near_product.1 = (f32[320,1280]{1,0:T(8,128)S(1)}, f32[320,1280]{1,0:T(8,128)S(1)}, f32[320,1280]{1,0:T(8,128)S(1)}, f32[320,1280]{1,0:T(8,128)S(1)}) custom-call(bf16[1280,512]{1,0:T(8,128)(2,1)S(1)} %constant_dynamic-update-slice_fusion.z0.refs_0_, bf16[1280,512]{1,0:T(8,128)(2,1)S(1)} %collective-permute-done.3.zp.refs_1_, ...), custom_call_target="tpu_custom_call" | custom-call | tf_op jit(solution)/shard_map/near_product/pallas_call | solution.py:126
  64.2 2.7 %collective-permute-done.12.refs_8_ = bf16[256,1280]{1,0:T(8,128)(2,1)S(1)} collective-permute-done((bf16[256,1280]{1,0:T(8,128)(2,1)S(1)}, bf16[256,1280]{1,0:T(8,128)(2,1)S(1)}, u32[]{:S(2)}, u32[]{:S(2)}) %collective-permute-start.12) | collective-permute-done | bytes 655392 | tf_op jit(solution)/shard_map/ppermute | solution.py:31
  66.9 3.3 %collective-permute-done.13.refs_9_ = bf16[256,1280]{1,0:T(8,128)(2,1)S(1)} collective-permute-done((bf16[256,1280]{1,0:T(8,128)(2,1)S(1)}, bf16[256,1280]{1,0:T(8,128)(2,1)S(1)}, u32[]{:S(2)}, u32[]{:S(2)}) %collective-permute-start.13) | collective-permute-done | bytes 655392 | tf_op jit(solution)/shard_map/ppermute | solution.py:31
  70.2 1.9 %collective-permute-done.5.refs_3_ = bf16[640,512]{1,0:T(8,128)(2,1)S(1)} collective-permute-done((bf16[640,512]{1,0:T(8,128)(2,1)S(1)}, bf16[640,512]{1,0:T(8,128)(2,1)S(1)}, u32[]{:S(2)}, u32[]{:S(2)}) %collective-permute-start.5) | collective-permute-done | bytes 655392 | tf_op jit(solution)/shard_map/ppermute | solution.py:31
  72.0 3.3 %collective-permute-done.6.refs_4_ = bf16[640,512]{1,0:T(8,128)(2,1)S(1)} collective-permute-done((bf16[640,512]{1,0:T(8,128)(2,1)S(1)}, bf16[640,512]{1,0:T(8,128)(2,1)S(1)}, u32[]{:S(2)}, u32[]{:S(2)}) %collective-permute-start.6) | collective-permute-done | bytes 655392 | tf_op jit(solution)/shard_map/ppermute | solution.py:31
  75.3 3.6 %far_product.1 = (f32[320,640]{1,0:T(8,128)S(1)}, f32[320,640]{1,0:T(8,128)S(1)}, f32[320,640]{1,0:T(8,128)S(1)}, f32[320,640]{1,0:T(8,128)S(1)}, f32[320,640]{1...) custom-call(bf16[1280,512]{1,0:T(8,128)(2,1)S(1)} %constant_dynamic-, ...), custom_call_target="tpu_custom_call" | custom-call | tf_op jit(solution)/shard_map/far_product/pallas_call | solution.py:160
  78.9 2.9 %collective-permute-start.16 = (f32[320,640]{1,0:T(8,128)S(1)}, f32[320,640]{1,0:T(8,128)S(1)}, u32[]{:S(2)}, u32[]{:S(2)}) collective-permute-start(f32[320,640]{1,0:T(8,128)S(1)} %get-tuple-element.65), channel_id=1, source_target_pairs={{0,16},{1,17},{2,18},{3,19},{4,20},{5,21},{6,22},{7,23},{8,24},{9,... | collective-permute-start | bytes 2457608 | tf_op jit(solution)/shard_map/ppermute | solution.py:31
  82.3 1.4 collective-permute-done.16
  83.9 1.7 %collective-permute-start.22 = (f32[160,640]{1,0:T(8,128)S(1)}, f32[160,640]{1,0:T(8,128)S(1)}, u32[]{:S(2)}, u32[]{:S(2)}) collective-permute-start(f32[160,640]{1,0:T(8,128)S(1)} %get-tuple-element.86), channel_id=1, source_target_pairs={{0,1},{1,2},{2,3},{3,0},{4,5},{5,6},{6,7},{7,4},{8,9},{9,10},{10,1... | collective-permute-start | bytes 1228808 | tf_op jit(solution)/shard_map/ppermute | solution.py:31
  86.3 1.4 collective-permute-start.17
  87.7 8.3 %collective-permute-done.22 = f32[160,640]{1,0:T(8,128)S(1)} collective-permute-done((f32[160,640]{1,0:T(8,128)S(1)}, f32[160,640]{1,0:T(8,128)S(1)}, u32[]{:S(2)}, u32[]{:S(2)}) %collective-permute-start.22) | collective-permute-done | bytes 409632 | tf_op jit(solution)/shard_map/ppermute | solution.py:31
  98.2 1.9 %collective-permute-start.18 = (f32[160,640]{1,0:T(8,128)S(1)}, f32[160,640]{1,0:T(8,128)S(1)}, u32[]{:S(2)}, u32[]{:S(2)}) collective-permute-start(f32[160,640]{1,0:T(8,128)S(1)} %get-tuple-element.89), channel_id=1, source_target_pairs={{0,3},{1,0},{2,1},{3,2},{4,7},{5,4},{6,5},{7,6},{8,11},{9,8},{10,9... | collective-permute-start | bytes 1228808 | tf_op jit(solution)/shard_map/ppermute | solution.py:31
  100.1 6.1 %collective-permute-done.24.refs_10_.refs_1_ = f32[320,640]{1,0:T(8,128)S(1)} collective-permute-done((f32[320,640]{1,0:T(8,128)S(1)}, f32[320,640]{1,0:T(8,128)S(1)}, u32[]{:S(2)}, u32[]{:S(2)}) %collective-permute-start.24) | collective-permute-done | bytes 819232 | tf_op jit(solution)/shard_map/ppermute | solution.py:31
  106.1 1.0 collective-permute-start.19
  108.0 7.7 %collective-permute-done.25.refs_11_.refs_2_ = f32[320,640]{1,0:T(8,128)S(1)} collective-permute-done((f32[320,640]{1,0:T(8,128)S(1)}, f32[320,640]{1,0:T(8,128)S(1)}, u32[]{:S(2)}, u32[]{:S(2)}) %collective-permute-start.25) | collective-permute-done | bytes 819232 | tf_op jit(solution)/shard_map/ppermute | solution.py:31
  116.0 1.7 %collective-permute-done.19.refs_3_ = f32[160,640]{1,0:T(8,128)S(1)} collective-permute-done((f32[160,640]{1,0:T(8,128)S(1)}, f32[160,640]{1,0:T(8,128)S(1)}, u32[]{:S(2)}, u32[]{:S(2)}) %collective-permute-start.19) | collective-permute-done | bytes 409632 | tf_op jit(solution)/shard_map/ppermute | solution.py:31
  117.7 1.5 update.1
  120.1 1.3 collective-permute-start.36
  121.6 2.0 %collective-permute-start.26 = (f32[16,128]{1,0:T(8,128)S(1)}, f32[16,128]{1,0:T(8,128)S(1)}, u32[]{:S(2)}, u32[]{:S(2)}) collective-permute-start(f32[16,128]{1,0:T(8,128)S(1)} %get-tuple-element.69), channel_id=1, source_target_pairs={{0,16},{1,17},{2,18},{3,19},{4,20},{5,21},{6,22},{7,23},{8,24},{9,... | collective-permute-start | bytes 24584 | tf_op jit(solution)/shard_map/ppermute | solution.py:31
  124.5 2.3 %collective-permute-start.27 = (f32[16,128]{1,0:T(8,128)S(1)}, f32[16,128]{1,0:T(8,128)S(1)}, u32[]{:S(2)}, u32[]{:S(2)}) collective-permute-start(f32[16,128]{1,0:T(8,128)S(1)} %add.62), channel_id=1, source_target_pairs={{0,8},{1,9},{2,10},{3,11},{4,12},{5,13},{6,14},{7,15},{8,0},{9,1},... | collective-permute-start | bytes 24584 | tf_op jit(solution)/shard_map/ppermute | solution.py:31
  127.7 1.8 %collective-permute-start.29 = (f32[16,128]{1,0:T(8,128)S(1)}, f32[16,128]{1,0:T(8,128)S(1)}, u32[]{:S(2)}, u32[]{:S(2)}) collective-permute-start(f32[16,128]{1,0:T(8,128)S(1)} %add.62), channel_id=1, source_target_pairs={{0,12},{1,13},{2,14},{3,15},{4,0},{5,1},{6,2},{7,3},{8,4},{9,5},{1... | collective-permute-start | bytes 24584 | tf_op jit(solution)/shard_map/ppermute | solution.py:31
  129.4 1.3 collective-permute-done.28
  130.8 2.3 %collective-permute-start.30 = (f32[16,128]{1,0:T(8,128)S(1)}, f32[16,128]{1,0:T(8,128)S(1)}, u32[]{:S(2)}, u32[]{:S(2)}) collective-permute-start(f32[16,128]{1,0:T(8,128)S(1)} %add_add_fusion.2), channel_id=1, source_target_pairs={{0,2},{1,3},{2,0},{3,1},{4,6},{5,7},{6,4},{7,5},{8,10},{9,11},{10,... | collective-permute-start | bytes 24584 | tf_op jit(solution)/shard_map/ppermute | solution.py:31
  133.1 1.8 %collective-permute-start.31 = (f32[16,128]{1,0:T(8,128)S(1)}, f32[16,128]{1,0:T(8,128)S(1)}, u32[]{:S(2)}, u32[]{:S(2)}) collective-permute-start(f32[16,128]{1,0:T(8,128)S(1)} %add_add_fusion.2), channel_id=1, source_target_pairs={{0,1},{1,2},{2,3},{3,0},{4,5},{5,6},{6,7},{7,4},{8,9},{9,10},{10,1... | collective-permute-start | bytes 24584 | tf_op jit(solution)/shard_map/ppermute | solution.py:31
  138.5 2.6 %collective-permute-start.34 = (f32[16,128]{1,0:T(8,128)S(1)}, f32[16,128]{1,0:T(8,128)S(1)}, u32[]{:S(2)}, u32[]{:S(2)}) collective-permute-start(f32[16,128]{1,0:T(8,128)S(1)} %add_add_fusion.1), channel_id=1, source_target_pairs={{0,32},{1,33},{2,34},{3,35},{4,36},{5,37},{6,38},{7,39},{8,40},{9,... | collective-permute-start | bytes 24584 | tf_op jit(solution)/shard_map/ppermute | solution.py:31
  142.7 1.0 collective-permute-done.35
  143.7 1.5 step.1
  145.3 4.7 %collective-permute-start.38 = (bf16[320,640]{1,0:T(8,128)(2,1)S(1)}, bf16[320,640]{1,0:T(8,128)(2,1)S(1)}, u32[]{:S(2)}, u32[]{:S(2)}) collective-permute-start(bf16[320,640]{1,0:T(8,128)(2,1)S(1)} %get-tuple-element.71.refs_0_.step), channel_id=1, source_target_pairs={{0,16},{1,17},{2,18},{3,19},{4,20},{5,21},{6,22},{7,23},{8,24},{9,... | collective-permute-start | bytes 1228808 | tf_op jit(solution)/shard_map/ppermute | solution.py:31
  150.5 1.6 collective-permute-start.41
  152.0 4.7 %new_state.1 = (f32[320,640]{1,0:T(8,128)}, f32[320,640]{1,0:T(8,128)}, f32[320,640]{1,0:T(8,128)}) custom-call(f32[16,128]{1,0:T(8,128)S(1)} %add_add_fusion.sums, f32[1]{0:T(128)} %bitcast.5.rate, f32[320,640]{1,0:T(8,128)} %bitcast.11, f32[320,640]{1,0:T(8,128)} %bitcast.15, f32[320,640]{1,0:T(8,128)} %bitcast.17, ...), custom_call_target="tpu_custom_call" | custom-call | tf_op jit(solution)/shard_map/new_state/pallas_call | solution.py:342
  156.7 1.5 placed.2.refs_4_
  158.3 1.3 collective-permute-done.42.refs_2_
  159.5 1.2 collective-permute-start.43
  160.7 1.1 collective-permute-done.43.refs_1_
  (88 shorter events, 13.9 us)
Async XLA Ops:
  2.7 12.1 %collective-permute-start.7 = (bf16[128,1280]{1,0:T(8,128)(2,1)S(1)}, bf16[128,1280]{1,0:T(8,128)(2,1)S(1)}, u32[]{:S(2)}, u32[]{:S(2)}) collective-permute-start(bf16[128,1280]{1,0:T(8,128)(2,1)S(1)} %get-tuple-element.53), channel_id=1, source_target_pairs={{0,32},{1,33},{2,34},{3,35},{4,36},{5,37},{6,38},{7,39},{8,40},{9,... | collective-permute-start | bytes 983048 | tf_op jit(solution)/shard_map/ppermute | solution.py:31
  5.3 17.4 %collective-permute-start.8 = (bf16[128,1280]{1,0:T(8,128)(2,1)S(1)}, bf16[128,1280]{1,0:T(8,128)(2,1)S(1)}, u32[]{:S(2)}, u32[]{:S(2)}) collective-permute-start(bf16[128,1280]{1,0:T(8,128)(2,1)S(1)} %get-tuple-element.54), channel_id=1, source_target_pairs={{0,64},{1,65},{2,66},{3,67},{4,68},{5,69},{6,70},{7,71},{8,72},{9,... | collective-permute-start | bytes 983048 | tf_op jit(solution)/shard_map/ppermute | solution.py:31
  8.6 14.2 %collective-permute-start.9 = (bf16[128,1280]{1,0:T(8,128)(2,1)S(1)}, bf16[128,1280]{1,0:T(8,128)(2,1)S(1)}, u32[]{:S(2)}, u32[]{:S(2)}) collective-permute-start(bf16[128,1280]{1,0:T(8,128)(2,1)S(1)} %get-tuple-element.55), channel_id=1, source_target_pairs={{0,96},{1,97},{2,98},{3,99},{4,100},{5,101},{6,102},{7,103},{8,104... | collective-permute-start | bytes 983048 | tf_op jit(solution)/shard_map/ppermute | solution.py:31
  9.3 16.0 %collective-permute-start = (bf16[320,512]{1,0:T(8,128)(2,1)S(1)}, bf16[320,512]{1,0:T(8,128)(2,1)S(1)}, u32[]{:S(2)}, u32[]{:S(2)}) collective-permute-start(bf16[320,512]{1,0:T(8,128)(2,1)S(1)} %get-tuple-element.45), channel_id=1, source_target_pairs={{0,1},{1,2},{2,3},{3,0},{4,5},{5,6},{6,7},{7,4},{8,9},{9,10},{10,1... | collective-permute-start | bytes 983048 | tf_op jit(solution)/shard_map/ppermute | solution.py:31
  10.6 15.9 %collective-permute-start.1 = (bf16[320,512]{1,0:T(8,128)(2,1)S(1)}, bf16[320,512]{1,0:T(8,128)(2,1)S(1)}, u32[]{:S(2)}, u32[]{:S(2)}) collective-permute-start(bf16[320,512]{1,0:T(8,128)(2,1)S(1)} %get-tuple-element.46), channel_id=1, source_target_pairs={{0,2},{1,3},{2,0},{3,1},{4,6},{5,7},{6,4},{7,5},{8,10},{9,11},{10,... | collective-permute-start | bytes 983048 | tf_op jit(solution)/shard_map/ppermute | solution.py:31
  14.8 11.7 %collective-permute-start.2 = (bf16[320,512]{1,0:T(8,128)(2,1)S(1)}, bf16[320,512]{1,0:T(8,128)(2,1)S(1)}, u32[]{:S(2)}, u32[]{:S(2)}) collective-permute-start(bf16[320,512]{1,0:T(8,128)(2,1)S(1)} %get-tuple-element.47), channel_id=1, source_target_pairs={{0,3},{1,0},{2,1},{3,2},{4,7},{5,4},{6,5},{7,6},{8,11},{9,8},{10,9... | collective-permute-start | bytes 983048 | tf_op jit(solution)/shard_map/ppermute | solution.py:31
  22.8 29.1 %collective-permute-start.10 = (bf16[512,1280]{1,0:T(8,128)(2,1)S(1)}, bf16[512,1280]{1,0:T(8,128)(2,1)S(1)}, u32[]{:S(2)}, u32[]{:S(2)}) collective-permute-start(bf16[512,1280]{1,0:T(8,128)(2,1)S(1)} %constant_dynamic-update-slice_fusion.4.x0.refs_5_), channel_id=1, source_target_pairs={{0,12},{1,13},{2,14},{3,15},{4,0},{5,1},{6,2},{7,3},{8,4},{9,5},{1... | collective-permute-start | bytes 3932168 | tf_op jit(solution)/shard_map/ppermute | solution.py:31
  25.3 30.1 %collective-permute-start.11 = (bf16[512,1280]{1,0:T(8,128)(2,1)S(1)}, bf16[512,1280]{1,0:T(8,128)(2,1)S(1)}, u32[]{:S(2)}, u32[]{:S(2)}) collective-permute-start(bf16[512,1280]{1,0:T(8,128)(2,1)S(1)} %constant_dynamic-update-slice_fusion.4.x0.refs_5_), channel_id=1, source_target_pairs={{0,4},{1,5},{2,6},{3,7},{4,8},{5,9},{6,10},{7,11},{8,12},{9,13},{1... | collective-permute-start | bytes 3932168 | tf_op jit(solution)/shard_map/ppermute | solution.py:31
  26.5 29.2 %collective-permute-start.3 = (bf16[1280,512]{1,0:T(8,128)(2,1)S(1)}, bf16[1280,512]{1,0:T(8,128)(2,1)S(1)}, u32[]{:S(2)}, u32[]{:S(2)}) collective-permute-start(bf16[1280,512]{1,0:T(8,128)(2,1)S(1)} %constant_dynamic-update-slice_fusion.z0.refs_0_), channel_id=1, source_target_pairs={{0,96},{1,97},{2,98},{3,99},{4,100},{5,101},{6,102},{7,103},{8,104... | collective-permute-start | bytes 3932168 | tf_op jit(solution)/shard_map/ppermute | solution.py:31
  28.4 31.3 %collective-permute-start.4 = (bf16[1280,512]{1,0:T(8,128)(2,1)S(1)}, bf16[1280,512]{1,0:T(8,128)(2,1)S(1)}, u32[]{:S(2)}, u32[]{:S(2)}) collective-permute-start(bf16[1280,512]{1,0:T(8,128)(2,1)S(1)} %constant_dynamic-update-slice_fusion.z0.refs_0_), channel_id=1, source_target_pairs={{0,32},{1,33},{2,34},{3,35},{4,36},{5,37},{6,38},{7,39},{8,40},{9,... | collective-permute-start | bytes 3932168 | tf_op jit(solution)/shard_map/ppermute | solution.py:31
  51.9 15.0 %collective-permute-start.12 = (bf16[256,1280]{1,0:T(8,128)(2,1)S(1)}, bf16[256,1280]{1,0:T(8,128)(2,1)S(1)}, u32[]{:S(2)}, u32[]{:S(2)}) collective-permute-start(bf16[256,1280]{1,0:T(8,128)(2,1)S(1)} %slice.66), channel_id=1, source_target_pairs={{0,12},{1,13},{2,14},{3,15},{4,0},{5,1},{6,2},{7,3},{8,4},{9,5},{1... | collective-permute-start | bytes 1966088 | tf_op jit(solution)/shard_map/ppermute | solution.py:31
  55.4 14.8 %collective-permute-start.13 = (bf16[256,1280]{1,0:T(8,128)(2,1)S(1)}, bf16[256,1280]{1,0:T(8,128)(2,1)S(1)}, u32[]{:S(2)}, u32[]{:S(2)}) collective-permute-start(bf16[256,1280]{1,0:T(8,128)(2,1)S(1)} %slice.67), channel_id=1, source_target_pairs={{0,4},{1,5},{2,6},{3,7},{4,8},{5,9},{6,10},{7,11},{8,12},{9,13},{1... | collective-permute-start | bytes 1966088 | tf_op jit(solution)/shard_map/ppermute | solution.py:31
  55.8 16.3 %collective-permute-start.5 = (bf16[640,512]{1,0:T(8,128)(2,1)S(1)}, bf16[640,512]{1,0:T(8,128)(2,1)S(1)}, u32[]{:S(2)}, u32[]{:S(2)}) collective-permute-start(bf16[640,512]{1,0:T(8,128)(2,1)S(1)} %slice.64), channel_id=1, source_target_pairs={{0,96},{1,97},{2,98},{3,99},{4,100},{5,101},{6,102},{7,103},{8,104... | collective-permute-start | bytes 1966088 | tf_op jit(solution)/shard_map/ppermute | solution.py:31
  59.7 15.6 %collective-permute-start.6 = (bf16[640,512]{1,0:T(8,128)(2,1)S(1)}, bf16[640,512]{1,0:T(8,128)(2,1)S(1)}, u32[]{:S(2)}, u32[]{:S(2)}) collective-permute-start(bf16[640,512]{1,0:T(8,128)(2,1)S(1)} %slice.65), channel_id=1, source_target_pairs={{0,32},{1,33},{2,34},{3,35},{4,36},{5,37},{6,38},{7,39},{8,40},{9,... | collective-permute-start | bytes 1966088 | tf_op jit(solution)/shard_map/ppermute | solution.py:31
  78.9 4.9 %collective-permute-start.16 = (f32[320,640]{1,0:T(8,128)S(1)}, f32[320,640]{1,0:T(8,128)S(1)}, u32[]{:S(2)}, u32[]{:S(2)}) collective-permute-start(f32[320,640]{1,0:T(8,128)S(1)} %get-tuple-element.65), channel_id=1, source_target_pairs={{0,16},{1,17},{2,18},{3,19},{4,20},{5,21},{6,22},{7,23},{8,24},{9,... | collective-permute-start | bytes 2457608 | tf_op jit(solution)/shard_map/ppermute | solution.py:31
  81.8 4.5 %collective-permute-start.20 = (f32[320,640]{1,0:T(8,128)S(1)}, f32[320,640]{1,0:T(8,128)S(1)}, u32[]{:S(2)}, u32[]{:S(2)}) collective-permute-start(f32[320,640]{1,0:T(8,128)S(1)} %get-tuple-element.67), channel_id=1, source_target_pairs={{0,16},{1,17},{2,18},{3,19},{4,20},{5,21},{6,22},{7,23},{8,24},{9,... | collective-permute-start | bytes 2457608 | tf_op jit(solution)/shard_map/ppermute | solution.py:31
  81.9 14.1 %collective-permute-start.15 = (f32[320,640]{1,0:T(8,128)S(1)}, f32[320,640]{1,0:T(8,128)S(1)}, u32[]{:S(2)}, u32[]{:S(2)}) collective-permute-start(f32[320,640]{1,0:T(8,128)S(1)} %get-tuple-element.63), channel_id=1, source_target_pairs={{0,16},{1,17},{2,18},{3,19},{4,20},{5,21},{6,22},{7,23},{8,24},{9,... | collective-permute-start | bytes 2457608 | tf_op jit(solution)/shard_map/ppermute | solution.py:31
  83.9 12.1 %collective-permute-start.22 = (f32[160,640]{1,0:T(8,128)S(1)}, f32[160,640]{1,0:T(8,128)S(1)}, u32[]{:S(2)}, u32[]{:S(2)}) collective-permute-start(f32[160,640]{1,0:T(8,128)S(1)} %get-tuple-element.86), channel_id=1, source_target_pairs={{0,1},{1,2},{2,3},{3,0},{4,5},{5,6},{6,7},{7,4},{8,9},{9,10},{10,1... | collective-permute-start | bytes 1228808 | tf_op jit(solution)/shard_map/ppermute | solution.py:31
  85.6 12.6 %collective-permute-start.14 = (f32[320,640]{1,0:T(8,128)S(1)}, f32[320,640]{1,0:T(8,128)S(1)}, u32[]{:S(2)}, u32[]{:S(2)}) collective-permute-start(f32[320,640]{1,0:T(8,128)S(1)} %get-tuple-element.61), channel_id=1, source_target_pairs={{0,16},{1,17},{2,18},{3,19},{4,20},{5,21},{6,22},{7,23},{8,24},{9,... | collective-permute-start | bytes 2457608 | tf_op jit(solution)/shard_map/ppermute | solution.py:31
  86.3 19.9 %collective-permute-start.24 = (f32[320,640]{1,0:T(8,128)S(1)}, f32[320,640]{1,0:T(8,128)S(1)}, u32[]{:S(2)}, u32[]{:S(2)}) collective-permute-start(f32[320,640]{1,0:T(8,128)S(1)} %get-tuple-element.68), channel_id=1, source_target_pairs={{0,96},{1,97},{2,98},{3,99},{4,100},{5,101},{6,102},{7,103},{8,104... | collective-permute-start | bytes 2457608 | tf_op jit(solution)/shard_map/ppermute | solution.py:31
  86.3 10.9 %collective-permute-start.17 = (f32[160,640]{1,0:T(8,128)S(1)}, f32[160,640]{1,0:T(8,128)S(1)}, u32[]{:S(2)}, u32[]{:S(2)}) collective-permute-start(f32[160,640]{1,0:T(8,128)S(1)} %get-tuple-element.87), channel_id=1, source_target_pairs={{0,3},{1,0},{2,1},{3,2},{4,7},{5,4},{6,5},{7,6},{8,11},{9,8},{10,9... | collective-permute-start | bytes 1228808 | tf_op jit(solution)/shard_map/ppermute | solution.py:31
  96.0 19.8 %collective-permute-start.25 = (f32[320,640]{1,0:T(8,128)S(1)}, f32[320,640]{1,0:T(8,128)S(1)}, u32[]{:S(2)}, u32[]{:S(2)}) collective-permute-start(f32[320,640]{1,0:T(8,128)S(1)} %get-tuple-element.68), channel_id=1, source_target_pairs={{0,32},{1,33},{2,34},{3,35},{4,36},{5,37},{6,38},{7,39},{8,40},{9,... | collective-permute-start | bytes 2457608 | tf_op jit(solution)/shard_map/ppermute | solution.py:31
  96.1 19.7 %collective-permute-start.21 = (f32[160,640]{1,0:T(8,128)S(1)}, f32[160,640]{1,0:T(8,128)S(1)}, u32[]{:S(2)}, u32[]{:S(2)}) collective-permute-start(f32[160,640]{1,0:T(8,128)S(1)} %get-tuple-element.85), channel_id=1, source_target_pairs={{0,1},{1,2},{2,3},{3,0},{4,5},{5,6},{6,7},{7,4},{8,9},{9,10},{10,1... | collective-permute-start | bytes 1228808 | tf_op jit(solution)/shard_map/ppermute | solution.py:31
  97.2 18.8 %collective-permute-start.23 = (f32[160,640]{1,0:T(8,128)S(1)}, f32[160,640]{1,0:T(8,128)S(1)}, u32[]{:S(2)}, u32[]{:S(2)}) collective-permute-start(f32[160,640]{1,0:T(8,128)S(1)} %get-tuple-element.84), channel_id=1, source_target_pairs={{0,1},{1,2},{2,3},{3,0},{4,5},{5,6},{6,7},{7,4},{8,9},{9,10},{10,1... | collective-permute-start | bytes 1228808 | tf_op jit(solution)/shard_map/ppermute | solution.py:31
  98.1 19.6 %copy-start.1 = (f32[640,320]{0,1:T(8,128)S(1)}, f32[640,320]{0,1:T(8,128)}, u32[]{:S(2)}) copy-start(f32[640,320]{0,1:T(8,128)} %param.11) | copy-start | bytes 2457604
  98.1 19.6 %copy-start.2 = (f32[640,320]{0,1:T(8,128)S(1)}, f32[640,320]{0,1:T(8,128)}, u32[]{:S(2)}) copy-start(f32[640,320]{0,1:T(8,128)} %param.12) | copy-start | bytes 2457604
  98.2 17.7 %collective-permute-start.18 = (f32[160,640]{1,0:T(8,128)S(1)}, f32[160,640]{1,0:T(8,128)S(1)}, u32[]{:S(2)}, u32[]{:S(2)}) collective-permute-start(f32[160,640]{1,0:T(8,128)S(1)} %get-tuple-element.89), channel_id=1, source_target_pairs={{0,3},{1,0},{2,1},{3,2},{4,7},{5,4},{6,5},{7,6},{8,11},{9,8},{10,9... | collective-permute-start | bytes 1228808 | tf_op jit(solution)/shard_map/ppermute | solution.py:31
  106.1 11.6 %collective-permute-start.19 = (f32[160,640]{1,0:T(8,128)S(1)}, f32[160,640]{1,0:T(8,128)S(1)}, u32[]{:S(2)}, u32[]{:S(2)}) collective-permute-start(f32[160,640]{1,0:T(8,128)S(1)} %get-tuple-element.88), channel_id=1, source_target_pairs={{0,3},{1,0},{2,1},{3,2},{4,7},{5,4},{6,5},{7,6},{8,11},{9,8},{10,9... | collective-permute-start | bytes 1228808 | tf_op jit(solution)/shard_map/ppermute | solution.py:31
  117.7 23.5 %copy-start.7 = (f32[8]{0:T(128)S(1)}, f32[8]{0:T(128)}, u32[]{:S(2)}) copy-start(f32[8]{0:T(128)} %param.15) | copy-start | bytes 100
  120.1 23.6 %collective-permute-start.36 = (f32[320,640]{1,0:T(8,128)S(1)}, f32[320,640]{1,0:T(8,128)S(1)}, u32[]{:S(2)}, u32[]{:S(2)}) collective-permute-start(f32[320,640]{1,0:T(8,128)S(1)} %get-tuple-element.70.refs_3_.update), channel_id=1, source_target_pairs={{0,96},{1,97},{2,98},{3,99},{4,100},{5,101},{6,102},{7,103},{8,104... | collective-permute-start | bytes 2457608 | tf_op jit(solution)/shard_map/ppermute | solution.py:31
  121.4 22.3 %collective-permute-start.37 = (f32[320,640]{1,0:T(8,128)S(1)}, f32[320,640]{1,0:T(8,128)S(1)}, u32[]{:S(2)}, u32[]{:S(2)}) collective-permute-start(f32[320,640]{1,0:T(8,128)S(1)} %get-tuple-element.70.refs_3_.update), channel_id=1, source_target_pairs={{0,32},{1,33},{2,34},{3,35},{4,36},{5,37},{6,38},{7,39},{8,40},{9,... | collective-permute-start | bytes 2457608 | tf_op jit(solution)/shard_map/ppermute | solution.py:31
  121.6 2.9 %collective-permute-start.26 = (f32[16,128]{1,0:T(8,128)S(1)}, f32[16,128]{1,0:T(8,128)S(1)}, u32[]{:S(2)}, u32[]{:S(2)}) collective-permute-start(f32[16,128]{1,0:T(8,128)S(1)} %get-tuple-element.69), channel_id=1, source_target_pairs={{0,16},{1,17},{2,18},{3,19},{4,20},{5,21},{6,22},{7,23},{8,24},{9,... | collective-permute-start | bytes 24584 | tf_op jit(solution)/shard_map/ppermute | solution.py:31
  124.5 5.0 %collective-permute-start.27 = (f32[16,128]{1,0:T(8,128)S(1)}, f32[16,128]{1,0:T(8,128)S(1)}, u32[]{:S(2)}, u32[]{:S(2)}) collective-permute-start(f32[16,128]{1,0:T(8,128)S(1)} %add.62), channel_id=1, source_target_pairs={{0,8},{1,9},{2,10},{3,11},{4,12},{5,13},{6,14},{7,15},{8,0},{9,1},... | collective-permute-start | bytes 24584 | tf_op jit(solution)/shard_map/ppermute | solution.py:31
  126.8 4.0 %collective-permute-start.28 = (f32[16,128]{1,0:T(8,128)S(1)}, f32[16,128]{1,0:T(8,128)S(1)}, u32[]{:S(2)}, u32[]{:S(2)}) collective-permute-start(f32[16,128]{1,0:T(8,128)S(1)} %add.62), channel_id=1, source_target_pairs={{0,4},{1,5},{2,6},{3,7},{4,8},{5,9},{6,10},{7,11},{8,12},{9,13},{1... | collective-permute-start | bytes 24584 | tf_op jit(solution)/shard_map/ppermute | solution.py:31
  127.7 3.1 %collective-permute-start.29 = (f32[16,128]{1,0:T(8,128)S(1)}, f32[16,128]{1,0:T(8,128)S(1)}, u32[]{:S(2)}, u32[]{:S(2)}) collective-permute-start(f32[16,128]{1,0:T(8,128)S(1)} %add.62), channel_id=1, source_target_pairs={{0,12},{1,13},{2,14},{3,15},{4,0},{5,1},{6,2},{7,3},{8,4},{9,5},{1... | collective-permute-start | bytes 24584 | tf_op jit(solution)/shard_map/ppermute | solution.py:31
  130.8 5.7 %collective-permute-start.30 = (f32[16,128]{1,0:T(8,128)S(1)}, f32[16,128]{1,0:T(8,128)S(1)}, u32[]{:S(2)}, u32[]{:S(2)}) collective-permute-start(f32[16,128]{1,0:T(8,128)S(1)} %add_add_fusion.2), channel_id=1, source_target_pairs={{0,2},{1,3},{2,0},{3,1},{4,6},{5,7},{6,4},{7,5},{8,10},{9,11},{10,... | collective-permute-start | bytes 24584 | tf_op jit(solution)/shard_map/ppermute | solution.py:31
  133.1 4.1 %collective-permute-start.31 = (f32[16,128]{1,0:T(8,128)S(1)}, f32[16,128]{1,0:T(8,128)S(1)}, u32[]{:S(2)}, u32[]{:S(2)}) collective-permute-start(f32[16,128]{1,0:T(8,128)S(1)} %add_add_fusion.2), channel_id=1, source_target_pairs={{0,1},{1,2},{2,3},{3,0},{4,5},{5,6},{6,7},{7,4},{8,9},{9,10},{10,1... | collective-permute-start | bytes 24584 | tf_op jit(solution)/shard_map/ppermute | solution.py:31
  134.8 2.8 %collective-permute-start.32 = (f32[16,128]{1,0:T(8,128)S(1)}, f32[16,128]{1,0:T(8,128)S(1)}, u32[]{:S(2)}, u32[]{:S(2)}) collective-permute-start(f32[16,128]{1,0:T(8,128)S(1)} %add_add_fusion.2), channel_id=1, source_target_pairs={{0,3},{1,0},{2,1},{3,2},{4,7},{5,4},{6,5},{7,6},{8,11},{9,8},{10,9... | collective-permute-start | bytes 24584 | tf_op jit(solution)/shard_map/ppermute | solution.py:31
  137.6 4.7 %collective-permute-start.33 = (f32[16,128]{1,0:T(8,128)S(1)}, f32[16,128]{1,0:T(8,128)S(1)}, u32[]{:S(2)}, u32[]{:S(2)}) collective-permute-start(f32[16,128]{1,0:T(8,128)S(1)} %add_add_fusion.1), channel_id=1, source_target_pairs={{0,64},{1,65},{2,66},{3,67},{4,68},{5,69},{6,70},{7,71},{8,72},{9,... | collective-permute-start | bytes 24584 | tf_op jit(solution)/shard_map/ppermute | solution.py:31
  138.5 4.2 %collective-permute-start.34 = (f32[16,128]{1,0:T(8,128)S(1)}, f32[16,128]{1,0:T(8,128)S(1)}, u32[]{:S(2)}, u32[]{:S(2)}) collective-permute-start(f32[16,128]{1,0:T(8,128)S(1)} %add_add_fusion.1), channel_id=1, source_target_pairs={{0,32},{1,33},{2,34},{3,35},{4,36},{5,37},{6,38},{7,39},{8,40},{9,... | collective-permute-start | bytes 24584 | tf_op jit(solution)/shard_map/ppermute | solution.py:31
  141.2 2.5 %collective-permute-start.35 = (f32[16,128]{1,0:T(8,128)S(1)}, f32[16,128]{1,0:T(8,128)S(1)}, u32[]{:S(2)}, u32[]{:S(2)}) collective-permute-start(f32[16,128]{1,0:T(8,128)S(1)} %add_add_fusion.1), channel_id=1, source_target_pairs={{0,96},{1,97},{2,98},{3,99},{4,100},{5,101},{6,102},{7,103},{8,104... | collective-permute-start | bytes 24584 | tf_op jit(solution)/shard_map/ppermute | solution.py:31
  145.3 11.4 %collective-permute-start.38 = (bf16[320,640]{1,0:T(8,128)(2,1)S(1)}, bf16[320,640]{1,0:T(8,128)(2,1)S(1)}, u32[]{:S(2)}, u32[]{:S(2)}) collective-permute-start(bf16[320,640]{1,0:T(8,128)(2,1)S(1)} %get-tuple-element.71.refs_0_.step), channel_id=1, source_target_pairs={{0,16},{1,17},{2,18},{3,19},{4,20},{5,21},{6,22},{7,23},{8,24},{9,... | collective-permute-start | bytes 1228808 | tf_op jit(solution)/shard_map/ppermute | solution.py:31
  150.0 6.8 %collective-permute-start.39 = (bf16[320,640]{1,0:T(8,128)(2,1)S(1)}, bf16[320,640]{1,0:T(8,128)(2,1)S(1)}, u32[]{:S(2)}, u32[]{:S(2)}) collective-permute-start(bf16[320,640]{1,0:T(8,128)(2,1)S(1)} %get-tuple-element.72.refs_2_), channel_id=1, source_target_pairs={{0,16},{1,17},{2,18},{3,19},{4,20},{5,21},{6,22},{7,23},{8,24},{9,... | collective-permute-start | bytes 1228808 | tf_op jit(solution)/shard_map/ppermute | solution.py:31
  150.0 6.7 %collective-permute-start.40 = (bf16[320,640]{1,0:T(8,128)(2,1)S(1)}, bf16[320,640]{1,0:T(8,128)(2,1)S(1)}, u32[]{:S(2)}, u32[]{:S(2)}) collective-permute-start(bf16[320,640]{1,0:T(8,128)(2,1)S(1)} %get-tuple-element.73.refs_4_), channel_id=1, source_target_pairs={{0,16},{1,17},{2,18},{3,19},{4,20},{5,21},{6,22},{7,23},{8,24},{9,... | collective-permute-start | bytes 1228808 | tf_op jit(solution)/shard_map/ppermute | solution.py:31
  150.5 7.8 %collective-permute-start.41 = (bf16[160,640]{1,0:T(8,128)(2,1)S(1)}, bf16[160,640]{1,0:T(8,128)(2,1)S(1)}, u32[]{:S(2)}, u32[]{:S(2)}) collective-permute-start(bf16[160,640]{1,0:T(8,128)(2,1)S(1)} %get-tuple-element.76), channel_id=1, source_target_pairs={{0,96},{1,97},{2,98},{3,99},{4,100},{5,101},{6,102},{7,103},{8,104... | collective-permute-start | bytes 614408 | tf_op jit(solution)/shard_map/ppermute | solution.py:31
  152.0 7.5 %collective-permute-start.42 = (bf16[160,640]{1,0:T(8,128)(2,1)S(1)}, bf16[160,640]{1,0:T(8,128)(2,1)S(1)}, u32[]{:S(2)}, u32[]{:S(2)}) collective-permute-start(bf16[160,640]{1,0:T(8,128)(2,1)S(1)} %get-tuple-element.77), channel_id=1, source_target_pairs={{0,32},{1,33},{2,34},{3,35},{4,36},{5,37},{6,38},{7,39},{8,40},{9,... | collective-permute-start | bytes 614408 | tf_op jit(solution)/shard_map/ppermute | solution.py:31
  159.5 2.3 %collective-permute-start.43 = (bf16[160,640]{1,0:T(8,128)(2,1)S(1)}, bf16[160,640]{1,0:T(8,128)(2,1)S(1)}, u32[]{:S(2)}, u32[]{:S(2)}) collective-permute-start(bf16[160,640]{1,0:T(8,128)(2,1)S(1)} %collective-permute-done.41.refs_0_), channel_id=1, source_target_pairs={{0,16},{1,17},{2,18},{3,19},{4,20},{5,21},{6,22},{7,23},{8,24},{9,... | collective-permute-start | bytes 614408 | tf_op jit(solution)/shard_map/ppermute | solution.py:31
  160.7 1.5 collective-permute-start.44
  (5 other events, 41.3 us)

commit v6 on v4

v6 whole, which is shorter than its diff:
```python
import functools

import jax
import jax.numpy as jnp
from jax import lax
from jax.experimental import pallas as pl
from jax.experimental.pallas import tpu as pltpu
from jax.sharding import PartitionSpec as P

beta_one = 0.9
beta_two = 0.999
epsilon = 1e-06
decay_weight = 0.1
base_rate = 0.25

ROWS = 640
COLS = 320
BLOCK = 128
GROUP = 2 * ROWS


def moved(array, dz=0, dc=0, dx=0, dy=0):
    pairs = []
    for z in range(4):
        for c in range(2):
            for x in range(4):
                for y in range(4):
                    src = (2 * z + c) * 16 + 4 * x + y
                    dst = (2 * ((z + dz) % 4) + (c + dc) % 2) * 16 + 4 * ((x + dx) % 4) + (y + dy) % 4
                    pairs.append((src, dst))
    return lax.ppermute(array, ("dp", "mp"), pairs)


def place():
    d = lax.axis_index("dp")
    m = lax.axis_index("mp")
    return d // 2, d % 2, m // 4, m % 4


HBM = pl.BlockSpec(memory_space=pltpu.HBM)
ANY = pl.BlockSpec(memory_space=pl.ANY)
VMEM = pl.BlockSpec(memory_space=pltpu.VMEM)
SMEM = pl.BlockSpec(memory_space=pltpu.SMEM)


def params(mib):
    return pltpu.CompilerParams(vmem_limit_bytes=mib * 2**20)


def copy_all(copies, sems):
    started = [pltpu.make_async_copy(src, dst, sems.at[k]) for k, (src, dst) in enumerate(copies)]
    for copy in started:
        copy.start()
    for copy in started:
        copy.wait()


def prepare_kernel(act, cot, *refs):
    acts, cots, sems = refs[:4], refs[4:8], refs[8]
    z, c, x, y = place()
    copies = []
    for kz, out in enumerate(acts):
        base = lax.rem(z + kz, 4) * GROUP
        for half, core in enumerate((c, 1 - c)):
            start = pl.multiple_of(base + core * ROWS, 128)
            copies.append((act.at[:, pl.ds(start, ROWS)], out.at[:, pl.ds(half * ROWS, ROWS)]))
    for ky, out in enumerate(cots):
        for dx in range(4):
            start = (4 * lax.rem(x + dx, 4) + lax.rem(y + ky, 4)) * BLOCK
            start = pl.multiple_of(start, 128)
            copies.append((cot.at[:, pl.ds(start, BLOCK)], out.at[:, pl.ds(dx * BLOCK, BLOCK)]))
    copy_all(copies, sems)


def prepare(activations, cotangent_t):
    bf16 = jnp.bfloat16
    return pl.pallas_call(
        prepare_kernel,
        out_shape=[jax.ShapeDtypeStruct((BLOCK, GROUP), bf16)] * 4
        + [jax.ShapeDtypeStruct((COLS, 4 * BLOCK), bf16)] * 4,
        in_specs=[HBM] * 2,
        out_specs=[VMEM] * 8,
        scratch_shapes=[pltpu.SemaphoreType.DMA((24,))],
        compiler_params=params(4),
        name="prepare",
    )(
        pltpu.with_memory_space_constraint(activations, pltpu.HBM),
        pltpu.with_memory_space_constraint(cotangent_t, pltpu.HBM),
    )


def keep_kernel(*refs):
    pass


def kept(arrays):
    count = len(arrays)
    return pl.pallas_call(
        keep_kernel,
        out_shape=[jax.ShapeDtypeStruct(a.shape, a.dtype) for a in arrays],
        in_specs=[ANY] * count,
        out_specs=[ANY] * count,
        input_output_aliases={k: k for k in range(count)},
        compiler_params=params(1),
        name="kept",
    )(*arrays)


def dot(a, b):
    return jnp.dot(a, b, preferred_element_type=jnp.float32)


def near_kernel(z0, zp, zm, x0, xp, xm, *outs):
    acts = jnp.concatenate(
        [x[kz * BLOCK : (kz + 1) * BLOCK, :] for kz in (0, 1, 3) for x in (x0, xp, xm)], axis=0
    )
    for ky, out in enumerate(outs):
        rows = slice(ky * COLS, (ky + 1) * COLS)
        parts = []
        for z in (z0, zm, zp):
            parts += [z[rows, : 2 * BLOCK], z[rows, 3 * BLOCK :]]
        out[...] = dot(jnp.concatenate(parts, axis=1), acts)


def near_product(z0, zp, zm, x0, xp, xm):
    return pl.pallas_call(
        near_kernel,
        out_shape=[jax.ShapeDtypeStruct((COLS, GROUP), jnp.float32)] * 4,
        in_specs=[VMEM] * 6,
        out_specs=[VMEM] * 4,
        compiler_params=params(14),
        name="near_product",
    )(z0, zp, zm, x0, xp, xm)


def far_kernel(order, *refs):
    z0, zp, zm, zd0, zd1, x0, xp, xm, xd0, xd1 = refs[:10]
    totals, outs = refs[10 : 10 + len(order)], refs[11 + len(order) : -1]
    refs[-1][...] = refs[10 + len(order)][...]
    acts = jnp.concatenate(
        [x[2 * BLOCK : 3 * BLOCK, :] for x in (x0, xp)]
        + [xd1[:BLOCK, :]]
        + [xm[2 * BLOCK : 3 * BLOCK, :]]
        + [xd0[:BLOCK, :], xd0[BLOCK:, :], xd1[BLOCK:, :]],
        axis=0,
    )
    middle = slice(2 * BLOCK, 3 * BLOCK)
    for k, ky in enumerate(order):
        rows = slice(ky * COLS, (ky + 1) * COLS)
        far = zd0 if ky < 2 else zd1
        parts = [far[(ky % 2) * COLS : (ky % 2 + 1) * COLS, :]]
        parts += [z[rows, middle] for z in (z0, zm, zp)]
        total = totals[k][...] + dot(jnp.concatenate(parts, axis=1), acts)
        outs[2 * k][...] = total[:, :ROWS]
        outs[2 * k + 1][...] = total[:, ROWS:]


def far_product(order, pieces, totals, also):
    outs = pl.pallas_call(
        functools.partial(far_kernel, order),
        out_shape=[jax.ShapeDtypeStruct((COLS, ROWS), jnp.float32)] * (2 * len(order))
        + [jax.ShapeDtypeStruct(also.shape, also.dtype)],
        in_specs=[VMEM] * (11 + len(order)),
        out_specs=[VMEM] * (2 * len(order) + 1),
        compiler_params=params(14),
        name="far_product",
    )(*pieces, *[totals[ky] for ky in order], also)
    return {ky: (outs[2 * k], outs[2 * k + 1]) for k, ky in enumerate(order)}, outs[-1]


def ring_gather(block, axis):
    half = block.shape[0] // 2
    plus = moved(block, **{axis: -1})
    minus = moved(block, **{axis: 1})
    far_first = moved(plus[:half], **{axis: -1})
    far_second = moved(minus[half:], **{axis: 1})
    return [block, plus, minus, far_first, far_second]


def exchanged(blocks, axis):
    parts = {k: moved(blocks[k], **{axis: k}) for k in (2, 1, 3)}
    return jnp.concatenate([blocks[0], parts[1], parts[2], parts[3]], axis=0)


def gradient_terms(activations, cotangent, weights):
    parts = prepare(activations, cotangent.T)
    c_block = exchanged(parts[4:], "dy")
    a_block = exchanged(kept(parts[:4]), "dz")
    c_pieces = ring_gather(c_block, "dz")
    a_pieces = ring_gather(a_block, "dx")
    totals = near_product(*c_pieces[:3], *a_pieces[:3])
    terms, weights = far_product((2,), c_pieces + a_pieces, totals, weights)
    half = COLS // 2
    far = moved(terms[2][1], dc=1)
    others, weights = far_product((1, 3, 0), c_pieces + a_pieces, totals, weights)
    terms |= others
    low = moved(terms[2][0][:half] + far[:half], dy=-1)
    high = moved(terms[2][0][half:] + far[half:], dy=1)
    down = terms[1][0] + moved(terms[1][1], dc=1)
    up = terms[3][0] + moved(terms[3][1], dc=1)
    own = moved(terms[0][1], dc=1)
    near = [moved(weights, dz=-1), moved(weights, dz=1)]
    down = jnp.concatenate([down[:half] + low, down[half:]], axis=0)
    up = jnp.concatenate([up[:half], up[half:] + high], axis=0)
    return [terms[0][0], own, moved(down, dy=-1), moved(up, dy=1)], near


STRIP = 32


def update_kernel(*refs):
    own0, own1, down, up, weights, first, second, scale = refs[:8]
    new_first, new_second, update, sums, held, sems = refs[10:]
    inv_one, inv_two = scale[0], scale[1]
    half = COLS // 2
    carry = (jnp.zeros((8, ROWS), jnp.float32),) * 2
    copies = []
    for base in (0, half):

        def strip(i, carry):
            rows = pl.ds(base + pl.multiple_of(i * STRIP, STRIP), STRIP)
            g = (own0[rows, :] + own1[rows, :]) + (down[rows, :] + up[rows, :])
            w = weights[rows, :]
            m = beta_one * first[rows, :] + (1.0 - beta_one) * g
            v = beta_two * second[rows, :] + (1.0 - beta_two) * g * g
            u = m * inv_one / (jnp.sqrt(v * inv_two) + epsilon) + decay_weight * w
            held[0, rows, :] = m
            held[1, rows, :] = v
            update[rows, :] = u
            out = []
            for total, term in zip(carry, (w * w, u * u)):
                part = term[:8]
                for k in range(8, STRIP, 8):
                    part = part + term[k : k + 8]
                out.append(total + part)
            return tuple(out)

        carry = lax.fori_loop(0, half // STRIP, strip, carry)
        for k, out in enumerate((new_first, new_second)):
            rows = pl.ds(base, half)
            copies.append(pltpu.make_async_copy(held.at[k, rows], out.at[rows], sems.at[len(copies)]))
            copies[-1].start()
    for k, total in enumerate(carry):
        part = total[:, :128]
        for j in range(128, ROWS, 128):
            part = part + total[:, j : j + 128]
        sums[8 * k : 8 * k + 8, :] = part
    for copy in copies:
        copy.wait()


def updated(terms, weights, first, second, scale, near):
    block = jax.ShapeDtypeStruct((COLS, ROWS), jnp.float32)
    return pl.pallas_call(
        update_kernel,
        out_shape=[block] * 3 + [jax.ShapeDtypeStruct((16, 128), jnp.float32)],
        in_specs=[VMEM] * 7 + [SMEM] + [ANY] * 2,
        out_specs=[HBM] * 2 + [VMEM] * 2,
        scratch_shapes=[
            pltpu.VMEM((2, COLS, ROWS), jnp.float32),
            pltpu.SemaphoreType.DMA((4,)),
        ],
        compiler_params=params(6),
        name="update",
    )(*terms, weights, first, second, scale, *near)


def total_over_devices(values):
    values = values + moved(values, dc=1)
    for axis in ("dx", "dy", "dz"):
        one, two, three = (moved(values, **{axis: k}) for k in (1, 2, 3))
        values = (values + two) + (one + three)
    return values


def scale_of(sums, rate):
    weight_sq = jnp.sum(jnp.sum(sums[:8, :], axis=0, keepdims=True), axis=1, keepdims=True)
    update_sq = jnp.sum(jnp.sum(sums[8:, :], axis=0, keepdims=True), axis=1, keepdims=True)
    return rate[0] * (jnp.sqrt(weight_sq) / jnp.sqrt(update_sq))


def step_kernel(sums, rate, weights, update, near0, near1, new_weights):
    scale = scale_of(sums, rate)

    def strip(i, carry):
        rows = pl.ds(pl.multiple_of(i * STRIP, STRIP), STRIP)
        new_weights[rows, :] = (weights[rows, :] - scale * update[rows, :]).astype(jnp.bfloat16)
        return carry

    lax.fori_loop(0, COLS // STRIP, strip, 0)


def own_step(sums, rate, weights, update, near):
    return pl.pallas_call(
        step_kernel,
        out_shape=jax.ShapeDtypeStruct((COLS, ROWS), jnp.bfloat16),
        in_specs=[VMEM, SMEM, VMEM, VMEM] + [ANY] * 2,
        out_specs=VMEM,
        compiler_params=params(6),
        name="own_step",
    )(sums, rate, weights, update, *near)


def near_step_kernel(sums, rate, w, wp, wm, u, up, um, own, new_master, plus, minus):
    scale = scale_of(sums, rate)

    def strip(i, carry):
        rows = pl.ds(pl.multiple_of(i * STRIP, STRIP), STRIP)
        new_master[rows, :] = w[rows, :] - scale * u[rows, :]
        plus[rows, :] = (wp[rows, :] - scale * up[rows, :]).astype(jnp.bfloat16)
        minus[rows, :] = (wm[rows, :] - scale * um[rows, :]).astype(jnp.bfloat16)
        return carry

    lax.fori_loop(0, COLS // STRIP, strip, 0)


def near_step(sums, rate, weights, updates, own):
    return pl.pallas_call(
        near_step_kernel,
        out_shape=[jax.ShapeDtypeStruct((COLS, ROWS), jnp.float32)]
        + [jax.ShapeDtypeStruct((COLS, ROWS), jnp.bfloat16)] * 2,
        in_specs=[VMEM, SMEM] + [VMEM] * 6 + [ANY],
        out_specs=[VMEM] * 3,
        compiler_params=params(6),
        name="near_step",
    )(sums, rate, *weights, *updates, own)


def place_kernel(offsets, *refs):
    pieces, out, sems = refs[: 2 * len(offsets)], refs[-2], refs[-1]
    z, c, x, y = place()
    copies = []
    for k, dz in enumerate(offsets):
        for half, core in enumerate((c, 1 - c)):
            start = pl.multiple_of((2 * lax.rem(z + dz, 4) + core) * ROWS, 128)
            copies.append((pieces[2 * k + half], out.at[:, pl.ds(start, ROWS)]))
    copy_all(copies, sems)


def placed(offsets, pieces, held=None):
    count = len(pieces)
    given = [] if held is None else [held]
    return pl.pallas_call(
        functools.partial(place_kernel, offsets),
        out_shape=jax.ShapeDtypeStruct((COLS, 8 * ROWS), jnp.bfloat16),
        in_specs=[VMEM] * count + [HBM] * len(given),
        out_specs=HBM,
        scratch_shapes=[pltpu.SemaphoreType.DMA((count,))],
        input_output_aliases={count: 0} if given else {},
        compiler_params=params(4),
        name="placed",
    )(*pieces, *given)


def on_device(
    activations,
    cotangent,
    master_weights,
    first_moment,
    second_moment,
    step_count,
    language_ids,
    language_rates,
):
    steps_done = step_count.astype(jnp.float32)
    corr_one = 1.0 - jnp.power(jnp.float32(beta_one), steps_done)
    corr_two = 1.0 - jnp.power(jnp.float32(beta_two), steps_done)
    scale = jnp.concatenate([1.0 / corr_one, 1.0 / corr_two])
    picked = jnp.arange(language_rates.shape[0], dtype=jnp.int32) == language_ids[0]
    rate = base_rate * jnp.sum(jnp.where(picked, language_rates, jnp.float32(0.0)))
    weights = master_weights.T
    rate = rate.reshape(1)
    terms, near_weights = gradient_terms(activations, cotangent, weights)
    new_first, new_second, update, sums = updated(
        terms, weights, first_moment.T, second_moment.T, scale, near_weights
    )
    near_updates = [moved(update, dz=-1), moved(update, dz=1)]
    sums = total_over_devices(sums)
    own = own_step(sums, rate, weights, update, near_updates)
    far = moved(own, dz=2)
    new_master, plus, minus = near_step(
        sums, rate, [weights] + near_weights, [update] + near_updates, own
    )
    pieces = []
    for block in (own, plus, minus):
        pieces += [block, moved(block, dc=1)]
    near = placed((0, 1, 3), pieces)
    new_weights = placed((2,), [far, moved(far, dc=1)], near)
    return (new_master.T, new_first.T, new_second.T, new_weights.T)


def solution(mesh):
    return jax.shard_map(
        on_device,
        mesh=mesh,
        in_specs=(
            P(("dp", "mp"), None),
            P("dp", "mp"),
            P("dp", "mp"),
            P("dp", "mp"),
            P("dp", "mp"),
            P(),
            P(),
            P(),
        ),
        out_specs=(P("dp", "mp"), P("dp", "mp"), P("dp", "mp"), P(None, "mp")),
        check_vma=False,
    )
```

time: 161 us -> 157 us (0.975)
  starting transfers between devices: 65.8 us -> 63.8 us
    pallas_call x4 -> x5, Pallas kernels: 9 us -> 6.12 us  [the longest x2 3.82 us: far_product(): pl.pallas_call(functools.partial(far_kernel, order), out_shape=[jax.Shape...]
    pallas_call x1, Pallas kernels: 0.38 us -> 2.66 us  [near_step(): pl.pallas_call(near_step_kernel, out_shape=[jax.ShapeDtypeStruct((COLS, R...]
    ppermute x41, starting transfers between devices: 65.8 us -> 63.8 us  [moved(): return lax.ppermute(array, ('dp', 'mp'), pairs)]
  transfers between devices with their start and end apart: 41 -> 41, of which waited for: 21 -> 20; matrix products, arithmetic and copies ran while one was open for 1% -> 1% of each run, Pallas kernels for 4% -> 7%
where the time goes in v6:
time: 157 us; the launch traced here: 156 us
  waiting for transfers between devices  69.9 us (45%)
  starting transfers between devices  63.8 us (41%)
  Pallas kernels  17.9 us (11%)
  between operations  3.22 us (2%)
    ppermute x41, waiting for transfers between devices, moved(): return lax.ppermute(array, ('dp', 'mp'), pairs)  69.9 us
    ppermute x41, starting transfers between devices, moved(): return lax.ppermute(array, ('dp', 'mp'), pairs)  63.8 us
    pallas_call x1, Pallas kernels, near_product(): pl.pallas_call(near_kernel, out_shape=[jax.ShapeDtypeStruct((COLS, GROUP)...  4.39 us
    pallas_call x2, Pallas kernels, far_product(): pl.pallas_call(functools.partial(far_kernel, order), out_shape=[jax.Shape...  3.82 us
  transfers between devices with their start and end apart: 41, of which 20 were waited for; matrix products, arithmetic and copies ran while one was open for 1% of the time, Pallas kernels for 7%

profile of v6, /device:TPU:1, one launch (start us, length us, event | category | flops | bytes accessed | tf_op | source)
XLA Modules:
  0.0 156.5 jit_solution(16515997176927514912)
XLA Ops:
  0.6 2.1 %prepare.1 = (bf16[128,1280]{1,0:T(8,128)(2,1)S(1)}, bf16[128,1280]{1,0:T(8,128)(2,1)S(1)}, bf16[128,1280]{1,0:T(8,128)(2,1)S(1)}, bf16[128,1280]{1,0:T(8,128)(2...) custom-call(bf16[128,5120]{1,0:T(8,128)(2,1)} %act.1, ...), custom_call_target="tpu_custom_call" | custom-call | tf_op jit(solution)/shard_map/prepare/pallas_call | solution.py:77
  2.7 2.5 %collective-permute-start.7 = (bf16[128,1280]{1,0:T(8,128)(2,1)S(1)}, bf16[128,1280]{1,0:T(8,128)(2,1)S(1)}, u32[]{:S(2)}, u32[]{:S(2)}) collective-permute-start(bf16[128,1280]{1,0:T(8,128)(2,1)S(1)} %get-tuple-element.46), channel_id=1, source_target_pairs={{0,32},{1,33},{2,34},{3,35},{4,36},{5,37},{6,38},{7,39},{8,40},{9,... | collective-permute-start | bytes 983048 | tf_op jit(solution)/shard_map/ppermute | solution.py:31
  5.3 3.3 %collective-permute-start.8 = (bf16[128,1280]{1,0:T(8,128)(2,1)S(1)}, bf16[128,1280]{1,0:T(8,128)(2,1)S(1)}, u32[]{:S(2)}, u32[]{:S(2)}) collective-permute-start(bf16[128,1280]{1,0:T(8,128)(2,1)S(1)} %get-tuple-element.47), channel_id=1, source_target_pairs={{0,64},{1,65},{2,66},{3,67},{4,68},{5,69},{6,70},{7,71},{8,72},{9,... | collective-permute-start | bytes 983048 | tf_op jit(solution)/shard_map/ppermute | solution.py:31
  9.3 1.3 collective-permute-start
  10.6 2.6 %collective-permute-start.1 = (bf16[320,512]{1,0:T(8,128)(2,1)S(1)}, bf16[320,512]{1,0:T(8,128)(2,1)S(1)}, u32[]{:S(2)}, u32[]{:S(2)}) collective-permute-start(bf16[320,512]{1,0:T(8,128)(2,1)S(1)} %get-tuple-element.39), channel_id=1, source_target_pairs={{0,2},{1,3},{2,0},{3,1},{4,6},{5,7},{6,4},{7,5},{8,10},{9,11},{10,... | collective-permute-start | bytes 983048 | tf_op jit(solution)/shard_map/ppermute | solution.py:31
  13.3 1.6 collective-permute-done.7
  14.8 2.7 %collective-permute-start.2 = (bf16[320,512]{1,0:T(8,128)(2,1)S(1)}, bf16[320,512]{1,0:T(8,128)(2,1)S(1)}, u32[]{:S(2)}, u32[]{:S(2)}) collective-permute-start(bf16[320,512]{1,0:T(8,128)(2,1)S(1)} %get-tuple-element.40), channel_id=1, source_target_pairs={{0,3},{1,0},{2,1},{3,2},{4,7},{5,4},{6,5},{7,6},{8,11},{9,8},{10,9... | collective-permute-start | bytes 983048 | tf_op jit(solution)/shard_map/ppermute | solution.py:31
  17.6 5.1 %collective-permute-done.8 = bf16[128,1280]{1,0:T(8,128)(2,1)S(1)} collective-permute-done((bf16[128,1280]{1,0:T(8,128)(2,1)S(1)}, bf16[128,1280]{1,0:T(8,128)(2,1)S(1)}, u32[]{:S(2)}, u32[]{:S(2)}) %collective-permute-start.8) | collective-permute-done | bytes 327712 | tf_op jit(solution)/shard_map/ppermute | solution.py:31
  22.8 2.5 %collective-permute-start.10 = (bf16[512,1280]{1,0:T(8,128)(2,1)S(1)}, bf16[512,1280]{1,0:T(8,128)(2,1)S(1)}, u32[]{:S(2)}, u32[]{:S(2)}) collective-permute-start(bf16[512,1280]{1,0:T(8,128)(2,1)S(1)} %constant_dynamic-update-slice_fusion.4.x0.refs_5_), channel_id=1, source_target_pairs={{0,12},{1,13},{2,14},{3,15},{4,0},{5,1},{6,2},{7,3},{8,4},{9,5},{1... | collective-permute-start | bytes 3932168 | tf_op jit(solution)/shard_map/ppermute | solution.py:31
  25.3 1.1 collective-permute-done.1
  26.5 1.9 %collective-permute-start.3 = (bf16[1280,512]{1,0:T(8,128)(2,1)S(1)}, bf16[1280,512]{1,0:T(8,128)(2,1)S(1)}, u32[]{:S(2)}, u32[]{:S(2)}) collective-permute-start(bf16[1280,512]{1,0:T(8,128)(2,1)S(1)} %constant_dynamic-update-slice_fusion.z0.refs_0_), channel_id=1, source_target_pairs={{0,96},{1,97},{2,98},{3,99},{4,100},{5,101},{6,102},{7,103},{8,104... | collective-permute-start | bytes 3932168 | tf_op jit(solution)/shard_map/ppermute | solution.py:31
  28.4 23.4 %collective-permute-done.10.xp.refs_6_ = bf16[512,1280]{1,0:T(8,128)(2,1)S(1)} collective-permute-done((bf16[512,1280]{1,0:T(8,128)(2,1)S(1)}, bf16[512,1280]{1,0:T(8,128)(2,1)S(1)}, u32[]{:S(2)}, u32[]{:S(2)}) %collective-permute-start.10) | collective-permute-done | bytes 1310752 | tf_op jit(solution)/shard_map/ppermute | solution.py:31
  51.9 3.5 %collective-permute-start.12 = (bf16[256,1280]{1,0:T(8,128)(2,1)S(1)}, bf16[256,1280]{1,0:T(8,128)(2,1)S(1)}, u32[]{:S(2)}, u32[]{:S(2)}) collective-permute-start(bf16[256,1280]{1,0:T(8,128)(2,1)S(1)} %slice.50), channel_id=1, source_target_pairs={{0,12},{1,13},{2,14},{3,15},{4,0},{5,1},{6,2},{7,3},{8,4},{9,5},{1... | collective-permute-start | bytes 1966088 | tf_op jit(solution)/shard_map/ppermute | solution.py:31
  55.8 3.9 %collective-permute-start.5 = (bf16[640,512]{1,0:T(8,128)(2,1)S(1)}, bf16[640,512]{1,0:T(8,128)(2,1)S(1)}, u32[]{:S(2)}, u32[]{:S(2)}) collective-permute-start(bf16[640,512]{1,0:T(8,128)(2,1)S(1)} %slice.48), channel_id=1, source_target_pairs={{0,96},{1,97},{2,98},{3,99},{4,100},{5,101},{6,102},{7,103},{8,104... | collective-permute-start | bytes 1966088 | tf_op jit(solution)/shard_map/ppermute | solution.py:31
  59.8 4.4 %near_product.1 = (f32[320,1280]{1,0:T(8,128)S(1)}, f32[320,1280]{1,0:T(8,128)S(1)}, f32[320,1280]{1,0:T(8,128)S(1)}, f32[320,1280]{1,0:T(8,128)S(1)}) custom-call(bf16[1280,512]{1,0:T(8,128)(2,1)S(1)} %constant_dynamic-update-slice_fusion.z0.refs_0_, bf16[1280,512]{1,0:T(8,128)(2,1)S(1)} %collective-permute-done.3.zp.refs_1_, ...), custom_call_target="tpu_custom_call" | custom-call | tf_op jit(solution)/shard_map/near_product/pallas_call | solution.py:126
  64.2 2.7 %collective-permute-done.12.refs_8_ = bf16[256,1280]{1,0:T(8,128)(2,1)S(1)} collective-permute-done((bf16[256,1280]{1,0:T(8,128)(2,1)S(1)}, bf16[256,1280]{1,0:T(8,128)(2,1)S(1)}, u32[]{:S(2)}, u32[]{:S(2)}) %collective-permute-start.12) | collective-permute-done | bytes 655392 | tf_op jit(solution)/shard_map/ppermute | solution.py:31
  66.9 3.3 %collective-permute-done.13.refs_9_ = bf16[256,1280]{1,0:T(8,128)(2,1)S(1)} collective-permute-done((bf16[256,1280]{1,0:T(8,128)(2,1)S(1)}, bf16[256,1280]{1,0:T(8,128)(2,1)S(1)}, u32[]{:S(2)}, u32[]{:S(2)}) %collective-permute-start.13) | collective-permute-done | bytes 655392 | tf_op jit(solution)/shard_map/ppermute | solution.py:31
  70.2 1.9 %collective-permute-done.5.refs_3_ = bf16[640,512]{1,0:T(8,128)(2,1)S(1)} collective-permute-done((bf16[640,512]{1,0:T(8,128)(2,1)S(1)}, bf16[640,512]{1,0:T(8,128)(2,1)S(1)}, u32[]{:S(2)}, u32[]{:S(2)}) %collective-permute-start.5) | collective-permute-done | bytes 655392 | tf_op jit(solution)/shard_map/ppermute | solution.py:31
  72.0 3.3 %collective-permute-done.6.refs_4_ = bf16[640,512]{1,0:T(8,128)(2,1)S(1)} collective-permute-done((bf16[640,512]{1,0:T(8,128)(2,1)S(1)}, bf16[640,512]{1,0:T(8,128)(2,1)S(1)}, u32[]{:S(2)}, u32[]{:S(2)}) %collective-permute-start.6) | collective-permute-done | bytes 655392 | tf_op jit(solution)/shard_map/ppermute | solution.py:31
  75.3 1.1 far_product.2
  76.4 2.9 %collective-permute-start.16 = (f32[320,640]{1,0:T(8,128)S(1)}, f32[320,640]{1,0:T(8,128)S(1)}, u32[]{:S(2)}, u32[]{:S(2)}) collective-permute-start(f32[320,640]{1,0:T(8,128)S(1)} %get-tuple-element.59), channel_id=1, source_target_pairs={{0,16},{1,17},{2,18},{3,19},{4,20},{5,21},{6,22},{7,23},{8,24},{9,... | collective-permute-start | bytes 2457608 | tf_op jit(solution)/shard_map/ppermute | solution.py:31
  79.3 2.8 %far_product.3 = (f32[320,640]{1,0:T(8,128)S(1)}, f32[320,640]{1,0:T(8,128)S(1)}, f32[320,640]{1,0:T(8,128)S(1)}, f32[320,640]{1,0:T(8,128)S(1)}, f32[320,640]{1...) custom-call(bf16[1280,512]{1,0:T(8,128)(2,1)S(1)} %constant_dynamic-update-slice_fusion.z0.refs_0_, ...), custom_call_target="tpu_custom_call" | custom-call | tf_op jit(solution)/shard_map/far_product/pallas_call | solution.py:159
  82.9 1.8 %collective-permute-start.20 = (f32[160,640]{1,0:T(8,128)S(1)}, f32[160,640]{1,0:T(8,128)S(1)}, u32[]{:S(2)}, u32[]{:S(2)}) collective-permute-start(f32[160,640]{1,0:T(8,128)S(1)} %get-tuple-element.70), channel_id=1, source_target_pairs={{0,1},{1,2},{2,3},{3,0},{4,5},{5,6},{6,7},{7,4},{8,9},{9,10},{10,1... | collective-permute-start | bytes 1228808 | tf_op jit(solution)/shard_map/ppermute | solution.py:31
  84.7 1.1 collective-permute-start.17
  85.8 1.5 collective-permute-start.23
  87.4 1.2 collective-permute-start.14
  88.6 6.7 %collective-permute-done.20 = f32[160,640]{1,0:T(8,128)S(1)} collective-permute-done((f32[160,640]{1,0:T(8,128)S(1)}, f32[160,640]{1,0:T(8,128)S(1)}, u32[]{:S(2)}, u32[]{:S(2)}) %collective-permute-start.20) | collective-permute-done | bytes 409632 | tf_op jit(solution)/shard_map/ppermute | solution.py:31
  96.0 2.4 %collective-permute-start.18 = (f32[320,640]{1,0:T(8,128)S(1)}, f32[320,640]{1,0:T(8,128)S(1)}, u32[]{:S(2)}, u32[]{:S(2)}) collective-permute-start(f32[320,640]{1,0:T(8,128)S(1)} %pad_maximum_fusion), channel_id=1, source_target_pairs={{0,3},{1,0},{2,1},{3,2},{4,7},{5,4},{6,5},{7,6},{8,11},{9,8},{10,9... | collective-permute-start | bytes 2457608 | tf_op jit(solution)/shard_map/ppermute | solution.py:31
  99.3 5.8 %collective-permute-done.22.refs_8_.wp = f32[320,640]{1,0:T(8,128)S(1)} collective-permute-done((f32[320,640]{1,0:T(8,128)S(1)}, f32[320,640]{1,0:T(8,128)S(1)}, u32[]{:S(2)}, u32[]{:S(2)}) %collective-permute-start.22) | collective-permute-done | bytes 819232 | tf_op jit(solution)/shard_map/ppermute | solution.py:31
  105.1 1.0 collective-permute-done.23.refs_9_.wm
  106.1 9.5 %collective-permute-done.21.refs_3_ = f32[320,640]{1,0:T(8,128)S(1)} collective-permute-done((f32[320,640]{1,0:T(8,128)S(1)}, f32[320,640]{1,0:T(8,128)S(1)}, u32[]{:S(2)}, u32[]{:S(2)}) %collective-permute-start.21) | collective-permute-done | bytes 819232 | tf_op jit(solution)/shard_map/ppermute | solution.py:31
  115.7 2.3 %update.1 = (f32[320,640]{1,0:T(8,128)}, f32[320,640]{1,0:T(8,128)}, f32[320,640]{1,0:T(8,128)S(1)}, f32[16,128]{1,0:T(8,128)S(1)}) custom-call(f32[320,640]{1,0:T(8,128)S(1)} %get-tuple-element.54.refs_0_, f32[320,640]{1,0:T(8,128)S(1)} %collective-permute-done.14.refs_1_, f32[320,640]{1,0:T(8,128)S(1)} %collective-permute-done.18.refs_2_, ...), custom_call_target="tpu_custom_call" | custom-call | tf_op jit(solution)/shard_map/update/pallas_call | solution.py:254
  118.1 1.5 collective-permute-start.35
  119.6 2.3 %collective-permute-start.24 = (f32[16,128]{1,0:T(8,128)S(1)}, f32[16,128]{1,0:T(8,128)S(1)}, u32[]{:S(2)}, u32[]{:S(2)}) collective-permute-start(f32[16,128]{1,0:T(8,128)S(1)} %get-tuple-element.63), channel_id=1, source_target_pairs={{0,16},{1,17},{2,18},{3,19},{4,20},{5,21},{6,22},{7,23},{8,24},{9,... | collective-permute-start | bytes 24584 | tf_op jit(solution)/shard_map/ppermute | solution.py:31
  122.7 2.1 %collective-permute-start.25 = (f32[16,128]{1,0:T(8,128)S(1)}, f32[16,128]{1,0:T(8,128)S(1)}, u32[]{:S(2)}, u32[]{:S(2)}) collective-permute-start(f32[16,128]{1,0:T(8,128)S(1)} %add.54), channel_id=1, source_target_pairs={{0,8},{1,9},{2,10},{3,11},{4,12},{5,13},{6,14},{7,15},{8,0},{9,1},... | collective-permute-start | bytes 24584 | tf_op jit(solution)/shard_map/ppermute | solution.py:31
  124.8 1.1 collective-permute-start.26
  125.9 1.6 collective-permute-start.27
  127.5 1.4 collective-permute-done.26
  128.9 1.5 collective-permute-start.28
  130.4 1.9 %collective-permute-start.29 = (f32[16,128]{1,0:T(8,128)S(1)}, f32[16,128]{1,0:T(8,128)S(1)}, u32[]{:S(2)}, u32[]{:S(2)}) collective-permute-start(f32[16,128]{1,0:T(8,128)S(1)} %add_add_fusion.2), channel_id=1, source_target_pairs={{0,1},{1,2},{2,3},{3,0},{4,5},{5,6},{6,7},{7,4},{8,9},{9,10},{10,1... | collective-permute-start | bytes 24584 | tf_op jit(solution)/shard_map/ppermute | solution.py:31
  135.2 1.7 %collective-permute-start.32 = (f32[16,128]{1,0:T(8,128)S(1)}, f32[16,128]{1,0:T(8,128)S(1)}, u32[]{:S(2)}, u32[]{:S(2)}) collective-permute-start(f32[16,128]{1,0:T(8,128)S(1)} %add_add_fusion.1), channel_id=1, source_target_pairs={{0,32},{1,33},{2,34},{3,35},{4,36},{5,37},{6,38},{7,39},{8,40},{9,... | collective-permute-start | bytes 24584 | tf_op jit(solution)/shard_map/ppermute | solution.py:31
  136.9 1.1 collective-permute-start.33
  140.0 1.3 collective-permute-start.36
  141.3 2.7 %near_step.1 = (f32[320,640]{1,0:T(8,128)}, bf16[320,640]{1,0:T(8,128)(2,1)S(1)}, bf16[320,640]{1,0:T(8,128)(2,1)S(1)}) custom-call(f32[16,128]{1,0:T(8,128)S(1)} %add_add_fusion.sums, f32[1]{0:T(128)} %bitcast.5.rate, f32[320,640]{1,0:T(8,128)S(1)} %bitcast.14, f32[320,640]{1,0:T(8,128)S(1)} %collective-permute-done.22.refs_8_.wp, ...), custom_call_target="tpu_custom_call" | custom-call | tf_op jit(solution)/shard_map/near_step/pallas_call | solution.py:318
  144.0 5.0 %collective-permute-start.39 = (bf16[320,640]{1,0:T(8,128)(2,1)S(1)}, bf16[320,640]{1,0:T(8,128)(2,1)S(1)}, u32[]{:S(2)}, u32[]{:S(2)}) collective-permute-start(bf16[320,640]{1,0:T(8,128)(2,1)S(1)} %get-tuple-element.68.refs_2_), channel_id=1, source_target_pairs={{0,16},{1,17},{2,18},{3,19},{4,20},{5,21},{6,22},{7,23},{8,24},{9,... | collective-permute-start | bytes 1228808 | tf_op jit(solution)/shard_map/ppermute | solution.py:31
  149.5 4.4 %collective-permute-start.37 = (bf16[320,640]{1,0:T(8,128)(2,1)S(1)}, bf16[320,640]{1,0:T(8,128)(2,1)S(1)}, u32[]{:S(2)}, u32[]{:S(2)}) collective-permute-start(bf16[320,640]{1,0:T(8,128)(2,1)S(1)} %collective-permute-done.36.refs_0_), channel_id=1, source_target_pairs={{0,16},{1,17},{2,18},{3,19},{4,20},{5,21},{6,22},{7,23},{8,24},{9,... | collective-permute-start | bytes 1228808 | tf_op jit(solution)/shard_map/ppermute | solution.py:31
  153.8 1.5 placed.2.refs_2_
  155.4 0.9 placed.3
  (77 shorter events, 8.4 us)
Async XLA Ops:
  2.7 12.1 %collective-permute-start.7 = (bf16[128,1280]{1,0:T(8,128)(2,1)S(1)}, bf16[128,1280]{1,0:T(8,128)(2,1)S(1)}, u32[]{:S(2)}, u32[]{:S(2)}) collective-permute-start(bf16[128,1280]{1,0:T(8,128)(2,1)S(1)} %get-tuple-element.46), channel_id=1, source_target_pairs={{0,32},{1,33},{2,34},{3,35},{4,36},{5,37},{6,38},{7,39},{8,40},{9,... | collective-permute-start | bytes 983048 | tf_op jit(solution)/shard_map/ppermute | solution.py:31
  5.3 17.4 %collective-permute-start.8 = (bf16[128,1280]{1,0:T(8,128)(2,1)S(1)}, bf16[128,1280]{1,0:T(8,128)(2,1)S(1)}, u32[]{:S(2)}, u32[]{:S(2)}) collective-permute-start(bf16[128,1280]{1,0:T(8,128)(2,1)S(1)} %get-tuple-element.47), channel_id=1, source_target_pairs={{0,64},{1,65},{2,66},{3,67},{4,68},{5,69},{6,70},{7,71},{8,72},{9,... | collective-permute-start | bytes 983048 | tf_op jit(solution)/shard_map/ppermute | solution.py:31
  8.6 14.2 %collective-permute-start.9 = (bf16[128,1280]{1,0:T(8,128)(2,1)S(1)}, bf16[128,1280]{1,0:T(8,128)(2,1)S(1)}, u32[]{:S(2)}, u32[]{:S(2)}) collective-permute-start(bf16[128,1280]{1,0:T(8,128)(2,1)S(1)} %get-tuple-element.48), channel_id=1, source_target_pairs={{0,96},{1,97},{2,98},{3,99},{4,100},{5,101},{6,102},{7,103},{8,104... | collective-permute-start | bytes 983048 | tf_op jit(solution)/shard_map/ppermute | solution.py:31
  9.3 16.0 %collective-permute-start = (bf16[320,512]{1,0:T(8,128)(2,1)S(1)}, bf16[320,512]{1,0:T(8,128)(2,1)S(1)}, u32[]{:S(2)}, u32[]{:S(2)}) collective-permute-start(bf16[320,512]{1,0:T(8,128)(2,1)S(1)} %get-tuple-element.38), channel_id=1, source_target_pairs={{0,1},{1,2},{2,3},{3,0},{4,5},{5,6},{6,7},{7,4},{8,9},{9,10},{10,1... | collective-permute-start | bytes 983048 | tf_op jit(solution)/shard_map/ppermute | solution.py:31
  10.6 15.9 %collective-permute-start.1 = (bf16[320,512]{1,0:T(8,128)(2,1)S(1)}, bf16[320,512]{1,0:T(8,128)(2,1)S(1)}, u32[]{:S(2)}, u32[]{:S(2)}) collective-permute-start(bf16[320,512]{1,0:T(8,128)(2,1)S(1)} %get-tuple-element.39), channel_id=1, source_target_pairs={{0,2},{1,3},{2,0},{3,1},{4,6},{5,7},{6,4},{7,5},{8,10},{9,11},{10,... | collective-permute-start | bytes 983048 | tf_op jit(solution)/shard_map/ppermute | solution.py:31
  14.8 11.7 %collective-permute-start.2 = (bf16[320,512]{1,0:T(8,128)(2,1)S(1)}, bf16[320,512]{1,0:T(8,128)(2,1)S(1)}, u32[]{:S(2)}, u32[]{:S(2)}) collective-permute-start(bf16[320,512]{1,0:T(8,128)(2,1)S(1)} %get-tuple-element.40), channel_id=1, source_target_pairs={{0,3},{1,0},{2,1},{3,2},{4,7},{5,4},{6,5},{7,6},{8,11},{9,8},{10,9... | collective-permute-start | bytes 983048 | tf_op jit(solution)/shard_map/ppermute | solution.py:31
  22.8 29.1 %collective-permute-start.10 = (bf16[512,1280]{1,0:T(8,128)(2,1)S(1)}, bf16[512,1280]{1,0:T(8,128)(2,1)S(1)}, u32[]{:S(2)}, u32[]{:S(2)}) collective-permute-start(bf16[512,1280]{1,0:T(8,128)(2,1)S(1)} %constant_dynamic-update-slice_fusion.4.x0.refs_5_), channel_id=1, source_target_pairs={{0,12},{1,13},{2,14},{3,15},{4,0},{5,1},{6,2},{7,3},{8,4},{9,5},{1... | collective-permute-start | bytes 3932168 | tf_op jit(solution)/shard_map/ppermute | solution.py:31
  25.3 30.1 %collective-permute-start.11 = (bf16[512,1280]{1,0:T(8,128)(2,1)S(1)}, bf16[512,1280]{1,0:T(8,128)(2,1)S(1)}, u32[]{:S(2)}, u32[]{:S(2)}) collective-permute-start(bf16[512,1280]{1,0:T(8,128)(2,1)S(1)} %constant_dynamic-update-slice_fusion.4.x0.refs_5_), channel_id=1, source_target_pairs={{0,4},{1,5},{2,6},{3,7},{4,8},{5,9},{6,10},{7,11},{8,12},{9,13},{1... | collective-permute-start | bytes 3932168 | tf_op jit(solution)/shard_map/ppermute | solution.py:31
  26.5 29.2 %collective-permute-start.3 = (bf16[1280,512]{1,0:T(8,128)(2,1)S(1)}, bf16[1280,512]{1,0:T(8,128)(2,1)S(1)}, u32[]{:S(2)}, u32[]{:S(2)}) collective-permute-start(bf16[1280,512]{1,0:T(8,128)(2,1)S(1)} %constant_dynamic-update-slice_fusion.z0.refs_0_), channel_id=1, source_target_pairs={{0,96},{1,97},{2,98},{3,99},{4,100},{5,101},{6,102},{7,103},{8,104... | collective-permute-start | bytes 3932168 | tf_op jit(solution)/shard_map/ppermute | solution.py:31
  28.4 31.3 %collective-permute-start.4 = (bf16[1280,512]{1,0:T(8,128)(2,1)S(1)}, bf16[1280,512]{1,0:T(8,128)(2,1)S(1)}, u32[]{:S(2)}, u32[]{:S(2)}) collective-permute-start(bf16[1280,512]{1,0:T(8,128)(2,1)S(1)} %constant_dynamic-update-slice_fusion.z0.refs_0_), channel_id=1, source_target_pairs={{0,32},{1,33},{2,34},{3,35},{4,36},{5,37},{6,38},{7,39},{8,40},{9,... | collective-permute-start | bytes 3932168 | tf_op jit(solution)/shard_map/ppermute | solution.py:31
  51.9 15.0 %collective-permute-start.12 = (bf16[256,1280]{1,0:T(8,128)(2,1)S(1)}, bf16[256,1280]{1,0:T(8,128)(2,1)S(1)}, u32[]{:S(2)}, u32[]{:S(2)}) collective-permute-start(bf16[256,1280]{1,0:T(8,128)(2,1)S(1)} %slice.50), channel_id=1, source_target_pairs={{0,12},{1,13},{2,14},{3,15},{4,0},{5,1},{6,2},{7,3},{8,4},{9,5},{1... | collective-permute-start | bytes 1966088 | tf_op jit(solution)/shard_map/ppermute | solution.py:31
  55.4 14.8 %collective-permute-start.13 = (bf16[256,1280]{1,0:T(8,128)(2,1)S(1)}, bf16[256,1280]{1,0:T(8,128)(2,1)S(1)}, u32[]{:S(2)}, u32[]{:S(2)}) collective-permute-start(bf16[256,1280]{1,0:T(8,128)(2,1)S(1)} %slice.51), channel_id=1, source_target_pairs={{0,4},{1,5},{2,6},{3,7},{4,8},{5,9},{6,10},{7,11},{8,12},{9,13},{1... | collective-permute-start | bytes 1966088 | tf_op jit(solution)/shard_map/ppermute | solution.py:31
  55.8 16.3 %collective-permute-start.5 = (bf16[640,512]{1,0:T(8,128)(2,1)S(1)}, bf16[640,512]{1,0:T(8,128)(2,1)S(1)}, u32[]{:S(2)}, u32[]{:S(2)}) collective-permute-start(bf16[640,512]{1,0:T(8,128)(2,1)S(1)} %slice.48), channel_id=1, source_target_pairs={{0,96},{1,97},{2,98},{3,99},{4,100},{5,101},{6,102},{7,103},{8,104... | collective-permute-start | bytes 1966088 | tf_op jit(solution)/shard_map/ppermute | solution.py:31
  59.7 15.6 %copy-start = (f32[640,320]{0,1:T(8,128)S(1)}, f32[640,320]{0,1:T(8,128)}, u32[]{:S(2)}) copy-start(f32[640,320]{0,1:T(8,128)} %param.10) | copy-start | bytes 2457604
  59.7 15.6 %collective-permute-start.6 = (bf16[640,512]{1,0:T(8,128)(2,1)S(1)}, bf16[640,512]{1,0:T(8,128)(2,1)S(1)}, u32[]{:S(2)}, u32[]{:S(2)}) collective-permute-start(bf16[640,512]{1,0:T(8,128)(2,1)S(1)} %slice.49), channel_id=1, source_target_pairs={{0,32},{1,33},{2,34},{3,35},{4,36},{5,37},{6,38},{7,39},{8,40},{9,... | collective-permute-start | bytes 1966088 | tf_op jit(solution)/shard_map/ppermute | solution.py:31
  76.4 6.4 %collective-permute-start.16 = (f32[320,640]{1,0:T(8,128)S(1)}, f32[320,640]{1,0:T(8,128)S(1)}, u32[]{:S(2)}, u32[]{:S(2)}) collective-permute-start(f32[320,640]{1,0:T(8,128)S(1)} %get-tuple-element.59), channel_id=1, source_target_pairs={{0,16},{1,17},{2,18},{3,19},{4,20},{5,21},{6,22},{7,23},{8,24},{9,... | collective-permute-start | bytes 2457608 | tf_op jit(solution)/shard_map/ppermute | solution.py:31
  82.0 3.8 %collective-permute-start.19 = (f32[320,640]{1,0:T(8,128)S(1)}, f32[320,640]{1,0:T(8,128)S(1)}, u32[]{:S(2)}, u32[]{:S(2)}) collective-permute-start(f32[320,640]{1,0:T(8,128)S(1)} %get-tuple-element.61), channel_id=1, source_target_pairs={{0,16},{1,17},{2,18},{3,19},{4,20},{5,21},{6,22},{7,23},{8,24},{9,... | collective-permute-start | bytes 2457608 | tf_op jit(solution)/shard_map/ppermute | solution.py:31
  82.3 5.0 %collective-permute-start.15 = (f32[320,640]{1,0:T(8,128)S(1)}, f32[320,640]{1,0:T(8,128)S(1)}, u32[]{:S(2)}, u32[]{:S(2)}) collective-permute-start(f32[320,640]{1,0:T(8,128)S(1)} %get-tuple-element.57), channel_id=1, source_target_pairs={{0,16},{1,17},{2,18},{3,19},{4,20},{5,21},{6,22},{7,23},{8,24},{9,... | collective-permute-start | bytes 2457608 | tf_op jit(solution)/shard_map/ppermute | solution.py:31
  82.9 12.4 %collective-permute-start.20 = (f32[160,640]{1,0:T(8,128)S(1)}, f32[160,640]{1,0:T(8,128)S(1)}, u32[]{:S(2)}, u32[]{:S(2)}) collective-permute-start(f32[160,640]{1,0:T(8,128)S(1)} %get-tuple-element.70), channel_id=1, source_target_pairs={{0,1},{1,2},{2,3},{3,0},{4,5},{5,6},{6,7},{7,4},{8,9},{9,10},{10,1... | collective-permute-start | bytes 1228808 | tf_op jit(solution)/shard_map/ppermute | solution.py:31
  84.7 11.2 %collective-permute-start.17 = (f32[160,640]{1,0:T(8,128)S(1)}, f32[160,640]{1,0:T(8,128)S(1)}, u32[]{:S(2)}, u32[]{:S(2)}) collective-permute-start(f32[160,640]{1,0:T(8,128)S(1)} %get-tuple-element.71), channel_id=1, source_target_pairs={{0,3},{1,0},{2,1},{3,2},{4,7},{5,4},{6,5},{7,6},{8,11},{9,8},{10,9... | collective-permute-start | bytes 1228808 | tf_op jit(solution)/shard_map/ppermute | solution.py:31
  85.8 19.3 %collective-permute-start.22 = (f32[320,640]{1,0:T(8,128)S(1)}, f32[320,640]{1,0:T(8,128)S(1)}, u32[]{:S(2)}, u32[]{:S(2)}) collective-permute-start(f32[320,640]{1,0:T(8,128)S(1)} %get-tuple-element.62), channel_id=1, source_target_pairs={{0,96},{1,97},{2,98},{3,99},{4,100},{5,101},{6,102},{7,103},{8,104... | collective-permute-start | bytes 2457608 | tf_op jit(solution)/shard_map/ppermute | solution.py:31
  85.8 20.3 %collective-permute-start.23 = (f32[320,640]{1,0:T(8,128)S(1)}, f32[320,640]{1,0:T(8,128)S(1)}, u32[]{:S(2)}, u32[]{:S(2)}) collective-permute-start(f32[320,640]{1,0:T(8,128)S(1)} %get-tuple-element.62), channel_id=1, source_target_pairs={{0,32},{1,33},{2,34},{3,35},{4,36},{5,37},{6,38},{7,39},{8,40},{9,... | collective-permute-start | bytes 2457608 | tf_op jit(solution)/shard_map/ppermute | solution.py:31
  87.4 12.0 %collective-permute-start.14 = (f32[320,640]{1,0:T(8,128)S(1)}, f32[320,640]{1,0:T(8,128)S(1)}, u32[]{:S(2)}, u32[]{:S(2)}) collective-permute-start(f32[320,640]{1,0:T(8,128)S(1)} %get-tuple-element.55), channel_id=1, source_target_pairs={{0,16},{1,17},{2,18},{3,19},{4,20},{5,21},{6,22},{7,23},{8,24},{9,... | collective-permute-start | bytes 2457608 | tf_op jit(solution)/shard_map/ppermute | solution.py:31
  95.5 20.2 %collective-permute-start.21 = (f32[320,640]{1,0:T(8,128)S(1)}, f32[320,640]{1,0:T(8,128)S(1)}, u32[]{:S(2)}, u32[]{:S(2)}) collective-permute-start(f32[320,640]{1,0:T(8,128)S(1)} %pad_maximum_fusion.1), channel_id=1, source_target_pairs={{0,1},{1,2},{2,3},{3,0},{4,5},{5,6},{6,7},{7,4},{8,9},{9,10},{10,1... | collective-permute-start | bytes 2457608 | tf_op jit(solution)/shard_map/ppermute | solution.py:31
  96.0 19.7 %copy-start.1 = (f32[640,320]{0,1:T(8,128)S(1)}, f32[640,320]{0,1:T(8,128)}, u32[]{:S(2)}) copy-start(f32[640,320]{0,1:T(8,128)} %param.11) | copy-start | bytes 2457604
  96.0 19.7 %copy-start.2 = (f32[640,320]{0,1:T(8,128)S(1)}, f32[640,320]{0,1:T(8,128)}, u32[]{:S(2)}) copy-start(f32[640,320]{0,1:T(8,128)} %param.12) | copy-start | bytes 2457604
  96.0 19.6 %collective-permute-start.18 = (f32[320,640]{1,0:T(8,128)S(1)}, f32[320,640]{1,0:T(8,128)S(1)}, u32[]{:S(2)}, u32[]{:S(2)}) collective-permute-start(f32[320,640]{1,0:T(8,128)S(1)} %pad_maximum_fusion), channel_id=1, source_target_pairs={{0,3},{1,0},{2,1},{3,2},{4,7},{5,4},{6,5},{7,6},{8,11},{9,8},{10,9... | collective-permute-start | bytes 2457608 | tf_op jit(solution)/shard_map/ppermute | solution.py:31
  115.7 22.3 %copy-start.3 = (f32[8]{0:T(128)S(1)}, f32[8]{0:T(128)}, u32[]{:S(2)}) copy-start(f32[8]{0:T(128)} %param.15) | copy-start | bytes 100
  118.0 21.7 %collective-permute-start.34 = (f32[320,640]{1,0:T(8,128)S(1)}, f32[320,640]{1,0:T(8,128)}, u32[]{:S(2)}, u32[]{:S(2)}) collective-permute-start(f32[320,640]{1,0:T(8,128)S(1)} %get-tuple-element.64.update.u), channel_id=1, source_target_pairs={{0,96},{1,97},{2,98},{3,99},{4,100},{5,101},{6,102},{7,103},{8,104... | collective-permute-start | bytes 2457608 | tf_op jit(solution)/shard_map/ppermute | solution.py:31
  118.1 21.6 %collective-permute-start.35 = (f32[320,640]{1,0:T(8,128)S(1)}, f32[320,640]{1,0:T(8,128)}, u32[]{:S(2)}, u32[]{:S(2)}) collective-permute-start(f32[320,640]{1,0:T(8,128)S(1)} %get-tuple-element.64.update.u), channel_id=1, source_target_pairs={{0,32},{1,33},{2,34},{3,35},{4,36},{5,37},{6,38},{7,39},{8,40},{9,... | collective-permute-start | bytes 2457608 | tf_op jit(solution)/shard_map/ppermute | solution.py:31
  119.6 3.1 %collective-permute-start.24 = (f32[16,128]{1,0:T(8,128)S(1)}, f32[16,128]{1,0:T(8,128)S(1)}, u32[]{:S(2)}, u32[]{:S(2)}) collective-permute-start(f32[16,128]{1,0:T(8,128)S(1)} %get-tuple-element.63), channel_id=1, source_target_pairs={{0,16},{1,17},{2,18},{3,19},{4,20},{5,21},{6,22},{7,23},{8,24},{9,... | collective-permute-start | bytes 24584 | tf_op jit(solution)/shard_map/ppermute | solution.py:31
  122.7 4.8 %collective-permute-start.25 = (f32[16,128]{1,0:T(8,128)S(1)}, f32[16,128]{1,0:T(8,128)S(1)}, u32[]{:S(2)}, u32[]{:S(2)}) collective-permute-start(f32[16,128]{1,0:T(8,128)S(1)} %add.54), channel_id=1, source_target_pairs={{0,8},{1,9},{2,10},{3,11},{4,12},{5,13},{6,14},{7,15},{8,0},{9,1},... | collective-permute-start | bytes 24584 | tf_op jit(solution)/shard_map/ppermute | solution.py:31
  124.8 4.1 %collective-permute-start.26 = (f32[16,128]{1,0:T(8,128)S(1)}, f32[16,128]{1,0:T(8,128)S(1)}, u32[]{:S(2)}, u32[]{:S(2)}) collective-permute-start(f32[16,128]{1,0:T(8,128)S(1)} %add.54), channel_id=1, source_target_pairs={{0,4},{1,5},{2,6},{3,7},{4,8},{5,9},{6,10},{7,11},{8,12},{9,13},{1... | collective-permute-start | bytes 24584 | tf_op jit(solution)/shard_map/ppermute | solution.py:31
  125.9 3.0 %collective-permute-start.27 = (f32[16,128]{1,0:T(8,128)S(1)}, f32[16,128]{1,0:T(8,128)S(1)}, u32[]{:S(2)}, u32[]{:S(2)}) collective-permute-start(f32[16,128]{1,0:T(8,128)S(1)} %add.54), channel_id=1, source_target_pairs={{0,12},{1,13},{2,14},{3,15},{4,0},{5,1},{6,2},{7,3},{8,4},{9,5},{1... | collective-permute-start | bytes 24584 | tf_op jit(solution)/shard_map/ppermute | solution.py:31
  128.9 4.8 %collective-permute-start.28 = (f32[16,128]{1,0:T(8,128)S(1)}, f32[16,128]{1,0:T(8,128)S(1)}, u32[]{:S(2)}, u32[]{:S(2)}) collective-permute-start(f32[16,128]{1,0:T(8,128)S(1)} %add_add_fusion.2), channel_id=1, source_target_pairs={{0,2},{1,3},{2,0},{3,1},{4,6},{5,7},{6,4},{7,5},{8,10},{9,11},{10,... | collective-permute-start | bytes 24584 | tf_op jit(solution)/shard_map/ppermute | solution.py:31
  130.4 4.1 %collective-permute-start.29 = (f32[16,128]{1,0:T(8,128)S(1)}, f32[16,128]{1,0:T(8,128)S(1)}, u32[]{:S(2)}, u32[]{:S(2)}) collective-permute-start(f32[16,128]{1,0:T(8,128)S(1)} %add_add_fusion.2), channel_id=1, source_target_pairs={{0,1},{1,2},{2,3},{3,0},{4,5},{5,6},{6,7},{7,4},{8,9},{9,10},{10,1... | collective-permute-start | bytes 24584 | tf_op jit(solution)/shard_map/ppermute | solution.py:31
  132.3 2.9 %collective-permute-start.30 = (f32[16,128]{1,0:T(8,128)S(1)}, f32[16,128]{1,0:T(8,128)S(1)}, u32[]{:S(2)}, u32[]{:S(2)}) collective-permute-start(f32[16,128]{1,0:T(8,128)S(1)} %add_add_fusion.2), channel_id=1, source_target_pairs={{0,3},{1,0},{2,1},{3,2},{4,7},{5,4},{6,5},{7,6},{8,11},{9,8},{10,9... | collective-permute-start | bytes 24584 | tf_op jit(solution)/shard_map/ppermute | solution.py:31
  135.2 4.1 %collective-permute-start.31 = (f32[16,128]{1,0:T(8,128)S(1)}, f32[16,128]{1,0:T(8,128)S(1)}, u32[]{:S(2)}, u32[]{:S(2)}) collective-permute-start(f32[16,128]{1,0:T(8,128)S(1)} %add_add_fusion.1), channel_id=1, source_target_pairs={{0,64},{1,65},{2,66},{3,67},{4,68},{5,69},{6,70},{7,71},{8,72},{9,... | collective-permute-start | bytes 24584 | tf_op jit(solution)/shard_map/ppermute | solution.py:31
  135.2 4.3 %collective-permute-start.32 = (f32[16,128]{1,0:T(8,128)S(1)}, f32[16,128]{1,0:T(8,128)S(1)}, u32[]{:S(2)}, u32[]{:S(2)}) collective-permute-start(f32[16,128]{1,0:T(8,128)S(1)} %add_add_fusion.1), channel_id=1, source_target_pairs={{0,32},{1,33},{2,34},{3,35},{4,36},{5,37},{6,38},{7,39},{8,40},{9,... | collective-permute-start | bytes 24584 | tf_op jit(solution)/shard_map/ppermute | solution.py:31
  136.9 2.9 %collective-permute-start.33 = (f32[16,128]{1,0:T(8,128)S(1)}, f32[16,128]{1,0:T(8,128)S(1)}, u32[]{:S(2)}, u32[]{:S(2)}) collective-permute-start(f32[16,128]{1,0:T(8,128)S(1)} %add_add_fusion.1), channel_id=1, source_target_pairs={{0,96},{1,97},{2,98},{3,99},{4,100},{5,101},{6,102},{7,103},{8,104... | collective-permute-start | bytes 24584 | tf_op jit(solution)/shard_map/ppermute | solution.py:31
  140.0 9.4 %collective-permute-start.36 = (bf16[320,640]{1,0:T(8,128)(2,1)S(1)}, bf16[320,640]{1,0:T(8,128)(2,1)S(1)}, u32[]{:S(2)}, u32[]{:S(2)}) collective-permute-start(bf16[320,640]{1,0:T(8,128)(2,1)S(1)} %own_step.1.own.refs_0_), channel_id=1, source_target_pairs={{0,64},{1,65},{2,66},{3,67},{4,68},{5,69},{6,70},{7,71},{8,72},{9,... | collective-permute-start | bytes 1228808 | tf_op jit(solution)/shard_map/ppermute | solution.py:31
  144.0 9.8 %collective-permute-start.39 = (bf16[320,640]{1,0:T(8,128)(2,1)S(1)}, bf16[320,640]{1,0:T(8,128)(2,1)S(1)}, u32[]{:S(2)}, u32[]{:S(2)}) collective-permute-start(bf16[320,640]{1,0:T(8,128)(2,1)S(1)} %get-tuple-element.68.refs_2_), channel_id=1, source_target_pairs={{0,16},{1,17},{2,18},{3,19},{4,20},{5,21},{6,22},{7,23},{8,24},{9,... | collective-permute-start | bytes 1228808 | tf_op jit(solution)/shard_map/ppermute | solution.py:31
  149.0 4.9 %collective-permute-start.40 = (bf16[320,640]{1,0:T(8,128)(2,1)S(1)}, bf16[320,640]{1,0:T(8,128)(2,1)S(1)}, u32[]{:S(2)}, u32[]{:S(2)}) collective-permute-start(bf16[320,640]{1,0:T(8,128)(2,1)S(1)} %get-tuple-element.69.refs_4_), channel_id=1, source_target_pairs={{0,16},{1,17},{2,18},{3,19},{4,20},{5,21},{6,22},{7,23},{8,24},{9,... | collective-permute-start | bytes 1228808 | tf_op jit(solution)/shard_map/ppermute | solution.py:31
  149.0 4.9 %collective-permute-start.38 = (bf16[320,640]{1,0:T(8,128)(2,1)S(1)}, bf16[320,640]{1,0:T(8,128)(2,1)S(1)}, u32[]{:S(2)}, u32[]{:S(2)}) collective-permute-start(bf16[320,640]{1,0:T(8,128)(2,1)S(1)} %own_step.1.own.refs_0_), channel_id=1, source_target_pairs={{0,16},{1,17},{2,18},{3,19},{4,20},{5,21},{6,22},{7,23},{8,24},{9,... | collective-permute-start | bytes 1228808 | tf_op jit(solution)/shard_map/ppermute | solution.py:31
  149.5 5.9 %collective-permute-start.37 = (bf16[320,640]{1,0:T(8,128)(2,1)S(1)}, bf16[320,640]{1,0:T(8,128)(2,1)S(1)}, u32[]{:S(2)}, u32[]{:S(2)}) collective-permute-start(bf16[320,640]{1,0:T(8,128)(2,1)S(1)} %collective-permute-done.36.refs_0_), channel_id=1, source_target_pairs={{0,16},{1,17},{2,18},{3,19},{4,20},{5,21},{6,22},{7,23},{8,24},{9,... | collective-permute-start | bytes 1228808 | tf_op jit(solution)/shard_map/ppermute | solution.py:31

commit v7 on v6

--- a/solution.py
+++ b/solution.py
@@ -133,35 +133,49 @@
     )(z0, zp, zm, x0, xp, xm)
 
 
+def middle_kernel(z0, zp, zm, x0, xp, xm, xd0, xd1, *refs):
+    del x0, xp, xm
+    rhs = jnp.concatenate([xd0[:BLOCK, :], xd0[BLOCK:, :], xd1[BLOCK:, :]], axis=0)
+    for ky in range(4):
+        rows = slice(ky * COLS, (ky + 1) * COLS)
+        parts = [z[rows, 2 * BLOCK : 3 * BLOCK] for z in (z0, zm, zp)]
+        refs[4 + ky][...] = refs[ky][...] + dot(jnp.concatenate(parts, axis=1), rhs)
+
+
+def middle_product(c_near, a_pieces, totals):
+    return pl.pallas_call(
+        middle_kernel,
+        out_shape=[jax.ShapeDtypeStruct((COLS, GROUP), jnp.float32)] * 4,
+        in_specs=[VMEM] * 12,
+        out_specs=[VMEM] * 4,
+        input_output_aliases={8 + k: k for k in range(4)},
+        compiler_params=params(14),
+        name="middle_product",
+    )(*c_near, *a_pieces, *totals)
+
+
 def far_kernel(order, *refs):
-    z0, zp, zm, zd0, zd1, x0, xp, xm, xd0, xd1 = refs[:10]
-    totals, outs = refs[10 : 10 + len(order)], refs[11 + len(order) : -1]
-    refs[-1][...] = refs[10 + len(order)][...]
-    acts = jnp.concatenate(
-        [x[2 * BLOCK : 3 * BLOCK, :] for x in (x0, xp)]
-        + [xd1[:BLOCK, :]]
-        + [xm[2 * BLOCK : 3 * BLOCK, :]]
-        + [xd0[:BLOCK, :], xd0[BLOCK:, :], xd1[BLOCK:, :]],
-        axis=0,
-    )
-    middle = slice(2 * BLOCK, 3 * BLOCK)
+    zd0, zd1, x0, xp, xm, xd0, xd1 = refs[:7]
+    count = len(order)
+    totals, outs = refs[7 : 7 + count], refs[8 + count : -1]
+    refs[-1][...] = refs[7 + count][...]
+    last = slice(2 * BLOCK, 3 * BLOCK)
+    rhs = jnp.concatenate([x0[last, :], xp[last, :], xd1[:BLOCK, :], xm[last, :]], axis=0)
     for k, ky in enumerate(order):
-        rows = slice(ky * COLS, (ky + 1) * COLS)
         far = zd0 if ky < 2 else zd1
-        parts = [far[(ky % 2) * COLS : (ky % 2 + 1) * COLS, :]]
-        parts += [z[rows, middle] for z in (z0, zm, zp)]
-        total = totals[k][...] + dot(jnp.concatenate(parts, axis=1), acts)
+        total = totals[k][...] + dot(far[(ky % 2) * COLS : (ky % 2 + 1) * COLS, :], rhs)
         outs[2 * k][...] = total[:, :ROWS]
         outs[2 * k + 1][...] = total[:, ROWS:]
 
 
 def far_product(order, pieces, totals, also):
+    count = len(order)
     outs = pl.pallas_call(
         functools.partial(far_kernel, order),
-        out_shape=[jax.ShapeDtypeStruct((COLS, ROWS), jnp.float32)] * (2 * len(order))
+        out_shape=[jax.ShapeDtypeStruct((COLS, ROWS), jnp.float32)] * (2 * count)
         + [jax.ShapeDtypeStruct(also.shape, also.dtype)],
-        in_specs=[VMEM] * (11 + len(order)),
-        out_specs=[VMEM] * (2 * len(order) + 1),
+        in_specs=[VMEM] * (8 + count),
+        out_specs=[VMEM] * (2 * count + 1),
         compiler_params=params(14),
         name="far_product",
     )(*pieces, *[totals[ky] for ky in order], also)
@@ -189,10 +203,12 @@
     c_pieces = ring_gather(c_block, "dz")
     a_pieces = ring_gather(a_block, "dx")
     totals = near_product(*c_pieces[:3], *a_pieces[:3])
-    terms, weights = far_product((2,), c_pieces + a_pieces, totals, weights)
+    totals = middle_product(c_pieces[:3], a_pieces, totals)
+    far_pieces = c_pieces[3:] + a_pieces
+    terms, weights = far_product((2,), far_pieces, totals, weights)
     half = COLS // 2
     far = moved(terms[2][1], dc=1)
-    others, weights = far_product((1, 3, 0), c_pieces + a_pieces, totals, weights)
+    others, weights = far_product((1, 3, 0), far_pieces, totals, weights)
     terms |= others
     low = moved(terms[2][0][:half] + far[:half], dy=-1)
     high = moved(terms[2][0][half:] + far[half:], dy=1)
@@ -333,7 +349,9 @@
     for k, dz in enumerate(offsets):
         for half, core in enumerate((c, 1 - c)):
             start = pl.multiple_of((2 * lax.rem(z + dz, 4) + core) * ROWS, 128)
-            copies.append((pieces[2 * k + half], out.at[:, pl.ds(start, ROWS)]))
+            for first in range(0, COLS, COLS // 2):
+                rows = pl.ds(first, COLS // 2)
+                copies.append((pieces[2 * k + half].at[rows], out.at[rows, pl.ds(start, ROWS)]))
     copy_all(copies, sems)
 
 
@@ -345,7 +363,7 @@
         out_shape=jax.ShapeDtypeStruct((COLS, 8 * ROWS), jnp.bfloat16),
         in_specs=[VMEM] * count + [HBM] * len(given),
         out_specs=HBM,
-        scratch_shapes=[pltpu.SemaphoreType.DMA((count,))],
+        scratch_shapes=[pltpu.SemaphoreType.DMA((2 * count,))],
         input_output_aliases={count: 0} if given else {},
         compiler_params=params(4),
         name="placed",

time: 157 us -> 155 us (0.987)
  waiting for transfers between devices: 69.9 us -> 67.3 us
    ppermute x41, waiting for transfers between devices: 69.9 us -> 67.3 us  [moved(): return lax.ppermute(array, ('dp', 'mp'), pairs)]
    pallas_call x0 -> x1, Pallas kernels: none -> 2.07 us  [middle_product(): pl.pallas_call(middle_kernel, out_shape=[jax.ShapeDtypeStruct((COLS, GROU...]
    pallas_call x2, Pallas kernels: 3.82 us -> 2.13 us  [far_product(): pl.pallas_call(functools.partial(far_kernel, order), out_shape=[jax.Shape...]
  transfers between devices with their start and end apart: 41 -> 41, of which waited for: 20 -> 19; matrix products, arithmetic and copies ran while one was open for 1% -> 1% of each run, Pallas kernels for 7% -> 8%
where the time goes in v7:
time: 155 us
  waiting for transfers between devices  67.3 us (43%)
  starting transfers between devices  64.2 us (41%)
  Pallas kernels  18.4 us (12%)
  between operations  3.22 us (2%)
    ppermute x41, waiting for transfers between devices, moved(): return lax.ppermute(array, ('dp', 'mp'), pairs)  67.3 us
    ppermute x41, starting transfers between devices, moved(): return lax.ppermute(array, ('dp', 'mp'), pairs)  64.2 us
    pallas_call x1, Pallas kernels, near_product(): pl.pallas_call(near_kernel, out_shape=[jax.ShapeDtypeStruct((COLS, GROUP)...  4.39 us
  transfers between devices with their start and end apart: 41, of which 19 were waited for; matrix products, arithmetic and copies ran while one was open for 1% of the time, Pallas kernels for 8%

profile of v7, /device:TPU:1, one launch (start us, length us, event | category | flops | bytes accessed | tf_op | source)
XLA Modules:
  0.0 154.7 jit_solution(2020626326794889636)
XLA Ops:
  0.6 2.1 %prepare.1 = (bf16[128,1280]{1,0:T(8,128)(2,1)S(1)}, bf16[128,1280]{1,0:T(8,128)(2,1)S(1)}, bf16[128,1280]{1,0:T(8,128)(2,1)S(1)}, bf16[128,1280]{1,0:T(8,128)(2...) custom-call(bf16[128,5120]{1,0:T(8,128)(2,1)} %act.1, ...), custom_call_target="tpu_custom_call" | custom-call | tf_op jit(solution)/shard_map/prepare/pallas_call | solution.py:77
  2.7 2.5 %collective-permute-start.7 = (bf16[128,1280]{1,0:T(8,128)(2,1)S(1)}, bf16[128,1280]{1,0:T(8,128)(2,1)S(1)}, u32[]{:S(2)}, u32[]{:S(2)}) collective-permute-start(bf16[128,1280]{1,0:T(8,128)(2,1)S(1)} %get-tuple-element.50), channel_id=1, source_target_pairs={{0,32},{1,33},{2,34},{3,35},{4,36},{5,37},{6,38},{7,39},{8,40},{9,... | collective-permute-start | bytes 983048 | tf_op jit(solution)/shard_map/ppermute | solution.py:31
  5.3 3.3 %collective-permute-start.8 = (bf16[128,1280]{1,0:T(8,128)(2,1)S(1)}, bf16[128,1280]{1,0:T(8,128)(2,1)S(1)}, u32[]{:S(2)}, u32[]{:S(2)}) collective-permute-start(bf16[128,1280]{1,0:T(8,128)(2,1)S(1)} %get-tuple-element.51), channel_id=1, source_target_pairs={{0,64},{1,65},{2,66},{3,67},{4,68},{5,69},{6,70},{7,71},{8,72},{9,... | collective-permute-start | bytes 983048 | tf_op jit(solution)/shard_map/ppermute | solution.py:31
  9.3 1.3 collective-permute-start
  10.6 2.6 %collective-permute-start.1 = (bf16[320,512]{1,0:T(8,128)(2,1)S(1)}, bf16[320,512]{1,0:T(8,128)(2,1)S(1)}, u32[]{:S(2)}, u32[]{:S(2)}) collective-permute-start(bf16[320,512]{1,0:T(8,128)(2,1)S(1)} %get-tuple-element.43), channel_id=1, source_target_pairs={{0,2},{1,3},{2,0},{3,1},{4,6},{5,7},{6,4},{7,5},{8,10},{9,11},{10,... | collective-permute-start | bytes 983048 | tf_op jit(solution)/shard_map/ppermute | solution.py:31
  13.3 1.6 %collective-permute-done.7 = bf16[128,1280]{1,0:T(8,128)(2,1)S(1)} collective-permute-done((bf16[128,1280]{1,0:T(8,128)(2,1)S(1)}, bf16[128,1280]{1,0:T(8,128)(2,1)S(1)}, u32[]{:S(2)}, u32[]{:S(2)}) %collective-permute-start.7) | collective-permute-done | bytes 327712 | tf_op jit(solution)/shard_map/ppermute | solution.py:31
  14.8 2.7 %collective-permute-start.2 = (bf16[320,512]{1,0:T(8,128)(2,1)S(1)}, bf16[320,512]{1,0:T(8,128)(2,1)S(1)}, u32[]{:S(2)}, u32[]{:S(2)}) collective-permute-start(bf16[320,512]{1,0:T(8,128)(2,1)S(1)} %get-tuple-element.44), channel_id=1, source_target_pairs={{0,3},{1,0},{2,1},{3,2},{4,7},{5,4},{6,5},{7,6},{8,11},{9,8},{10,9... | collective-permute-start | bytes 983048 | tf_op jit(solution)/shard_map/ppermute | solution.py:31
  17.6 5.1 %collective-permute-done.8 = bf16[128,1280]{1,0:T(8,128)(2,1)S(1)} collective-permute-done((bf16[128,1280]{1,0:T(8,128)(2,1)S(1)}, bf16[128,1280]{1,0:T(8,128)(2,1)S(1)}, u32[]{:S(2)}, u32[]{:S(2)}) %collective-permute-start.8) | collective-permute-done | bytes 327712 | tf_op jit(solution)/shard_map/ppermute | solution.py:31
  22.8 2.5 %collective-permute-start.10 = (bf16[512,1280]{1,0:T(8,128)(2,1)S(1)}, bf16[512,1280]{1,0:T(8,128)(2,1)S(1)}, u32[]{:S(2)}, u32[]{:S(2)}) collective-permute-start(bf16[512,1280]{1,0:T(8,128)(2,1)S(1)} %constant_dynamic-update-slice_fusion.4.x0.refs_2_), channel_id=1, source_target_pairs={{0,12},{1,13},{2,14},{3,15},{4,0},{5,1},{6,2},{7,3},{8,4},{9,5},{1... | collective-permute-start | bytes 3932168 | tf_op jit(solution)/shard_map/ppermute | solution.py:31
  25.3 1.1 collective-permute-done.1
  26.5 1.9 %collective-permute-start.3 = (bf16[1280,512]{1,0:T(8,128)(2,1)S(1)}, bf16[1280,512]{1,0:T(8,128)(2,1)S(1)}, u32[]{:S(2)}, u32[]{:S(2)}) collective-permute-start(bf16[1280,512]{1,0:T(8,128)(2,1)S(1)} %constant_dynamic-update-slice_fusion.z0), channel_id=1, source_target_pairs={{0,96},{1,97},{2,98},{3,99},{4,100},{5,101},{6,102},{7,103},{8,104... | collective-permute-start | bytes 3932168 | tf_op jit(solution)/shard_map/ppermute | solution.py:31
  28.4 23.4 %collective-permute-done.10.xp.refs_3_ = bf16[512,1280]{1,0:T(8,128)(2,1)S(1)} collective-permute-done((bf16[512,1280]{1,0:T(8,128)(2,1)S(1)}, bf16[512,1280]{1,0:T(8,128)(2,1)S(1)}, u32[]{:S(2)}, u32[]{:S(2)}) %collective-permute-start.10) | collective-permute-done | bytes 1310752 | tf_op jit(solution)/shard_map/ppermute | solution.py:31
  51.9 3.5 %collective-permute-start.12 = (bf16[256,1280]{1,0:T(8,128)(2,1)S(1)}, bf16[256,1280]{1,0:T(8,128)(2,1)S(1)}, u32[]{:S(2)}, u32[]{:S(2)}) collective-permute-start(bf16[256,1280]{1,0:T(8,128)(2,1)S(1)} %slice.50), channel_id=1, source_target_pairs={{0,12},{1,13},{2,14},{3,15},{4,0},{5,1},{6,2},{7,3},{8,4},{9,5},{1... | collective-permute-start | bytes 1966088 | tf_op jit(solution)/shard_map/ppermute | solution.py:31
  55.8 3.9 %collective-permute-start.4 = (bf16[640,512]{1,0:T(8,128)(2,1)S(1)}, bf16[640,512]{1,0:T(8,128)(2,1)S(1)}, u32[]{:S(2)}, u32[]{:S(2)}) collective-permute-start(bf16[640,512]{1,0:T(8,128)(2,1)S(1)} %slice.48), channel_id=1, source_target_pairs={{0,96},{1,97},{2,98},{3,99},{4,100},{5,101},{6,102},{7,103},{8,104... | collective-permute-start | bytes 1966088 | tf_op jit(solution)/shard_map/ppermute | solution.py:31
  59.8 4.4 %near_product.1 = (f32[320,1280]{1,0:T(8,128)S(1)}, f32[320,1280]{1,0:T(8,128)S(1)}, f32[320,1280]{1,0:T(8,128)S(1)}, f32[320,1280]{1,0:T(8,128)S(1)}) custom-call(bf16[1280,512]{1,0:T(8,128)(2,1)S(1)} %constant_dynamic-update-slice_fusion.z0, bf16[1280,512]{1,0:T(8,128)(2,1)S(1)} %collective-permute-done.3.zp, ...), custom_call_target="tpu_custom_call" | custom-call | tf_op jit(solution)/shard_map/near_product/pallas_call | solution.py:126
  64.2 2.7 %collective-permute-done.12.xd0.refs_5_ = bf16[256,1280]{1,0:T(8,128)(2,1)S(1)} collective-permute-done((bf16[256,1280]{1,0:T(8,128)(2,1)S(1)}, bf16[256,1280]{1,0:T(8,128)(2,1)S(1)}, u32[]{:S(2)}, u32[]{:S(2)}) %collective-permute-start.12) | collective-permute-done | bytes 655392 | tf_op jit(solution)/shard_map/ppermute | solution.py:31
  66.9 3.3 %collective-permute-done.13.xd1.refs_6_ = bf16[256,1280]{1,0:T(8,128)(2,1)S(1)} collective-permute-done((bf16[256,1280]{1,0:T(8,128)(2,1)S(1)}, bf16[256,1280]{1,0:T(8,128)(2,1)S(1)}, u32[]{:S(2)}, u32[]{:S(2)}) %collective-permute-start.13) | collective-permute-done | bytes 655392 | tf_op jit(solution)/shard_map/ppermute | solution.py:31
  70.2 2.1 %middle_product.1 = (f32[320,1280]{1,0:T(8,128)S(1)}, f32[320,1280]{1,0:T(8,128)S(1)}, f32[320,1280]{1,0:T(8,128)S(1)}, f32[320,1280]{1,0:T(8,128)S(1)}) custom-call(bf16[1280,512]{1,0:T(8,128)(2,1)S(1)} %constant_dynamic-update-slice_fusion.z0, ...), custom_call_target="tpu_custom_call", output_to_operand_aliasing={{0}: (8, {}), {1}: (9, {}), {2}: (10, {}), {3}: (11, {})} | custom-call | tf_op jit(solution)/shard_map/middle_product/pallas_call | solution.py:146
  72.3 3.0 %collective-permute-done.6.refs_1_ = bf16[640,512]{1,0:T(8,128)(2,1)S(1)} collective-permute-done((bf16[640,512]{1,0:T(8,128)(2,1)S(1)}, bf16[640,512]{1,0:T(8,128)(2,1)S(1)}, u32[]{:S(2)}, u32[]{:S(2)}) %collective-permute-start.6) | collective-permute-done | bytes 655392 | tf_op jit(solution)/shard_map/ppermute | solution.py:31
  76.0 3.1 %collective-permute-start.16 = (f32[320,640]{1,0:T(8,128)S(1)}, f32[320,640]{1,0:T(8,128)S(1)}, u32[]{:S(2)}, u32[]{:S(2)}) collective-permute-start(f32[320,640]{1,0:T(8,128)S(1)} %get-tuple-element.67), channel_id=1, source_target_pairs={{0,16},{1,17},{2,18},{3,19},{4,20},{5,21},{6,22},{7,23},{8,24},{9,... | collective-permute-start | bytes 2457608 | tf_op jit(solution)/shard_map/ppermute | solution.py:31
  79.0 1.5 far_product.3
  81.2 1.7 %collective-permute-start.20 = (f32[160,640]{1,0:T(8,128)S(1)}, f32[160,640]{1,0:T(8,128)S(1)}, u32[]{:S(2)}, u32[]{:S(2)}) collective-permute-start(f32[160,640]{1,0:T(8,128)S(1)} %get-tuple-element.78), channel_id=1, source_target_pairs={{0,1},{1,2},{2,3},{3,0},{4,5},{5,6},{6,7},{7,4},{8,9},{9,10},{10,1... | collective-permute-start | bytes 1228808 | tf_op jit(solution)/shard_map/ppermute | solution.py:31
  83.0 1.1 collective-permute-start.17
  84.1 1.8 %collective-permute-start.22 = (f32[320,640]{1,0:T(8,128)S(1)}, f32[320,640]{1,0:T(8,128)S(1)}, u32[]{:S(2)}, u32[]{:S(2)}) collective-permute-start(f32[320,640]{1,0:T(8,128)S(1)} %get-tuple-element.70), channel_id=1, source_target_pairs={{0,96},{1,97},{2,98},{3,99},{4,100},{5,101},{6,102},{7,103},{8,104... | collective-permute-start | bytes 2457608 | tf_op jit(solution)/shard_map/ppermute | solution.py:31
  86.0 1.0 collective-permute-start.14
  87.2 6.3 %collective-permute-done.20 = f32[160,640]{1,0:T(8,128)S(1)} collective-permute-done((f32[160,640]{1,0:T(8,128)S(1)}, f32[160,640]{1,0:T(8,128)S(1)}, u32[]{:S(2)}, u32[]{:S(2)}) %collective-permute-start.20) | collective-permute-done | bytes 409632 | tf_op jit(solution)/shard_map/ppermute | solution.py:31
  94.2 2.4 %collective-permute-start.18 = (f32[320,640]{1,0:T(8,128)S(1)}, f32[320,640]{1,0:T(8,128)S(1)}, u32[]{:S(2)}, u32[]{:S(2)}) collective-permute-start(f32[320,640]{1,0:T(8,128)S(1)} %pad_maximum_fusion), channel_id=1, source_target_pairs={{0,3},{1,0},{2,1},{3,2},{4,7},{5,4},{6,5},{7,6},{8,11},{9,8},{10,9... | collective-permute-start | bytes 2457608 | tf_op jit(solution)/shard_map/ppermute | solution.py:31
  97.5 5.8 %collective-permute-done.22.refs_8_.wp = f32[320,640]{1,0:T(8,128)S(1)} collective-permute-done((f32[320,640]{1,0:T(8,128)S(1)}, f32[320,640]{1,0:T(8,128)S(1)}, u32[]{:S(2)}, u32[]{:S(2)}) %collective-permute-start.22) | collective-permute-done | bytes 819232 | tf_op jit(solution)/shard_map/ppermute | solution.py:31
  103.2 2.7 %collective-permute-done.23.refs_9_.wm = f32[320,640]{1,0:T(8,128)S(1)} collective-permute-done((f32[320,640]{1,0:T(8,128)S(1)}, f32[320,640]{1,0:T(8,128)S(1)}, u32[]{:S(2)}, u32[]{:S(2)}) %collective-permute-start.23) | collective-permute-done | bytes 819232 | tf_op jit(solution)/shard_map/ppermute | solution.py:31
  106.0 7.7 %collective-permute-done.21.refs_3_ = f32[320,640]{1,0:T(8,128)S(1)} collective-permute-done((f32[320,640]{1,0:T(8,128)S(1)}, f32[320,640]{1,0:T(8,128)S(1)}, u32[]{:S(2)}, u32[]{:S(2)}) %collective-permute-start.21) | collective-permute-done | bytes 819232 | tf_op jit(solution)/shard_map/ppermute | solution.py:31
  113.7 2.4 %update.1 = (f32[320,640]{1,0:T(8,128)}, f32[320,640]{1,0:T(8,128)}, f32[320,640]{1,0:T(8,128)S(1)}, f32[16,128]{1,0:T(8,128)S(1)}) custom-call(f32[320,640]{1,0:T(8,128)S(1)} %get-tuple-element.62.refs_0_, f32[320,640]{1,0:T(8,128)S(1)} %collective-permute-done.14.refs_1_, f32[320,640]{1,0:T(8,128)S(1)} %collective-permute-done.18.refs_2_, ...), custom_call_target="tpu_custom_call" | custom-call | tf_op jit(solution)/shard_map/update/pallas_call | solution.py:270
  116.0 1.9 %collective-permute-start.34 = (f32[320,640]{1,0:T(8,128)S(1)}, f32[320,640]{1,0:T(8,128)}, u32[]{:S(2)}, u32[]{:S(2)}) collective-permute-start(f32[320,640]{1,0:T(8,128)S(1)} %get-tuple-element.72.update.u), channel_id=1, source_target_pairs={{0,96},{1,97},{2,98},{3,99},{4,100},{5,101},{6,102},{7,103},{8,104... | collective-permute-start | bytes 2457608 | tf_op jit(solution)/shard_map/ppermute | solution.py:31
  118.0 2.2 %collective-permute-start.24 = (f32[16,128]{1,0:T(8,128)S(1)}, f32[16,128]{1,0:T(8,128)S(1)}, u32[]{:S(2)}, u32[]{:S(2)}) collective-permute-start(f32[16,128]{1,0:T(8,128)S(1)} %get-tuple-element.71), channel_id=1, source_target_pairs={{0,16},{1,17},{2,18},{3,19},{4,20},{5,21},{6,22},{7,23},{8,24},{9,... | collective-permute-start | bytes 24584 | tf_op jit(solution)/shard_map/ppermute | solution.py:31
  120.1 0.8 collective-permute-done.24
  121.0 2.0 %collective-permute-start.25 = (f32[16,128]{1,0:T(8,128)S(1)}, f32[16,128]{1,0:T(8,128)S(1)}, u32[]{:S(2)}, u32[]{:S(2)}) collective-permute-start(f32[16,128]{1,0:T(8,128)S(1)} %add.54), channel_id=1, source_target_pairs={{0,8},{1,9},{2,10},{3,11},{4,12},{5,13},{6,14},{7,15},{8,0},{9,1},... | collective-permute-start | bytes 24584 | tf_op jit(solution)/shard_map/ppermute | solution.py:31
  123.0 1.1 collective-permute-start.26
  124.1 1.5 collective-permute-start.27
  125.6 1.4 collective-permute-done.26
  127.1 1.5 collective-permute-start.28
  128.6 1.9 %collective-permute-start.29 = (f32[16,128]{1,0:T(8,128)S(1)}, f32[16,128]{1,0:T(8,128)S(1)}, u32[]{:S(2)}, u32[]{:S(2)}) collective-permute-start(f32[16,128]{1,0:T(8,128)S(1)} %add_add_fusion.2), channel_id=1, source_target_pairs={{0,1},{1,2},{2,3},{3,0},{4,5},{5,6},{6,7},{7,4},{8,9},{9,10},{10,1... | collective-permute-start | bytes 24584 | tf_op jit(solution)/shard_map/ppermute | solution.py:31
  133.4 1.7 %collective-permute-start.32 = (f32[16,128]{1,0:T(8,128)S(1)}, f32[16,128]{1,0:T(8,128)S(1)}, u32[]{:S(2)}, u32[]{:S(2)}) collective-permute-start(f32[16,128]{1,0:T(8,128)S(1)} %add_add_fusion.1), channel_id=1, source_target_pairs={{0,32},{1,33},{2,34},{3,35},{4,36},{5,37},{6,38},{7,39},{8,40},{9,... | collective-permute-start | bytes 24584 | tf_op jit(solution)/shard_map/ppermute | solution.py:31
  135.1 1.1 collective-permute-start.33
  138.3 1.3 collective-permute-start.36
  139.5 2.7 %near_step.1 = (f32[320,640]{1,0:T(8,128)}, bf16[320,640]{1,0:T(8,128)(2,1)S(1)}, bf16[320,640]{1,0:T(8,128)(2,1)S(1)}) custom-call(f32[16,128]{1,0:T(8,128)S(1)} %add_add_fusion.sums, f32[1]{0:T(128)} %bitcast.5.rate, f32[320,640]{1,0:T(8,128)S(1)} %bitcast.14, f32[320,640]{1,0:T(8,128)S(1)} %collective-permute-done.22.refs_8_.wp, ...), custom_call_target="tpu_custom_call" | custom-call | tf_op jit(solution)/shard_map/near_step/pallas_call | solution.py:334
  142.2 5.0 %collective-permute-start.39 = (bf16[320,640]{1,0:T(8,128)(2,1)S(1)}, bf16[320,640]{1,0:T(8,128)(2,1)S(1)}, u32[]{:S(2)}, u32[]{:S(2)}) collective-permute-start(bf16[320,640]{1,0:T(8,128)(2,1)S(1)} %get-tuple-element.76.refs_2_), channel_id=1, source_target_pairs={{0,16},{1,17},{2,18},{3,19},{4,20},{5,21},{6,22},{7,23},{8,24},{9,... | collective-permute-start | bytes 1228808 | tf_op jit(solution)/shard_map/ppermute | solution.py:31
  147.7 4.4 %collective-permute-start.37 = (bf16[320,640]{1,0:T(8,128)(2,1)S(1)}, bf16[320,640]{1,0:T(8,128)(2,1)S(1)}, u32[]{:S(2)}, u32[]{:S(2)}) collective-permute-start(bf16[320,640]{1,0:T(8,128)(2,1)S(1)} %collective-permute-done.36.refs_0_), channel_id=1, source_target_pairs={{0,16},{1,17},{2,18},{3,19},{4,20},{5,21},{6,22},{7,23},{8,24},{9,... | collective-permute-start | bytes 1228808 | tf_op jit(solution)/shard_map/ppermute | solution.py:31
  152.1 1.6 %placed.2.refs_2_ = bf16[320,5120]{1,0:T(8,128)(2,1)} custom-call(bf16[320,640]{1,0:T(8,128)(2,1)S(1)} %own_step.1.own.refs_0_, bf16[320,640]{1,0:T(8,128)(2,1)S(1)} %collective-permute-done.38.refs_1_, bf16[320,640]{1,0:T(8,128)(2,1)S(1)} %get-tuple-element.76.refs_2_, bf16[320,640]{1,0:T(8,128)(2,1)S(1)} %collective-permute-done.39.refs_3_, ...), custom_call_target="tpu_custom_call" | custom-call | tf_op jit(solution)/shard_map/placed/pallas_call | solution.py:361
  153.6 0.9 placed.3
  (78 shorter events, 8.0 us)
Async XLA Ops:
  2.7 12.1 %collective-permute-start.7 = (bf16[128,1280]{1,0:T(8,128)(2,1)S(1)}, bf16[128,1280]{1,0:T(8,128)(2,1)S(1)}, u32[]{:S(2)}, u32[]{:S(2)}) collective-permute-start(bf16[128,1280]{1,0:T(8,128)(2,1)S(1)} %get-tuple-element.50), channel_id=1, source_target_pairs={{0,32},{1,33},{2,34},{3,35},{4,36},{5,37},{6,38},{7,39},{8,40},{9,... | collective-permute-start | bytes 983048 | tf_op jit(solution)/shard_map/ppermute | solution.py:31
  5.3 17.4 %collective-permute-start.8 = (bf16[128,1280]{1,0:T(8,128)(2,1)S(1)}, bf16[128,1280]{1,0:T(8,128)(2,1)S(1)}, u32[]{:S(2)}, u32[]{:S(2)}) collective-permute-start(bf16[128,1280]{1,0:T(8,128)(2,1)S(1)} %get-tuple-element.51), channel_id=1, source_target_pairs={{0,64},{1,65},{2,66},{3,67},{4,68},{5,69},{6,70},{7,71},{8,72},{9,... | collective-permute-start | bytes 983048 | tf_op jit(solution)/shard_map/ppermute | solution.py:31
  8.6 14.2 %collective-permute-start.9 = (bf16[128,1280]{1,0:T(8,128)(2,1)S(1)}, bf16[128,1280]{1,0:T(8,128)(2,1)S(1)}, u32[]{:S(2)}, u32[]{:S(2)}) collective-permute-start(bf16[128,1280]{1,0:T(8,128)(2,1)S(1)} %get-tuple-element.52), channel_id=1, source_target_pairs={{0,96},{1,97},{2,98},{3,99},{4,100},{5,101},{6,102},{7,103},{8,104... | collective-permute-start | bytes 983048 | tf_op jit(solution)/shard_map/ppermute | solution.py:31
  9.3 16.0 %collective-permute-start = (bf16[320,512]{1,0:T(8,128)(2,1)S(1)}, bf16[320,512]{1,0:T(8,128)(2,1)S(1)}, u32[]{:S(2)}, u32[]{:S(2)}) collective-permute-start(bf16[320,512]{1,0:T(8,128)(2,1)S(1)} %get-tuple-element.42), channel_id=1, source_target_pairs={{0,1},{1,2},{2,3},{3,0},{4,5},{5,6},{6,7},{7,4},{8,9},{9,10},{10,1... | collective-permute-start | bytes 983048 | tf_op jit(solution)/shard_map/ppermute | solution.py:31
  10.6 15.9 %collective-permute-start.1 = (bf16[320,512]{1,0:T(8,128)(2,1)S(1)}, bf16[320,512]{1,0:T(8,128)(2,1)S(1)}, u32[]{:S(2)}, u32[]{:S(2)}) collective-permute-start(bf16[320,512]{1,0:T(8,128)(2,1)S(1)} %get-tuple-element.43), channel_id=1, source_target_pairs={{0,2},{1,3},{2,0},{3,1},{4,6},{5,7},{6,4},{7,5},{8,10},{9,11},{10,... | collective-permute-start | bytes 983048 | tf_op jit(solution)/shard_map/ppermute | solution.py:31
  14.8 11.7 %collective-permute-start.2 = (bf16[320,512]{1,0:T(8,128)(2,1)S(1)}, bf16[320,512]{1,0:T(8,128)(2,1)S(1)}, u32[]{:S(2)}, u32[]{:S(2)}) collective-permute-start(bf16[320,512]{1,0:T(8,128)(2,1)S(1)} %get-tuple-element.44), channel_id=1, source_target_pairs={{0,3},{1,0},{2,1},{3,2},{4,7},{5,4},{6,5},{7,6},{8,11},{9,8},{10,9... | collective-permute-start | bytes 983048 | tf_op jit(solution)/shard_map/ppermute | solution.py:31
  22.8 29.1 %collective-permute-start.10 = (bf16[512,1280]{1,0:T(8,128)(2,1)S(1)}, bf16[512,1280]{1,0:T(8,128)(2,1)S(1)}, u32[]{:S(2)}, u32[]{:S(2)}) collective-permute-start(bf16[512,1280]{1,0:T(8,128)(2,1)S(1)} %constant_dynamic-update-slice_fusion.4.x0.refs_2_), channel_id=1, source_target_pairs={{0,12},{1,13},{2,14},{3,15},{4,0},{5,1},{6,2},{7,3},{8,4},{9,5},{1... | collective-permute-start | bytes 3932168 | tf_op jit(solution)/shard_map/ppermute | solution.py:31
  25.3 30.1 %collective-permute-start.11 = (bf16[512,1280]{1,0:T(8,128)(2,1)S(1)}, bf16[512,1280]{1,0:T(8,128)(2,1)S(1)}, u32[]{:S(2)}, u32[]{:S(2)}) collective-permute-start(bf16[512,1280]{1,0:T(8,128)(2,1)S(1)} %constant_dynamic-update-slice_fusion.4.x0.refs_2_), channel_id=1, source_target_pairs={{0,4},{1,5},{2,6},{3,7},{4,8},{5,9},{6,10},{7,11},{8,12},{9,13},{1... | collective-permute-start | bytes 3932168 | tf_op jit(solution)/shard_map/ppermute | solution.py:31
  26.5 29.2 %collective-permute-start.3 = (bf16[1280,512]{1,0:T(8,128)(2,1)S(1)}, bf16[1280,512]{1,0:T(8,128)(2,1)S(1)}, u32[]{:S(2)}, u32[]{:S(2)}) collective-permute-start(bf16[1280,512]{1,0:T(8,128)(2,1)S(1)} %constant_dynamic-update-slice_fusion.z0), channel_id=1, source_target_pairs={{0,96},{1,97},{2,98},{3,99},{4,100},{5,101},{6,102},{7,103},{8,104... | collective-permute-start | bytes 3932168 | tf_op jit(solution)/shard_map/ppermute | solution.py:31
  28.4 31.3 %collective-permute-start.5 = (bf16[1280,512]{1,0:T(8,128)(2,1)S(1)}, bf16[1280,512]{1,0:T(8,128)(2,1)S(1)}, u32[]{:S(2)}, u32[]{:S(2)}) collective-permute-start(bf16[1280,512]{1,0:T(8,128)(2,1)S(1)} %constant_dynamic-update-slice_fusion.z0), channel_id=1, source_target_pairs={{0,32},{1,33},{2,34},{3,35},{4,36},{5,37},{6,38},{7,39},{8,40},{9,... | collective-permute-start | bytes 3932168 | tf_op jit(solution)/shard_map/ppermute | solution.py:31
  51.9 15.0 %collective-permute-start.12 = (bf16[256,1280]{1,0:T(8,128)(2,1)S(1)}, bf16[256,1280]{1,0:T(8,128)(2,1)S(1)}, u32[]{:S(2)}, u32[]{:S(2)}) collective-permute-start(bf16[256,1280]{1,0:T(8,128)(2,1)S(1)} %slice.50), channel_id=1, source_target_pairs={{0,12},{1,13},{2,14},{3,15},{4,0},{5,1},{6,2},{7,3},{8,4},{9,5},{1... | collective-permute-start | bytes 1966088 | tf_op jit(solution)/shard_map/ppermute | solution.py:31
  55.4 14.8 %collective-permute-start.13 = (bf16[256,1280]{1,0:T(8,128)(2,1)S(1)}, bf16[256,1280]{1,0:T(8,128)(2,1)S(1)}, u32[]{:S(2)}, u32[]{:S(2)}) collective-permute-start(bf16[256,1280]{1,0:T(8,128)(2,1)S(1)} %slice.51), channel_id=1, source_target_pairs={{0,4},{1,5},{2,6},{3,7},{4,8},{5,9},{6,10},{7,11},{8,12},{9,13},{1... | collective-permute-start | bytes 1966088 | tf_op jit(solution)/shard_map/ppermute | solution.py:31
  55.8 16.5 %collective-permute-start.4 = (bf16[640,512]{1,0:T(8,128)(2,1)S(1)}, bf16[640,512]{1,0:T(8,128)(2,1)S(1)}, u32[]{:S(2)}, u32[]{:S(2)}) collective-permute-start(bf16[640,512]{1,0:T(8,128)(2,1)S(1)} %slice.48), channel_id=1, source_target_pairs={{0,96},{1,97},{2,98},{3,99},{4,100},{5,101},{6,102},{7,103},{8,104... | collective-permute-start | bytes 1966088 | tf_op jit(solution)/shard_map/ppermute | solution.py:31
  59.7 15.6 %collective-permute-start.6 = (bf16[640,512]{1,0:T(8,128)(2,1)S(1)}, bf16[640,512]{1,0:T(8,128)(2,1)S(1)}, u32[]{:S(2)}, u32[]{:S(2)}) collective-permute-start(bf16[640,512]{1,0:T(8,128)(2,1)S(1)} %slice.49), channel_id=1, source_target_pairs={{0,32},{1,33},{2,34},{3,35},{4,36},{5,37},{6,38},{7,39},{8,40},{9,... | collective-permute-start | bytes 1966088 | tf_op jit(solution)/shard_map/ppermute | solution.py:31
  70.2 5.1 %copy-start = (f32[640,320]{0,1:T(8,128)S(1)}, f32[640,320]{0,1:T(8,128)}, u32[]{:S(2)}) copy-start(f32[640,320]{0,1:T(8,128)} %param.10) | copy-start | bytes 2457604
  76.0 5.2 %collective-permute-start.16 = (f32[320,640]{1,0:T(8,128)S(1)}, f32[320,640]{1,0:T(8,128)S(1)}, u32[]{:S(2)}, u32[]{:S(2)}) collective-permute-start(f32[320,640]{1,0:T(8,128)S(1)} %get-tuple-element.67), channel_id=1, source_target_pairs={{0,16},{1,17},{2,18},{3,19},{4,20},{5,21},{6,22},{7,23},{8,24},{9,... | collective-permute-start | bytes 2457608 | tf_op jit(solution)/shard_map/ppermute | solution.py:31
  80.5 5.4 %collective-permute-start.19 = (f32[320,640]{1,0:T(8,128)S(1)}, f32[320,640]{1,0:T(8,128)S(1)}, u32[]{:S(2)}, u32[]{:S(2)}) collective-permute-start(f32[320,640]{1,0:T(8,128)S(1)} %get-tuple-element.69), channel_id=1, source_target_pairs={{0,16},{1,17},{2,18},{3,19},{4,20},{5,21},{6,22},{7,23},{8,24},{9,... | collective-permute-start | bytes 2457608 | tf_op jit(solution)/shard_map/ppermute | solution.py:31
  80.6 5.4 %collective-permute-start.15 = (f32[320,640]{1,0:T(8,128)S(1)}, f32[320,640]{1,0:T(8,128)S(1)}, u32[]{:S(2)}, u32[]{:S(2)}) collective-permute-start(f32[320,640]{1,0:T(8,128)S(1)} %get-tuple-element.65), channel_id=1, source_target_pairs={{0,16},{1,17},{2,18},{3,19},{4,20},{5,21},{6,22},{7,23},{8,24},{9,... | collective-permute-start | bytes 2457608 | tf_op jit(solution)/shard_map/ppermute | solution.py:31
  81.2 12.2 %collective-permute-start.20 = (f32[160,640]{1,0:T(8,128)S(1)}, f32[160,640]{1,0:T(8,128)S(1)}, u32[]{:S(2)}, u32[]{:S(2)}) collective-permute-start(f32[160,640]{1,0:T(8,128)S(1)} %get-tuple-element.78), channel_id=1, source_target_pairs={{0,1},{1,2},{2,3},{3,0},{4,5},{5,6},{6,7},{7,4},{8,9},{9,10},{10,1... | collective-permute-start | bytes 1228808 | tf_op jit(solution)/shard_map/ppermute | solution.py:31
  83.0 11.0 %collective-permute-start.17 = (f32[160,640]{1,0:T(8,128)S(1)}, f32[160,640]{1,0:T(8,128)S(1)}, u32[]{:S(2)}, u32[]{:S(2)}) collective-permute-start(f32[160,640]{1,0:T(8,128)S(1)} %get-tuple-element.79), channel_id=1, source_target_pairs={{0,3},{1,0},{2,1},{3,2},{4,7},{5,4},{6,5},{7,6},{8,11},{9,8},{10,9... | collective-permute-start | bytes 1228808 | tf_op jit(solution)/shard_map/ppermute | solution.py:31
  84.1 19.1 %collective-permute-start.22 = (f32[320,640]{1,0:T(8,128)S(1)}, f32[320,640]{1,0:T(8,128)S(1)}, u32[]{:S(2)}, u32[]{:S(2)}) collective-permute-start(f32[320,640]{1,0:T(8,128)S(1)} %get-tuple-element.70), channel_id=1, source_target_pairs={{0,96},{1,97},{2,98},{3,99},{4,100},{5,101},{6,102},{7,103},{8,104... | collective-permute-start | bytes 2457608 | tf_op jit(solution)/shard_map/ppermute | solution.py:31
  85.9 20.0 %collective-permute-start.23 = (f32[320,640]{1,0:T(8,128)S(1)}, f32[320,640]{1,0:T(8,128)S(1)}, u32[]{:S(2)}, u32[]{:S(2)}) collective-permute-start(f32[320,640]{1,0:T(8,128)S(1)} %get-tuple-element.70), channel_id=1, source_target_pairs={{0,32},{1,33},{2,34},{3,35},{4,36},{5,37},{6,38},{7,39},{8,40},{9,... | collective-permute-start | bytes 2457608 | tf_op jit(solution)/shard_map/ppermute | solution.py:31
  86.0 11.4 %collective-permute-start.14 = (f32[320,640]{1,0:T(8,128)S(1)}, f32[320,640]{1,0:T(8,128)S(1)}, u32[]{:S(2)}, u32[]{:S(2)}) collective-permute-start(f32[320,640]{1,0:T(8,128)S(1)} %get-tuple-element.63), channel_id=1, source_target_pairs={{0,16},{1,17},{2,18},{3,19},{4,20},{5,21},{6,22},{7,23},{8,24},{9,... | collective-permute-start | bytes 2457608 | tf_op jit(solution)/shard_map/ppermute | solution.py:31
  93.6 20.0 %collective-permute-start.21 = (f32[320,640]{1,0:T(8,128)S(1)}, f32[320,640]{1,0:T(8,128)S(1)}, u32[]{:S(2)}, u32[]{:S(2)}) collective-permute-start(f32[320,640]{1,0:T(8,128)S(1)} %pad_maximum_fusion.1), channel_id=1, source_target_pairs={{0,1},{1,2},{2,3},{3,0},{4,5},{5,6},{6,7},{7,4},{8,9},{9,10},{10,1... | collective-permute-start | bytes 2457608 | tf_op jit(solution)/shard_map/ppermute | solution.py:31
  94.1 19.6 %copy-start.1 = (f32[640,320]{0,1:T(8,128)S(1)}, f32[640,320]{0,1:T(8,128)}, u32[]{:S(2)}) copy-start(f32[640,320]{0,1:T(8,128)} %param.11) | copy-start | bytes 2457604
  94.1 19.6 %copy-start.2 = (f32[640,320]{0,1:T(8,128)S(1)}, f32[640,320]{0,1:T(8,128)}, u32[]{:S(2)}) copy-start(f32[640,320]{0,1:T(8,128)} %param.12) | copy-start | bytes 2457604
  94.2 19.5 %collective-permute-start.18 = (f32[320,640]{1,0:T(8,128)S(1)}, f32[320,640]{1,0:T(8,128)S(1)}, u32[]{:S(2)}, u32[]{:S(2)}) collective-permute-start(f32[320,640]{1,0:T(8,128)S(1)} %pad_maximum_fusion), channel_id=1, source_target_pairs={{0,3},{1,0},{2,1},{3,2},{4,7},{5,4},{6,5},{7,6},{8,11},{9,8},{10,9... | collective-permute-start | bytes 2457608 | tf_op jit(solution)/shard_map/ppermute | solution.py:31
  113.6 22.5 %copy-start.3 = (f32[8]{0:T(128)S(1)}, f32[8]{0:T(128)}, u32[]{:S(2)}) copy-start(f32[8]{0:T(128)} %param.15) | copy-start | bytes 100
  116.0 22.0 %collective-permute-start.34 = (f32[320,640]{1,0:T(8,128)S(1)}, f32[320,640]{1,0:T(8,128)}, u32[]{:S(2)}, u32[]{:S(2)}) collective-permute-start(f32[320,640]{1,0:T(8,128)S(1)} %get-tuple-element.72.update.u), channel_id=1, source_target_pairs={{0,96},{1,97},{2,98},{3,99},{4,100},{5,101},{6,102},{7,103},{8,104... | collective-permute-start | bytes 2457608 | tf_op jit(solution)/shard_map/ppermute | solution.py:31
  118.0 20.1 %collective-permute-start.35 = (f32[320,640]{1,0:T(8,128)S(1)}, f32[320,640]{1,0:T(8,128)}, u32[]{:S(2)}, u32[]{:S(2)}) collective-permute-start(f32[320,640]{1,0:T(8,128)S(1)} %get-tuple-element.72.update.u), channel_id=1, source_target_pairs={{0,32},{1,33},{2,34},{3,35},{4,36},{5,37},{6,38},{7,39},{8,40},{9,... | collective-permute-start | bytes 2457608 | tf_op jit(solution)/shard_map/ppermute | solution.py:31
  118.0 3.0 %collective-permute-start.24 = (f32[16,128]{1,0:T(8,128)S(1)}, f32[16,128]{1,0:T(8,128)S(1)}, u32[]{:S(2)}, u32[]{:S(2)}) collective-permute-start(f32[16,128]{1,0:T(8,128)S(1)} %get-tuple-element.71), channel_id=1, source_target_pairs={{0,16},{1,17},{2,18},{3,19},{4,20},{5,21},{6,22},{7,23},{8,24},{9,... | collective-permute-start | bytes 24584 | tf_op jit(solution)/shard_map/ppermute | solution.py:31
  121.0 4.7 %collective-permute-start.25 = (f32[16,128]{1,0:T(8,128)S(1)}, f32[16,128]{1,0:T(8,128)S(1)}, u32[]{:S(2)}, u32[]{:S(2)}) collective-permute-start(f32[16,128]{1,0:T(8,128)S(1)} %add.54), channel_id=1, source_target_pairs={{0,8},{1,9},{2,10},{3,11},{4,12},{5,13},{6,14},{7,15},{8,0},{9,1},... | collective-permute-start | bytes 24584 | tf_op jit(solution)/shard_map/ppermute | solution.py:31
  123.0 4.1 %collective-permute-start.26 = (f32[16,128]{1,0:T(8,128)S(1)}, f32[16,128]{1,0:T(8,128)S(1)}, u32[]{:S(2)}, u32[]{:S(2)}) collective-permute-start(f32[16,128]{1,0:T(8,128)S(1)} %add.54), channel_id=1, source_target_pairs={{0,4},{1,5},{2,6},{3,7},{4,8},{5,9},{6,10},{7,11},{8,12},{9,13},{1... | collective-permute-start | bytes 24584 | tf_op jit(solution)/shard_map/ppermute | solution.py:31
  124.1 3.0 %collective-permute-start.27 = (f32[16,128]{1,0:T(8,128)S(1)}, f32[16,128]{1,0:T(8,128)S(1)}, u32[]{:S(2)}, u32[]{:S(2)}) collective-permute-start(f32[16,128]{1,0:T(8,128)S(1)} %add.54), channel_id=1, source_target_pairs={{0,12},{1,13},{2,14},{3,15},{4,0},{5,1},{6,2},{7,3},{8,4},{9,5},{1... | collective-permute-start | bytes 24584 | tf_op jit(solution)/shard_map/ppermute | solution.py:31
  127.1 4.8 %collective-permute-start.28 = (f32[16,128]{1,0:T(8,128)S(1)}, f32[16,128]{1,0:T(8,128)S(1)}, u32[]{:S(2)}, u32[]{:S(2)}) collective-permute-start(f32[16,128]{1,0:T(8,128)S(1)} %add_add_fusion.2), channel_id=1, source_target_pairs={{0,2},{1,3},{2,0},{3,1},{4,6},{5,7},{6,4},{7,5},{8,10},{9,11},{10,... | collective-permute-start | bytes 24584 | tf_op jit(solution)/shard_map/ppermute | solution.py:31
  128.6 4.1 %collective-permute-start.29 = (f32[16,128]{1,0:T(8,128)S(1)}, f32[16,128]{1,0:T(8,128)S(1)}, u32[]{:S(2)}, u32[]{:S(2)}) collective-permute-start(f32[16,128]{1,0:T(8,128)S(1)} %add_add_fusion.2), channel_id=1, source_target_pairs={{0,1},{1,2},{2,3},{3,0},{4,5},{5,6},{6,7},{7,4},{8,9},{9,10},{10,1... | collective-permute-start | bytes 24584 | tf_op jit(solution)/shard_map/ppermute | solution.py:31
  130.5 2.9 %collective-permute-start.30 = (f32[16,128]{1,0:T(8,128)S(1)}, f32[16,128]{1,0:T(8,128)S(1)}, u32[]{:S(2)}, u32[]{:S(2)}) collective-permute-start(f32[16,128]{1,0:T(8,128)S(1)} %add_add_fusion.2), channel_id=1, source_target_pairs={{0,3},{1,0},{2,1},{3,2},{4,7},{5,4},{6,5},{7,6},{8,11},{9,8},{10,9... | collective-permute-start | bytes 24584 | tf_op jit(solution)/shard_map/ppermute | solution.py:31
  133.4 4.2 %collective-permute-start.31 = (f32[16,128]{1,0:T(8,128)S(1)}, f32[16,128]{1,0:T(8,128)S(1)}, u32[]{:S(2)}, u32[]{:S(2)}) collective-permute-start(f32[16,128]{1,0:T(8,128)S(1)} %add_add_fusion.1), channel_id=1, source_target_pairs={{0,64},{1,65},{2,66},{3,67},{4,68},{5,69},{6,70},{7,71},{8,72},{9,... | collective-permute-start | bytes 24584 | tf_op jit(solution)/shard_map/ppermute | solution.py:31
  133.4 4.3 %collective-permute-start.32 = (f32[16,128]{1,0:T(8,128)S(1)}, f32[16,128]{1,0:T(8,128)S(1)}, u32[]{:S(2)}, u32[]{:S(2)}) collective-permute-start(f32[16,128]{1,0:T(8,128)S(1)} %add_add_fusion.1), channel_id=1, source_target_pairs={{0,32},{1,33},{2,34},{3,35},{4,36},{5,37},{6,38},{7,39},{8,40},{9,... | collective-permute-start | bytes 24584 | tf_op jit(solution)/shard_map/ppermute | solution.py:31
  135.1 2.9 %collective-permute-start.33 = (f32[16,128]{1,0:T(8,128)S(1)}, f32[16,128]{1,0:T(8,128)S(1)}, u32[]{:S(2)}, u32[]{:S(2)}) collective-permute-start(f32[16,128]{1,0:T(8,128)S(1)} %add_add_fusion.1), channel_id=1, source_target_pairs={{0,96},{1,97},{2,98},{3,99},{4,100},{5,101},{6,102},{7,103},{8,104... | collective-permute-start | bytes 24584 | tf_op jit(solution)/shard_map/ppermute | solution.py:31
  138.3 9.4 %collective-permute-start.36 = (bf16[320,640]{1,0:T(8,128)(2,1)S(1)}, bf16[320,640]{1,0:T(8,128)(2,1)S(1)}, u32[]{:S(2)}, u32[]{:S(2)}) collective-permute-start(bf16[320,640]{1,0:T(8,128)(2,1)S(1)} %own_step.1.own.refs_0_), channel_id=1, source_target_pairs={{0,64},{1,65},{2,66},{3,67},{4,68},{5,69},{6,70},{7,71},{8,72},{9,... | collective-permute-start | bytes 1228808 | tf_op jit(solution)/shard_map/ppermute | solution.py:31
  142.2 9.9 %collective-permute-start.39 = (bf16[320,640]{1,0:T(8,128)(2,1)S(1)}, bf16[320,640]{1,0:T(8,128)(2,1)S(1)}, u32[]{:S(2)}, u32[]{:S(2)}) collective-permute-start(bf16[320,640]{1,0:T(8,128)(2,1)S(1)} %get-tuple-element.76.refs_2_), channel_id=1, source_target_pairs={{0,16},{1,17},{2,18},{3,19},{4,20},{5,21},{6,22},{7,23},{8,24},{9,... | collective-permute-start | bytes 1228808 | tf_op jit(solution)/shard_map/ppermute | solution.py:31
  147.1 4.9 %collective-permute-start.40 = (bf16[320,640]{1,0:T(8,128)(2,1)S(1)}, bf16[320,640]{1,0:T(8,128)(2,1)S(1)}, u32[]{:S(2)}, u32[]{:S(2)}) collective-permute-start(bf16[320,640]{1,0:T(8,128)(2,1)S(1)} %get-tuple-element.77.refs_4_), channel_id=1, source_target_pairs={{0,16},{1,17},{2,18},{3,19},{4,20},{5,21},{6,22},{7,23},{8,24},{9,... | collective-permute-start | bytes 1228808 | tf_op jit(solution)/shard_map/ppermute | solution.py:31
  147.2 4.9 %collective-permute-start.38 = (bf16[320,640]{1,0:T(8,128)(2,1)S(1)}, bf16[320,640]{1,0:T(8,128)(2,1)S(1)}, u32[]{:S(2)}, u32[]{:S(2)}) collective-permute-start(bf16[320,640]{1,0:T(8,128)(2,1)S(1)} %own_step.1.own.refs_0_), channel_id=1, source_target_pairs={{0,16},{1,17},{2,18},{3,19},{4,20},{5,21},{6,22},{7,23},{8,24},{9,... | collective-permute-start | bytes 1228808 | tf_op jit(solution)/shard_map/ppermute | solution.py:31
  147.7 6.0 %collective-permute-start.37 = (bf16[320,640]{1,0:T(8,128)(2,1)S(1)}, bf16[320,640]{1,0:T(8,128)(2,1)S(1)}, u32[]{:S(2)}, u32[]{:S(2)}) collective-permute-start(bf16[320,640]{1,0:T(8,128)(2,1)S(1)} %collective-permute-done.36.refs_0_), channel_id=1, source_target_pairs={{0,16},{1,17},{2,18},{3,19},{4,20},{5,21},{6,22},{7,23},{8,24},{9,... | collective-permute-start | bytes 1228808 | tf_op jit(solution)/shard_map/ppermute | solution.py:31

commit v8 on v7

--- a/solution.py
+++ b/solution.py
@@ -221,7 +221,7 @@
     return [terms[0][0], own, moved(down, dy=-1), moved(up, dy=1)], near
 
 
-STRIP = 32
+STRIP = 80
 
 
 def update_kernel(*refs):

time: 155 us -> 155 us (level)
  no operation moved by 1% of the time
where the time goes in v8:
time: 155 us
  waiting for transfers between devices  67.3 us (43%)
  starting transfers between devices  64.2 us (41%)
  Pallas kernels  18.2 us (12%)
  between operations  3.22 us (2%)
    ppermute x41, waiting for transfers between devices, moved(): return lax.ppermute(array, ('dp', 'mp'), pairs)  67.3 us
    ppermute x41, starting transfers between devices, moved(): return lax.ppermute(array, ('dp', 'mp'), pairs)  64.2 us
    pallas_call x1, Pallas kernels, near_product(): pl.pallas_call(near_kernel, out_shape=[jax.ShapeDtypeStruct((COLS, GROUP)...  4.39 us
  transfers between devices with their start and end apart: 41, of which 19 were waited for; matrix products, arithmetic and copies ran while one was open for 1% of the time, Pallas kernels for 8%

profile of v8, /device:TPU:1, one launch (start us, length us, event | category | flops | bytes accessed | tf_op | source)
XLA Modules:
  0.0 154.6 jit_solution(17792534140265498903)
XLA Ops:
  0.6 2.1 %prepare.1 = (bf16[128,1280]{1,0:T(8,128)(2,1)S(1)}, bf16[128,1280]{1,0:T(8,128)(2,1)S(1)}, bf16[128,1280]{1,0:T(8,128)(2,1)S(1)}, bf16[128,1280]{1,0:T(8,128)(2...) custom-call(bf16[128,5120]{1,0:T(8,128)(2,1)} %act.1, ...), custom_call_target="tpu_custom_call" | custom-call | tf_op jit(solution)/shard_map/prepare/pallas_call | solution.py:77
  2.7 2.5 %collective-permute-start.7 = (bf16[128,1280]{1,0:T(8,128)(2,1)S(1)}, bf16[128,1280]{1,0:T(8,128)(2,1)S(1)}, u32[]{:S(2)}, u32[]{:S(2)}) collective-permute-start(bf16[128,1280]{1,0:T(8,128)(2,1)S(1)} %get-tuple-element.50), channel_id=1, source_target_pairs={{0,32},{1,33},{2,34},{3,35},{4,36},{5,37},{6,38},{7,39},{8,40},{9,... | collective-permute-start | bytes 983048 | tf_op jit(solution)/shard_map/ppermute | solution.py:31
  5.3 3.3 %collective-permute-start.8 = (bf16[128,1280]{1,0:T(8,128)(2,1)S(1)}, bf16[128,1280]{1,0:T(8,128)(2,1)S(1)}, u32[]{:S(2)}, u32[]{:S(2)}) collective-permute-start(bf16[128,1280]{1,0:T(8,128)(2,1)S(1)} %get-tuple-element.51), channel_id=1, source_target_pairs={{0,64},{1,65},{2,66},{3,67},{4,68},{5,69},{6,70},{7,71},{8,72},{9,... | collective-permute-start | bytes 983048 | tf_op jit(solution)/shard_map/ppermute | solution.py:31
  9.3 1.3 collective-permute-start
  10.6 2.6 %collective-permute-start.1 = (bf16[320,512]{1,0:T(8,128)(2,1)S(1)}, bf16[320,512]{1,0:T(8,128)(2,1)S(1)}, u32[]{:S(2)}, u32[]{:S(2)}) collective-permute-start(bf16[320,512]{1,0:T(8,128)(2,1)S(1)} %get-tuple-element.43), channel_id=1, source_target_pairs={{0,2},{1,3},{2,0},{3,1},{4,6},{5,7},{6,4},{7,5},{8,10},{9,11},{10,... | collective-permute-start | bytes 983048 | tf_op jit(solution)/shard_map/ppermute | solution.py:31
  13.3 1.6 %collective-permute-done.7 = bf16[128,1280]{1,0:T(8,128)(2,1)S(1)} collective-permute-done((bf16[128,1280]{1,0:T(8,128)(2,1)S(1)}, bf16[128,1280]{1,0:T(8,128)(2,1)S(1)}, u32[]{:S(2)}, u32[]{:S(2)}) %collective-permute-start.7) | collective-permute-done | bytes 327712 | tf_op jit(solution)/shard_map/ppermute | solution.py:31
  14.8 2.7 %collective-permute-start.2 = (bf16[320,512]{1,0:T(8,128)(2,1)S(1)}, bf16[320,512]{1,0:T(8,128)(2,1)S(1)}, u32[]{:S(2)}, u32[]{:S(2)}) collective-permute-start(bf16[320,512]{1,0:T(8,128)(2,1)S(1)} %get-tuple-element.44), channel_id=1, source_target_pairs={{0,3},{1,0},{2,1},{3,2},{4,7},{5,4},{6,5},{7,6},{8,11},{9,8},{10,9... | collective-permute-start | bytes 983048 | tf_op jit(solution)/shard_map/ppermute | solution.py:31
  17.6 5.1 %collective-permute-done.8 = bf16[128,1280]{1,0:T(8,128)(2,1)S(1)} collective-permute-done((bf16[128,1280]{1,0:T(8,128)(2,1)S(1)}, bf16[128,1280]{1,0:T(8,128)(2,1)S(1)}, u32[]{:S(2)}, u32[]{:S(2)}) %collective-permute-start.8) | collective-permute-done | bytes 327712 | tf_op jit(solution)/shard_map/ppermute | solution.py:31
  22.8 2.5 %collective-permute-start.10 = (bf16[512,1280]{1,0:T(8,128)(2,1)S(1)}, bf16[512,1280]{1,0:T(8,128)(2,1)S(1)}, u32[]{:S(2)}, u32[]{:S(2)}) collective-permute-start(bf16[512,1280]{1,0:T(8,128)(2,1)S(1)} %constant_dynamic-update-slice_fusion.4.x0.refs_2_), channel_id=1, source_target_pairs={{0,12},{1,13},{2,14},{3,15},{4,0},{5,1},{6,2},{7,3},{8,4},{9,5},{1... | collective-permute-start | bytes 3932168 | tf_op jit(solution)/shard_map/ppermute | solution.py:31
  25.3 1.1 collective-permute-done.1
  26.5 1.9 %collective-permute-start.3 = (bf16[1280,512]{1,0:T(8,128)(2,1)S(1)}, bf16[1280,512]{1,0:T(8,128)(2,1)S(1)}, u32[]{:S(2)}, u32[]{:S(2)}) collective-permute-start(bf16[1280,512]{1,0:T(8,128)(2,1)S(1)} %constant_dynamic-update-slice_fusion.z0), channel_id=1, source_target_pairs={{0,96},{1,97},{2,98},{3,99},{4,100},{5,101},{6,102},{7,103},{8,104... | collective-permute-start | bytes 3932168 | tf_op jit(solution)/shard_map/ppermute | solution.py:31
  28.4 23.4 %collective-permute-done.10.xp.refs_3_ = bf16[512,1280]{1,0:T(8,128)(2,1)S(1)} collective-permute-done((bf16[512,1280]{1,0:T(8,128)(2,1)S(1)}, bf16[512,1280]{1,0:T(8,128)(2,1)S(1)}, u32[]{:S(2)}, u32[]{:S(2)}) %collective-permute-start.10) | collective-permute-done | bytes 1310752 | tf_op jit(solution)/shard_map/ppermute | solution.py:31
  51.9 3.5 %collective-permute-start.12 = (bf16[256,1280]{1,0:T(8,128)(2,1)S(1)}, bf16[256,1280]{1,0:T(8,128)(2,1)S(1)}, u32[]{:S(2)}, u32[]{:S(2)}) collective-permute-start(bf16[256,1280]{1,0:T(8,128)(2,1)S(1)} %slice.50), channel_id=1, source_target_pairs={{0,12},{1,13},{2,14},{3,15},{4,0},{5,1},{6,2},{7,3},{8,4},{9,5},{1... | collective-permute-start | bytes 1966088 | tf_op jit(solution)/shard_map/ppermute | solution.py:31
  55.8 3.9 %collective-permute-start.4 = (bf16[640,512]{1,0:T(8,128)(2,1)S(1)}, bf16[640,512]{1,0:T(8,128)(2,1)S(1)}, u32[]{:S(2)}, u32[]{:S(2)}) collective-permute-start(bf16[640,512]{1,0:T(8,128)(2,1)S(1)} %slice.48), channel_id=1, source_target_pairs={{0,96},{1,97},{2,98},{3,99},{4,100},{5,101},{6,102},{7,103},{8,104... | collective-permute-start | bytes 1966088 | tf_op jit(solution)/shard_map/ppermute | solution.py:31
  59.8 4.4 %near_product.1 = (f32[320,1280]{1,0:T(8,128)S(1)}, f32[320,1280]{1,0:T(8,128)S(1)}, f32[320,1280]{1,0:T(8,128)S(1)}, f32[320,1280]{1,0:T(8,128)S(1)}) custom-call(bf16[1280,512]{1,0:T(8,128)(2,1)S(1)} %constant_dynamic-update-slice_fusion.z0, bf16[1280,512]{1,0:T(8,128)(2,1)S(1)} %collective-permute-done.3.zp, ...), custom_call_target="tpu_custom_call" | custom-call | tf_op jit(solution)/shard_map/near_product/pallas_call | solution.py:126
  64.2 2.7 %collective-permute-done.12.xd0.refs_5_ = bf16[256,1280]{1,0:T(8,128)(2,1)S(1)} collective-permute-done((bf16[256,1280]{1,0:T(8,128)(2,1)S(1)}, bf16[256,1280]{1,0:T(8,128)(2,1)S(1)}, u32[]{:S(2)}, u32[]{:S(2)}) %collective-permute-start.12) | collective-permute-done | bytes 655392 | tf_op jit(solution)/shard_map/ppermute | solution.py:31
  66.9 3.3 %collective-permute-done.13.xd1.refs_6_ = bf16[256,1280]{1,0:T(8,128)(2,1)S(1)} collective-permute-done((bf16[256,1280]{1,0:T(8,128)(2,1)S(1)}, bf16[256,1280]{1,0:T(8,128)(2,1)S(1)}, u32[]{:S(2)}, u32[]{:S(2)}) %collective-permute-start.13) | collective-permute-done | bytes 655392 | tf_op jit(solution)/shard_map/ppermute | solution.py:31
  70.2 2.1 %middle_product.1 = (f32[320,1280]{1,0:T(8,128)S(1)}, f32[320,1280]{1,0:T(8,128)S(1)}, f32[320,1280]{1,0:T(8,128)S(1)}, f32[320,1280]{1,0:T(8,128)S(1)}) custom-call(bf16[1280,512]{1,0:T(8,128)(2,1)S(1)} %constant_dynamic-update-slice_fusion.z0, ...), custom_call_target="tpu_custom_call", output_to_operand_aliasing={{0}: (8, {}), {1}: (9, {}), {2}: (10, {}), {3}: (11, {})} | custom-call | tf_op jit(solution)/shard_map/middle_product/pallas_call | solution.py:146
  72.3 3.0 %collective-permute-done.6.refs_1_ = bf16[640,512]{1,0:T(8,128)(2,1)S(1)} collective-permute-done((bf16[640,512]{1,0:T(8,128)(2,1)S(1)}, bf16[640,512]{1,0:T(8,128)(2,1)S(1)}, u32[]{:S(2)}, u32[]{:S(2)}) %collective-permute-start.6) | collective-permute-done | bytes 655392 | tf_op jit(solution)/shard_map/ppermute | solution.py:31
  76.0 3.1 %collective-permute-start.16 = (f32[320,640]{1,0:T(8,128)S(1)}, f32[320,640]{1,0:T(8,128)S(1)}, u32[]{:S(2)}, u32[]{:S(2)}) collective-permute-start(f32[320,640]{1,0:T(8,128)S(1)} %get-tuple-element.67), channel_id=1, source_target_pairs={{0,16},{1,17},{2,18},{3,19},{4,20},{5,21},{6,22},{7,23},{8,24},{9,... | collective-permute-start | bytes 2457608 | tf_op jit(solution)/shard_map/ppermute | solution.py:31
  79.0 1.5 far_product.3
  81.2 1.7 %collective-permute-start.20 = (f32[160,640]{1,0:T(8,128)S(1)}, f32[160,640]{1,0:T(8,128)S(1)}, u32[]{:S(2)}, u32[]{:S(2)}) collective-permute-start(f32[160,640]{1,0:T(8,128)S(1)} %get-tuple-element.78), channel_id=1, source_target_pairs={{0,1},{1,2},{2,3},{3,0},{4,5},{5,6},{6,7},{7,4},{8,9},{9,10},{10,1... | collective-permute-start | bytes 1228808 | tf_op jit(solution)/shard_map/ppermute | solution.py:31
  83.0 1.1 collective-permute-start.17
  84.1 1.8 %collective-permute-start.22 = (f32[320,640]{1,0:T(8,128)S(1)}, f32[320,640]{1,0:T(8,128)S(1)}, u32[]{:S(2)}, u32[]{:S(2)}) collective-permute-start(f32[320,640]{1,0:T(8,128)S(1)} %get-tuple-element.70), channel_id=1, source_target_pairs={{0,96},{1,97},{2,98},{3,99},{4,100},{5,101},{6,102},{7,103},{8,104... | collective-permute-start | bytes 2457608 | tf_op jit(solution)/shard_map/ppermute | solution.py:31
  86.0 1.0 collective-permute-start.14
  87.2 6.3 %collective-permute-done.20 = f32[160,640]{1,0:T(8,128)S(1)} collective-permute-done((f32[160,640]{1,0:T(8,128)S(1)}, f32[160,640]{1,0:T(8,128)S(1)}, u32[]{:S(2)}, u32[]{:S(2)}) %collective-permute-start.20) | collective-permute-done | bytes 409632 | tf_op jit(solution)/shard_map/ppermute | solution.py:31
  94.2 2.4 %collective-permute-start.18 = (f32[320,640]{1,0:T(8,128)S(1)}, f32[320,640]{1,0:T(8,128)S(1)}, u32[]{:S(2)}, u32[]{:S(2)}) collective-permute-start(f32[320,640]{1,0:T(8,128)S(1)} %pad_maximum_fusion), channel_id=1, source_target_pairs={{0,3},{1,0},{2,1},{3,2},{4,7},{5,4},{6,5},{7,6},{8,11},{9,8},{10,9... | collective-permute-start | bytes 2457608 | tf_op jit(solution)/shard_map/ppermute | solution.py:31
  97.5 5.8 %collective-permute-done.22.refs_8_.wp = f32[320,640]{1,0:T(8,128)S(1)} collective-permute-done((f32[320,640]{1,0:T(8,128)S(1)}, f32[320,640]{1,0:T(8,128)S(1)}, u32[]{:S(2)}, u32[]{:S(2)}) %collective-permute-start.22) | collective-permute-done | bytes 819232 | tf_op jit(solution)/shard_map/ppermute | solution.py:31
  103.2 2.7 %collective-permute-done.23.refs_9_.wm = f32[320,640]{1,0:T(8,128)S(1)} collective-permute-done((f32[320,640]{1,0:T(8,128)S(1)}, f32[320,640]{1,0:T(8,128)S(1)}, u32[]{:S(2)}, u32[]{:S(2)}) %collective-permute-start.23) | collective-permute-done | bytes 819232 | tf_op jit(solution)/shard_map/ppermute | solution.py:31
  106.0 7.7 %collective-permute-done.21.refs_3_ = f32[320,640]{1,0:T(8,128)S(1)} collective-permute-done((f32[320,640]{1,0:T(8,128)S(1)}, f32[320,640]{1,0:T(8,128)S(1)}, u32[]{:S(2)}, u32[]{:S(2)}) %collective-permute-start.21) | collective-permute-done | bytes 819232 | tf_op jit(solution)/shard_map/ppermute | solution.py:31
  113.7 2.3 %update.1 = (f32[320,640]{1,0:T(8,128)}, f32[320,640]{1,0:T(8,128)}, f32[320,640]{1,0:T(8,128)S(1)}, f32[16,128]{1,0:T(8,128)S(1)}) custom-call(f32[320,640]{1,0:T(8,128)S(1)} %get-tuple-element.62.refs_0_, f32[320,640]{1,0:T(8,128)S(1)} %collective-permute-done.14.refs_1_, f32[320,640]{1,0:T(8,128)S(1)} %collective-permute-done.18.refs_2_, ...), custom_call_target="tpu_custom_call" | custom-call | tf_op jit(solution)/shard_map/update/pallas_call | solution.py:270
  115.9 1.9 %collective-permute-start.34 = (f32[320,640]{1,0:T(8,128)S(1)}, f32[320,640]{1,0:T(8,128)}, u32[]{:S(2)}, u32[]{:S(2)}) collective-permute-start(f32[320,640]{1,0:T(8,128)S(1)} %get-tuple-element.72.update.u), channel_id=1, source_target_pairs={{0,96},{1,97},{2,98},{3,99},{4,100},{5,101},{6,102},{7,103},{8,104... | collective-permute-start | bytes 2457608 | tf_op jit(solution)/shard_map/ppermute | solution.py:31
  117.8 2.2 %collective-permute-start.24 = (f32[16,128]{1,0:T(8,128)S(1)}, f32[16,128]{1,0:T(8,128)S(1)}, u32[]{:S(2)}, u32[]{:S(2)}) collective-permute-start(f32[16,128]{1,0:T(8,128)S(1)} %get-tuple-element.71), channel_id=1, source_target_pairs={{0,16},{1,17},{2,18},{3,19},{4,20},{5,21},{6,22},{7,23},{8,24},{9,... | collective-permute-start | bytes 24584 | tf_op jit(solution)/shard_map/ppermute | solution.py:31
  120.0 0.8 collective-permute-done.24
  120.9 2.0 %collective-permute-start.25 = (f32[16,128]{1,0:T(8,128)S(1)}, f32[16,128]{1,0:T(8,128)S(1)}, u32[]{:S(2)}, u32[]{:S(2)}) collective-permute-start(f32[16,128]{1,0:T(8,128)S(1)} %add.54), channel_id=1, source_target_pairs={{0,8},{1,9},{2,10},{3,11},{4,12},{5,13},{6,14},{7,15},{8,0},{9,1},... | collective-permute-start | bytes 24584 | tf_op jit(solution)/shard_map/ppermute | solution.py:31
  122.8 1.1 collective-permute-start.26
  124.0 1.5 collective-permute-start.27
  125.5 1.4 collective-permute-done.26
  127.0 1.5 collective-permute-start.28
  128.5 1.9 %collective-permute-start.29 = (f32[16,128]{1,0:T(8,128)S(1)}, f32[16,128]{1,0:T(8,128)S(1)}, u32[]{:S(2)}, u32[]{:S(2)}) collective-permute-start(f32[16,128]{1,0:T(8,128)S(1)} %add_add_fusion.2), channel_id=1, source_target_pairs={{0,1},{1,2},{2,3},{3,0},{4,5},{5,6},{6,7},{7,4},{8,9},{9,10},{10,1... | collective-permute-start | bytes 24584 | tf_op jit(solution)/shard_map/ppermute | solution.py:31
  133.3 1.7 %collective-permute-start.32 = (f32[16,128]{1,0:T(8,128)S(1)}, f32[16,128]{1,0:T(8,128)S(1)}, u32[]{:S(2)}, u32[]{:S(2)}) collective-permute-start(f32[16,128]{1,0:T(8,128)S(1)} %add_add_fusion.1), channel_id=1, source_target_pairs={{0,32},{1,33},{2,34},{3,35},{4,36},{5,37},{6,38},{7,39},{8,40},{9,... | collective-permute-start | bytes 24584 | tf_op jit(solution)/shard_map/ppermute | solution.py:31
  135.0 1.1 collective-permute-start.33
  138.1 1.3 collective-permute-start.36
  139.4 2.6 %near_step.1 = (f32[320,640]{1,0:T(8,128)}, bf16[320,640]{1,0:T(8,128)(2,1)S(1)}, bf16[320,640]{1,0:T(8,128)(2,1)S(1)}) custom-call(f32[16,128]{1,0:T(8,128)S(1)} %add_add_fusion.sums, f32[1]{0:T(128)} %bitcast.5.rate, f32[320,640]{1,0:T(8,128)S(1)} %bitcast.14, f32[320,640]{1,0:T(8,128)S(1)} %collective-permute-done.22.refs_8_.wp, ...), custom_call_target="tpu_custom_call" | custom-call | tf_op jit(solution)/shard_map/near_step/pallas_call | solution.py:334
  142.0 5.0 %collective-permute-start.39 = (bf16[320,640]{1,0:T(8,128)(2,1)S(1)}, bf16[320,640]{1,0:T(8,128)(2,1)S(1)}, u32[]{:S(2)}, u32[]{:S(2)}) collective-permute-start(bf16[320,640]{1,0:T(8,128)(2,1)S(1)} %get-tuple-element.76.refs_2_), channel_id=1, source_target_pairs={{0,16},{1,17},{2,18},{3,19},{4,20},{5,21},{6,22},{7,23},{8,24},{9,... | collective-permute-start | bytes 1228808 | tf_op jit(solution)/shard_map/ppermute | solution.py:31
  147.5 4.4 %collective-permute-start.37 = (bf16[320,640]{1,0:T(8,128)(2,1)S(1)}, bf16[320,640]{1,0:T(8,128)(2,1)S(1)}, u32[]{:S(2)}, u32[]{:S(2)}) collective-permute-start(bf16[320,640]{1,0:T(8,128)(2,1)S(1)} %collective-permute-done.36.refs_0_), channel_id=1, source_target_pairs={{0,16},{1,17},{2,18},{3,19},{4,20},{5,21},{6,22},{7,23},{8,24},{9,... | collective-permute-start | bytes 1228808 | tf_op jit(solution)/shard_map/ppermute | solution.py:31
  151.9 1.6 %placed.2.refs_2_ = bf16[320,5120]{1,0:T(8,128)(2,1)} custom-call(bf16[320,640]{1,0:T(8,128)(2,1)S(1)} %own_step.1.own.refs_0_, bf16[320,640]{1,0:T(8,128)(2,1)S(1)} %collective-permute-done.38.refs_1_, bf16[320,640]{1,0:T(8,128)(2,1)S(1)} %get-tuple-element.76.refs_2_, bf16[320,640]{1,0:T(8,128)(2,1)S(1)} %collective-permute-done.39.refs_3_, ...), custom_call_target="tpu_custom_call" | custom-call | tf_op jit(solution)/shard_map/placed/pallas_call | solution.py:361
  153.5 0.9 placed.3
  (78 shorter events, 7.9 us)
Async XLA Ops:
  2.7 12.1 %collective-permute-start.7 = (bf16[128,1280]{1,0:T(8,128)(2,1)S(1)}, bf16[128,1280]{1,0:T(8,128)(2,1)S(1)}, u32[]{:S(2)}, u32[]{:S(2)}) collective-permute-start(bf16[128,1280]{1,0:T(8,128)(2,1)S(1)} %get-tuple-element.50), channel_id=1, source_target_pairs={{0,32},{1,33},{2,34},{3,35},{4,36},{5,37},{6,38},{7,39},{8,40},{9,... | collective-permute-start | bytes 983048 | tf_op jit(solution)/shard_map/ppermute | solution.py:31
  5.3 17.4 %collective-permute-start.8 = (bf16[128,1280]{1,0:T(8,128)(2,1)S(1)}, bf16[128,1280]{1,0:T(8,128)(2,1)S(1)}, u32[]{:S(2)}, u32[]{:S(2)}) collective-permute-start(bf16[128,1280]{1,0:T(8,128)(2,1)S(1)} %get-tuple-element.51), channel_id=1, source_target_pairs={{0,64},{1,65},{2,66},{3,67},{4,68},{5,69},{6,70},{7,71},{8,72},{9,... | collective-permute-start | bytes 983048 | tf_op jit(solution)/shard_map/ppermute | solution.py:31
  8.6 14.2 %collective-permute-start.9 = (bf16[128,1280]{1,0:T(8,128)(2,1)S(1)}, bf16[128,1280]{1,0:T(8,128)(2,1)S(1)}, u32[]{:S(2)}, u32[]{:S(2)}) collective-permute-start(bf16[128,1280]{1,0:T(8,128)(2,1)S(1)} %get-tuple-element.52), channel_id=1, source_target_pairs={{0,96},{1,97},{2,98},{3,99},{4,100},{5,101},{6,102},{7,103},{8,104... | collective-permute-start | bytes 983048 | tf_op jit(solution)/shard_map/ppermute | solution.py:31
  9.3 16.0 %collective-permute-start = (bf16[320,512]{1,0:T(8,128)(2,1)S(1)}, bf16[320,512]{1,0:T(8,128)(2,1)S(1)}, u32[]{:S(2)}, u32[]{:S(2)}) collective-permute-start(bf16[320,512]{1,0:T(8,128)(2,1)S(1)} %get-tuple-element.42), channel_id=1, source_target_pairs={{0,1},{1,2},{2,3},{3,0},{4,5},{5,6},{6,7},{7,4},{8,9},{9,10},{10,1... | collective-permute-start | bytes 983048 | tf_op jit(solution)/shard_map/ppermute | solution.py:31
  10.6 15.9 %collective-permute-start.1 = (bf16[320,512]{1,0:T(8,128)(2,1)S(1)}, bf16[320,512]{1,0:T(8,128)(2,1)S(1)}, u32[]{:S(2)}, u32[]{:S(2)}) collective-permute-start(bf16[320,512]{1,0:T(8,128)(2,1)S(1)} %get-tuple-element.43), channel_id=1, source_target_pairs={{0,2},{1,3},{2,0},{3,1},{4,6},{5,7},{6,4},{7,5},{8,10},{9,11},{10,... | collective-permute-start | bytes 983048 | tf_op jit(solution)/shard_map/ppermute | solution.py:31
  14.8 11.7 %collective-permute-start.2 = (bf16[320,512]{1,0:T(8,128)(2,1)S(1)}, bf16[320,512]{1,0:T(8,128)(2,1)S(1)}, u32[]{:S(2)}, u32[]{:S(2)}) collective-permute-start(bf16[320,512]{1,0:T(8,128)(2,1)S(1)} %get-tuple-element.44), channel_id=1, source_target_pairs={{0,3},{1,0},{2,1},{3,2},{4,7},{5,4},{6,5},{7,6},{8,11},{9,8},{10,9... | collective-permute-start | bytes 983048 | tf_op jit(solution)/shard_map/ppermute | solution.py:31
  22.8 29.1 %collective-permute-start.10 = (bf16[512,1280]{1,0:T(8,128)(2,1)S(1)}, bf16[512,1280]{1,0:T(8,128)(2,1)S(1)}, u32[]{:S(2)}, u32[]{:S(2)}) collective-permute-start(bf16[512,1280]{1,0:T(8,128)(2,1)S(1)} %constant_dynamic-update-slice_fusion.4.x0.refs_2_), channel_id=1, source_target_pairs={{0,12},{1,13},{2,14},{3,15},{4,0},{5,1},{6,2},{7,3},{8,4},{9,5},{1... | collective-permute-start | bytes 3932168 | tf_op jit(solution)/shard_map/ppermute | solution.py:31
  25.3 30.1 %collective-permute-start.11 = (bf16[512,1280]{1,0:T(8,128)(2,1)S(1)}, bf16[512,1280]{1,0:T(8,128)(2,1)S(1)}, u32[]{:S(2)}, u32[]{:S(2)}) collective-permute-start(bf16[512,1280]{1,0:T(8,128)(2,1)S(1)} %constant_dynamic-update-slice_fusion.4.x0.refs_2_), channel_id=1, source_target_pairs={{0,4},{1,5},{2,6},{3,7},{4,8},{5,9},{6,10},{7,11},{8,12},{9,13},{1... | collective-permute-start | bytes 3932168 | tf_op jit(solution)/shard_map/ppermute | solution.py:31
  26.5 29.2 %collective-permute-start.3 = (bf16[1280,512]{1,0:T(8,128)(2,1)S(1)}, bf16[1280,512]{1,0:T(8,128)(2,1)S(1)}, u32[]{:S(2)}, u32[]{:S(2)}) collective-permute-start(bf16[1280,512]{1,0:T(8,128)(2,1)S(1)} %constant_dynamic-update-slice_fusion.z0), channel_id=1, source_target_pairs={{0,96},{1,97},{2,98},{3,99},{4,100},{5,101},{6,102},{7,103},{8,104... | collective-permute-start | bytes 3932168 | tf_op jit(solution)/shard_map/ppermute | solution.py:31
  28.4 31.3 %collective-permute-start.5 = (bf16[1280,512]{1,0:T(8,128)(2,1)S(1)}, bf16[1280,512]{1,0:T(8,128)(2,1)S(1)}, u32[]{:S(2)}, u32[]{:S(2)}) collective-permute-start(bf16[1280,512]{1,0:T(8,128)(2,1)S(1)} %constant_dynamic-update-slice_fusion.z0), channel_id=1, source_target_pairs={{0,32},{1,33},{2,34},{3,35},{4,36},{5,37},{6,38},{7,39},{8,40},{9,... | collective-permute-start | bytes 3932168 | tf_op jit(solution)/shard_map/ppermute | solution.py:31
  51.9 15.0 %collective-permute-start.12 = (bf16[256,1280]{1,0:T(8,128)(2,1)S(1)}, bf16[256,1280]{1,0:T(8,128)(2,1)S(1)}, u32[]{:S(2)}, u32[]{:S(2)}) collective-permute-start(bf16[256,1280]{1,0:T(8,128)(2,1)S(1)} %slice.50), channel_id=1, source_target_pairs={{0,12},{1,13},{2,14},{3,15},{4,0},{5,1},{6,2},{7,3},{8,4},{9,5},{1... | collective-permute-start | bytes 1966088 | tf_op jit(solution)/shard_map/ppermute | solution.py:31
  55.4 14.8 %collective-permute-start.13 = (bf16[256,1280]{1,0:T(8,128)(2,1)S(1)}, bf16[256,1280]{1,0:T(8,128)(2,1)S(1)}, u32[]{:S(2)}, u32[]{:S(2)}) collective-permute-start(bf16[256,1280]{1,0:T(8,128)(2,1)S(1)} %slice.51), channel_id=1, source_target_pairs={{0,4},{1,5},{2,6},{3,7},{4,8},{5,9},{6,10},{7,11},{8,12},{9,13},{1... | collective-permute-start | bytes 1966088 | tf_op jit(solution)/shard_map/ppermute | solution.py:31
  55.8 16.5 %collective-permute-start.4 = (bf16[640,512]{1,0:T(8,128)(2,1)S(1)}, bf16[640,512]{1,0:T(8,128)(2,1)S(1)}, u32[]{:S(2)}, u32[]{:S(2)}) collective-permute-start(bf16[640,512]{1,0:T(8,128)(2,1)S(1)} %slice.48), channel_id=1, source_target_pairs={{0,96},{1,97},{2,98},{3,99},{4,100},{5,101},{6,102},{7,103},{8,104... | collective-permute-start | bytes 1966088 | tf_op jit(solution)/shard_map/ppermute | solution.py:31
  59.7 15.6 %collective-permute-start.6 = (bf16[640,512]{1,0:T(8,128)(2,1)S(1)}, bf16[640,512]{1,0:T(8,128)(2,1)S(1)}, u32[]{:S(2)}, u32[]{:S(2)}) collective-permute-start(bf16[640,512]{1,0:T(8,128)(2,1)S(1)} %slice.49), channel_id=1, source_target_pairs={{0,32},{1,33},{2,34},{3,35},{4,36},{5,37},{6,38},{7,39},{8,40},{9,... | collective-permute-start | bytes 1966088 | tf_op jit(solution)/shard_map/ppermute | solution.py:31
  70.2 5.1 %copy-start = (f32[640,320]{0,1:T(8,128)S(1)}, f32[640,320]{0,1:T(8,128)}, u32[]{:S(2)}) copy-start(f32[640,320]{0,1:T(8,128)} %param.10) | copy-start | bytes 2457604
  76.0 5.2 %collective-permute-start.16 = (f32[320,640]{1,0:T(8,128)S(1)}, f32[320,640]{1,0:T(8,128)S(1)}, u32[]{:S(2)}, u32[]{:S(2)}) collective-permute-start(f32[320,640]{1,0:T(8,128)S(1)} %get-tuple-element.67), channel_id=1, source_target_pairs={{0,16},{1,17},{2,18},{3,19},{4,20},{5,21},{6,22},{7,23},{8,24},{9,... | collective-permute-start | bytes 2457608 | tf_op jit(solution)/shard_map/ppermute | solution.py:31
  80.5 5.4 %collective-permute-start.19 = (f32[320,640]{1,0:T(8,128)S(1)}, f32[320,640]{1,0:T(8,128)S(1)}, u32[]{:S(2)}, u32[]{:S(2)}) collective-permute-start(f32[320,640]{1,0:T(8,128)S(1)} %get-tuple-element.69), channel_id=1, source_target_pairs={{0,16},{1,17},{2,18},{3,19},{4,20},{5,21},{6,22},{7,23},{8,24},{9,... | collective-permute-start | bytes 2457608 | tf_op jit(solution)/shard_map/ppermute | solution.py:31
  80.6 5.4 %collective-permute-start.15 = (f32[320,640]{1,0:T(8,128)S(1)}, f32[320,640]{1,0:T(8,128)S(1)}, u32[]{:S(2)}, u32[]{:S(2)}) collective-permute-start(f32[320,640]{1,0:T(8,128)S(1)} %get-tuple-element.65), channel_id=1, source_target_pairs={{0,16},{1,17},{2,18},{3,19},{4,20},{5,21},{6,22},{7,23},{8,24},{9,... | collective-permute-start | bytes 2457608 | tf_op jit(solution)/shard_map/ppermute | solution.py:31
  81.2 12.2 %collective-permute-start.20 = (f32[160,640]{1,0:T(8,128)S(1)}, f32[160,640]{1,0:T(8,128)S(1)}, u32[]{:S(2)}, u32[]{:S(2)}) collective-permute-start(f32[160,640]{1,0:T(8,128)S(1)} %get-tuple-element.78), channel_id=1, source_target_pairs={{0,1},{1,2},{2,3},{3,0},{4,5},{5,6},{6,7},{7,4},{8,9},{9,10},{10,1... | collective-permute-start | bytes 1228808 | tf_op jit(solution)/shard_map/ppermute | solution.py:31
  83.0 11.0 %collective-permute-start.17 = (f32[160,640]{1,0:T(8,128)S(1)}, f32[160,640]{1,0:T(8,128)S(1)}, u32[]{:S(2)}, u32[]{:S(2)}) collective-permute-start(f32[160,640]{1,0:T(8,128)S(1)} %get-tuple-element.79), channel_id=1, source_target_pairs={{0,3},{1,0},{2,1},{3,2},{4,7},{5,4},{6,5},{7,6},{8,11},{9,8},{10,9... | collective-permute-start | bytes 1228808 | tf_op jit(solution)/shard_map/ppermute | solution.py:31
  84.1 19.1 %collective-permute-start.22 = (f32[320,640]{1,0:T(8,128)S(1)}, f32[320,640]{1,0:T(8,128)S(1)}, u32[]{:S(2)}, u32[]{:S(2)}) collective-permute-start(f32[320,640]{1,0:T(8,128)S(1)} %get-tuple-element.70), channel_id=1, source_target_pairs={{0,96},{1,97},{2,98},{3,99},{4,100},{5,101},{6,102},{7,103},{8,104... | collective-permute-start | bytes 2457608 | tf_op jit(solution)/shard_map/ppermute | solution.py:31
  85.9 20.0 %collective-permute-start.23 = (f32[320,640]{1,0:T(8,128)S(1)}, f32[320,640]{1,0:T(8,128)S(1)}, u32[]{:S(2)}, u32[]{:S(2)}) collective-permute-start(f32[320,640]{1,0:T(8,128)S(1)} %get-tuple-element.70), channel_id=1, source_target_pairs={{0,32},{1,33},{2,34},{3,35},{4,36},{5,37},{6,38},{7,39},{8,40},{9,... | collective-permute-start | bytes 2457608 | tf_op jit(solution)/shard_map/ppermute | solution.py:31
  86.0 11.4 %collective-permute-start.14 = (f32[320,640]{1,0:T(8,128)S(1)}, f32[320,640]{1,0:T(8,128)S(1)}, u32[]{:S(2)}, u32[]{:S(2)}) collective-permute-start(f32[320,640]{1,0:T(8,128)S(1)} %get-tuple-element.63), channel_id=1, source_target_pairs={{0,16},{1,17},{2,18},{3,19},{4,20},{5,21},{6,22},{7,23},{8,24},{9,... | collective-permute-start | bytes 2457608 | tf_op jit(solution)/shard_map/ppermute | solution.py:31
  93.6 20.0 %collective-permute-start.21 = (f32[320,640]{1,0:T(8,128)S(1)}, f32[320,640]{1,0:T(8,128)S(1)}, u32[]{:S(2)}, u32[]{:S(2)}) collective-permute-start(f32[320,640]{1,0:T(8,128)S(1)} %pad_maximum_fusion.1), channel_id=1, source_target_pairs={{0,1},{1,2},{2,3},{3,0},{4,5},{5,6},{6,7},{7,4},{8,9},{9,10},{10,1... | collective-permute-start | bytes 2457608 | tf_op jit(solution)/shard_map/ppermute | solution.py:31
  94.1 19.6 %copy-start.1 = (f32[640,320]{0,1:T(8,128)S(1)}, f32[640,320]{0,1:T(8,128)}, u32[]{:S(2)}) copy-start(f32[640,320]{0,1:T(8,128)} %param.11) | copy-start | bytes 2457604
  94.1 19.6 %copy-start.2 = (f32[640,320]{0,1:T(8,128)S(1)}, f32[640,320]{0,1:T(8,128)}, u32[]{:S(2)}) copy-start(f32[640,320]{0,1:T(8,128)} %param.12) | copy-start | bytes 2457604
  94.2 19.5 %collective-permute-start.18 = (f32[320,640]{1,0:T(8,128)S(1)}, f32[320,640]{1,0:T(8,128)S(1)}, u32[]{:S(2)}, u32[]{:S(2)}) collective-permute-start(f32[320,640]{1,0:T(8,128)S(1)} %pad_maximum_fusion), channel_id=1, source_target_pairs={{0,3},{1,0},{2,1},{3,2},{4,7},{5,4},{6,5},{7,6},{8,11},{9,8},{10,9... | collective-permute-start | bytes 2457608 | tf_op jit(solution)/shard_map/ppermute | solution.py:31
  113.6 22.4 %copy-start.3 = (f32[8]{0:T(128)S(1)}, f32[8]{0:T(128)}, u32[]{:S(2)}) copy-start(f32[8]{0:T(128)} %param.15) | copy-start | bytes 100
  115.9 22.0 %collective-permute-start.34 = (f32[320,640]{1,0:T(8,128)S(1)}, f32[320,640]{1,0:T(8,128)}, u32[]{:S(2)}, u32[]{:S(2)}) collective-permute-start(f32[320,640]{1,0:T(8,128)S(1)} %get-tuple-element.72.update.u), channel_id=1, source_target_pairs={{0,96},{1,97},{2,98},{3,99},{4,100},{5,101},{6,102},{7,103},{8,104... | collective-permute-start | bytes 2457608 | tf_op jit(solution)/shard_map/ppermute | solution.py:31
  117.8 20.1 %collective-permute-start.35 = (f32[320,640]{1,0:T(8,128)S(1)}, f32[320,640]{1,0:T(8,128)}, u32[]{:S(2)}, u32[]{:S(2)}) collective-permute-start(f32[320,640]{1,0:T(8,128)S(1)} %get-tuple-element.72.update.u), channel_id=1, source_target_pairs={{0,32},{1,33},{2,34},{3,35},{4,36},{5,37},{6,38},{7,39},{8,40},{9,... | collective-permute-start | bytes 2457608 | tf_op jit(solution)/shard_map/ppermute | solution.py:31
  117.8 3.0 %collective-permute-start.24 = (f32[16,128]{1,0:T(8,128)S(1)}, f32[16,128]{1,0:T(8,128)S(1)}, u32[]{:S(2)}, u32[]{:S(2)}) collective-permute-start(f32[16,128]{1,0:T(8,128)S(1)} %get-tuple-element.71), channel_id=1, source_target_pairs={{0,16},{1,17},{2,18},{3,19},{4,20},{5,21},{6,22},{7,23},{8,24},{9,... | collective-permute-start | bytes 24584 | tf_op jit(solution)/shard_map/ppermute | solution.py:31
  120.9 4.7 %collective-permute-start.25 = (f32[16,128]{1,0:T(8,128)S(1)}, f32[16,128]{1,0:T(8,128)S(1)}, u32[]{:S(2)}, u32[]{:S(2)}) collective-permute-start(f32[16,128]{1,0:T(8,128)S(1)} %add.54), channel_id=1, source_target_pairs={{0,8},{1,9},{2,10},{3,11},{4,12},{5,13},{6,14},{7,15},{8,0},{9,1},... | collective-permute-start | bytes 24584 | tf_op jit(solution)/shard_map/ppermute | solution.py:31
  122.8 4.1 %collective-permute-start.26 = (f32[16,128]{1,0:T(8,128)S(1)}, f32[16,128]{1,0:T(8,128)S(1)}, u32[]{:S(2)}, u32[]{:S(2)}) collective-permute-start(f32[16,128]{1,0:T(8,128)S(1)} %add.54), channel_id=1, source_target_pairs={{0,4},{1,5},{2,6},{3,7},{4,8},{5,9},{6,10},{7,11},{8,12},{9,13},{1... | collective-permute-start | bytes 24584 | tf_op jit(solution)/shard_map/ppermute | solution.py:31
  124.0 3.0 %collective-permute-start.27 = (f32[16,128]{1,0:T(8,128)S(1)}, f32[16,128]{1,0:T(8,128)S(1)}, u32[]{:S(2)}, u32[]{:S(2)}) collective-permute-start(f32[16,128]{1,0:T(8,128)S(1)} %add.54), channel_id=1, source_target_pairs={{0,12},{1,13},{2,14},{3,15},{4,0},{5,1},{6,2},{7,3},{8,4},{9,5},{1... | collective-permute-start | bytes 24584 | tf_op jit(solution)/shard_map/ppermute | solution.py:31
  127.0 4.8 %collective-permute-start.28 = (f32[16,128]{1,0:T(8,128)S(1)}, f32[16,128]{1,0:T(8,128)S(1)}, u32[]{:S(2)}, u32[]{:S(2)}) collective-permute-start(f32[16,128]{1,0:T(8,128)S(1)} %add_add_fusion.2), channel_id=1, source_target_pairs={{0,2},{1,3},{2,0},{3,1},{4,6},{5,7},{6,4},{7,5},{8,10},{9,11},{10,... | collective-permute-start | bytes 24584 | tf_op jit(solution)/shard_map/ppermute | solution.py:31
  128.5 4.1 %collective-permute-start.29 = (f32[16,128]{1,0:T(8,128)S(1)}, f32[16,128]{1,0:T(8,128)S(1)}, u32[]{:S(2)}, u32[]{:S(2)}) collective-permute-start(f32[16,128]{1,0:T(8,128)S(1)} %add_add_fusion.2), channel_id=1, source_target_pairs={{0,1},{1,2},{2,3},{3,0},{4,5},{5,6},{6,7},{7,4},{8,9},{9,10},{10,1... | collective-permute-start | bytes 24584 | tf_op jit(solution)/shard_map/ppermute | solution.py:31
  130.4 2.9 %collective-permute-start.30 = (f32[16,128]{1,0:T(8,128)S(1)}, f32[16,128]{1,0:T(8,128)S(1)}, u32[]{:S(2)}, u32[]{:S(2)}) collective-permute-start(f32[16,128]{1,0:T(8,128)S(1)} %add_add_fusion.2), channel_id=1, source_target_pairs={{0,3},{1,0},{2,1},{3,2},{4,7},{5,4},{6,5},{7,6},{8,11},{9,8},{10,9... | collective-permute-start | bytes 24584 | tf_op jit(solution)/shard_map/ppermute | solution.py:31
  133.3 4.2 %collective-permute-start.31 = (f32[16,128]{1,0:T(8,128)S(1)}, f32[16,128]{1,0:T(8,128)S(1)}, u32[]{:S(2)}, u32[]{:S(2)}) collective-permute-start(f32[16,128]{1,0:T(8,128)S(1)} %add_add_fusion.1), channel_id=1, source_target_pairs={{0,64},{1,65},{2,66},{3,67},{4,68},{5,69},{6,70},{7,71},{8,72},{9,... | collective-permute-start | bytes 24584 | tf_op jit(solution)/shard_map/ppermute | solution.py:31
  133.3 4.3 %collective-permute-start.32 = (f32[16,128]{1,0:T(8,128)S(1)}, f32[16,128]{1,0:T(8,128)S(1)}, u32[]{:S(2)}, u32[]{:S(2)}) collective-permute-start(f32[16,128]{1,0:T(8,128)S(1)} %add_add_fusion.1), channel_id=1, source_target_pairs={{0,32},{1,33},{2,34},{3,35},{4,36},{5,37},{6,38},{7,39},{8,40},{9,... | collective-permute-start | bytes 24584 | tf_op jit(solution)/shard_map/ppermute | solution.py:31
  135.0 2.9 %collective-permute-start.33 = (f32[16,128]{1,0:T(8,128)S(1)}, f32[16,128]{1,0:T(8,128)S(1)}, u32[]{:S(2)}, u32[]{:S(2)}) collective-permute-start(f32[16,128]{1,0:T(8,128)S(1)} %add_add_fusion.1), channel_id=1, source_target_pairs={{0,96},{1,97},{2,98},{3,99},{4,100},{5,101},{6,102},{7,103},{8,104... | collective-permute-start | bytes 24584 | tf_op jit(solution)/shard_map/ppermute | solution.py:31
  138.1 9.4 %collective-permute-start.36 = (bf16[320,640]{1,0:T(8,128)(2,1)S(1)}, bf16[320,640]{1,0:T(8,128)(2,1)S(1)}, u32[]{:S(2)}, u32[]{:S(2)}) collective-permute-start(bf16[320,640]{1,0:T(8,128)(2,1)S(1)} %own_step.1.own.refs_0_), channel_id=1, source_target_pairs={{0,64},{1,65},{2,66},{3,67},{4,68},{5,69},{6,70},{7,71},{8,72},{9,... | collective-permute-start | bytes 1228808 | tf_op jit(solution)/shard_map/ppermute | solution.py:31
  142.0 9.9 %collective-permute-start.39 = (bf16[320,640]{1,0:T(8,128)(2,1)S(1)}, bf16[320,640]{1,0:T(8,128)(2,1)S(1)}, u32[]{:S(2)}, u32[]{:S(2)}) collective-permute-start(bf16[320,640]{1,0:T(8,128)(2,1)S(1)} %get-tuple-element.76.refs_2_), channel_id=1, source_target_pairs={{0,16},{1,17},{2,18},{3,19},{4,20},{5,21},{6,22},{7,23},{8,24},{9,... | collective-permute-start | bytes 1228808 | tf_op jit(solution)/shard_map/ppermute | solution.py:31
  147.0 4.9 %collective-permute-start.40 = (bf16[320,640]{1,0:T(8,128)(2,1)S(1)}, bf16[320,640]{1,0:T(8,128)(2,1)S(1)}, u32[]{:S(2)}, u32[]{:S(2)}) collective-permute-start(bf16[320,640]{1,0:T(8,128)(2,1)S(1)} %get-tuple-element.77.refs_4_), channel_id=1, source_target_pairs={{0,16},{1,17},{2,18},{3,19},{4,20},{5,21},{6,22},{7,23},{8,24},{9,... | collective-permute-start | bytes 1228808 | tf_op jit(solution)/shard_map/ppermute | solution.py:31
  147.0 4.9 %collective-permute-start.38 = (bf16[320,640]{1,0:T(8,128)(2,1)S(1)}, bf16[320,640]{1,0:T(8,128)(2,1)S(1)}, u32[]{:S(2)}, u32[]{:S(2)}) collective-permute-start(bf16[320,640]{1,0:T(8,128)(2,1)S(1)} %own_step.1.own.refs_0_), channel_id=1, source_target_pairs={{0,16},{1,17},{2,18},{3,19},{4,20},{5,21},{6,22},{7,23},{8,24},{9,... | collective-permute-start | bytes 1228808 | tf_op jit(solution)/shard_map/ppermute | solution.py:31
  147.5 6.0 %collective-permute-start.37 = (bf16[320,640]{1,0:T(8,128)(2,1)S(1)}, bf16[320,640]{1,0:T(8,128)(2,1)S(1)}, u32[]{:S(2)}, u32[]{:S(2)}) collective-permute-start(bf16[320,640]{1,0:T(8,128)(2,1)S(1)} %collective-permute-done.36.refs_0_), channel_id=1, source_target_pairs={{0,16},{1,17},{2,18},{3,19},{4,20},{5,21},{6,22},{7,23},{8,24},{9,... | collective-permute-start | bytes 1228808 | tf_op jit(solution)/shard_map/ppermute | solution.py:31
